TPU v7x, 32 devices: a whole 2x2x4 slice. The times are simulated.
32 devices in a mesh: dp: 16 (over z, y, x), inner: 2 (over core).
Axes of the slice: x: 2, y: 2, z: 4, core: 2. Of those that a mesh axis runs over, the one named last changes fastest.
Arguments:
- features: bfloat16 [8192, 2048], P(('dp', 'inner')), may hold values from -12 to 12
- kv_cotangent: bfloat16 [8192, 512], P(('dp', 'inner')), may hold values from -0.0625 to 0.0625
- owner_of_block: int32 [64], replicated, may hold values from 0 to 15, as said below
- first_moment: float32 [16, 4, 128, 128], P('dp'), may hold values from -1.25 to 1.25
- second_moment: float32 [16, 4, 128, 128], P('dp'), may hold values from 0.05 to 1
- left_stat: float32 [16, 4, 128, 128], P('dp')
- right_stat: float32 [16, 4, 128, 128], P('dp')
- left_basis: bfloat16 [16, 4, 128, 128], P('dp')
- right_basis: bfloat16 [16, 4, 128, 128], P('dp')
Outputs:
- update: bfloat16 [2048, 512], replicated
- new_left_basis: bfloat16 [16, 4, 128, 128], P('dp')
- new_right_basis: bfloat16 [16, 4, 128, 128], P('dp')
Inputs may be any that keep to these rules, and one draw needn't show every extreme that they name: `owner_of_block`: each index of dp owns at most 4 tiles, and one index owns exactly 4.
All inputs are finite; a program needn't handle non-finite values.
Results may differ from a plain program's by a relative error of at most 0.001.
Values may be sent and summed in bfloat16 or wider, within the bound.
No kernel may reach another device: no remote copies, remote signals or barrier semaphores. Data moves between devices by JAX's collectives and lax.ppermute only.
A program may use at most 64 MiB of HBM per device.

v0:
```python
import jax
import jax.numpy as jnp
from jax import lax
from jax.sharding import PartitionSpec as P

NS_STEPS = 12


highest = lax.Precision.HIGHEST


def rotate_in(basis_left, matrix, basis_right):
    half = jnp.einsum("sji,sjk->sik", basis_left, matrix, precision=highest)
    return jnp.einsum("sij,sjk->sik", half, basis_right, precision=highest)


def rotate_out(basis_left, matrix, basis_right):
    half = jnp.einsum("sij,sjk->sik", basis_left, matrix, precision=highest)
    return jnp.einsum("sij,skj->sik", half, basis_right, precision=highest)


def orthogonalize(stat, basis):
    power = jnp.einsum("sij,sjk->sik", stat, basis, precision=highest)
    scale = jnp.sqrt(jnp.sum(power * power, axis=(1, 2), keepdims=True) + 1e-06)
    iterate = power / scale
    for sweep in range(NS_STEPS):
        gram = jnp.einsum("sji,sjk->sik", iterate, iterate, precision=highest)
        iterate = 1.5 * iterate - 0.5 * jnp.einsum("sij,sjk->sik", iterate, gram, precision=highest)
    return iterate


def soap_tiles(grads, first, second, stat_left, stat_right, basis_left, basis_right):
    rotated = rotate_in(basis_left, grads, basis_right)
    moment = 0.95 * first + 0.05 * grads
    moment_rot = rotate_in(basis_left, moment, basis_right)
    second_new = 0.95 * second + 0.05 * rotated * rotated
    direction = rotate_out(basis_left, moment_rot / (jnp.sqrt(second_new) + 1e-08), basis_right)
    left_new = 0.95 * stat_left + 0.05 * jnp.einsum("sij,skj->sik", grads, grads, precision=highest)
    right_new = 0.95 * stat_right + 0.05 * jnp.einsum(
        "sji,sjk->sik", grads, grads, precision=highest
    )
    return (direction, orthogonalize(left_new, basis_left), orthogonalize(right_new, basis_right))


def per_device(
    features,
    kv_cotangent,
    owner_of_block,
    first_moment,
    second_moment,
    left_stat,
    right_stat,
    left_basis,
    right_basis,
):
    tile = left_basis.shape[-1]
    capacity = left_basis.shape[1]
    d_win = features.shape[1]
    width = kv_cotangent.shape[1]
    row_tiles = d_win // tile
    col_tiles = width // tile
    nblocks = owner_of_block.shape[0]
    owner_here = lax.axis_index("dp")
    block_ids = jnp.arange(nblocks, dtype=jnp.int32)
    same = owner_of_block[:, None] == owner_of_block[None, :]
    earlier = block_ids[None, :] < block_ids[:, None]
    slot = jnp.sum((same & earlier).astype(jnp.int32), axis=1)
    slot_ids = jnp.arange(capacity, dtype=jnp.int32)
    match = (owner_of_block[None, :] == owner_here) & (slot[None, :] == slot_ids[:, None])
    live = jnp.any(match, axis=1)
    which = jnp.sum(jnp.where(match, block_ids[None, :], 0), axis=1)
    row_start = which // col_tiles * tile
    col_start = which % col_tiles * tile
    partial_grad = lax.dot_general(
        features, kv_cotangent, (((0,), (0,)), ((), ())), preferred_element_type=jnp.float32
    )
    grad = lax.psum(partial_grad, ("dp", "inner"))
    fetched = [
        lax.dynamic_slice(grad, (row_start[slot_index], col_start[slot_index]), (tile, tile))
        for slot_index in range(capacity)
    ]
    grads = jnp.stack(fetched)
    basis_left = left_basis[0].astype(jnp.float32)
    basis_right = right_basis[0].astype(jnp.float32)
    direction, left_iter, right_iter = soap_tiles(
        grads,
        first_moment[0],
        second_moment[0],
        left_stat[0],
        right_stat[0],
        basis_left,
        basis_right,
    )
    direction_low = direction.astype(jnp.bfloat16)
    everyone = lax.all_gather(direction_low[None], "dp", axis=0, tiled=True)
    tiles = everyone[owner_of_block, slot]
    update = (
        tiles.reshape(row_tiles, col_tiles, tile, tile).transpose(0, 2, 1, 3).reshape(d_win, width)
    )
    keep = live[:, None, None]
    new_left = jnp.where(keep, left_iter.astype(jnp.bfloat16), left_basis[0])
    new_right = jnp.where(keep, right_iter.astype(jnp.bfloat16), right_basis[0])
    return (update, new_left[None], new_right[None])


def solution(mesh):
    return jax.shard_map(
        per_device,
        mesh=mesh,
        in_specs=(
            P(("dp", "inner"), None),
            P(("dp", "inner"), None),
            P(),
            P("dp", None, None, None),
            P("dp", None, None, None),
            P("dp", None, None, None),
            P("dp", None, None, None),
            P("dp", None, None, None),
            P("dp", None, None, None),
        ),
        out_specs=(P(), P("dp", None, None, None), P("dp", None, None, None)),
        check_vma=False,
    )
```

profile of v0, /device:TPU:0, one launch (start us, length us, event | category | flops | bytes accessed | tf_op | source)
XLA Modules:
  0.0 234.5 jit_solution(13853577143957279118)
XLA Ops:
  7.2 1.2 copy-done
  8.4 3.6 %fusion.71 = f32[2048,512]{1,0:T(8,128)} fusion(bf16[256,2048]{1,0:T(8,128)(2,1)S(1)} %copy-done, bf16[256,512]{1,0:T(8,128)(2,1)} %param.10), kind=kOutput, calls=%fused_computation.126 | convolution fusion | flops 536870912 | bytes 5505024 | tf_op jit(solution)/shard_map/dot_general | solution.py:74
  12.2 0.5 copy-done.7
  13.0 0.7 fusion.69
  28.8 129.2 %all-reduce.2.cloned.1.call-done = f32[2048,512]{1,0:T(8,128)} async-done(((f32[2048,512]{1,0:T(8,128)}), f32[2048,512]{1,0:T(8,128)}) %all-reduce.2.cloned.1.call-update) | async-done | bytes 4194320 | tf_op jit(solution)/shard_map/psum | solution.py:77
  158.0 1.2 dynamic-slice_bitcast_fusion.3
  160.8 1.0 convolution_convert_fusion
  161.9 0.7 fusion.25
  162.9 0.7 fusion.53
  163.6 0.4 fusion.24
  164.1 0.6 fusion.72
  164.7 0.4 fusion.23
  165.1 0.6 fusion.73
  165.7 0.4 fusion.22
  166.1 0.6 fusion.74
  166.7 0.4 fusion.21
  167.1 0.6 fusion.75
  168.1 0.6 fusion.76
  169.2 0.6 fusion.77
  170.2 0.6 fusion.78
  171.2 0.6 fusion.79
  172.2 0.6 fusion.80
  172.8 0.6 fusion.15
  173.4 0.6 fusion.81
  174.4 0.6 fusion.82
  175.0 0.6 fusion.12
  176.0 0.7 fusion.54
  176.7 0.4 fusion.11
  177.2 0.6 fusion.83
  178.2 0.6 fusion.84
  179.2 0.6 fusion.85
  179.8 0.4 fusion.8
  180.2 1.1 fusion.31
  181.3 0.6 fusion.86
  182.3 0.6 fusion.87
  182.9 0.4 fusion.6
  183.3 0.6 fusion.88
  183.9 0.4 fusion.5
  184.4 0.6 fusion.89
  185.4 0.6 fusion.90
  186.4 0.6 fusion.91
  187.4 0.8 fusion.92
  188.6 0.6 fusion.93
  189.2 1.1 fusion.29
  190.3 31.3 %all-gather.3.cloned.1.call-done = bf16[64,128,128]{2,1,0:T(8,128)(2,1)} async-done(((bf16[4,128,128]{2,1,0:T(8,128)(2,1)}), bf16[64,128,128]{2,1,0:T(8,128)(2,1)}) %all-gather.3.cloned.1.call-update) | async-done | bytes 2097168 | tf_op jit(solution)/shard_map/all_gather | solution.py:95
  221.6 2.5 %gather_fusion = bf16[64,128,128]{2,1,0:T(8,128)(2,1)S(1)} fusion(bf16[16,4,128,128]{3,2,1,0:T(8,128)(2,1)} %bitcast.173, s32[64]{0:T(128)S(1)} %fusion.65), kind=kCustom, calls=%fused_computation | custom fusion | bytes 4194816 | tf_op jit(solution)/shard_map/gather | solution.py:96
  224.2 1.8 copy.20
  226.0 1.7 copy.79
  (46 shorter events, 8.1 us)
Async XLA Ops:
  7.2 1.2 copy-start
  7.2 150.8 %all-reduce.2.cloned.1.call-start = ((), (), s32[]{:S(2)}) async-start(), calls=%async_computation | async-start | bytes 8388608 | tf_op jit(solution)/shard_map/psum | solution.py:77
  12.0 0.7 copy-start.7
  12.0 147.2 %copy-start.1 = (bf16[1,4,128,128]{3,2,1,0:T(8,128)(2,1)S(1)}, bf16[1,4,128,128]{3,2,1,0:T(8,128)(2,1)}, u32[]{:S(2)}) copy-start(bf16[1,4,128,128]{3,2,1,0:T(8,128)(2,1)} %param.16) | copy-start | bytes 393220
  12.0 147.5 %copy-start.3 = (f32[1,4,128,128]{3,2,1,0:T(8,128)S(1)}, f32[1,4,128,128]{3,2,1,0:T(8,128)}, u32[]{:S(2)}) copy-start(f32[1,4,128,128]{3,2,1,0:T(8,128)} %param.12) | copy-start | bytes 786436
  12.1 147.9 %copy-start.2 = (bf16[1,4,128,128]{3,2,1,0:T(8,128)(2,1)S(1)}, bf16[1,4,128,128]{3,2,1,0:T(8,128)(2,1)}, u32[]{:S(2)}) copy-start(bf16[1,4,128,128]{3,2,1,0:T(8,128)(2,1)} %param.17) | copy-start | bytes 393220
  12.1 148.1 %copy-start.6 = (f32[1,4,128,128]{3,2,1,0:T(8,128)S(1)}, f32[1,4,128,128]{3,2,1,0:T(8,128)}, u32[]{:S(2)}) copy-start(f32[1,4,128,128]{3,2,1,0:T(8,128)} %param.13) | copy-start | bytes 786436
  12.1 209.5 %all-gather.3.cloned.1.call-start = ((), (), s32[]{:S(2)}) async-start(), calls=%async_computation.1 | async-start | bytes 2228224 | tf_op jit(solution)/shard_map/all_gather | solution.py:95
  159.6 2.3 copy-start.4
  172.2 2.8 %copy-start.5 = (f32[1,4,128,128]{3,2,1,0:T(8,128)S(1)}, f32[1,4,128,128]{3,2,1,0:T(8,128)}, u32[]{:S(2)}) copy-start(f32[1,4,128,128]{3,2,1,0:T(8,128)} %param.15) | copy-start | bytes 786436
Sparse Core Ops, SparseCore 0:
  13.5 144.4 all-reduce.1
  162.0 59.5 all-gather.2
where the time goes:
time: 235 us; the launch traced here: 234 us
  waiting for transfers between devices  161 us (69%)
  matrix products  34.2 us (15%)
  between operations  29.5 us (13%)
  local copies, waits for them, and re-layouts  9.65 us (4%)
    psum x1, waiting for transfers between devices, per_device(): grad = lax.psum(partial_grad, ('dp', 'inner'))  129 us
    all_gather x1, waiting for transfers between devices, per_device(): everyone = lax.all_gather(direction_low[None], 'dp', axis=0, tiled=True)  31.3 us
    dot_general x24, matrix products, orthogonalize(): gram = jnp.einsum('sji,sjk->sik', iterate, iterate, precision=highest)  14.8 us
    dot_general x24, matrix products, orthogonalize(): jnp.einsum('sij,sjk->sik', iterate, gram, precision=highest)  11.3 us
  transfers between devices with their start and end apart: 2, of which 2 were waited for; matrix products, arithmetic and copies ran while one was open for 12% of the time, Pallas kernels for 0%

commit v1 on v0

--- a/solution.py
+++ b/solution.py
@@ -1,6 +1,10 @@
+import functools
+
 import jax
 import jax.numpy as jnp
 from jax import lax
+from jax.experimental import pallas as pl
+from jax.experimental.pallas import tpu as pltpu
 from jax.sharding import PartitionSpec as P
 
 NS_STEPS = 12
@@ -42,7 +46,7 @@
     return (direction, orthogonalize(left_new, basis_left), orthogonalize(right_new, basis_right))
 
 
-def per_device(
+def per_device_plain(
     features,
     kv_cotangent,
     owner_of_block,
@@ -103,7 +107,312 @@
     return (update, new_left[None], new_right[None])
 
 
+def swap_along(values, axis, size, bit):
+    return lax.ppermute(values, axis, [(i, i ^ bit) for i in range(size)])
+
+
+def product(left, right, dims):
+    return lax.dot_general(
+        left, right, (dims, ((), ())), precision=highest, preferred_element_type=jnp.float32
+    )
+
+
+MM = ((1,), (0,))
+MT = ((1,), (1,))
+TM = ((0,), (0,))
+
+
+def grad_kernel(col_tiles, near, order_ref, f_own, f_sib, kv_own, kv_sib, *outs):
+    tile = outs[0].shape[-1]
+    rows = f_own.shape[0]
+    kv_rows = outs[-1]
+    kv_rows[:, :rows] = kv_own[...].T
+    kv_rows[:, rows:] = kv_sib[...].T
+    half = outs[0].shape[0]
+    for part, out in enumerate(outs[:-1]):
+
+        def one(index, carry, part=part, out=out):
+            block = order_ref[part * half + index]
+            row = pl.multiple_of(block // col_tiles * tile, tile)
+            col = pl.multiple_of(block % col_tiles * tile, tile)
+            cots = kv_rows[pl.ds(col, tile), :]
+            total = jnp.dot(
+                cots[:, :rows], f_own[:, pl.ds(row, tile)], preferred_element_type=jnp.float32
+            )
+            total += jnp.dot(
+                cots[:, rows:], f_sib[:, pl.ds(row, tile)], preferred_element_type=jnp.float32
+            )
+            out[index] = total
+            return carry
+
+        lax.fori_loop(0, half, one, 0, unroll=4)
+
+
+def grad_parts(order, f_own, f_sib, kv_own, kv_sib, tile, col_tiles, owners):
+    shape = jax.ShapeDtypeStruct((owners // 2, tile, tile), jnp.float32)
+    vmem = pl.BlockSpec(memory_space=pltpu.VMEM)
+    rows, width = kv_own.shape
+    return pl.pallas_call(
+        functools.partial(grad_kernel, col_tiles, None),
+        out_shape=(shape,) * 4,
+        in_specs=[pl.BlockSpec(memory_space=pltpu.SMEM)] + [vmem] * 4,
+        out_specs=(vmem,) * 4,
+        scratch_shapes=[pltpu.VMEM((width, 2 * rows), jnp.bfloat16)],
+        compiler_params=pltpu.CompilerParams(vmem_limit_bytes=32 * 2**20),
+        name="grad_parts",
+    )(order, f_own, f_sib, kv_own, kv_sib)
+
+
+def direction_kernel(side_ref, a_ref, b_ref, m_ref, v_ref, ql_ref, qr_ref, dir_ref, grad_ref):
+    for k in range(2):
+        grad_t = a_ref[k] + b_ref[k]
+        grad = grad_t.T
+        grad_ref[k] = grad
+        left = ql_ref[0, k].astype(jnp.float32)
+        right = qr_ref[0, k].astype(jnp.float32)
+        rotated = product(product(left, grad, TM), right, MM)
+        moment = 0.95 * m_ref[0, k] + 0.05 * grad
+        moment_rot = product(product(left, moment, TM), right, MM)
+        second = 0.95 * v_ref[0, k] + 0.05 * rotated * rotated
+        scaled = moment_rot / (jnp.sqrt(second) + 1e-08)
+        out = product(product(left, scaled, MM), right, MT)
+        dir_ref[k] = out.astype(dir_ref.dtype)
+
+
+def slots_of(side, *arrays):
+    tile = arrays[0].shape[-1]
+    return [pl.BlockSpec((1, 2, tile, tile), lambda i, s: (0, s[0], 0, 0)) for _ in arrays]
+
+
+def whole(shape):
+    return pl.BlockSpec(shape, lambda i, s: (0,) * len(shape))
+
+
+def directions(side, kept, got, first, second, basis_left, basis_right):
+    tile = first.shape[-1]
+    pair = (2, tile, tile)
+    return pl.pallas_call(
+        direction_kernel,
+        out_shape=(
+            jax.ShapeDtypeStruct(pair, jnp.bfloat16),
+            jax.ShapeDtypeStruct(pair, jnp.float32),
+        ),
+        grid_spec=pltpu.PrefetchScalarGridSpec(
+            num_scalar_prefetch=1,
+            grid=(1,),
+            in_specs=[whole(pair), whole(pair)]
+            + slots_of(side, first, second, basis_left, basis_right),
+            out_specs=(whole(pair), whole(pair)),
+        ),
+        name="directions",
+    )(side, kept, got, first, second, basis_left, basis_right)
+
+
+def refresh_kernel(side_ref, g_ref, l_ref, r_ref, ql_ref, qr_ref, left_ref, right_ref):
+    iterates = []
+    for k in range(2):
+        grad = g_ref[k]
+        for stat, basis, dims in ((l_ref, ql_ref, MT), (r_ref, qr_ref, TM)):
+            new = 0.95 * stat[0, k] + 0.05 * product(grad, grad, dims)
+            power = product(new, basis[0, k].astype(jnp.float32), MM)
+            iterates.append(power / jnp.sqrt(jnp.sum(power * power) + 1e-06))
+
+    def sweep(step, values):
+        grams = [product(x, x, TM) for x in values]
+        return tuple(1.5 * x - 0.5 * product(x, g, MM) for x, g in zip(values, grams))
+
+    values = lax.fori_loop(0, NS_STEPS, sweep, tuple(iterates))
+    for k in range(2):
+        left_ref[k] = values[2 * k].astype(left_ref.dtype)
+        right_ref[k] = values[2 * k + 1].astype(right_ref.dtype)
+
+
+def refreshed(side, grads, stat_left, stat_right, basis_left, basis_right):
+    tile = stat_left.shape[-1]
+    pair = (2, tile, tile)
+    return pl.pallas_call(
+        refresh_kernel,
+        out_shape=(jax.ShapeDtypeStruct(pair, jnp.bfloat16),) * 2,
+        grid_spec=pltpu.PrefetchScalarGridSpec(
+            num_scalar_prefetch=1,
+            grid=(1,),
+            in_specs=[whole(pair)]
+            + slots_of(side, stat_left, stat_right, basis_left, basis_right),
+            out_specs=(whole(pair), whole(pair)),
+        ),
+        cost_estimate=pl.CostEstimate(
+            flops=4 * 26 * 6 * 2 * tile**3, bytes_accessed=800_000, transcendentals=0
+        ),
+        name="refreshed",
+    )(side, grads, stat_left, stat_right, basis_left, basis_right)
+
+
+def place_kernel(col_tiles, order_ref, live_ref, *refs):
+    sources, out, sems = refs[:-2], refs[-2], refs[-1]
+    tile = sources[0].shape[-1]
+    half = sources[0].shape[0]
+
+    def copy(source, index, entry):
+        block = order_ref[entry]
+        row = pl.multiple_of(block // col_tiles * tile, tile)
+        col = pl.multiple_of(block % col_tiles * tile, tile)
+        return pltpu.make_async_copy(
+            source.at[index], out.at[pl.ds(row, tile), pl.ds(col, tile)], sems.at[entry]
+        )
+
+    for number, source in enumerate(sources):
+        for index in range(half):
+            entry = number * half + index
+
+            @pl.when(live_ref[entry] == 1)
+            def _():
+                copy(source, index, entry).start()
+
+    for number, source in enumerate(sources):
+        for index in range(half):
+            entry = number * half + index
+
+            @pl.when(live_ref[entry] == 1)
+            def _():
+                copy(source, index, entry).wait()
+
+
+def placed(order, live, sources, d_win, width):
+    tile = sources[0].shape[-1]
+    smem = pl.BlockSpec(memory_space=pltpu.SMEM)
+    anywhere = pl.BlockSpec(memory_space=pl.ANY)
+    return pl.pallas_call(
+        functools.partial(place_kernel, width // tile),
+        out_shape=jax.ShapeDtypeStruct((d_win, width), jnp.bfloat16),
+        in_specs=[smem, smem] + [anywhere] * len(sources),
+        out_specs=anywhere,
+        scratch_shapes=[pltpu.SemaphoreType.DMA((order.shape[0],))],
+        name="placed",
+    )(order, live, *sources)
+
+
+def per_device_dealt(
+    owners,
+    features,
+    kv_cotangent,
+    owner_of_block,
+    first_moment,
+    second_moment,
+    left_stat,
+    right_stat,
+    left_basis,
+    right_basis,
+):
+    tile = left_basis.shape[-1]
+    capacity = left_basis.shape[1]
+    d_win = features.shape[1]
+    width = kv_cotangent.shape[1]
+    nblocks = owner_of_block.shape[0]
+    here = lax.axis_index("dp")
+    core = lax.axis_index("inner")
+    bits = owners.bit_length() - 1
+    orders = ([0, 1] + list(range(2, bits)), [1, 0] + list(range(2, bits)))
+
+    f_sib = swap_along(features, "inner", 2, 1)
+    kv_sib = swap_along(kv_cotangent, "inner", 2, 1)
+
+    offsets = []
+    for order in orders:
+        offsets.append(
+            [
+                sum(((p >> (bits - 1 - i)) & 1) << bit for i, bit in enumerate(order))
+                for p in range(owners)
+            ]
+        )
+    block_ids = jnp.arange(nblocks, dtype=jnp.int32)
+    same = owner_of_block[:, None] == owner_of_block[None, :]
+    earlier = block_ids[None, :] < block_ids[:, None]
+    slot = jnp.sum((same & earlier).astype(jnp.int32), axis=1)
+    offset = jnp.array(offsets, dtype=jnp.int32)[None, :, :]
+    owner_at = jnp.broadcast_to(here ^ offset, (2, 2, owners))
+    side_at = core ^ lax.broadcasted_iota(jnp.int32, (2, 2, owners), 0)
+    slot_at = 2 * side_at + lax.broadcasted_iota(jnp.int32, (2, 2, owners), 1)
+    match = (owner_of_block == owner_at[..., None]) & (slot == slot_at[..., None])
+    which = jnp.sum(jnp.where(match, block_ids, 0), axis=-1)
+    live = jnp.sum(match.astype(jnp.int32), axis=-1)
+
+    near = owners // 2
+    kept_a, sent_a, kept_b, sent_b = grad_parts(
+        which[0].reshape(-1),
+        features,
+        f_sib,
+        kv_cotangent,
+        kv_sib,
+        tile,
+        width // tile,
+        owners,
+    )
+    got_a = swap_along(sent_a, "dp", owners, 1 << orders[0][0])
+    got_b = swap_along(sent_b, "dp", owners, 1 << orders[1][0])
+    half = near // 2
+    next_a = swap_along(kept_a[half:] + got_a[half:], "dp", owners, 1 << orders[0][1])
+    next_b = swap_along(kept_b[half:] + got_b[half:], "dp", owners, 1 << orders[1][1])
+    kept = jnp.stack([kept_a[:half] + got_a[:half], kept_b[:half] + got_b[:half]], axis=1)
+    got = jnp.stack([next_a, next_b], axis=1)
+    for bit in orders[0][2:]:
+        half = kept.shape[0] // 2
+        sent = kept[half:] + got[half:]
+        kept = kept[:half] + got[:half]
+        got = swap_along(sent, "dp", owners, 1 << bit)
+    side = core.reshape(1).astype(jnp.int32)
+    direction, grads = directions(
+        side, kept[0], got[0], first_moment, second_moment, left_basis, right_basis
+    )
+
+    tiles = direction[None]
+    for bit in orders[0][:1:-1]:
+        other = swap_along(tiles, "dp", owners, 1 << bit)
+        tiles = jnp.concatenate([tiles, other], axis=0)
+    gathered = []
+    for stream, order in enumerate(orders):
+        mine = tiles[:, stream]
+        other = swap_along(mine, "dp", owners, 1 << order[1])
+        mine = jnp.concatenate([mine, other], axis=0)
+        other = swap_along(mine, "dp", owners, 1 << order[0])
+        gathered += [mine, other]
+    from_sib = [swap_along(part, "inner", 2, 1) for part in gathered]
+
+    left_iter, right_iter = refreshed(
+        side, grads, left_stat, right_stat, left_basis, right_basis
+    )
+    left_sib = swap_along(left_iter, "inner", 2, 1)
+    right_sib = swap_along(right_iter, "inner", 2, 1)
+
+    update = placed(which.reshape(-1), live.reshape(-1), gathered + from_sib, d_win, width)
+
+    here_live = jnp.any(
+        (owner_of_block == here) & (slot == jnp.arange(capacity, dtype=jnp.int32)[:, None]), axis=1
+    )
+    keep = here_live[:, None, None]
+
+    def merged(own, sib, basis):
+        both = jnp.where(
+            core == 0, jnp.concatenate([own, sib], axis=0), jnp.concatenate([sib, own], axis=0)
+        )
+        return jnp.where(keep, both, basis[0])[None]
+
+    return (
+        update,
+        merged(left_iter, left_sib, left_basis),
+        merged(right_iter, right_sib, right_basis),
+    )
+
+
 def solution(mesh):
+    owners = mesh.shape["dp"]
+    inner = mesh.shape["inner"]
+
+    def per_device(*args):
+        capacity = args[-1].shape[1]
+        if inner == 2 and capacity == 4 and owners >= 4 and owners & (owners - 1) == 0:
+            return per_device_dealt(owners, *args)
+        return per_device_plain(*args)
+
     return jax.shard_map(
         per_device,
         mesh=mesh,

time: 235 us -> 158 us (0.67)
  waiting for transfers between devices: 161 us -> 39.1 us
  Pallas kernels: 0 us -> 84.6 us
  matrix products: 34.2 us -> 0 us
  between operations: 29.5 us -> 0.8 us
  starting transfers between devices: 0.08 us -> 20.7 us
  other arithmetic: 0.46 us -> 7.11 us
  local copies, waits for them, and re-layouts: 9.65 us -> 5.74 us
    psum x1 -> x0, waiting for transfers between devices: 129 us -> none  [per_device(): grad = lax.psum(partial_grad, ('dp', 'inner'))]
    pallas_call x0 -> x4, Pallas kernels: none -> 84.6 us  [the longest x1 65.9 us: placed(): pl.pallas_call(functools.partial(place_kernel, width // tile), out_shape=...]
    ppermute x0 -> x20, waiting for transfers between devices: none -> 39.1 us  [swap_along(): return lax.ppermute(values, axis, [(i, i ^ bit) for i in range(size)])]
    dot_general x59 -> x0, matrix products: 34.2 us -> none  [the longest x24 14.8 us: orthogonalize(): gram = jnp.einsum('sji,sjk->sik', iterate, iterate, precision=highest)]
    all_gather x1 -> x0, waiting for transfers between devices: 31.3 us -> none  [per_device(): everyone = lax.all_gather(direction_low[None], 'dp', axis=0, tiled=True)]
    ppermute x0 -> x20, starting transfers between devices: none -> 20.7 us  [swap_along(): return lax.ppermute(values, axis, [(i, i ^ bit) for i in range(size)])]
    gather x1 -> x0, local copies, waits for them, and re-layouts: 2.55 us -> none  [per_device(): tiles = everyone[owner_of_block, slot]]
  transfers between devices with their start and end apart: 2 -> 20, of which waited for: 2 -> 10; matrix products, arithmetic and copies ran while one was open for 12% -> 4% of each run, Pallas kernels for 0% -> 7%
where the time goes in v1:
time: 158 us
  Pallas kernels  84.6 us (54%)
  waiting for transfers between devices  39.1 us (25%)
  starting transfers between devices  20.7 us (13%)
  other arithmetic  7.11 us (4%)
  local copies, waits for them, and re-layouts  5.74 us (4%)
    pallas_call x1, Pallas kernels, placed(): pl.pallas_call(functools.partial(place_kernel, width // tile), out_shape=...  65.9 us
    ppermute x20, waiting for transfers between devices, swap_along(): return lax.ppermute(values, axis, [(i, i ^ bit) for i in range(size)])  39.1 us
    ppermute x20, starting transfers between devices, swap_along(): return lax.ppermute(values, axis, [(i, i ^ bit) for i in range(size)])  20.7 us
    pallas_call x1, Pallas kernels, refreshed(): pl.pallas_call(refresh_kernel, out_shape=(jax.ShapeDtypeStruct(pair, jnp....  11.6 us
    unnamed x28, local copies, waits for them, and re-layouts  4.39 us
    pallas_call x1, Pallas kernels, directions(): pl.pallas_call(direction_kernel, out_shape=(jax.ShapeDtypeStruct(pair, jn...  3.64 us
    pallas_call x1, Pallas kernels, grad_parts(): pl.pallas_call(functools.partial(grad_kernel, col_tiles, None), out_shape...  3.46 us
  transfers between devices with their start and end apart: 20, of which 10 were waited for; matrix products, arithmetic and copies ran while one was open for 4% of the time, Pallas kernels for 7%

profile of v1, /device:TPU:0, one launch (start us, length us, event | category | flops | bytes accessed | tf_op | source)
XLA Modules:
  0.0 158.0 jit_solution(1868370609931681466)
XLA Ops:
  0.6 0.5 collective-permute-start
  1.1 0.1 collective-permute-start.1
  1.3 0.7 broadcast_xor_fusion
  2.0 0.9 convert_reduce_fusion.1
  2.9 1.0 convert_reduce_fusion
  3.9 0.1 reshape_squeeze.3.order_ref
  4.0 1.2 copy-done
  5.3 0.9 copy-done.1
  6.2 3.5 %grad_parts.1 = (f32[8,128,128]{2,1,0:T(8,128)S(1)}, f32[8,128,128]{2,1,0:T(8,128)S(1)}, f32[8,128,128]{2,1,0:T(8,128)S(1)}, f32[8,128,128]{2,1,0:T(8,128)S(1)}) custom-call(s32[32]{0:T(128)S(1)} %reshape_squeeze.3.order_ref, bf16[256,2048]{1,0:T(8,128)(2,1)S(1)} %copy-done, bf16[256,2048]{1,0:T(8,128)(2,1)S(1)} %collective-permute-done.f_sib, ...), custom_call_target="tpu_custom_call" | custom-call | tf_op jit(solution)/shard_map/grad_parts/pallas_call | solution.py:155
  9.7 2.9 %collective-permute-start.2 = (f32[8,128,128]{2,1,0:T(8,128)S(1)}, f32[8,128,128]{2,1,0:T(8,128)S(1)}, u32[]{:S(2)}, u32[]{:S(2)}) collective-permute-start(f32[8,128,128]{2,1,0:T(8,128)S(1)} %get-tuple-element.12), channel_id=1, source_target_pairs={{0,2},{2,0},{4,6},{6,4},{8,10},{10,8},{12,14},{14,12},{16,18},{18,... | collective-permute-start | bytes 1572872 | tf_op jit(solution)/shard_map/ppermute | solution.py:111
  12.6 1.5 collective-permute-start.3
  14.1 10.7 %collective-permute-done.2 = f32[8,128,128]{2,1,0:T(8,128)S(1)} collective-permute-done((f32[8,128,128]{2,1,0:T(8,128)S(1)}, f32[8,128,128]{2,1,0:T(8,128)S(1)}, u32[]{:S(2)}, u32[]{:S(2)}) %collective-permute-start.2) | collective-permute-done | bytes 524320 | tf_op jit(solution)/shard_map/ppermute | solution.py:111
  24.9 1.8 %collective-permute-start.4 = (f32[4,128,128]{2,1,0:T(8,128)S(1)}, f32[4,128,128]{2,1,0:T(8,128)S(1)}, u32[]{:S(2)}, u32[]{:S(2)}) collective-permute-start(f32[4,128,128]{2,1,0:T(8,128)S(1)} %get-tuple-element.24), channel_id=1, source_target_pairs={{0,4},{2,6},{4,0},{6,2},{8,12},{10,14},{12,8},{14,10},{16,20},{18,... | collective-permute-start | bytes 786440 | tf_op jit(solution)/shard_map/ppermute | solution.py:111
  26.8 1.6 collective-permute-start.5
  28.3 4.4 %collective-permute-done.4 = f32[4,128,128]{2,1,0:T(8,128)S(1)} collective-permute-done((f32[4,128,128]{2,1,0:T(8,128)S(1)}, f32[4,128,128]{2,1,0:T(8,128)S(1)}, u32[]{:S(2)}, u32[]{:S(2)}) %collective-permute-start.4) | collective-permute-done | bytes 262176 | tf_op jit(solution)/shard_map/ppermute | solution.py:111
  32.8 1.3 collective-permute-done.5
  34.1 1.6 %collective-permute-start.6 = (f32[2,2,128,128]{3,2,1,0:T(8,128)S(1)}, f32[2,2,128,128]{3,2,1,0:T(8,128)S(1)}, u32[]{:S(2)}, u32[]{:S(2)}) collective-permute-start(f32[2,2,128,128]{3,2,1,0:T(8,128)S(1)} %get-tuple-element.22), channel_id=1, source_target_pairs={{0,8},{2,10},{4,12},{6,14},{8,0},{10,2},{12,4},{14,6},{16,24},{18,... | collective-permute-start | bytes 786440 | tf_op jit(solution)/shard_map/ppermute | solution.py:111
  35.8 4.8 %collective-permute-done.6 = f32[2,2,128,128]{3,2,1,0:T(8,128)S(1)} collective-permute-done((f32[2,2,128,128]{3,2,1,0:T(8,128)S(1)}, f32[2,2,128,128]{3,2,1,0:T(8,128)S(1)}, u32[]{:S(2)}, u32[]{:S(2)}) %collective-permute-start.6) | collective-permute-done | bytes 262176 | tf_op jit(solution)/shard_map/ppermute | solution.py:111
  40.6 0.7 slice_add_fusion.4
  41.3 2.6 %collective-permute-start.7 = (f32[1,2,128,128]{3,2,1,0:T(8,128)S(1)}, f32[1,2,128,128]{3,2,1,0:T(8,128)S(1)}, u32[]{:S(2)}, u32[]{:S(2)}) collective-permute-start(f32[1,2,128,128]{3,2,1,0:T(8,128)S(1)} %get-tuple-element.27), channel_id=1, source_target_pairs={{0,16},{2,18},{4,20},{6,22},{8,24},{10,26},{12,28},{14,30},{16,0},... | collective-permute-start | bytes 393224 | tf_op jit(solution)/shard_map/ppermute | solution.py:111
  43.8 4.7 %collective-permute-done.7 = f32[1,2,128,128]{3,2,1,0:T(8,128)S(1)} collective-permute-done((f32[1,2,128,128]{3,2,1,0:T(8,128)S(1)}, f32[1,2,128,128]{3,2,1,0:T(8,128)S(1)}, u32[]{:S(2)}, u32[]{:S(2)}) %collective-permute-start.7) | collective-permute-done | bytes 131104 | tf_op jit(solution)/shard_map/ppermute | solution.py:111
  48.5 0.7 copy-done.12
  49.2 3.6 %directions.1 = (bf16[2,128,128]{2,1,0:T(8,128)(2,1)}, f32[2,128,128]{2,1,0:T(8,128)}) custom-call(s32[1]{0:T(128)} %bitcast.side_ref, f32[2,128,128]{2,1,0:T(8,128)} %get-tuple-element.28.a_ref, f32[2,128,128]{2,1,0:T(8,128)} %bitcast.28, f32[1,4,128,128]{3,2,1,0:T(8,128)} %m_ref.1, f32[1,4,128,128]{3,2,1,0:T(8,128)} %v_ref.1, ...), custom_call_target="tpu_custom_call" | custom-call | tf_op jit(solution)/shard_map/directions/pallas_call | solution.py:194
  52.8 1.3 collective-permute-start.8
  54.1 4.3 %collective-permute-done.8 = bf16[1,2,128,128]{3,2,0,1:T(8,128)(2,1)S(1)} collective-permute-done((bf16[1,2,128,128]{3,2,0,1:T(8,128)(2,1)}, bf16[1,2,128,128]{3,2,0,1:T(8,128)(2,1)S(1)}, u32[]{:S(2)}, u32[]{:S(2)}) %collective-permute-start.8) | collective-permute-done | bytes 65568 | tf_op jit(solution)/shard_map/ppermute | solution.py:111
  58.4 0.9 pad_maximum_fusion.5
  59.3 1.6 %collective-permute-start.9 = (bf16[2,2,128,128]{3,2,0,1:T(8,128)(2,1)S(1)}, bf16[2,2,128,128]{3,2,0,1:T(8,128)(2,1)S(1)}, u32[]{:S(2)}, u32[]{:S(2)}) collective-permute-start(bf16[2,2,128,128]{3,2,0,1:T(8,128)(2,1)S(1)} %pad_maximum_fusion.5), channel_id=1, source_target_pairs={{0,8},{2,10},{4,12},{6,14},{8,0},{10,2},{12,4},{14,6},{16,24},{18,... | collective-permute-start | bytes 393224 | tf_op jit(solution)/shard_map/ppermute | solution.py:111
  60.9 3.4 %collective-permute-done.9 = bf16[2,2,128,128]{3,2,0,1:T(8,128)(2,1)S(1)} collective-permute-done((bf16[2,2,128,128]{3,2,0,1:T(8,128)(2,1)S(1)}, bf16[2,2,128,128]{3,2,0,1:T(8,128)(2,1)S(1)}, u32[]{:S(2)}, u32[]{:S(2)}) %collective-permute-start.9) | collective-permute-done | bytes 131104 | tf_op jit(solution)/shard_map/ppermute | solution.py:111
  64.3 0.9 pad_maximum_fusion.2
  65.2 1.1 collective-permute-start.10
  66.2 1.0 collective-permute-start.12
  67.2 4.4 %collective-permute-done.10 = bf16[4,128,128]{2,1,0:T(8,128)(2,1)S(1)} collective-permute-done((bf16[4,128,128]{2,1,0:T(8,128)(2,1)S(1)}, bf16[4,128,128]{2,1,0:T(8,128)(2,1)S(1)}, u32[]{:S(2)}, u32[]{:S(2)}) %collective-permute-start.10) | collective-permute-done | bytes 131104 | tf_op jit(solution)/shard_map/ppermute | solution.py:111
  71.7 0.8 collective-permute-start.11
  72.5 1.1 collective-permute-start.13
  73.7 11.6 %refreshed.1 = (bf16[2,128,128]{2,1,0:T(8,128)(2,1)}, bf16[2,128,128]{2,1,0:T(8,128)(2,1)}) custom-call(s32[1]{0:T(128)} %bitcast.side_ref, f32[2,128,128]{2,1,0:T(8,128)} %get-tuple-element.16.g_ref, f32[1,4,128,128]{3,2,1,0:T(8,128)} %l_ref.1, f32[1,4,128,128]{3,2,1,0:T(8,128)} %r_ref.1, bf16[1,4,128,128]{3,2,1,0:T(8,128)(2,1)} %ql_ref.3, ...), custom_call_target="tpu_custom_call" | custom-call | flops 2617245696 | bytes 800000 | tf_op jit(solution)/shard_map/refreshed/pallas_call | solution.py:233
  85.3 0.5 collective-permute-start.18
  85.9 0.9 collective-permute-done.19
  86.7 0.2 collective-permute-start.16
  86.9 0.4 collective-permute-start.15
  87.2 0.2 collective-permute-start.17
  87.4 0.1 fusion.11
  87.5 0.7 reshape.139.order_ref
  88.2 0.6 reshape.140.live_ref
  88.8 1.7 %fusion.8 = (bf16[1,4,128,128]{3,2,1,0:T(8,128)(2,1)}, bf16[1,4,128,128]{3,2,1,0:T(8,128)(2,1)}) fusion(bf16[1,4,128,128]{3,2,1,0:T(8,128)(2,1)S(1)} %copy-done.5, bf16[1,2,128,128]{3,2,1,0:T(8,128)(2,1)S(1)} %bitcast.31, bf16[1,2,128,128]{3,2,1,0:T(8,128)(2,1)} %bitcast.30, pred[4]{0:T(512)(128)(4,1)S(1)} %fusion.11, pred[]{:T(512)S(6)} %eq.70, ...), kind=kLoop, calls=%fused_computation.28 | loop fusion | flops 524288 | bytes 786437 | tf_op jit(solution)/shard_map/jit(_where)/select_n | solution.py:397
  90.6 0.6 copy-done.8
  91.2 0.1 copy-done.9
  91.4 0.7 copy-done.11
  92.1 65.9 %placed.1 = bf16[2048,512]{1,0:T(8,128)(2,1)} custom-call(s32[64]{0:T(128)} %reshape.139.order_ref, s32[64]{0:T(128)} %reshape.140.live_ref, bf16[8,128,128]{2,1,0:T(8,128)(2,1)} %copy-done.2, bf16[8,128,128]{2,1,0:T(8,128)(2,1)} %copy-done.6, bf16[8,128,128]{2,1,0:T(8,128)(2,1)} %copy-done.3, bf16[8,128,128]{2,1,0:T(8,128)(2,1)} %copy-done.7, ...), custom_call_target="tpu_custom_call" | custom-call | tf_op jit(solution)/shard_map/placed/pallas_call | solution.py:284
  (45 shorter events, 0.6 us)
Async XLA Ops:
  0.6 3.4 %collective-permute-start = (bf16[256,2048]{1,0:T(8,128)(2,1)}, bf16[256,2048]{1,0:T(8,128)(2,1)S(1)}, u32[]{:S(2)}, u32[]{:S(2)}) collective-permute-start(bf16[256,2048]{1,0:T(8,128)(2,1)} %f_own.1), channel_id=1, source_target_pairs={{0,1},{1,0},{2,3},{3,2},{4,5},{5,4},{6,7},{7,6},{8,9},{9,8},{10,11... | collective-permute-start | bytes 3145736 | tf_op jit(solution)/shard_map/ppermute | solution.py:111
  1.1 2.9 %collective-permute-start.1 = (bf16[256,512]{1,0:T(8,128)(2,1)}, bf16[256,512]{1,0:T(8,128)(2,1)S(1)}, u32[]{:S(2)}, u32[]{:S(2)}) collective-permute-start(bf16[256,512]{1,0:T(8,128)(2,1)} %kv_own.1), channel_id=1, source_target_pairs={{0,1},{1,0},{2,3},{3,2},{4,5},{5,4},{6,7},{7,6},{8,9},{9,8},{10,11... | collective-permute-start | bytes 786440 | tf_op jit(solution)/shard_map/ppermute | solution.py:111
  4.0 1.2 copy-start
  5.2 0.9 copy-start.1
  9.7 15.1 %collective-permute-start.2 = (f32[8,128,128]{2,1,0:T(8,128)S(1)}, f32[8,128,128]{2,1,0:T(8,128)S(1)}, u32[]{:S(2)}, u32[]{:S(2)}) collective-permute-start(f32[8,128,128]{2,1,0:T(8,128)S(1)} %get-tuple-element.12), channel_id=1, source_target_pairs={{0,2},{2,0},{4,6},{6,4},{8,10},{10,8},{12,14},{14,12},{16,18},{18,... | collective-permute-start | bytes 1572872 | tf_op jit(solution)/shard_map/ppermute | solution.py:111
  12.6 14.1 %collective-permute-start.3 = (f32[8,128,128]{2,1,0:T(8,128)S(1)}, f32[8,128,128]{2,1,0:T(8,128)S(1)}, u32[]{:S(2)}, u32[]{:S(2)}) collective-permute-start(f32[8,128,128]{2,1,0:T(8,128)S(1)} %get-tuple-element.14), channel_id=1, source_target_pairs={{0,4},{2,6},{4,0},{6,2},{8,12},{10,14},{12,8},{14,10},{16,20},{18,... | collective-permute-start | bytes 1572872 | tf_op jit(solution)/shard_map/ppermute | solution.py:111
  24.9 7.9 %collective-permute-start.4 = (f32[4,128,128]{2,1,0:T(8,128)S(1)}, f32[4,128,128]{2,1,0:T(8,128)S(1)}, u32[]{:S(2)}, u32[]{:S(2)}) collective-permute-start(f32[4,128,128]{2,1,0:T(8,128)S(1)} %get-tuple-element.24), channel_id=1, source_target_pairs={{0,4},{2,6},{4,0},{6,2},{8,12},{10,14},{12,8},{14,10},{16,20},{18,... | collective-permute-start | bytes 786440 | tf_op jit(solution)/shard_map/ppermute | solution.py:111
  26.8 7.3 %collective-permute-start.5 = (f32[4,128,128]{2,1,0:T(8,128)S(1)}, f32[4,128,128]{2,1,0:T(8,128)S(1)}, u32[]{:S(2)}, u32[]{:S(2)}) collective-permute-start(f32[4,128,128]{2,1,0:T(8,128)S(1)} %get-tuple-element.26), channel_id=1, source_target_pairs={{0,2},{2,0},{4,6},{6,4},{8,10},{10,8},{12,14},{14,12},{16,18},{18,... | collective-permute-start | bytes 786440 | tf_op jit(solution)/shard_map/ppermute | solution.py:111
  34.1 6.4 %collective-permute-start.6 = (f32[2,2,128,128]{3,2,1,0:T(8,128)S(1)}, f32[2,2,128,128]{3,2,1,0:T(8,128)S(1)}, u32[]{:S(2)}, u32[]{:S(2)}) collective-permute-start(f32[2,2,128,128]{3,2,1,0:T(8,128)S(1)} %get-tuple-element.22), channel_id=1, source_target_pairs={{0,8},{2,10},{4,12},{6,14},{8,0},{10,2},{12,4},{14,6},{16,24},{18,... | collective-permute-start | bytes 786440 | tf_op jit(solution)/shard_map/ppermute | solution.py:111
  41.3 7.3 %collective-permute-start.7 = (f32[1,2,128,128]{3,2,1,0:T(8,128)S(1)}, f32[1,2,128,128]{3,2,1,0:T(8,128)S(1)}, u32[]{:S(2)}, u32[]{:S(2)}) collective-permute-start(f32[1,2,128,128]{3,2,1,0:T(8,128)S(1)} %get-tuple-element.27), channel_id=1, source_target_pairs={{0,16},{2,18},{4,20},{6,22},{8,24},{10,26},{12,28},{14,30},{16,0},... | collective-permute-start | bytes 393224 | tf_op jit(solution)/shard_map/ppermute | solution.py:111
  48.5 0.7 copy-start.12
  52.8 5.6 %collective-permute-start.8 = (bf16[1,2,128,128]{3,2,0,1:T(8,128)(2,1)}, bf16[1,2,128,128]{3,2,0,1:T(8,128)(2,1)S(1)}, u32[]{:S(2)}, u32[]{:S(2)}) collective-permute-start(bf16[1,2,128,128]{3,2,0,1:T(8,128)(2,1)} %bitcast.25), channel_id=1, source_target_pairs={{0,16},{2,18},{4,20},{6,22},{8,24},{10,26},{12,28},{14,30},{16,0},... | collective-permute-start | bytes 196616 | tf_op jit(solution)/shard_map/ppermute | solution.py:111
  59.3 5.0 %collective-permute-start.9 = (bf16[2,2,128,128]{3,2,0,1:T(8,128)(2,1)S(1)}, bf16[2,2,128,128]{3,2,0,1:T(8,128)(2,1)S(1)}, u32[]{:S(2)}, u32[]{:S(2)}) collective-permute-start(bf16[2,2,128,128]{3,2,0,1:T(8,128)(2,1)S(1)} %pad_maximum_fusion.5), channel_id=1, source_target_pairs={{0,8},{2,10},{4,12},{6,14},{8,0},{10,2},{12,4},{14,6},{16,24},{18,... | collective-permute-start | bytes 393224 | tf_op jit(solution)/shard_map/ppermute | solution.py:111
  65.2 6.5 %collective-permute-start.10 = (bf16[4,128,128]{2,1,0:T(8,128)(2,1)S(1)}, bf16[4,128,128]{2,1,0:T(8,128)(2,1)S(1)}, u32[]{:S(2)}, u32[]{:S(2)}) collective-permute-start(bf16[4,128,128]{2,1,0:T(8,128)(2,1)S(1)} %get-tuple-element.30), channel_id=1, source_target_pairs={{0,4},{2,6},{4,0},{6,2},{8,12},{10,14},{12,8},{14,10},{16,20},{18,... | collective-permute-start | bytes 393224 | tf_op jit(solution)/shard_map/ppermute | solution.py:111
  66.2 6.2 %collective-permute-start.12 = (bf16[4,128,128]{2,1,0:T(8,128)(2,1)S(1)}, bf16[4,128,128]{2,1,0:T(8,128)(2,1)S(1)}, u32[]{:S(2)}, u32[]{:S(2)}) collective-permute-start(bf16[4,128,128]{2,1,0:T(8,128)(2,1)S(1)} %get-tuple-element.29), channel_id=1, source_target_pairs={{0,2},{2,0},{4,6},{6,4},{8,10},{10,8},{12,14},{14,12},{16,18},{18,... | collective-permute-start | bytes 393224 | tf_op jit(solution)/shard_map/ppermute | solution.py:111
  71.7 14.1 %copy-start.2 = (bf16[8,128,128]{2,1,0:T(8,128)(2,1)}, bf16[8,128,128]{2,1,0:T(8,128)(2,1)S(1)}, u32[]{:S(2)}) copy-start(bf16[8,128,128]{2,1,0:T(8,128)(2,1)S(1)} %pad_maximum_fusion.3.refs_0_) | copy-start | bytes 786436
  71.7 15.2 %collective-permute-start.11 = (bf16[8,128,128]{2,1,0:T(8,128)(2,1)S(1)}, bf16[8,128,128]{2,1,0:T(8,128)(2,1)S(1)}, u32[]{:S(2)}, u32[]{:S(2)}) collective-permute-start(bf16[8,128,128]{2,1,0:T(8,128)(2,1)S(1)} %pad_maximum_fusion.3.refs_0_), channel_id=1, source_target_pairs={{0,2},{2,0},{4,6},{6,4},{8,10},{10,8},{12,14},{14,12},{16,18},{18,... | collective-permute-start | bytes 786440 | tf_op jit(solution)/shard_map/ppermute | solution.py:111
  72.5 14.2 %copy-start.3 = (bf16[8,128,128]{2,1,0:T(8,128)(2,1)}, bf16[8,128,128]{2,1,0:T(8,128)(2,1)S(1)}, u32[]{:S(2)}) copy-start(bf16[8,128,128]{2,1,0:T(8,128)(2,1)S(1)} %pad_maximum_fusion.4.refs_2_) | copy-start | bytes 786436
  72.5 14.7 %collective-permute-start.13 = (bf16[8,128,128]{2,1,0:T(8,128)(2,1)S(1)}, bf16[8,128,128]{2,1,0:T(8,128)(2,1)S(1)}, u32[]{:S(2)}, u32[]{:S(2)}) collective-permute-start(bf16[8,128,128]{2,1,0:T(8,128)(2,1)S(1)} %pad_maximum_fusion.4.refs_2_), channel_id=1, source_target_pairs={{0,4},{2,6},{4,0},{6,2},{8,12},{10,14},{12,8},{14,10},{16,20},{18,... | collective-permute-start | bytes 786440 | tf_op jit(solution)/shard_map/ppermute | solution.py:111
  73.7 11.6 %copy-start.13 = (s32[64]{0:T(128)S(1)}, s32[64]{0:T(128)}, u32[]{:S(2)}) copy-start(s32[64]{0:T(128)} %param.12) | copy-start | bytes 772
  73.7 15.1 %copy-start.4 = (bf16[1,4,128,128]{3,2,1,0:T(8,128)(2,1)S(1)}, bf16[1,4,128,128]{3,2,1,0:T(8,128)(2,1)}, u32[]{:S(2)}) copy-start(bf16[1,4,128,128]{3,2,1,0:T(8,128)(2,1)} %ql_ref.3) | copy-start | bytes 393220
  73.7 15.1 %copy-start.5 = (bf16[1,4,128,128]{3,2,1,0:T(8,128)(2,1)S(1)}, bf16[1,4,128,128]{3,2,1,0:T(8,128)(2,1)}, u32[]{:S(2)}) copy-start(bf16[1,4,128,128]{3,2,1,0:T(8,128)(2,1)} %qr_ref.3) | copy-start | bytes 393220
  85.3 1.5 collective-permute-start.19
  85.3 3.5 %collective-permute-start.18 = (bf16[2,128,128]{2,1,0:T(8,128)(2,1)}, bf16[2,128,128]{2,1,0:T(8,128)(2,1)S(1)}, u32[]{:S(2)}, u32[]{:S(2)}) collective-permute-start(bf16[2,128,128]{2,1,0:T(8,128)(2,1)} %get-tuple-element.17), channel_id=1, source_target_pairs={{0,1},{1,0},{2,3},{3,2},{4,5},{5,4},{6,7},{7,6},{8,9},{9,8},{10,11... | collective-permute-start | bytes 196616 | tf_op jit(solution)/shard_map/ppermute | solution.py:111
  85.8 4.7 %collective-permute-start.14 = (bf16[8,128,128]{2,1,0:T(8,128)(2,1)S(1)}, bf16[8,128,128]{2,1,0:T(8,128)(2,1)S(1)}, u32[]{:S(2)}, u32[]{:S(2)}) collective-permute-start(bf16[8,128,128]{2,1,0:T(8,128)(2,1)S(1)} %pad_maximum_fusion.3.refs_0_), channel_id=1, source_target_pairs={{0,1},{1,0},{2,3},{3,2},{4,5},{5,4},{6,7},{7,6},{8,9},{9,8},{10,11... | collective-permute-start | bytes 786440 | tf_op jit(solution)/shard_map/ppermute | solution.py:111
  86.7 3.8 %collective-permute-start.16 = (bf16[8,128,128]{2,1,0:T(8,128)(2,1)S(1)}, bf16[8,128,128]{2,1,0:T(8,128)(2,1)S(1)}, u32[]{:S(2)}, u32[]{:S(2)}) collective-permute-start(bf16[8,128,128]{2,1,0:T(8,128)(2,1)S(1)} %pad_maximum_fusion.4.refs_2_), channel_id=1, source_target_pairs={{0,1},{1,0},{2,3},{3,2},{4,5},{5,4},{6,7},{7,6},{8,9},{9,8},{10,11... | collective-permute-start | bytes 786440 | tf_op jit(solution)/shard_map/ppermute | solution.py:111
  86.9 3.7 %copy-start.6 = (bf16[8,128,128]{2,1,0:T(8,128)(2,1)}, bf16[8,128,128]{2,1,0:T(8,128)(2,1)S(1)}, u32[]{:S(2)}) copy-start(bf16[8,128,128]{2,1,0:T(8,128)(2,1)S(1)} %collective-permute-done.11.refs_1_) | copy-start | bytes 786436
  86.9 3.7 %collective-permute-start.15 = (bf16[8,128,128]{2,1,0:T(8,128)(2,1)S(1)}, bf16[8,128,128]{2,1,0:T(8,128)(2,1)S(1)}, u32[]{:S(2)}, u32[]{:S(2)}) collective-permute-start(bf16[8,128,128]{2,1,0:T(8,128)(2,1)S(1)} %collective-permute-done.11.refs_1_), channel_id=1, source_target_pairs={{0,1},{1,0},{2,3},{3,2},{4,5},{5,4},{6,7},{7,6},{8,9},{9,8},{10,11... | collective-permute-start | bytes 786440 | tf_op jit(solution)/shard_map/ppermute | solution.py:111
  87.2 3.3 %copy-start.7 = (bf16[8,128,128]{2,1,0:T(8,128)(2,1)}, bf16[8,128,128]{2,1,0:T(8,128)(2,1)S(1)}, u32[]{:S(2)}) copy-start(bf16[8,128,128]{2,1,0:T(8,128)(2,1)S(1)} %collective-permute-done.13.refs_3_) | copy-start | bytes 786436
  87.2 3.3 %collective-permute-start.17 = (bf16[8,128,128]{2,1,0:T(8,128)(2,1)S(1)}, bf16[8,128,128]{2,1,0:T(8,128)(2,1)S(1)}, u32[]{:S(2)}, u32[]{:S(2)}) collective-permute-start(bf16[8,128,128]{2,1,0:T(8,128)(2,1)S(1)} %collective-permute-done.13.refs_3_), channel_id=1, source_target_pairs={{0,1},{1,0},{2,3},{3,2},{4,5},{5,4},{6,7},{7,6},{8,9},{9,8},{10,11... | collective-permute-start | bytes 786440 | tf_op jit(solution)/shard_map/ppermute | solution.py:111
  90.5 0.7 copy-start.8
  90.5 0.8 copy-start.9
  90.5 0.9 copy-start.10
  91.4 0.7 copy-start.11

commit v2 on v0

--- a/solution.py
+++ b/solution.py
@@ -1,6 +1,10 @@
+import functools
+
 import jax
 import jax.numpy as jnp
 from jax import lax
+from jax.experimental import pallas as pl
+from jax.experimental.pallas import tpu as pltpu
 from jax.sharding import PartitionSpec as P
 
 NS_STEPS = 12
@@ -42,7 +46,7 @@
     return (direction, orthogonalize(left_new, basis_left), orthogonalize(right_new, basis_right))
 
 
-def per_device(
+def per_device_plain(
     features,
     kv_cotangent,
     owner_of_block,
@@ -103,7 +107,412 @@
     return (update, new_left[None], new_right[None])
 
 
+MM = ((1,), (0,))
+MT = ((1,), (1,))
+TM = ((0,), (0,))
+
+
+def swap_along(values, axis, size, bit):
+    return lax.ppermute(values, axis, [(i, i ^ bit) for i in range(size)])
+
+
+def dot(left, right, dims):
+    return lax.dot_general(left, right, (dims, ((), ())), preferred_element_type=jnp.float32)
+
+
+def halves(x):
+    high = x.astype(jnp.bfloat16)
+    return high, (x - high.astype(jnp.float32)).astype(jnp.bfloat16)
+
+
+def beside(a, b):
+    return jnp.concatenate([a, b], axis=1)
+
+
+def above(a, b):
+    return jnp.concatenate([a, b], axis=0)
+
+
+def folded(both):
+    n = both.shape[1] // 2
+    return both[:, :n] + both[:, n:]
+
+
+def pair_product(left, right, dims):
+    if dims == TM:
+        rows = above(*left)
+    else:
+        rows = beside(*left)
+    if dims == MT:
+        return folded(dot(rows, above(beside(right[0], right[0]), beside(right[1], right[1])), MT))
+    return folded(dot(rows, above(beside(*right), beside(*right)), dims))
+
+
+def low_times(low, x, dims):
+    high, rest = halves(x)
+    if dims == MT:
+        return dot(beside(low, low), beside(high, rest), MT)
+    return dot(beside(low, low), above(high, rest), MM)
+
+
+def times_low(x, low):
+    high, rest = halves(x)
+    return dot(beside(high, rest), above(low, low), MM)
+
+
+def stream_offsets(owners):
+    bits = owners.bit_length() - 1
+    orders = ([0, 1] + list(range(2, bits)), [1, 0] + list(range(2, bits)))
+    offsets = [
+        [sum(((p >> (bits - 1 - i)) & 1) << bit for i, bit in enumerate(order)) for p in range(owners)]
+        for order in orders
+    ]
+    return orders, offsets
+
+
+def tile_terms(block, col_tiles, kv_rows, f_ref):
+    tile = kv_rows.shape[0] // col_tiles
+    row = pl.multiple_of(block // col_tiles * tile, tile)
+    col = pl.multiple_of(block % col_tiles * tile, tile)
+    return dot(kv_rows[pl.ds(col, tile), :], f_ref[:, pl.ds(row, tile)], MM)
+
+
+def first_kernel(owners, capacity, col_tiles, place_ref, owner_ref, f_ref, kv_ref, *rest):
+    table_ref, sent_a, sent_b, kv_rows, count, held = rest
+    nblocks = owner_ref.shape[0]
+    for o in range(owners):
+        count[o] = 0
+
+    def enter(b, carry):
+        o = owner_ref[b]
+        s = count[o]
+        count[o] = s + 1
+        held[o * capacity + s] = b
+        return carry
+
+    lax.fori_loop(0, nblocks, enter, 0, unroll=8)
+    here, core = place_ref[0], place_ref[1]
+    offsets = stream_offsets(owners)[1]
+    for side in range(2):
+        first_slot = 2 * (core ^ side)
+        for stream in range(2):
+            for p in range(owners):
+                entry = (side * 2 + stream) * owners + p
+                table_ref[entry] = held[(here ^ offsets[stream][p]) * capacity + first_slot + stream]
+    kv_rows[...] = kv_ref[...].T
+    near = owners // 2
+    for stream, out in enumerate((sent_a, sent_b)):
+
+        def one(i, carry, stream=stream, out=out):
+            block = table_ref[stream * owners + near + i]
+            out[i] = tile_terms(block, col_tiles, kv_rows, f_ref)
+            return carry
+
+        lax.fori_loop(0, near, one, 0, unroll=4)
+
+
+def second_kernel(owners, col_tiles, table_ref, f_ref, kv_ref, part_a, part_b, sent_a, sent_b, kv_rows):
+    kv_rows[...] = kv_ref[...].T
+    near = owners // 2
+    for stream, (part, out) in enumerate(((part_a, sent_a), (part_b, sent_b))):
+
+        def one(i, carry, stream=stream, part=part, out=out):
+            block = table_ref[stream * owners + near + i]
+            out[i] = part[i] + tile_terms(block, col_tiles, kv_rows, f_ref)
+            return carry
+
+        lax.fori_loop(0, near, one, 0, unroll=4)
+
+
+def third_kernel(owners, col_tiles, table_ref, f_own, f_sib, kv_own, kv_sib, kept_a, kept_b, *rows):
+    rows[0][...] = kv_own[...].T
+    rows[1][...] = kv_sib[...].T
+    near = owners // 2
+    for stream, out in enumerate((kept_a, kept_b)):
+
+        def one(i, carry, stream=stream, out=out):
+            block = table_ref[stream * owners + i]
+            out[i] = tile_terms(block, col_tiles, rows[0], f_own) + tile_terms(
+                block, col_tiles, rows[1], f_sib
+            )
+            return carry
+
+        lax.fori_loop(0, near, one, 0, unroll=4)
+
+
+SMEM = pl.BlockSpec(memory_space=pltpu.SMEM)
+
+
+def whole(shape):
+    return pl.BlockSpec(shape, lambda *g: (0,) * len(shape))
+
+
+def wholes(arrays):
+    return [whole(a.shape) for a in arrays]
+
+
+BIG = pltpu.CompilerParams(vmem_limit_bytes=40 * 2**20)
+
+
+def rotated_kernel(side_ref, m_ref, v_ref, ql_ref, qr_ref, rot_ref, second_ref):
+    for k in range(2):
+        half = times_low(m_ref[0, k].T, ql_ref[0, k])
+        rot_ref[k] = 0.95 * low_times(qr_ref[0, k].T, half, MM)
+        second_ref[k] = 0.95 * v_ref[0, k].T
+
+
+def direction_kernel(side_ref, a_ref, b_ref, m_ref, v_ref, ql_ref, qr_ref, dir_ref, grad_ref):
+    for k in range(2):
+        grad = a_ref[k] + b_ref[k]
+        grad_ref[k] = grad
+        left = ql_ref[0, k]
+        right = qr_ref[0, k]
+        rotated = low_times(right.T, times_low(grad, left), MM)
+        moment_rot = m_ref[k] + 0.05 * rotated
+        second = v_ref[k] + 0.05 * rotated * rotated
+        scaled = moment_rot / (jnp.sqrt(second) + 1e-08)
+        out = low_times(left, low_times(right, scaled, MM), MT)
+        dir_ref[k] = out.astype(dir_ref.dtype)
+
+
+def slots_of(*arrays):
+    tile = arrays[0].shape[-1]
+    return [pl.BlockSpec((1, 2, tile, tile), lambda i, s: (0, s[0], 0, 0)) for _ in arrays]
+
+
+def on_slots(kernel, side, plain, slotted, outs, flops):
+    return pl.pallas_call(
+        kernel,
+        out_shape=tuple(outs),
+        grid_spec=pltpu.PrefetchScalarGridSpec(
+            num_scalar_prefetch=1,
+            grid=(1,),
+            in_specs=wholes(plain) + slots_of(*slotted),
+            out_specs=tuple(wholes(outs)),
+        ),
+        cost_estimate=pl.CostEstimate(flops=flops, bytes_accessed=800_000, transcendentals=0),
+        name=kernel.__name__.removesuffix("_kernel"),
+    )(side, *plain, *slotted)
+
+
+def sweep(values):
+    pairs = [halves(y) for y in values]
+    grams = [halves(pair_product(p, p, MT)) for p in pairs]
+    return tuple(
+        1.5 * y - 0.5 * pair_product(g, p, MM) for y, g, p in zip(values, grams, pairs)
+    )
+
+
+def sweeps(values, count):
+    return lax.fori_loop(0, count, lambda i, v: sweep(v), tuple(values), unroll=2)
+
+
+def refresh_kernel(side_ref, g_ref, l_ref, r_ref, ql_ref, qr_ref, iter_ref):
+    values = []
+    for k in range(2):
+        grad = halves(g_ref[k])
+        for stat, basis, dims in ((l_ref, ql_ref, TM), (r_ref, qr_ref, MT)):
+            new = 0.95 * stat[0, k] + 0.05 * pair_product(grad, grad, dims)
+            power = times_low(new, basis[0, k])
+            values.append((power / jnp.sqrt(jnp.sum(power * power) + 1e-06)).T)
+    for i, y in enumerate(sweeps(values, NS_STEPS // 2)):
+        iter_ref[i] = y
+
+
+def finish_kernel(iter_ref, out_ref):
+    values = [iter_ref[i] for i in range(4)]
+    for i, y in enumerate(sweeps(values, NS_STEPS - NS_STEPS // 2)):
+        out_ref[i] = y.T.astype(out_ref.dtype)
+
+
+def bases_kernel(place_ref, own_ref, sib_ref, left_ref, right_ref):
+    core = place_ref[1]
+    for source, first in ((own_ref, 2 * core), (sib_ref, 2 - 2 * core)):
+        for k in range(2):
+            left_ref[0, first + k] = source[2 * k]
+            right_ref[0, first + k] = source[2 * k + 1]
+
+
+def place_kernel(col_tiles, table_ref, *refs):
+    sources, out = refs[:-1], refs[-1]
+    half, tile = sources[0].shape[:2]
+    for number, source in enumerate(sources):
+        for i in range(half):
+            block = table_ref[number * half + i]
+            row = pl.multiple_of(block // col_tiles * tile, tile)
+            col = pl.multiple_of(block % col_tiles * tile, tile)
+            out[pl.ds(row, tile), pl.ds(col, tile)] = source[i]
+
+
+def per_device_dealt(
+    owners,
+    features,
+    kv_cotangent,
+    owner_of_block,
+    first_moment,
+    second_moment,
+    left_stat,
+    right_stat,
+    left_basis,
+    right_basis,
+):
+    tile = left_basis.shape[-1]
+    capacity = left_basis.shape[1]
+    rows, d_win = features.shape
+    width = kv_cotangent.shape[1]
+    col_tiles = width // tile
+    here = lax.axis_index("dp")
+    core = lax.axis_index("inner")
+    place = jnp.stack([here, core]).astype(jnp.int32)
+    side = core.reshape(1).astype(jnp.int32)
+    orders = stream_offsets(owners)[0]
+    near = owners // 2
+
+    f_sib = swap_along(features, "inner", 2, 1)
+    kv_sib = swap_along(kv_cotangent, "inner", 2, 1)
+    flipped = pltpu.VMEM((width, rows), jnp.bfloat16)
+    part = jax.ShapeDtypeStruct((near, tile, tile), jnp.float32)
+    f32_pair = jax.ShapeDtypeStruct((2, tile, tile), jnp.float32)
+    term_flops = 2 * near * 2 * tile * tile * rows
+
+    table, part_a, part_b = pl.pallas_call(
+        functools.partial(first_kernel, owners, capacity, col_tiles),
+        out_shape=(jax.ShapeDtypeStruct((4 * owners,), jnp.int32), part, part),
+        grid=(1,),
+        in_specs=[SMEM, SMEM] + wholes((features, kv_cotangent)),
+        out_specs=(SMEM, whole(part.shape), whole(part.shape)),
+        scratch_shapes=[
+            flipped,
+            pltpu.SMEM((owners,), jnp.int32),
+            pltpu.SMEM((owners * capacity,), jnp.int32),
+        ],
+        compiler_params=BIG,
+        cost_estimate=pl.CostEstimate(
+            flops=term_flops, bytes_accessed=2_500_000, transcendentals=0
+        ),
+        name="first",
+    )(place, owner_of_block, features, kv_cotangent)
+    sent_a, sent_b = pl.pallas_call(
+        functools.partial(second_kernel, owners, col_tiles),
+        out_shape=(part, part),
+        grid=(1,),
+        in_specs=[SMEM] + wholes((f_sib, kv_sib, part_a, part_b)),
+        out_specs=(whole(part.shape), whole(part.shape)),
+        scratch_shapes=[flipped],
+        compiler_params=BIG,
+        cost_estimate=pl.CostEstimate(
+            flops=term_flops, bytes_accessed=3_500_000, transcendentals=0
+        ),
+        name="second",
+    )(table, f_sib, kv_sib, part_a, part_b)
+    got_a = swap_along(sent_a, "dp", owners, 1 << orders[0][0])
+    got_b = swap_along(sent_b, "dp", owners, 1 << orders[1][0])
+    kept_a, kept_b = pl.pallas_call(
+        functools.partial(third_kernel, owners, col_tiles),
+        out_shape=(part, part),
+        grid=(1,),
+        in_specs=[SMEM] + wholes((features, f_sib, kv_cotangent, kv_sib)),
+        out_specs=(whole(part.shape), whole(part.shape)),
+        scratch_shapes=[flipped, flipped],
+        compiler_params=BIG,
+        cost_estimate=pl.CostEstimate(
+            flops=2 * term_flops, bytes_accessed=3_500_000, transcendentals=0
+        ),
+        name="third",
+    )(table, features, f_sib, kv_cotangent, kv_sib)
+    moment_rot, second = on_slots(
+        rotated_kernel,
+        side,
+        (),
+        (first_moment, second_moment, left_basis, right_basis),
+        (f32_pair, f32_pair),
+        8 * 2 * tile**3,
+    )
+
+    half = near // 2
+    next_a = swap_along(kept_a[half:] + got_a[half:], "dp", owners, 1 << orders[0][1])
+    next_b = swap_along(kept_b[half:] + got_b[half:], "dp", owners, 1 << orders[1][1])
+    kept = jnp.stack([kept_a[:half] + got_a[:half], kept_b[:half] + got_b[:half]], axis=1)
+    got = jnp.stack([next_a, next_b], axis=1)
+    for bit in orders[0][2:]:
+        half = kept.shape[0] // 2
+        sent = kept[half:] + got[half:]
+        kept = kept[:half] + got[:half]
+        got = swap_along(sent, "dp", owners, 1 << bit)
+    direction, grads = on_slots(
+        direction_kernel,
+        side,
+        (kept[0], got[0], moment_rot, second),
+        (left_basis, right_basis),
+        (jax.ShapeDtypeStruct(f32_pair.shape, jnp.bfloat16), f32_pair),
+        16 * 2 * tile**3,
+    )
+
+    bits = len(orders[0])
+    high = owners // 4
+    tiles = []
+    for p in range(high):
+        offset = sum(((p >> (bits - 3 - i)) & 1) << bit for i, bit in enumerate(orders[0][2:]))
+        tiles.append(swap_along(direction, "dp", owners, offset) if offset else direction)
+    iterates = on_slots(
+        refresh_kernel,
+        side,
+        (grads,),
+        (left_stat, right_stat, left_basis, right_basis),
+        (jax.ShapeDtypeStruct((4, tile, tile), jnp.float32),),
+        4 * 14 * 4 * 2 * tile**3,
+    )[0]
+    fresh = pl.pallas_call(
+        finish_kernel,
+        out_shape=jax.ShapeDtypeStruct(iterates.shape, jnp.bfloat16),
+        cost_estimate=pl.CostEstimate(
+            flops=4 * 12 * 4 * 2 * tile**3, bytes_accessed=400_000, transcendentals=0
+        ),
+        name="finish",
+    )(iterates)
+    fresh_sib = swap_along(fresh, "inner", 2, 1)
+    basis = jax.ShapeDtypeStruct(left_basis.shape, left_basis.dtype)
+    new_left, new_right = pl.pallas_call(
+        bases_kernel,
+        out_shape=(basis, basis),
+        grid=(1,),
+        in_specs=[SMEM] + wholes((fresh, fresh_sib)),
+        out_specs=tuple(wholes((basis, basis))),
+        cost_estimate=pl.CostEstimate(flops=0, bytes_accessed=600_000, transcendentals=0),
+        name="bases",
+    )(place, fresh, fresh_sib)
+
+    gathered = []
+    for stream, order in enumerate(orders):
+        mine = jnp.stack([t[stream] for t in tiles])
+        other = swap_along(mine, "dp", owners, 1 << order[1])
+        mine = jnp.concatenate([mine, other], axis=0)
+        other = swap_along(mine, "dp", owners, 1 << order[0])
+        gathered += [mine, other]
+    sources = gathered + [swap_along(g, "inner", 2, 1) for g in gathered]
+    update = pl.pallas_call(
+        functools.partial(place_kernel, col_tiles),
+        out_shape=jax.ShapeDtypeStruct((d_win, width), jnp.bfloat16),
+        grid=(1,),
+        in_specs=[SMEM] + wholes(sources),
+        out_specs=whole((d_win, width)),
+        compiler_params=BIG,
+        name="placed",
+    )(table, *sources)
+    return update, new_left, new_right
+
+
 def solution(mesh):
+    owners = mesh.shape["dp"]
+    inner = mesh.shape["inner"]
+
+    def per_device(*args):
+        capacity = args[-1].shape[1]
+        full = args[2].shape[0] == owners * capacity
+        if full and inner == 2 and capacity == 4 and owners >= 8 and owners & (owners - 1) == 0:
+            return per_device_dealt(owners, *args)
+        return per_device_plain(*args)
+
     return jax.shard_map(
         per_device,
         mesh=mesh,

time: 235 us -> 89.5 us (0.38)
  waiting for transfers between devices: 161 us -> 35.5 us
  matrix products: 34.2 us -> 0 us
  between operations: 29.5 us -> 0.79 us
  Pallas kernels: 0 us -> 24.5 us
  starting transfers between devices: 0.08 us -> 22.3 us
  local copies, waits for them, and re-layouts: 9.65 us -> 5.07 us
    psum x1 -> x0, waiting for transfers between devices: 129 us -> none  [per_device(): grad = lax.psum(partial_grad, ('dp', 'inner'))]
    ppermute x0 -> x20, waiting for transfers between devices: none -> 35.5 us  [swap_along(): return lax.ppermute(values, axis, [(i, i ^ bit) for i in range(size)])]
    dot_general x59 -> x0, matrix products: 34.2 us -> none  [the longest x24 14.8 us: orthogonalize(): gram = jnp.einsum('sji,sjk->sik', iterate, iterate, precision=highest)]
    all_gather x1 -> x0, waiting for transfers between devices: 31.3 us -> none  [per_device(): everyone = lax.all_gather(direction_low[None], 'dp', axis=0, tiled=True)]
    pallas_call x0 -> x9, Pallas kernels: none -> 24.5 us  [the longest x3 10.1 us: on_slots(): pl.pallas_call(kernel, out_shape=tuple(outs), grid_spec=pltpu.PrefetchSca...]
    ppermute x0 -> x20, starting transfers between devices: none -> 22.3 us  [swap_along(): return lax.ppermute(values, axis, [(i, i ^ bit) for i in range(size)])]
    gather x1 -> x0, local copies, waits for them, and re-layouts: 2.55 us -> none  [per_device(): tiles = everyone[owner_of_block, slot]]
  transfers between devices with their start and end apart: 2 -> 20, of which waited for: 2 -> 10; matrix products, arithmetic and copies ran while one was open for 12% -> 1% of each run, Pallas kernels for 0% -> 20%
where the time goes in v2:
time: 89.5 us; the launch traced here: 89.1 us
  waiting for transfers between devices  35.5 us (40%)
  Pallas kernels  24.5 us (27%)
  starting transfers between devices  22.3 us (25%)
  local copies, waits for them, and re-layouts  5.07 us (6%)
  other arithmetic  0.97 us (1%)
    ppermute x20, waiting for transfers between devices, swap_along(): return lax.ppermute(values, axis, [(i, i ^ bit) for i in range(size)])  35.5 us
    ppermute x20, starting transfers between devices, swap_along(): return lax.ppermute(values, axis, [(i, i ^ bit) for i in range(size)])  22.3 us
    pallas_call x3, Pallas kernels, on_slots(): pl.pallas_call(kernel, out_shape=tuple(outs), grid_spec=pltpu.PrefetchSca...  10.1 us
    unnamed x16, local copies, waits for them, and re-layouts  4.15 us
    pallas_call x1, Pallas kernels, per_device_dealt(): pl.pallas_call(finish_kernel, out_shape=jax.ShapeDtypeStruct(iterates.sha...  4.09 us
    pallas_call x1, Pallas kernels, per_device_dealt(): pl.pallas_call(functools.partial(first_kernel, owners, capacity, col_tile...  2.42 us
    pallas_call x1, Pallas kernels, per_device_dealt(): pl.pallas_call(functools.partial(place_kernel, col_tiles), out_shape=jax....  2.36 us
    pallas_call x1, Pallas kernels, per_device_dealt(): pl.pallas_call(functools.partial(third_kernel, owners, col_tiles), out_sh...  2.14 us
  transfers between devices with their start and end apart: 20, of which 10 were waited for; matrix products, arithmetic and copies ran while one was open for 1% of the time, Pallas kernels for 20%

profile of v2, /device:TPU:0, one launch (start us, length us, event | category | flops | bytes accessed | tf_op | source)
XLA Modules:
  0.0 89.1 jit_solution(5695080573435090830)
XLA Ops:
  0.6 0.5 collective-permute-start
  1.1 0.1 collective-permute-start.1
  1.2 0.1 pad_add_fusion.place_ref
  1.3 1.2 %copy-done = bf16[256,2048]{1,0:T(8,128)(2,1)S(1)} copy-done((bf16[256,2048]{1,0:T(8,128)(2,1)S(1)}, bf16[256,2048]{1,0:T(8,128)(2,1)}, u32[]{:S(2)}) %copy-start) | copy-done | bytes 1048600
  2.5 0.9 %copy-done.2 = bf16[256,512]{1,0:T(8,128)(2,1)S(1)} copy-done((bf16[256,512]{1,0:T(8,128)(2,1)S(1)}, bf16[256,512]{1,0:T(8,128)(2,1)}, u32[]{:S(2)}) %copy-start.2) | copy-done | bytes 262168
  3.5 0.7 copy-done.5
  4.1 2.4 %first.1 = (s32[64]{0:T(128)S(1)}, f32[8,128,128]{2,1,0:T(8,128)S(1)}, f32[8,128,128]{2,1,0:T(8,128)S(1)}) custom-call(s32[2]{0:T(128)S(1)} %pad_add_fusion.place_ref, s32[64]{0:T(128)S(1)} %copy-done.5, bf16[256,2048]{1,0:T(8,128)(2,1)S(1)} %copy-done, bf16[256,512]{1,0:T(8,128)(2,1)S(1)} %copy-done.2), custom_call_target="tpu_custom_call" | custom-call | flops 134217728 | bytes 2500000 | tf_op jit(solution)/shard_map/first/pallas_call | solution.py:378
  6.6 0.0 collective-permute-done.1.kv_sib.kv_ref
  6.6 0.0 collective-permute-done.f_sib.f_ref
  6.6 1.7 %second.1 = (f32[8,128,128]{2,1,0:T(8,128)S(1)}, f32[8,128,128]{2,1,0:T(8,128)S(1)}) custom-call(s32[64]{0:T(128)S(1)} %get-tuple-element.16.table_ref, bf16[256,2048]{1,0:T(8,128)(2,1)S(1)} %collective-permute-done.f_sib.f_ref, bf16[256,512]{1,0:T(8,128)(2,1)S(1)} %collective-permute-done.1.kv_sib.kv_ref, f32[8,128,128]{2,1,0:T(8,128)S(1)} %get-tuple-element.18.part_a, ...), custom_call_target="tpu_custom_call" | custom-call | flops 134217728 | bytes 3500000 | tf_op jit(solution)/shard_map/second/pallas_call | solution.py:395
  8.3 3.0 %collective-permute-start.2 = (f32[8,128,128]{2,1,0:T(8,128)S(1)}, f32[8,128,128]{2,1,0:T(8,128)S(1)}, u32[]{:S(2)}, u32[]{:S(2)}) collective-permute-start(f32[8,128,128]{2,1,0:T(8,128)S(1)} %get-tuple-element.20), channel_id=1, source_target_pairs={{0,2},{2,0},{4,6},{6,4},{8,10},{10,8},{12,14},{14,12},{16,18},{18,... | collective-permute-start | bytes 1572872 | tf_op jit(solution)/shard_map/ppermute | solution.py:116
  11.3 1.5 %collective-permute-start.3 = (f32[8,128,128]{2,1,0:T(8,128)S(1)}, f32[8,128,128]{2,1,0:T(8,128)S(1)}, u32[]{:S(2)}, u32[]{:S(2)}) collective-permute-start(f32[8,128,128]{2,1,0:T(8,128)S(1)} %get-tuple-element.22), channel_id=1, source_target_pairs={{0,4},{2,6},{4,0},{6,2},{8,12},{10,14},{12,8},{14,10},{16,20},{18,... | collective-permute-start | bytes 1572872 | tf_op jit(solution)/shard_map/ppermute | solution.py:116
  12.8 2.1 %third.1 = (f32[8,128,128]{2,1,0:T(8,128)S(1)}, f32[8,128,128]{2,1,0:T(8,128)S(1)}) custom-call(s32[64]{0:T(128)S(1)} %get-tuple-element.16.table_ref, bf16[256,2048]{1,0:T(8,128)(2,1)S(1)} %copy-done.1, bf16[256,2048]{1,0:T(8,128)(2,1)S(1)} %collective-permute-done.f_sib.f_ref, bf16[256,512]{1,0:T(8,128)(2,1)S(1)} %copy-done.3, ...), custom_call_target="tpu_custom_call" | custom-call | flops 268435456 | bytes 3500000 | tf_op jit(solution)/shard_map/third/pallas_call | solution.py:410
  15.0 8.5 %collective-permute-done.2 = f32[8,128,128]{2,1,0:T(8,128)S(1)} collective-permute-done((f32[8,128,128]{2,1,0:T(8,128)S(1)}, f32[8,128,128]{2,1,0:T(8,128)S(1)}, u32[]{:S(2)}, u32[]{:S(2)}) %collective-permute-start.2) | collective-permute-done | bytes 524320 | tf_op jit(solution)/shard_map/ppermute | solution.py:116
  23.5 0.1 fusion.5
  23.5 1.8 %collective-permute-start.4 = (f32[4,128,128]{2,1,0:T(8,128)S(1)}, f32[4,128,128]{2,1,0:T(8,128)S(1)}, u32[]{:S(2)}, u32[]{:S(2)}) collective-permute-start(f32[4,128,128]{2,1,0:T(8,128)S(1)} %get-tuple-element.32), channel_id=1, source_target_pairs={{0,4},{2,6},{4,0},{6,2},{8,12},{10,14},{12,8},{14,10},{16,20},{18,... | collective-permute-start | bytes 786440 | tf_op jit(solution)/shard_map/ppermute | solution.py:116
  25.4 0.1 fusion.4
  25.4 1.6 %collective-permute-start.5 = (f32[4,128,128]{2,1,0:T(8,128)S(1)}, f32[4,128,128]{2,1,0:T(8,128)S(1)}, u32[]{:S(2)}, u32[]{:S(2)}) collective-permute-start(f32[4,128,128]{2,1,0:T(8,128)S(1)} %get-tuple-element.34), channel_id=1, source_target_pairs={{0,2},{2,0},{4,6},{6,4},{8,10},{10,8},{12,14},{14,12},{16,18},{18,... | collective-permute-start | bytes 786440 | tf_op jit(solution)/shard_map/ppermute | solution.py:116
  27.0 4.4 %collective-permute-done.4 = f32[4,128,128]{2,1,0:T(8,128)S(1)} collective-permute-done((f32[4,128,128]{2,1,0:T(8,128)S(1)}, f32[4,128,128]{2,1,0:T(8,128)S(1)}, u32[]{:S(2)}, u32[]{:S(2)}) %collective-permute-start.4) | collective-permute-done | bytes 262176 | tf_op jit(solution)/shard_map/ppermute | solution.py:116
  31.4 1.3 %collective-permute-done.5 = f32[4,128,128]{2,1,0:T(8,128)S(1)} collective-permute-done((f32[4,128,128]{2,1,0:T(8,128)S(1)}, f32[4,128,128]{2,1,0:T(8,128)S(1)}, u32[]{:S(2)}, u32[]{:S(2)}) %collective-permute-start.5) | collective-permute-done | bytes 262176 | tf_op jit(solution)/shard_map/ppermute | solution.py:116
  32.7 0.1 fusion.1
  32.8 1.6 %collective-permute-start.6 = (f32[2,2,128,128]{3,2,1,0:T(8,128)S(1)}, f32[2,2,128,128]{3,2,1,0:T(8,128)S(1)}, u32[]{:S(2)}, u32[]{:S(2)}) collective-permute-start(f32[2,2,128,128]{3,2,1,0:T(8,128)S(1)} %get-tuple-element.30), channel_id=1, source_target_pairs={{0,8},{2,10},{4,12},{6,14},{8,0},{10,2},{12,4},{14,6},{16,24},{18,... | collective-permute-start | bytes 786440 | tf_op jit(solution)/shard_map/ppermute | solution.py:116
  34.4 4.8 %collective-permute-done.6 = f32[2,2,128,128]{3,2,1,0:T(8,128)S(1)} collective-permute-done((f32[2,2,128,128]{3,2,1,0:T(8,128)S(1)}, f32[2,2,128,128]{3,2,1,0:T(8,128)S(1)}, u32[]{:S(2)}, u32[]{:S(2)}) %collective-permute-start.6) | collective-permute-done | bytes 262176 | tf_op jit(solution)/shard_map/ppermute | solution.py:116
  39.2 0.7 slice_add_fusion.4
  39.9 2.6 %collective-permute-start.7 = (f32[1,2,128,128]{3,2,1,0:T(8,128)S(1)}, f32[1,2,128,128]{3,2,1,0:T(8,128)S(1)}, u32[]{:S(2)}, u32[]{:S(2)}) collective-permute-start(f32[1,2,128,128]{3,2,1,0:T(8,128)S(1)} %get-tuple-element.35), channel_id=1, source_target_pairs={{0,16},{2,18},{4,20},{6,22},{8,24},{10,26},{12,28},{14,30},{16,0},... | collective-permute-start | bytes 393224 | tf_op jit(solution)/shard_map/ppermute | solution.py:116
  42.5 2.1 %rotated.1 = (f32[2,128,128]{2,1,0:T(8,128)}, f32[2,128,128]{2,1,0:T(8,128)}) custom-call(s32[1]{0:T(128)} %bitcast.1.side_ref, f32[1,4,128,128]{3,2,1,0:T(8,128)} %m_ref.1, f32[1,4,128,128]{3,2,1,0:T(8,128)} %v_ref.1, bf16[1,4,128,128]{3,2,1,0:T(8,128)(2,1)} %ql_ref.5, bf16[1,4,128,128]{3,2,1,0:T(8,128)(2,1)} %qr_ref.5), custom_call_target="tpu_custom_call" | custom-call | flops 33554432 | bytes 800000 | tf_op jit(solution)/shard_map/rotated/pallas_call | solution.py:284
  44.5 2.6 %collective-permute-done.7 = f32[1,2,128,128]{3,2,1,0:T(8,128)S(1)} collective-permute-done((f32[1,2,128,128]{3,2,1,0:T(8,128)S(1)}, f32[1,2,128,128]{3,2,1,0:T(8,128)S(1)}, u32[]{:S(2)}, u32[]{:S(2)}) %collective-permute-start.7) | collective-permute-done | bytes 131104 | tf_op jit(solution)/shard_map/ppermute | solution.py:116
  47.2 0.7 copy-done.7
  47.8 2.8 %direction.1 = (bf16[2,128,128]{2,1,0:T(8,128)(2,1)}, f32[2,128,128]{2,1,0:T(8,128)}) custom-call(s32[1]{0:T(128)} %bitcast.1.side_ref, f32[2,128,128]{2,1,0:T(8,128)} %get-tuple-element.36.a_ref, f32[2,128,128]{2,1,0:T(8,128)} %bitcast.17, f32[2,128,128]{2,1,0:T(8,128)} %get-tuple-element.23.m_ref, f32[2,128,128]{2,1,0:T(8,128)} %get-tuple-element.24.v_ref, ...), custom_call_target="tpu_custom_call" | custom-call | flops 67108864 | bytes 800000 | tf_op jit(solution)/shard_map/direction/pallas_call | solution.py:284
  50.6 3.5 %collective-permute-start.10 = (bf16[2,128,128]{2,1,0:T(8,128)(2,1)}, bf16[2,128,128]{2,1,0:T(8,128)(2,1)S(1)}, u32[]{:S(2)}, u32[]{:S(2)}) collective-permute-start(bf16[2,128,128]{2,1,0:T(8,128)(2,1)} %get-tuple-element.25), channel_id=1, source_target_pairs={{0,24},{2,26},{4,28},{6,30},{8,16},{10,18},{12,20},{14,22},{16,8},... | collective-permute-start | bytes 196616 | tf_op jit(solution)/shard_map/ppermute | solution.py:116
  54.1 0.9 %collective-permute-start.8 = (bf16[2,128,128]{2,1,0:T(8,128)(2,1)}, bf16[2,128,128]{2,1,0:T(8,128)(2,1)S(1)}, u32[]{:S(2)}, u32[]{:S(2)}) collective-permute-start(bf16[2,128,128]{2,1,0:T(8,128)(2,1)} %get-tuple-element.25), channel_id=1, source_target_pairs={{0,16},{2,18},{4,20},{6,22},{8,24},{10,26},{12,28},{14,30},{16,0},... | collective-permute-start | bytes 196616 | tf_op jit(solution)/shard_map/ppermute | solution.py:116
  55.0 0.8 fusion.7
  55.8 3.7 %collective-permute-done.8 = bf16[2,128,128]{2,1,0:T(8,128)(2,1)S(1)} collective-permute-done((bf16[2,128,128]{2,1,0:T(8,128)(2,1)}, bf16[2,128,128]{2,1,0:T(8,128)(2,1)S(1)}, u32[]{:S(2)}, u32[]{:S(2)}) %collective-permute-start.8) | collective-permute-done | bytes 65568 | tf_op jit(solution)/shard_map/ppermute | solution.py:116
  59.6 1.1 %collective-permute-start.11 = (bf16[4,128,128]{2,1,0:T(8,128)(2,1)S(1)}, bf16[4,128,128]{2,1,0:T(8,128)(2,1)S(1)}, u32[]{:S(2)}, u32[]{:S(2)}) collective-permute-start(bf16[4,128,128]{2,1,0:T(8,128)(2,1)S(1)} %pad_maximum_fusion.2), channel_id=1, source_target_pairs={{0,4},{2,6},{4,0},{6,2},{8,12},{10,14},{12,8},{14,10},{16,20},{18,... | collective-permute-start | bytes 393224 | tf_op jit(solution)/shard_map/ppermute | solution.py:116
  60.7 1.0 %collective-permute-start.13 = (bf16[4,128,128]{2,1,0:T(8,128)(2,1)S(1)}, bf16[4,128,128]{2,1,0:T(8,128)(2,1)S(1)}, u32[]{:S(2)}, u32[]{:S(2)}) collective-permute-start(bf16[4,128,128]{2,1,0:T(8,128)(2,1)S(1)} %pad_maximum_fusion.3), channel_id=1, source_target_pairs={{0,2},{2,0},{4,6},{6,4},{8,10},{10,8},{12,14},{14,12},{16,18},{18,... | collective-permute-start | bytes 393224 | tf_op jit(solution)/shard_map/ppermute | solution.py:116
  61.7 4.4 %collective-permute-done.11 = bf16[4,128,128]{2,1,0:T(8,128)(2,1)S(1)} collective-permute-done((bf16[4,128,128]{2,1,0:T(8,128)(2,1)S(1)}, bf16[4,128,128]{2,1,0:T(8,128)(2,1)S(1)}, u32[]{:S(2)}, u32[]{:S(2)}) %collective-permute-start.11) | collective-permute-done | bytes 131104 | tf_op jit(solution)/shard_map/ppermute | solution.py:116
  66.1 0.8 collective-permute-start.12
  66.9 1.2 %collective-permute-start.14 = (bf16[8,128,128]{2,1,0:T(8,128)(2,1)S(1)}, bf16[8,128,128]{2,1,0:T(8,128)(2,1)S(1)}, u32[]{:S(2)}, u32[]{:S(2)}) collective-permute-start(bf16[8,128,128]{2,1,0:T(8,128)(2,1)S(1)} %constant_dynamic-update-slice_fusion.5.refs_2_), channel_id=1, source_target_pairs={{0,4},{2,6},{4,0},{6,2},{8,12},{10,14},{12,8},{14,10},{16,20},{18,... | collective-permute-start | bytes 786440 | tf_op jit(solution)/shard_map/ppermute | solution.py:116
  68.2 0.5 collective-permute-start.17
  68.7 3.8 %collective-permute-done.12.refs_1_ = bf16[8,128,128]{2,1,0:T(8,128)(2,1)S(1)} collective-permute-done((bf16[8,128,128]{2,1,0:T(8,128)(2,1)S(1)}, bf16[8,128,128]{2,1,0:T(8,128)(2,1)S(1)}, u32[]{:S(2)}, u32[]{:S(2)}) %collective-permute-start.12) | collective-permute-done | bytes 262176 | tf_op jit(solution)/shard_map/ppermute | solution.py:116
  72.5 0.9 collective-permute-done.14.refs_3_
  73.4 5.2 %refresh.1.iter_ref = f32[4,128,128]{2,1,0:T(8,128)} custom-call(s32[1]{0:T(128)} %bitcast.1.side_ref, f32[2,128,128]{2,1,0:T(8,128)} %get-tuple-element.26.g_ref, f32[1,4,128,128]{3,2,1,0:T(8,128)} %l_ref.1, f32[1,4,128,128]{3,2,1,0:T(8,128)} %r_ref.1, bf16[1,4,128,128]{3,2,1,0:T(8,128)(2,1)} %ql_ref.5, bf16[1,4,128,128]{3,2,1,0:T(8,128)(2,1)} %qr_ref.5), custom_call_target="tpu_custom_call" | custom-call | flops 939524096 | bytes 800000 | tf_op jit(solution)/shard_map/refresh/pallas_call | solution.py:284
  78.6 4.1 %finish.1.own_ref = bf16[4,128,128]{2,1,0:T(8,128)(2,1)} custom-call(f32[4,128,128]{2,1,0:T(8,128)} %refresh.1.iter_ref), custom_call_target="tpu_custom_call" | custom-call | flops 805306368 | bytes 400000 | tf_op jit(solution)/shard_map/finish/pallas_call | solution.py:465
  82.7 0.5 collective-permute-start.19
  83.2 1.2 %collective-permute-done.19.sib_ref = bf16[4,128,128]{2,1,0:T(8,128)(2,1)S(1)} collective-permute-done((bf16[4,128,128]{2,1,0:T(8,128)(2,1)}, bf16[4,128,128]{2,1,0:T(8,128)(2,1)S(1)}, u32[]{:S(2)}, u32[]{:S(2)}) %collective-permute-start.19) | collective-permute-done | bytes 131104 | tf_op jit(solution)/shard_map/ppermute | solution.py:116
  84.4 0.7 copy-done.6
  85.0 1.7 %bases.1 = (bf16[1,4,128,128]{3,2,1,0:T(8,128)(2,1)}, bf16[1,4,128,128]{3,2,1,0:T(8,128)(2,1)}) custom-call(s32[2]{0:T(128)} %copy-done.4, bf16[4,128,128]{2,1,0:T(8,128)(2,1)} %finish.1.own_ref, bf16[4,128,128]{2,1,0:T(8,128)(2,1)} %copy-done.6), custom_call_target="tpu_custom_call" | custom-call | bytes 600000 | tf_op jit(solution)/shard_map/bases/pallas_call | solution.py:475
  86.8 2.4 %placed.1 = bf16[2048,512]{1,0:T(8,128)(2,1)} custom-call(s32[64]{0:T(128)S(1)} %get-tuple-element.16.table_ref, bf16[8,128,128]{2,1,0:T(8,128)(2,1)S(1)} %constant_dynamic-update-slice_fusion.refs_0_, bf16[8,128,128]{2,1,0:T(8,128)(2,1)S(1)} %collective-permute-done.12.refs_1_, bf16[8,128,128]{2,1,0:T(8,128)(2,1)S(1)} %constant_dynamic-update-slice_fusion.5.refs_2_, ...), custom_call_target="tpu_custom_call" | custom-call | tf_op jit(solution)/shard_map/placed/pallas_call | solution.py:493
  (30 shorter events, 0.2 us)
Async XLA Ops:
  0.6 6.0 %collective-permute-start = (bf16[256,2048]{1,0:T(8,128)(2,1)}, bf16[256,2048]{1,0:T(8,128)(2,1)S(1)}, u32[]{:S(2)}, u32[]{:S(2)}) collective-permute-start(bf16[256,2048]{1,0:T(8,128)(2,1)} %f_own.1), channel_id=1, source_target_pairs={{0,1},{1,0},{2,3},{3,2},{4,5},{5,4},{6,7},{7,6},{8,9},{9,8},{10,11... | collective-permute-start | bytes 3145736 | tf_op jit(solution)/shard_map/ppermute | solution.py:116
  1.1 5.4 %collective-permute-start.1 = (bf16[256,512]{1,0:T(8,128)(2,1)}, bf16[256,512]{1,0:T(8,128)(2,1)S(1)}, u32[]{:S(2)}, u32[]{:S(2)}) collective-permute-start(bf16[256,512]{1,0:T(8,128)(2,1)} %kv_own.1), channel_id=1, source_target_pairs={{0,1},{1,0},{2,3},{3,2},{4,5},{5,4},{6,7},{7,6},{8,9},{9,8},{10,11... | collective-permute-start | bytes 786440 | tf_op jit(solution)/shard_map/ppermute | solution.py:116
  1.3 1.2 %copy-start = (bf16[256,2048]{1,0:T(8,128)(2,1)S(1)}, bf16[256,2048]{1,0:T(8,128)(2,1)}, u32[]{:S(2)}) copy-start(bf16[256,2048]{1,0:T(8,128)(2,1)} %f_own.1) | copy-start | bytes 3145732
  2.5 0.9 %copy-start.2 = (bf16[256,512]{1,0:T(8,128)(2,1)S(1)}, bf16[256,512]{1,0:T(8,128)(2,1)}, u32[]{:S(2)}) copy-start(bf16[256,512]{1,0:T(8,128)(2,1)} %kv_own.1) | copy-start | bytes 786436
  3.5 0.7 copy-start.5
  4.1 10.9 %copy-start.4 = (s32[2]{0:T(128)}, s32[2]{0:T(128)S(1)}, u32[]{:S(2)}) copy-start(s32[2]{0:T(128)S(1)} %pad_add_fusion.place_ref) | copy-start | bytes 28
  4.1 8.7 %copy-start.1 = (bf16[256,2048]{1,0:T(8,128)(2,1)S(1)}, bf16[256,2048]{1,0:T(8,128)(2,1)}, u32[]{:S(2)}) copy-start(bf16[256,2048]{1,0:T(8,128)(2,1)} %f_own.1) | copy-start | bytes 3145732
  4.1 8.7 %copy-start.3 = (bf16[256,512]{1,0:T(8,128)(2,1)S(1)}, bf16[256,512]{1,0:T(8,128)(2,1)}, u32[]{:S(2)}) copy-start(bf16[256,512]{1,0:T(8,128)(2,1)} %kv_own.1) | copy-start | bytes 786436
  8.3 15.2 %collective-permute-start.2 = (f32[8,128,128]{2,1,0:T(8,128)S(1)}, f32[8,128,128]{2,1,0:T(8,128)S(1)}, u32[]{:S(2)}, u32[]{:S(2)}) collective-permute-start(f32[8,128,128]{2,1,0:T(8,128)S(1)} %get-tuple-element.20), channel_id=1, source_target_pairs={{0,2},{2,0},{4,6},{6,4},{8,10},{10,8},{12,14},{14,12},{16,18},{18,... | collective-permute-start | bytes 1572872 | tf_op jit(solution)/shard_map/ppermute | solution.py:116
  11.3 14.1 %collective-permute-start.3 = (f32[8,128,128]{2,1,0:T(8,128)S(1)}, f32[8,128,128]{2,1,0:T(8,128)S(1)}, u32[]{:S(2)}, u32[]{:S(2)}) collective-permute-start(f32[8,128,128]{2,1,0:T(8,128)S(1)} %get-tuple-element.22), channel_id=1, source_target_pairs={{0,4},{2,6},{4,0},{6,2},{8,12},{10,14},{12,8},{14,10},{16,20},{18,... | collective-permute-start | bytes 1572872 | tf_op jit(solution)/shard_map/ppermute | solution.py:116
  23.5 7.8 %collective-permute-start.4 = (f32[4,128,128]{2,1,0:T(8,128)S(1)}, f32[4,128,128]{2,1,0:T(8,128)S(1)}, u32[]{:S(2)}, u32[]{:S(2)}) collective-permute-start(f32[4,128,128]{2,1,0:T(8,128)S(1)} %get-tuple-element.32), channel_id=1, source_target_pairs={{0,4},{2,6},{4,0},{6,2},{8,12},{10,14},{12,8},{14,10},{16,20},{18,... | collective-permute-start | bytes 786440 | tf_op jit(solution)/shard_map/ppermute | solution.py:116
  25.4 7.3 %collective-permute-start.5 = (f32[4,128,128]{2,1,0:T(8,128)S(1)}, f32[4,128,128]{2,1,0:T(8,128)S(1)}, u32[]{:S(2)}, u32[]{:S(2)}) collective-permute-start(f32[4,128,128]{2,1,0:T(8,128)S(1)} %get-tuple-element.34), channel_id=1, source_target_pairs={{0,2},{2,0},{4,6},{6,4},{8,10},{10,8},{12,14},{14,12},{16,18},{18,... | collective-permute-start | bytes 786440 | tf_op jit(solution)/shard_map/ppermute | solution.py:116
  32.8 6.4 %collective-permute-start.6 = (f32[2,2,128,128]{3,2,1,0:T(8,128)S(1)}, f32[2,2,128,128]{3,2,1,0:T(8,128)S(1)}, u32[]{:S(2)}, u32[]{:S(2)}) collective-permute-start(f32[2,2,128,128]{3,2,1,0:T(8,128)S(1)} %get-tuple-element.30), channel_id=1, source_target_pairs={{0,8},{2,10},{4,12},{6,14},{8,0},{10,2},{12,4},{14,6},{16,24},{18,... | collective-permute-start | bytes 786440 | tf_op jit(solution)/shard_map/ppermute | solution.py:116
  39.9 7.3 %collective-permute-start.7 = (f32[1,2,128,128]{3,2,1,0:T(8,128)S(1)}, f32[1,2,128,128]{3,2,1,0:T(8,128)S(1)}, u32[]{:S(2)}, u32[]{:S(2)}) collective-permute-start(f32[1,2,128,128]{3,2,1,0:T(8,128)S(1)} %get-tuple-element.35), channel_id=1, source_target_pairs={{0,16},{2,18},{4,20},{6,22},{8,24},{10,26},{12,28},{14,30},{16,0},... | collective-permute-start | bytes 393224 | tf_op jit(solution)/shard_map/ppermute | solution.py:116
  47.2 0.7 copy-start.7
  50.6 8.9 %collective-permute-start.10 = (bf16[2,128,128]{2,1,0:T(8,128)(2,1)}, bf16[2,128,128]{2,1,0:T(8,128)(2,1)S(1)}, u32[]{:S(2)}, u32[]{:S(2)}) collective-permute-start(bf16[2,128,128]{2,1,0:T(8,128)(2,1)} %get-tuple-element.25), channel_id=1, source_target_pairs={{0,24},{2,26},{4,28},{6,30},{8,16},{10,18},{12,20},{14,22},{16,8},... | collective-permute-start | bytes 196616 | tf_op jit(solution)/shard_map/ppermute | solution.py:116
  54.1 5.4 %collective-permute-start.9 = (bf16[2,128,128]{2,1,0:T(8,128)(2,1)}, bf16[2,128,128]{2,1,0:T(8,128)(2,1)S(1)}, u32[]{:S(2)}, u32[]{:S(2)}) collective-permute-start(bf16[2,128,128]{2,1,0:T(8,128)(2,1)} %get-tuple-element.25), channel_id=1, source_target_pairs={{0,8},{2,10},{4,12},{6,14},{8,0},{10,2},{12,4},{14,6},{16,24},{18,... | collective-permute-start | bytes 196616 | tf_op jit(solution)/shard_map/ppermute | solution.py:116
  54.1 5.4 %collective-permute-start.8 = (bf16[2,128,128]{2,1,0:T(8,128)(2,1)}, bf16[2,128,128]{2,1,0:T(8,128)(2,1)S(1)}, u32[]{:S(2)}, u32[]{:S(2)}) collective-permute-start(bf16[2,128,128]{2,1,0:T(8,128)(2,1)} %get-tuple-element.25), channel_id=1, source_target_pairs={{0,16},{2,18},{4,20},{6,22},{8,24},{10,26},{12,28},{14,30},{16,0},... | collective-permute-start | bytes 196616 | tf_op jit(solution)/shard_map/ppermute | solution.py:116
  59.6 6.5 %collective-permute-start.11 = (bf16[4,128,128]{2,1,0:T(8,128)(2,1)S(1)}, bf16[4,128,128]{2,1,0:T(8,128)(2,1)S(1)}, u32[]{:S(2)}, u32[]{:S(2)}) collective-permute-start(bf16[4,128,128]{2,1,0:T(8,128)(2,1)S(1)} %pad_maximum_fusion.2), channel_id=1, source_target_pairs={{0,4},{2,6},{4,0},{6,2},{8,12},{10,14},{12,8},{14,10},{16,20},{18,... | collective-permute-start | bytes 393224 | tf_op jit(solution)/shard_map/ppermute | solution.py:116
  60.7 6.2 %collective-permute-start.13 = (bf16[4,128,128]{2,1,0:T(8,128)(2,1)S(1)}, bf16[4,128,128]{2,1,0:T(8,128)(2,1)S(1)}, u32[]{:S(2)}, u32[]{:S(2)}) collective-permute-start(bf16[4,128,128]{2,1,0:T(8,128)(2,1)S(1)} %pad_maximum_fusion.3), channel_id=1, source_target_pairs={{0,2},{2,0},{4,6},{6,4},{8,10},{10,8},{12,14},{14,12},{16,18},{18,... | collective-permute-start | bytes 393224 | tf_op jit(solution)/shard_map/ppermute | solution.py:116
  66.1 6.4 %collective-permute-start.12 = (bf16[8,128,128]{2,1,0:T(8,128)(2,1)S(1)}, bf16[8,128,128]{2,1,0:T(8,128)(2,1)S(1)}, u32[]{:S(2)}, u32[]{:S(2)}) collective-permute-start(bf16[8,128,128]{2,1,0:T(8,128)(2,1)S(1)} %constant_dynamic-update-slice_fusion.refs_0_), channel_id=1, source_target_pairs={{0,2},{2,0},{4,6},{6,4},{8,10},{10,8},{12,14},{14,12},{16,18},{18,... | collective-permute-start | bytes 786440 | tf_op jit(solution)/shard_map/ppermute | solution.py:116
  66.9 6.4 %collective-permute-start.14 = (bf16[8,128,128]{2,1,0:T(8,128)(2,1)S(1)}, bf16[8,128,128]{2,1,0:T(8,128)(2,1)S(1)}, u32[]{:S(2)}, u32[]{:S(2)}) collective-permute-start(bf16[8,128,128]{2,1,0:T(8,128)(2,1)S(1)} %constant_dynamic-update-slice_fusion.5.refs_2_), channel_id=1, source_target_pairs={{0,4},{2,6},{4,0},{6,2},{8,12},{10,14},{12,8},{14,10},{16,20},{18,... | collective-permute-start | bytes 786440 | tf_op jit(solution)/shard_map/ppermute | solution.py:116
  68.2 18.6 %collective-permute-start.15 = (bf16[8,128,128]{2,1,0:T(8,128)(2,1)S(1)}, bf16[8,128,128]{2,1,0:T(8,128)(2,1)S(1)}, u32[]{:S(2)}, u32[]{:S(2)}) collective-permute-start(bf16[8,128,128]{2,1,0:T(8,128)(2,1)S(1)} %constant_dynamic-update-slice_fusion.refs_0_), channel_id=1, source_target_pairs={{0,1},{1,0},{2,3},{3,2},{4,5},{5,4},{6,7},{7,6},{8,9},{9,8},{10,11... | collective-permute-start | bytes 786440 | tf_op jit(solution)/shard_map/ppermute | solution.py:116
  68.2 18.6 %collective-permute-start.17 = (bf16[8,128,128]{2,1,0:T(8,128)(2,1)S(1)}, bf16[8,128,128]{2,1,0:T(8,128)(2,1)S(1)}, u32[]{:S(2)}, u32[]{:S(2)}) collective-permute-start(bf16[8,128,128]{2,1,0:T(8,128)(2,1)S(1)} %constant_dynamic-update-slice_fusion.5.refs_2_), channel_id=1, source_target_pairs={{0,1},{1,0},{2,3},{3,2},{4,5},{5,4},{6,7},{7,6},{8,9},{9,8},{10,11... | collective-permute-start | bytes 786440 | tf_op jit(solution)/shard_map/ppermute | solution.py:116
  72.5 14.2 %collective-permute-start.16 = (bf16[8,128,128]{2,1,0:T(8,128)(2,1)S(1)}, bf16[8,128,128]{2,1,0:T(8,128)(2,1)S(1)}, u32[]{:S(2)}, u32[]{:S(2)}) collective-permute-start(bf16[8,128,128]{2,1,0:T(8,128)(2,1)S(1)} %collective-permute-done.12.refs_1_), channel_id=1, source_target_pairs={{0,1},{1,0},{2,3},{3,2},{4,5},{5,4},{6,7},{7,6},{8,9},{9,8},{10,11... | collective-permute-start | bytes 786440 | tf_op jit(solution)/shard_map/ppermute | solution.py:116
  73.4 13.4 %collective-permute-start.18 = (bf16[8,128,128]{2,1,0:T(8,128)(2,1)S(1)}, bf16[8,128,128]{2,1,0:T(8,128)(2,1)S(1)}, u32[]{:S(2)}, u32[]{:S(2)}) collective-permute-start(bf16[8,128,128]{2,1,0:T(8,128)(2,1)S(1)} %collective-permute-done.14.refs_3_), channel_id=1, source_target_pairs={{0,1},{1,0},{2,3},{3,2},{4,5},{5,4},{6,7},{7,6},{8,9},{9,8},{10,11... | collective-permute-start | bytes 786440 | tf_op jit(solution)/shard_map/ppermute | solution.py:116
  82.7 1.7 %collective-permute-start.19 = (bf16[4,128,128]{2,1,0:T(8,128)(2,1)}, bf16[4,128,128]{2,1,0:T(8,128)(2,1)S(1)}, u32[]{:S(2)}, u32[]{:S(2)}) collective-permute-start(bf16[4,128,128]{2,1,0:T(8,128)(2,1)} %finish.1.own_ref), channel_id=1, source_target_pairs={{0,1},{1,0},{2,3},{3,2},{4,5},{5,4},{6,7},{7,6},{8,9},{9,8},{10,11... | collective-permute-start | bytes 393224 | tf_op jit(solution)/shard_map/ppermute | solution.py:116
  84.4 0.7 copy-start.6

commit v3 on v2

--- a/solution.py
+++ b/solution.py
@@ -177,21 +177,29 @@
     return dot(kv_rows[pl.ds(col, tile), :], f_ref[:, pl.ds(row, tile)], MM)
 
 
-def first_kernel(owners, capacity, col_tiles, place_ref, owner_ref, f_ref, kv_ref, *rest):
-    table_ref, sent_a, sent_b, kv_rows, count, held = rest
-    nblocks = owner_ref.shape[0]
+def chunked(source, target, sems, first, count):
+    rows = source.shape[0] // count
+    return [
+        pltpu.make_async_copy(
+            source.at[pl.ds(i * rows, rows)], target.at[pl.ds(i * rows, rows)], sems.at[first + i]
+        )
+        for i in range(count)
+    ]
+
+
+def table_kernel(owners, capacity, meta_ref, table_ref, count, held):
     for o in range(owners):
         count[o] = 0
 
     def enter(b, carry):
-        o = owner_ref[b]
+        o = meta_ref[2 + b]
         s = count[o]
         count[o] = s + 1
         held[o * capacity + s] = b
         return carry
 
-    lax.fori_loop(0, nblocks, enter, 0, unroll=8)
-    here, core = place_ref[0], place_ref[1]
+    lax.fori_loop(0, owners * capacity, enter, 0, unroll=8)
+    here, core = meta_ref[0], meta_ref[1]
     offsets = stream_offsets(owners)[1]
     for side in range(2):
         first_slot = 2 * (core ^ side)
@@ -199,48 +207,26 @@
             for p in range(owners):
                 entry = (side * 2 + stream) * owners + p
                 table_ref[entry] = held[(here ^ offsets[stream][p]) * capacity + first_slot + stream]
-    kv_rows[...] = kv_ref[...].T
-    near = owners // 2
-    for stream, out in enumerate((sent_a, sent_b)):
+
+
+def tiles_kernel(owners, col_tiles, first, table_ref, f_own, f_sib, kv_own, kv_sib, *rest):
+    out_a, out_b, own_rows, sib_rows = rest
+    own_rows[...] = kv_own[...].T
+    sib_rows[...] = kv_sib[...].T
+    for stream, out in enumerate((out_a, out_b)):
 
         def one(i, carry, stream=stream, out=out):
-            block = table_ref[stream * owners + near + i]
-            out[i] = tile_terms(block, col_tiles, kv_rows, f_ref)
-            return carry
-
-        lax.fori_loop(0, near, one, 0, unroll=4)
-
-
-def second_kernel(owners, col_tiles, table_ref, f_ref, kv_ref, part_a, part_b, sent_a, sent_b, kv_rows):
-    kv_rows[...] = kv_ref[...].T
-    near = owners // 2
-    for stream, (part, out) in enumerate(((part_a, sent_a), (part_b, sent_b))):
-
-        def one(i, carry, stream=stream, part=part, out=out):
-            block = table_ref[stream * owners + near + i]
-            out[i] = part[i] + tile_terms(block, col_tiles, kv_rows, f_ref)
-            return carry
-
-        lax.fori_loop(0, near, one, 0, unroll=4)
-
-
-def third_kernel(owners, col_tiles, table_ref, f_own, f_sib, kv_own, kv_sib, kept_a, kept_b, *rows):
-    rows[0][...] = kv_own[...].T
-    rows[1][...] = kv_sib[...].T
-    near = owners // 2
-    for stream, out in enumerate((kept_a, kept_b)):
-
-        def one(i, carry, stream=stream, out=out):
-            block = table_ref[stream * owners + i]
-            out[i] = tile_terms(block, col_tiles, rows[0], f_own) + tile_terms(
-                block, col_tiles, rows[1], f_sib
+            block = table_ref[stream * owners + first + i]
+            out[i] = tile_terms(block, col_tiles, own_rows, f_own) + tile_terms(
+                block, col_tiles, sib_rows, f_sib
             )
             return carry
 
-        lax.fori_loop(0, near, one, 0, unroll=4)
+        lax.fori_loop(0, owners // 2, one, 0, unroll=4)
 
 
 SMEM = pl.BlockSpec(memory_space=pltpu.SMEM)
+HBM = pl.BlockSpec(memory_space=pltpu.HBM)
 
 
 def whole(shape):
@@ -254,25 +240,36 @@
 BIG = pltpu.CompilerParams(vmem_limit_bytes=40 * 2**20)
 
 
-def rotated_kernel(side_ref, m_ref, v_ref, ql_ref, qr_ref, rot_ref, second_ref):
+def rotated_kernel(side_ref, m_ref, v_ref, l_ref, r_ref, ql_ref, qr_ref, *outs):
+    rot_ref, second_ref, power_ref = outs
     for k in range(2):
-        half = times_low(m_ref[0, k].T, ql_ref[0, k])
-        rot_ref[k] = 0.95 * low_times(qr_ref[0, k].T, half, MM)
-        second_ref[k] = 0.95 * v_ref[0, k].T
-
-
-def direction_kernel(side_ref, a_ref, b_ref, m_ref, v_ref, ql_ref, qr_ref, dir_ref, grad_ref):
-    for k in range(2):
-        grad = a_ref[k] + b_ref[k]
-        grad_ref[k] = grad
         left = ql_ref[0, k]
         right = qr_ref[0, k]
-        rotated = low_times(right.T, times_low(grad, left), MM)
-        moment_rot = m_ref[k] + 0.05 * rotated
-        second = v_ref[k] + 0.05 * rotated * rotated
-        scaled = moment_rot / (jnp.sqrt(second) + 1e-08)
-        out = low_times(left, low_times(right, scaled, MM), MT)
-        dir_ref[k] = out.astype(dir_ref.dtype)
+        half = times_low(m_ref[0, k].T, left)
+        rot_ref[k] = 0.95 * low_times(right.T, half, MM)
+        second_ref[k] = 0.95 * v_ref[0, k].T
+        power_ref[2 * k] = 0.95 * times_low(l_ref[0, k], left)
+        power_ref[2 * k + 1] = 0.95 * times_low(r_ref[0, k], right)
+
+
+def direction_kernel(side_ref, a_ref, b_ref, m_ref, v_ref, ql_ref, qr_ref, dir_ref, grad_ref):
+    pair = range(2)
+    lefts = [ql_ref[0, k] for k in pair]
+    rights = [qr_ref[0, k] for k in pair]
+    turned = [right.T for right in rights]
+    grads = [a_ref[k] + b_ref[k] for k in pair]
+    rots = [times_low(grads[k], lefts[k]) for k in pair]
+    rots = [low_times(turned[k], rots[k], MM) for k in pair]
+    scaled = []
+    for k in pair:
+        moment_rot = m_ref[k] + 0.05 * rots[k]
+        second = v_ref[k] + 0.05 * rots[k] * rots[k]
+        scaled.append(moment_rot / (jnp.sqrt(second) + 1e-08))
+    outs = [low_times(rights[k], scaled[k], MM) for k in pair]
+    outs = [low_times(lefts[k], outs[k], MT) for k in pair]
+    for k in pair:
+        dir_ref[k] = outs[k].astype(dir_ref.dtype)
+        grad_ref[k] = grads[k]
 
 
 def slots_of(*arrays):
@@ -307,34 +304,47 @@
     return lax.fori_loop(0, count, lambda i, v: sweep(v), tuple(values), unroll=2)
 
 
-def refresh_kernel(side_ref, g_ref, l_ref, r_ref, ql_ref, qr_ref, iter_ref):
+STAGES = (3, 4, NS_STEPS - 7)
+
+
+def refresh_kernel(side_ref, g_ref, power_ref, ql_ref, qr_ref, iter_ref):
     values = []
     for k in range(2):
-        grad = halves(g_ref[k])
-        for stat, basis, dims in ((l_ref, ql_ref, TM), (r_ref, qr_ref, MT)):
-            new = 0.95 * stat[0, k] + 0.05 * pair_product(grad, grad, dims)
-            power = times_low(new, basis[0, k])
+        turned = g_ref[k]
+        grad = turned.T
+        for i, rows, columns, basis in ((0, grad, turned, ql_ref), (1, turned, grad, qr_ref)):
+            half = times_low(columns, basis[0, k])
+            power = power_ref[2 * k + i] + 0.05 * pair_product(halves(rows), halves(half), MM)
             values.append((power / jnp.sqrt(jnp.sum(power * power) + 1e-06)).T)
-    for i, y in enumerate(sweeps(values, NS_STEPS // 2)):
+    for i, y in enumerate(sweeps(values, STAGES[0])):
         iter_ref[i] = y
 
 
+def middle_kernel(iter_ref, out_ref):
+    for i, y in enumerate(sweeps([iter_ref[i] for i in range(4)], STAGES[1])):
+        out_ref[i] = y
+
+
 def finish_kernel(iter_ref, out_ref):
-    values = [iter_ref[i] for i in range(4)]
-    for i, y in enumerate(sweeps(values, NS_STEPS - NS_STEPS // 2)):
+    for i, y in enumerate(sweeps([iter_ref[i] for i in range(4)], STAGES[2])):
         out_ref[i] = y.T.astype(out_ref.dtype)
 
 
-def bases_kernel(place_ref, own_ref, sib_ref, left_ref, right_ref):
-    core = place_ref[1]
-    for source, first in ((own_ref, 2 * core), (sib_ref, 2 - 2 * core)):
-        for k in range(2):
-            left_ref[0, first + k] = source[2 * k]
-            right_ref[0, first + k] = source[2 * k + 1]
-
-
-def place_kernel(col_tiles, table_ref, *refs):
-    sources, out = refs[:-1], refs[-1]
+def sweeping(kernel, values, dtype, count):
+    tile = values.shape[-1]
+    return pl.pallas_call(
+        kernel,
+        out_shape=jax.ShapeDtypeStruct(values.shape, dtype),
+        cost_estimate=pl.CostEstimate(
+            flops=4 * 2 * count * 4 * 2 * tile**3, bytes_accessed=400_000, transcendentals=0
+        ),
+        name=kernel.__name__.removesuffix("_kernel"),
+    )(values)
+
+
+def place_kernel(col_tiles, table_ref, place_ref, own_ref, sib_ref, *refs):
+    sources = refs[:-5]
+    out_hbm, left_ref, right_ref, out, sems = refs[-5:]
     half, tile = sources[0].shape[:2]
     for number, source in enumerate(sources):
         for i in range(half):
@@ -342,6 +352,16 @@
             row = pl.multiple_of(block // col_tiles * tile, tile)
             col = pl.multiple_of(block % col_tiles * tile, tile)
             out[pl.ds(row, tile), pl.ds(col, tile)] = source[i]
+    copies = chunked(out, out_hbm, sems, 0, 8)
+    for copy in copies:
+        copy.start()
+    core = place_ref[1]
+    for source, first in ((own_ref, 2 * core), (sib_ref, 2 - 2 * core)):
+        for k in range(2):
+            left_ref[0, first + k] = source[2 * k]
+            right_ref[0, first + k] = source[2 * k + 1]
+    for copy in copies:
+        copy.wait()
 
 
 def per_device_dealt(
@@ -363,7 +383,7 @@
     col_tiles = width // tile
     here = lax.axis_index("dp")
     core = lax.axis_index("inner")
-    place = jnp.stack([here, core]).astype(jnp.int32)
+    meta = jnp.concatenate([jnp.stack([here, core]).astype(jnp.int32), owner_of_block])
     side = core.reshape(1).astype(jnp.int32)
     orders = stream_offsets(owners)[0]
     near = owners // 2
@@ -373,60 +393,49 @@
     flipped = pltpu.VMEM((width, rows), jnp.bfloat16)
     part = jax.ShapeDtypeStruct((near, tile, tile), jnp.float32)
     f32_pair = jax.ShapeDtypeStruct((2, tile, tile), jnp.float32)
-    term_flops = 2 * near * 2 * tile * tile * rows
-
-    table, part_a, part_b = pl.pallas_call(
-        functools.partial(first_kernel, owners, capacity, col_tiles),
-        out_shape=(jax.ShapeDtypeStruct((4 * owners,), jnp.int32), part, part),
-        grid=(1,),
-        in_specs=[SMEM, SMEM] + wholes((features, kv_cotangent)),
-        out_specs=(SMEM, whole(part.shape), whole(part.shape)),
+    table = pl.pallas_call(
+        functools.partial(table_kernel, owners, capacity),
+        out_shape=jax.ShapeDtypeStruct((4 * owners,), jnp.int32),
+        in_specs=[SMEM],
+        out_specs=SMEM,
         scratch_shapes=[
-            flipped,
             pltpu.SMEM((owners,), jnp.int32),
             pltpu.SMEM((owners * capacity,), jnp.int32),
         ],
-        compiler_params=BIG,
-        cost_estimate=pl.CostEstimate(
-            flops=term_flops, bytes_accessed=2_500_000, transcendentals=0
-        ),
-        name="first",
-    )(place, owner_of_block, features, kv_cotangent)
-    sent_a, sent_b = pl.pallas_call(
-        functools.partial(second_kernel, owners, col_tiles),
-        out_shape=(part, part),
-        grid=(1,),
-        in_specs=[SMEM] + wholes((f_sib, kv_sib, part_a, part_b)),
-        out_specs=(whole(part.shape), whole(part.shape)),
-        scratch_shapes=[flipped],
-        compiler_params=BIG,
-        cost_estimate=pl.CostEstimate(
-            flops=term_flops, bytes_accessed=3_500_000, transcendentals=0
-        ),
-        name="second",
-    )(table, f_sib, kv_sib, part_a, part_b)
+        cost_estimate=pl.CostEstimate(flops=0, bytes_accessed=1_000_000, transcendentals=0),
+        name="table",
+    )(meta)
+
+    def tiles_from(first):
+        inputs = (features, f_sib, kv_cotangent, kv_sib)
+        return pl.pallas_call(
+            functools.partial(tiles_kernel, owners, col_tiles, first),
+            out_shape=(part, part),
+            grid=(1,),
+            in_specs=[SMEM] + wholes(inputs),
+            out_specs=(whole(part.shape), whole(part.shape)),
+            scratch_shapes=[flipped, flipped],
+            compiler_params=BIG,
+            cost_estimate=pl.CostEstimate(
+                flops=2 * owners * 2 * tile * tile * 2 * rows,
+                bytes_accessed=3_500_000,
+                transcendentals=0,
+            ),
+            name="tiles",
+        )(table, *inputs)
+
+    sent_a, sent_b = tiles_from(near)
     got_a = swap_along(sent_a, "dp", owners, 1 << orders[0][0])
     got_b = swap_along(sent_b, "dp", owners, 1 << orders[1][0])
-    kept_a, kept_b = pl.pallas_call(
-        functools.partial(third_kernel, owners, col_tiles),
-        out_shape=(part, part),
-        grid=(1,),
-        in_specs=[SMEM] + wholes((features, f_sib, kv_cotangent, kv_sib)),
-        out_specs=(whole(part.shape), whole(part.shape)),
-        scratch_shapes=[flipped, flipped],
-        compiler_params=BIG,
-        cost_estimate=pl.CostEstimate(
-            flops=2 * term_flops, bytes_accessed=3_500_000, transcendentals=0
-        ),
-        name="third",
-    )(table, features, f_sib, kv_cotangent, kv_sib)
-    moment_rot, second = on_slots(
+    kept_a, kept_b = tiles_from(0)
+    quad = jax.ShapeDtypeStruct((4, tile, tile), jnp.float32)
+    moment_rot, second, power = on_slots(
         rotated_kernel,
         side,
         (),
-        (first_moment, second_moment, left_basis, right_basis),
-        (f32_pair, f32_pair),
-        8 * 2 * tile**3,
+        (first_moment, second_moment, left_stat, right_stat, left_basis, right_basis),
+        (f32_pair, f32_pair, quad),
+        16 * 2 * tile**3,
     )
 
     half = near // 2
@@ -438,11 +447,13 @@
         half = kept.shape[0] // 2
         sent = kept[half:] + got[half:]
         kept = kept[:half] + got[:half]
+        if half == 1:
+            sent, kept = sent[0], kept[0]
         got = swap_along(sent, "dp", owners, 1 << bit)
     direction, grads = on_slots(
         direction_kernel,
         side,
-        (kept[0], got[0], moment_rot, second),
+        (kept, got, moment_rot, second),
         (left_basis, right_basis),
         (jax.ShapeDtypeStruct(f32_pair.shape, jnp.bfloat16), f32_pair),
         16 * 2 * tile**3,
@@ -454,52 +465,40 @@
     for p in range(high):
         offset = sum(((p >> (bits - 3 - i)) & 1) << bit for i, bit in enumerate(orders[0][2:]))
         tiles.append(swap_along(direction, "dp", owners, offset) if offset else direction)
-    iterates = on_slots(
+    values = on_slots(
         refresh_kernel,
         side,
-        (grads,),
-        (left_stat, right_stat, left_basis, right_basis),
-        (jax.ShapeDtypeStruct((4, tile, tile), jnp.float32),),
-        4 * 14 * 4 * 2 * tile**3,
+        (grads, power),
+        (left_basis, right_basis),
+        (quad,),
+        4 * (4 + 2 * STAGES[0]) * 4 * 2 * tile**3,
     )[0]
-    fresh = pl.pallas_call(
-        finish_kernel,
-        out_shape=jax.ShapeDtypeStruct(iterates.shape, jnp.bfloat16),
-        cost_estimate=pl.CostEstimate(
-            flops=4 * 12 * 4 * 2 * tile**3, bytes_accessed=400_000, transcendentals=0
-        ),
-        name="finish",
-    )(iterates)
+    mine = [jnp.stack([t[stream] for t in tiles]) for stream in range(2)]
+    mine, values = lax.optimization_barrier((mine, values))
+    other = [swap_along(m, "dp", owners, 1 << order[1]) for m, order in zip(mine, orders)]
+    values = sweeping(middle_kernel, values, jnp.float32, STAGES[1])
+    mine = [jnp.concatenate(both, axis=0) for both in zip(mine, other)]
+    mine, values = lax.optimization_barrier((mine, values))
+    other = [swap_along(m, "dp", owners, 1 << order[0]) for m, order in zip(mine, orders)]
+    fresh = sweeping(finish_kernel, values, jnp.bfloat16, STAGES[2])
+    other, fresh = lax.optimization_barrier((other, fresh))
     fresh_sib = swap_along(fresh, "inner", 2, 1)
+    gathered = [part for both in zip(mine, other) for part in both]
+    sources = gathered + [swap_along(g, "inner", 2, 1) for g in gathered]
     basis = jax.ShapeDtypeStruct(left_basis.shape, left_basis.dtype)
-    new_left, new_right = pl.pallas_call(
-        bases_kernel,
-        out_shape=(basis, basis),
+    return pl.pallas_call(
+        functools.partial(place_kernel, col_tiles),
+        out_shape=(jax.ShapeDtypeStruct((d_win, width), jnp.bfloat16), basis, basis),
         grid=(1,),
-        in_specs=[SMEM] + wholes((fresh, fresh_sib)),
-        out_specs=tuple(wholes((basis, basis))),
-        cost_estimate=pl.CostEstimate(flops=0, bytes_accessed=600_000, transcendentals=0),
-        name="bases",
-    )(place, fresh, fresh_sib)
-
-    gathered = []
-    for stream, order in enumerate(orders):
-        mine = jnp.stack([t[stream] for t in tiles])
-        other = swap_along(mine, "dp", owners, 1 << order[1])
-        mine = jnp.concatenate([mine, other], axis=0)
-        other = swap_along(mine, "dp", owners, 1 << order[0])
-        gathered += [mine, other]
-    sources = gathered + [swap_along(g, "inner", 2, 1) for g in gathered]
-    update = pl.pallas_call(
-        functools.partial(place_kernel, col_tiles),
-        out_shape=jax.ShapeDtypeStruct((d_win, width), jnp.bfloat16),
-        grid=(1,),
-        in_specs=[SMEM] + wholes(sources),
-        out_specs=whole((d_win, width)),
+        in_specs=[SMEM, SMEM] + wholes([fresh, fresh_sib] + sources),
+        out_specs=(HBM, whole(basis.shape), whole(basis.shape)),
+        scratch_shapes=[
+            pltpu.VMEM((d_win, width), jnp.bfloat16),
+            pltpu.SemaphoreType.DMA((8,)),
+        ],
         compiler_params=BIG,
         name="placed",
-    )(table, *sources)
-    return update, new_left, new_right
+    )(table, meta, fresh, fresh_sib, *sources)
 
 
 def solution(mesh):

time: 89.5 us -> 82 us (0.916)
  waiting for transfers between devices: 35.5 us -> 26.6 us
  other arithmetic: 0.97 us -> 2.15 us
    ppermute x20, waiting for transfers between devices: 35.5 us -> 26.6 us  [swap_along(): return lax.ppermute(values, axis, [(i, i ^ bit) for i in range(size)])]
    pallas_call x3, Pallas kernels: 10.1 us -> 8.18 us  [on_slots(): pl.pallas_call(kernel, out_shape=tuple(outs), grid_spec=pltpu.PrefetchSca...]
    pallas_call x6, Pallas kernels: 14.4 us -> 16 us  [the longest x2 6.97 us: sweeping(): pl.pallas_call(kernel, out_shape=jax.ShapeDtypeStruct(values.shape, dtype...]
    concatenate x0 -> x3, other arithmetic: none -> 1.26 us  [the longest x1 1.21 us: per_device_dealt(): jnp.concatenate([jnp.stack([here, core]).astype(jnp.int32), owner_of_block])]
    unnamed x16 -> x14, local copies, waits for them, and re-layouts: 4.15 us -> 4.39 us
  transfers between devices with their start and end apart: 20 -> 20, of which waited for: 10 -> 11; matrix products, arithmetic and copies ran while one was open for 1% -> 3% of each run, Pallas kernels for 20% -> 20%
where the time goes in v3:
time: 82 us; the launch traced here: 81.5 us
  waiting for transfers between devices  26.6 us (32%)
  Pallas kernels  24.1 us (29%)
  starting transfers between devices  22.7 us (28%)
  local copies, waits for them, and re-layouts  5.21 us (6%)
  other arithmetic  2.15 us (3%)
    ppermute x20, waiting for transfers between devices, swap_along(): return lax.ppermute(values, axis, [(i, i ^ bit) for i in range(size)])  26.6 us
    ppermute x20, starting transfers between devices, swap_along(): return lax.ppermute(values, axis, [(i, i ^ bit) for i in range(size)])  22.7 us
    pallas_call x3, Pallas kernels, on_slots(): pl.pallas_call(kernel, out_shape=tuple(outs), grid_spec=pltpu.PrefetchSca...  8.18 us
    pallas_call x2, Pallas kernels, sweeping(): pl.pallas_call(kernel, out_shape=jax.ShapeDtypeStruct(values.shape, dtype...  6.97 us
    unnamed x14, local copies, waits for them, and re-layouts  4.39 us
    pallas_call x2, Pallas kernels, tiles_from(): pl.pallas_call(functools.partial(tiles_kernel, owners, col_tiles, first),...  4.28 us
    pallas_call x1, Pallas kernels, per_device_dealt(): pl.pallas_call(functools.partial(place_kernel, col_tiles), out_shape=(jax...  3.11 us
  transfers between devices with their start and end apart: 20, of which 11 were waited for; matrix products, arithmetic and copies ran while one was open for 3% of the time, Pallas kernels for 20%

profile of v3, /device:TPU:0, one launch (start us, length us, event | category | flops | bytes accessed | tf_op | source)
XLA Modules:
  0.0 81.5 jit_solution(10946180733010376582)
XLA Ops:
  0.6 0.5 collective-permute-start
  1.1 0.1 collective-permute-start.1
  1.2 1.2 %pad_add_fusion.meta_ref.place_ref = s32[66]{0:T(128)} fusion(s32[64]{0:T(128)} %param.11, s32[1]{0:T(128)} %bitcast.1.side_ref, s32[1]{0:T(128)} %bitcast), kind=kLoop, calls=%fused_computation.24 | loop fusion | flops 132 | bytes 528 | tf_op jit(solution)/shard_map/concatenate | solution.py:386
  2.4 1.6 %table.1.table_ref = s32[64]{0:T(128)} custom-call(s32[66]{0:T(128)} %pad_add_fusion.meta_ref.place_ref), custom_call_target="tpu_custom_call" | custom-call | bytes 1000000 | tf_op jit(solution)/shard_map/table/pallas_call | solution.py:396
  4.1 0.0 copy-start
  4.1 1.2 %copy-done = bf16[256,2048]{1,0:T(8,128)(2,1)S(1)} copy-done((bf16[256,2048]{1,0:T(8,128)(2,1)S(1)}, bf16[256,2048]{1,0:T(8,128)(2,1)}, u32[]{:S(2)}) %copy-start) | copy-done | bytes 1048600
  5.3 0.9 %copy-done.1 = bf16[256,512]{1,0:T(8,128)(2,1)S(1)} copy-done((bf16[256,512]{1,0:T(8,128)(2,1)S(1)}, bf16[256,512]{1,0:T(8,128)(2,1)}, u32[]{:S(2)}) %copy-start.1) | copy-done | bytes 262168
  6.2 0.7 copy-done.3
  6.9 2.1 %tiles.3 = (f32[8,128,128]{2,1,0:T(8,128)S(1)}, f32[8,128,128]{2,1,0:T(8,128)S(1)}) custom-call(s32[64]{0:T(128)S(1)} %copy-done.3, bf16[256,2048]{1,0:T(8,128)(2,1)S(1)} %copy-done, bf16[256,2048]{1,0:T(8,128)(2,1)S(1)} %collective-permute-done.f_sib, bf16[256,512]{1,0:T(8,128)(2,1)S(1)} %copy-done.1, bf16[256,512]{1,0:T(8,128)(2,1)S(1)} %collective-permute-done.1.kv_sib), custom_call_target="tpu_custom_call" | custom-call | flops 536870912 | bytes 3500000 | tf_op jit(solution)/shard_map/tiles/pallas_call | solution.py:411
  9.1 3.0 %collective-permute-start.2 = (f32[8,128,128]{2,1,0:T(8,128)S(1)}, f32[8,128,128]{2,1,0:T(8,128)S(1)}, u32[]{:S(2)}, u32[]{:S(2)}) collective-permute-start(f32[8,128,128]{2,1,0:T(8,128)S(1)} %get-tuple-element.22), channel_id=1, source_target_pairs={{0,2},{2,0},{4,6},{6,4},{8,10},{10,8},{12,14},{14,12},{16,18},{18,... | collective-permute-start | bytes 1572872 | tf_op jit(solution)/shard_map/ppermute | solution.py:116
  12.0 1.5 %collective-permute-start.3 = (f32[8,128,128]{2,1,0:T(8,128)S(1)}, f32[8,128,128]{2,1,0:T(8,128)S(1)}, u32[]{:S(2)}, u32[]{:S(2)}) collective-permute-start(f32[8,128,128]{2,1,0:T(8,128)S(1)} %get-tuple-element.24), channel_id=1, source_target_pairs={{0,4},{2,6},{4,0},{6,2},{8,12},{10,14},{12,8},{14,10},{16,20},{18,... | collective-permute-start | bytes 1572872 | tf_op jit(solution)/shard_map/ppermute | solution.py:116
  13.6 2.1 %tiles.2 = (f32[8,128,128]{2,1,0:T(8,128)S(1)}, f32[8,128,128]{2,1,0:T(8,128)S(1)}) custom-call(s32[64]{0:T(128)S(1)} %copy-done.3, bf16[256,2048]{1,0:T(8,128)(2,1)S(1)} %copy-done, bf16[256,2048]{1,0:T(8,128)(2,1)S(1)} %collective-permute-done.f_sib, bf16[256,512]{1,0:T(8,128)(2,1)S(1)} %copy-done.1, bf16[256,512]{1,0:T(8,128)(2,1)S(1)} %collective-permute-done.1.kv_sib), custom_call_target="tpu_custom_call" | custom-call | flops 536870912 | bytes 3500000 | tf_op jit(solution)/shard_map/tiles/pallas_call | solution.py:411
  15.7 8.5 %collective-permute-done.2 = f32[8,128,128]{2,1,0:T(8,128)S(1)} collective-permute-done((f32[8,128,128]{2,1,0:T(8,128)S(1)}, f32[8,128,128]{2,1,0:T(8,128)S(1)}, u32[]{:S(2)}, u32[]{:S(2)}) %collective-permute-start.2) | collective-permute-done | bytes 524320 | tf_op jit(solution)/shard_map/ppermute | solution.py:116
  24.2 0.1 fusion.5
  24.3 1.8 %collective-permute-start.4 = (f32[4,128,128]{2,1,0:T(8,128)S(1)}, f32[4,128,128]{2,1,0:T(8,128)S(1)}, u32[]{:S(2)}, u32[]{:S(2)}) collective-permute-start(f32[4,128,128]{2,1,0:T(8,128)S(1)} %get-tuple-element.42), channel_id=1, source_target_pairs={{0,4},{2,6},{4,0},{6,2},{8,12},{10,14},{12,8},{14,10},{16,20},{18,... | collective-permute-start | bytes 786440 | tf_op jit(solution)/shard_map/ppermute | solution.py:116
  26.1 0.1 fusion.4
  26.2 1.6 %collective-permute-start.5 = (f32[4,128,128]{2,1,0:T(8,128)S(1)}, f32[4,128,128]{2,1,0:T(8,128)S(1)}, u32[]{:S(2)}, u32[]{:S(2)}) collective-permute-start(f32[4,128,128]{2,1,0:T(8,128)S(1)} %get-tuple-element.44), channel_id=1, source_target_pairs={{0,2},{2,0},{4,6},{6,4},{8,10},{10,8},{12,14},{14,12},{16,18},{18,... | collective-permute-start | bytes 786440 | tf_op jit(solution)/shard_map/ppermute | solution.py:116
  27.7 4.4 %collective-permute-done.4 = f32[4,128,128]{2,1,0:T(8,128)S(1)} collective-permute-done((f32[4,128,128]{2,1,0:T(8,128)S(1)}, f32[4,128,128]{2,1,0:T(8,128)S(1)}, u32[]{:S(2)}, u32[]{:S(2)}) %collective-permute-start.4) | collective-permute-done | bytes 262176 | tf_op jit(solution)/shard_map/ppermute | solution.py:116
  32.1 1.3 %collective-permute-done.5 = f32[4,128,128]{2,1,0:T(8,128)S(1)} collective-permute-done((f32[4,128,128]{2,1,0:T(8,128)S(1)}, f32[4,128,128]{2,1,0:T(8,128)S(1)}, u32[]{:S(2)}, u32[]{:S(2)}) %collective-permute-start.5) | collective-permute-done | bytes 262176 | tf_op jit(solution)/shard_map/ppermute | solution.py:116
  33.4 0.1 fusion.1
  33.5 1.7 %collective-permute-start.6 = (f32[2,2,128,128]{3,2,1,0:T(8,128)S(1)}, f32[2,2,128,128]{3,2,1,0:T(8,128)S(1)}, u32[]{:S(2)}, u32[]{:S(2)}) collective-permute-start(f32[2,2,128,128]{3,2,1,0:T(8,128)S(1)} %get-tuple-element.40), channel_id=1, source_target_pairs={{0,8},{2,10},{4,12},{6,14},{8,0},{10,2},{12,4},{14,6},{16,24},{18,... | collective-permute-start | bytes 786440 | tf_op jit(solution)/shard_map/ppermute | solution.py:116
  35.1 4.8 %collective-permute-done.6 = f32[2,2,128,128]{3,2,1,0:T(8,128)S(1)} collective-permute-done((f32[2,2,128,128]{3,2,1,0:T(8,128)S(1)}, f32[2,2,128,128]{3,2,1,0:T(8,128)S(1)}, u32[]{:S(2)}, u32[]{:S(2)}) %collective-permute-start.6) | collective-permute-done | bytes 262176 | tf_op jit(solution)/shard_map/ppermute | solution.py:116
  39.9 0.7 fusion.6
  40.6 2.6 %collective-permute-start.7 = (f32[2,128,128]{2,1,0:T(8,128)S(1)}, f32[2,128,128]{2,1,0:T(8,128)S(1)}, u32[]{:S(2)}, u32[]{:S(2)}) collective-permute-start(f32[2,128,128]{2,1,0:T(8,128)S(1)} %get-tuple-element.45), channel_id=1, source_target_pairs={{0,16},{2,18},{4,20},{6,22},{8,24},{10,26},{12,28},{14,30},{16,0},... | collective-permute-start | bytes 393224 | tf_op jit(solution)/shard_map/ppermute | solution.py:116
  43.2 2.3 %rotated.1 = (f32[2,128,128]{2,1,0:T(8,128)}, f32[2,128,128]{2,1,0:T(8,128)}, f32[4,128,128]{2,1,0:T(8,128)}) custom-call(s32[1]{0:T(128)} %bitcast.1.side_ref, f32[1,4,128,128]{3,2,1,0:T(8,128)} %m_ref.1, f32[1,4,128,128]{3,2,1,0:T(8,128)} %v_ref.1, f32[1,4,128,128]{3,2,1,0:T(8,128)} %l_ref.1, f32[1,4,128,128]{3,2,1,0:T(8,128)} %r_ref.1, ...), custom_call_target="tpu_custom_call" | custom-call | flops 67108864 | bytes 800000 | tf_op jit(solution)/shard_map/rotated/pallas_call | solution.py:281
  45.5 2.3 %collective-permute-done.7.b_ref = f32[2,128,128]{2,1,0:T(8,128)S(1)} collective-permute-done((f32[2,128,128]{2,1,0:T(8,128)S(1)}, f32[2,128,128]{2,1,0:T(8,128)S(1)}, u32[]{:S(2)}, u32[]{:S(2)}) %collective-permute-start.7) | collective-permute-done | bytes 131104 | tf_op jit(solution)/shard_map/ppermute | solution.py:116
  47.9 0.7 copy-done.6
  48.5 2.4 %direction.1 = (bf16[2,128,128]{2,1,0:T(8,128)(2,1)}, f32[2,128,128]{2,1,0:T(8,128)}) custom-call(s32[1]{0:T(128)} %bitcast.1.side_ref, f32[2,128,128]{2,1,0:T(8,128)} %get-tuple-element.46.a_ref, f32[2,128,128]{2,1,0:T(8,128)} %copy-done.6, f32[2,128,128]{2,1,0:T(8,128)} %get-tuple-element.25.m_ref, f32[2,128,128]{2,1,0:T(8,128)} %get-tuple-element.26.v_ref, ...), custom_call_target="tpu_custom_call" | custom-call | flops 67108864 | bytes 800000 | tf_op jit(solution)/shard_map/direction/pallas_call | solution.py:281
  51.0 3.5 %collective-permute-start.10 = (bf16[2,128,128]{2,1,0:T(8,128)(2,1)}, bf16[2,128,128]{2,1,0:T(8,128)(2,1)S(1)}, u32[]{:S(2)}, u32[]{:S(2)}) collective-permute-start(bf16[2,128,128]{2,1,0:T(8,128)(2,1)} %get-tuple-element.27), channel_id=1, source_target_pairs={{0,24},{2,26},{4,28},{6,30},{8,16},{10,18},{12,20},{14,22},{16,8},... | collective-permute-start | bytes 196616 | tf_op jit(solution)/shard_map/ppermute | solution.py:116
  54.5 0.8 fusion.8
  55.3 0.9 %collective-permute-start.8 = (bf16[2,128,128]{2,1,0:T(8,128)(2,1)}, bf16[2,128,128]{2,1,0:T(8,128)(2,1)S(1)}, u32[]{:S(2)}, u32[]{:S(2)}) collective-permute-start(bf16[2,128,128]{2,1,0:T(8,128)(2,1)} %get-tuple-element.27), channel_id=1, source_target_pairs={{0,16},{2,18},{4,20},{6,22},{8,24},{10,26},{12,28},{14,30},{16,0},... | collective-permute-start | bytes 196616 | tf_op jit(solution)/shard_map/ppermute | solution.py:116
  56.2 3.4 %refresh.1.iter_ref = f32[4,128,128]{2,1,0:T(8,128)} custom-call(s32[1]{0:T(128)} %bitcast.1.side_ref, f32[2,128,128]{2,1,0:T(8,128)} %get-tuple-element.28.g_ref, f32[4,128,128]{2,1,0:T(8,128)} %get-tuple-element.29.power_ref, bf16[1,4,128,128]{3,2,1,0:T(8,128)(2,1)} %ql_ref.5, bf16[1,4,128,128]{3,2,1,0:T(8,128)(2,1)} %qr_ref.5), custom_call_target="tpu_custom_call" | custom-call | flops 671088640 | bytes 800000 | tf_op jit(solution)/shard_map/refresh/pallas_call | solution.py:281
  59.6 0.2 collective-permute-done.9
  59.8 1.0 %collective-permute-done.8 = bf16[2,128,128]{2,1,0:T(8,128)(2,1)S(1)} collective-permute-done((bf16[2,128,128]{2,1,0:T(8,128)(2,1)}, bf16[2,128,128]{2,1,0:T(8,128)(2,1)S(1)}, u32[]{:S(2)}, u32[]{:S(2)}) %collective-permute-start.8) | collective-permute-done | bytes 65568 | tf_op jit(solution)/shard_map/ppermute | solution.py:116
  60.8 1.1 %collective-permute-start.11 = (bf16[4,128,128]{2,1,0:T(8,128)(2,1)S(1)}, bf16[4,128,128]{2,1,0:T(8,128)(2,1)S(1)}, u32[]{:S(2)}, u32[]{:S(2)}) collective-permute-start(bf16[4,128,128]{2,1,0:T(8,128)(2,1)S(1)} %get-tuple-element.30), channel_id=1, source_target_pairs={{0,4},{2,6},{4,0},{6,2},{8,12},{10,14},{12,8},{14,10},{16,20},{18,... | collective-permute-start | bytes 393224 | tf_op jit(solution)/shard_map/ppermute | solution.py:116
  61.9 0.9 %collective-permute-start.12 = (bf16[4,128,128]{2,1,0:T(8,128)(2,1)S(1)}, bf16[4,128,128]{2,1,0:T(8,128)(2,1)S(1)}, u32[]{:S(2)}, u32[]{:S(2)}) collective-permute-start(bf16[4,128,128]{2,1,0:T(8,128)(2,1)S(1)} %get-tuple-element.31), channel_id=1, source_target_pairs={{0,2},{2,0},{4,6},{6,4},{8,10},{10,8},{12,14},{14,12},{16,18},{18,... | collective-permute-start | bytes 393224 | tf_op jit(solution)/shard_map/ppermute | solution.py:116
  62.8 3.3 %middle.1.iter_ref = f32[4,128,128]{2,1,0:T(8,128)} custom-call(f32[4,128,128]{2,1,0:T(8,128)} %refresh.1.iter_ref), custom_call_target="tpu_custom_call" | custom-call | flops 536870912 | bytes 400000 | tf_op jit(solution)/shard_map/middle/pallas_call | solution.py:335
  66.1 1.1 %collective-permute-done.11 = bf16[4,128,128]{2,1,0:T(8,128)(2,1)S(1)} collective-permute-done((bf16[4,128,128]{2,1,0:T(8,128)(2,1)S(1)}, bf16[4,128,128]{2,1,0:T(8,128)(2,1)S(1)}, u32[]{:S(2)}, u32[]{:S(2)}) %collective-permute-start.11) | collective-permute-done | bytes 131104 | tf_op jit(solution)/shard_map/ppermute | solution.py:116
  67.2 0.1 collective-permute-done.12
  67.3 1.5 %collective-permute-start.13 = (bf16[8,128,128]{2,1,0:T(8,128)(2,1)S(1)}, bf16[8,128,128]{2,1,0:T(8,128)(2,1)S(1)}, u32[]{:S(2)}, u32[]{:S(2)}) collective-permute-start(bf16[8,128,128]{2,1,0:T(8,128)(2,1)S(1)} %pad_maximum_fusion.2.refs_0_), channel_id=1, source_target_pairs={{0,2},{2,0},{4,6},{6,4},{8,10},{10,8},{12,14},{14,12},{16,18},{18,... | collective-permute-start | bytes 786440 | tf_op jit(solution)/shard_map/ppermute | solution.py:116
  68.8 1.0 %collective-permute-start.14 = (bf16[8,128,128]{2,1,0:T(8,128)(2,1)S(1)}, bf16[8,128,128]{2,1,0:T(8,128)(2,1)S(1)}, u32[]{:S(2)}, u32[]{:S(2)}) collective-permute-start(bf16[8,128,128]{2,1,0:T(8,128)(2,1)S(1)} %pad_maximum_fusion.3.refs_2_), channel_id=1, source_target_pairs={{0,4},{2,6},{4,0},{6,2},{8,12},{10,14},{12,8},{14,10},{16,20},{18,... | collective-permute-start | bytes 786440 | tf_op jit(solution)/shard_map/ppermute | solution.py:116
  69.8 0.5 collective-permute-start.18
  70.3 3.7 %finish.1.own_ref = bf16[4,128,128]{2,1,0:T(8,128)(2,1)} custom-call(f32[4,128,128]{2,1,0:T(8,128)} %middle.1.iter_ref), custom_call_target="tpu_custom_call" | custom-call | flops 671088640 | bytes 400000 | tf_op jit(solution)/shard_map/finish/pallas_call | solution.py:335
  74.0 1.2 %collective-permute-done.14.refs_3_ = bf16[8,128,128]{2,1,0:T(8,128)(2,1)S(1)} collective-permute-done((bf16[8,128,128]{2,1,0:T(8,128)(2,1)S(1)}, bf16[8,128,128]{2,1,0:T(8,128)(2,1)S(1)}, u32[]{:S(2)}, u32[]{:S(2)}) %collective-permute-start.14) | collective-permute-done | bytes 262176 | tf_op jit(solution)/shard_map/ppermute | solution.py:116
  75.2 0.5 collective-permute-start.19
  75.7 1.8 %collective-permute-done.15.sib_ref = bf16[4,128,128]{2,1,0:T(8,128)(2,1)S(1)} collective-permute-done((bf16[4,128,128]{2,1,0:T(8,128)(2,1)}, bf16[4,128,128]{2,1,0:T(8,128)(2,1)S(1)}, u32[]{:S(2)}, u32[]{:S(2)}) %collective-permute-start.15) | collective-permute-done | bytes 131104 | tf_op jit(solution)/shard_map/ppermute | solution.py:116
  77.5 0.9 %copy-done.2 = bf16[4,128,128]{2,1,0:T(8,128)(2,1)S(1)} copy-done((bf16[4,128,128]{2,1,0:T(8,128)(2,1)S(1)}, bf16[4,128,128]{2,1,0:T(8,128)(2,1)}, u32[]{:S(2)}) %copy-start.2) | copy-done | bytes 131096
  78.4 3.1 %placed.1 = (bf16[2048,512]{1,0:T(8,128)(2,1)}, bf16[1,4,128,128]{3,2,1,0:T(8,128)(2,1)}, bf16[1,4,128,128]{3,2,1,0:T(8,128)(2,1)}) custom-call(s32[64]{0:T(128)S(1)} %copy-done.4, s32[66]{0:T(128)S(1)} %copy-done.5, bf16[4,128,128]{2,1,0:T(8,128)(2,1)S(1)} %copy-done.2, bf16[4,128,128]{2,1,0:T(8,128)(2,1)S(1)} %collective-permute-done.15.sib_ref, ...), custom_call_target="tpu_custom_call" | custom-call | tf_op jit(solution)/shard_map/placed/pallas_call | solution.py:489
  (27 shorter events, 0.1 us)
Async XLA Ops:
  0.6 3.4 %collective-permute-start = (bf16[256,2048]{1,0:T(8,128)(2,1)}, bf16[256,2048]{1,0:T(8,128)(2,1)S(1)}, u32[]{:S(2)}, u32[]{:S(2)}) collective-permute-start(bf16[256,2048]{1,0:T(8,128)(2,1)} %f_own.3), channel_id=1, source_target_pairs={{0,1},{1,0},{2,3},{3,2},{4,5},{5,4},{6,7},{7,6},{8,9},{9,8},{10,11... | collective-permute-start | bytes 3145736 | tf_op jit(solution)/shard_map/ppermute | solution.py:116
  1.1 2.9 %collective-permute-start.1 = (bf16[256,512]{1,0:T(8,128)(2,1)}, bf16[256,512]{1,0:T(8,128)(2,1)S(1)}, u32[]{:S(2)}, u32[]{:S(2)}) collective-permute-start(bf16[256,512]{1,0:T(8,128)(2,1)} %kv_own.3), channel_id=1, source_target_pairs={{0,1},{1,0},{2,3},{3,2},{4,5},{5,4},{6,7},{7,6},{8,9},{9,8},{10,11... | collective-permute-start | bytes 786440 | tf_op jit(solution)/shard_map/ppermute | solution.py:116
  4.1 1.2 %copy-start = (bf16[256,2048]{1,0:T(8,128)(2,1)S(1)}, bf16[256,2048]{1,0:T(8,128)(2,1)}, u32[]{:S(2)}) copy-start(bf16[256,2048]{1,0:T(8,128)(2,1)} %f_own.3) | copy-start | bytes 3145732
  5.3 0.9 %copy-start.1 = (bf16[256,512]{1,0:T(8,128)(2,1)S(1)}, bf16[256,512]{1,0:T(8,128)(2,1)}, u32[]{:S(2)}) copy-start(bf16[256,512]{1,0:T(8,128)(2,1)} %kv_own.3) | copy-start | bytes 786436
  6.2 0.7 copy-start.3
  9.1 15.2 %collective-permute-start.2 = (f32[8,128,128]{2,1,0:T(8,128)S(1)}, f32[8,128,128]{2,1,0:T(8,128)S(1)}, u32[]{:S(2)}, u32[]{:S(2)}) collective-permute-start(f32[8,128,128]{2,1,0:T(8,128)S(1)} %get-tuple-element.22), channel_id=1, source_target_pairs={{0,2},{2,0},{4,6},{6,4},{8,10},{10,8},{12,14},{14,12},{16,18},{18,... | collective-permute-start | bytes 1572872 | tf_op jit(solution)/shard_map/ppermute | solution.py:116
  12.0 14.1 %collective-permute-start.3 = (f32[8,128,128]{2,1,0:T(8,128)S(1)}, f32[8,128,128]{2,1,0:T(8,128)S(1)}, u32[]{:S(2)}, u32[]{:S(2)}) collective-permute-start(f32[8,128,128]{2,1,0:T(8,128)S(1)} %get-tuple-element.24), channel_id=1, source_target_pairs={{0,4},{2,6},{4,0},{6,2},{8,12},{10,14},{12,8},{14,10},{16,20},{18,... | collective-permute-start | bytes 1572872 | tf_op jit(solution)/shard_map/ppermute | solution.py:116
  24.3 7.8 %collective-permute-start.4 = (f32[4,128,128]{2,1,0:T(8,128)S(1)}, f32[4,128,128]{2,1,0:T(8,128)S(1)}, u32[]{:S(2)}, u32[]{:S(2)}) collective-permute-start(f32[4,128,128]{2,1,0:T(8,128)S(1)} %get-tuple-element.42), channel_id=1, source_target_pairs={{0,4},{2,6},{4,0},{6,2},{8,12},{10,14},{12,8},{14,10},{16,20},{18,... | collective-permute-start | bytes 786440 | tf_op jit(solution)/shard_map/ppermute | solution.py:116
  26.2 7.2 %collective-permute-start.5 = (f32[4,128,128]{2,1,0:T(8,128)S(1)}, f32[4,128,128]{2,1,0:T(8,128)S(1)}, u32[]{:S(2)}, u32[]{:S(2)}) collective-permute-start(f32[4,128,128]{2,1,0:T(8,128)S(1)} %get-tuple-element.44), channel_id=1, source_target_pairs={{0,2},{2,0},{4,6},{6,4},{8,10},{10,8},{12,14},{14,12},{16,18},{18,... | collective-permute-start | bytes 786440 | tf_op jit(solution)/shard_map/ppermute | solution.py:116
  33.5 6.4 %collective-permute-start.6 = (f32[2,2,128,128]{3,2,1,0:T(8,128)S(1)}, f32[2,2,128,128]{3,2,1,0:T(8,128)S(1)}, u32[]{:S(2)}, u32[]{:S(2)}) collective-permute-start(f32[2,2,128,128]{3,2,1,0:T(8,128)S(1)} %get-tuple-element.40), channel_id=1, source_target_pairs={{0,8},{2,10},{4,12},{6,14},{8,0},{10,2},{12,4},{14,6},{16,24},{18,... | collective-permute-start | bytes 786440 | tf_op jit(solution)/shard_map/ppermute | solution.py:116
  40.6 7.3 %collective-permute-start.7 = (f32[2,128,128]{2,1,0:T(8,128)S(1)}, f32[2,128,128]{2,1,0:T(8,128)S(1)}, u32[]{:S(2)}, u32[]{:S(2)}) collective-permute-start(f32[2,128,128]{2,1,0:T(8,128)S(1)} %get-tuple-element.45), channel_id=1, source_target_pairs={{0,16},{2,18},{4,20},{6,22},{8,24},{10,26},{12,28},{14,30},{16,0},... | collective-permute-start | bytes 393224 | tf_op jit(solution)/shard_map/ppermute | solution.py:116
  47.9 0.7 copy-start.6
  51.0 8.6 %collective-permute-start.10 = (bf16[2,128,128]{2,1,0:T(8,128)(2,1)}, bf16[2,128,128]{2,1,0:T(8,128)(2,1)S(1)}, u32[]{:S(2)}, u32[]{:S(2)}) collective-permute-start(bf16[2,128,128]{2,1,0:T(8,128)(2,1)} %get-tuple-element.27), channel_id=1, source_target_pairs={{0,24},{2,26},{4,28},{6,30},{8,16},{10,18},{12,20},{14,22},{16,8},... | collective-permute-start | bytes 196616 | tf_op jit(solution)/shard_map/ppermute | solution.py:116
  55.3 4.5 %collective-permute-start.9 = (bf16[2,128,128]{2,1,0:T(8,128)(2,1)}, bf16[2,128,128]{2,1,0:T(8,128)(2,1)S(1)}, u32[]{:S(2)}, u32[]{:S(2)}) collective-permute-start(bf16[2,128,128]{2,1,0:T(8,128)(2,1)} %get-tuple-element.27), channel_id=1, source_target_pairs={{0,8},{2,10},{4,12},{6,14},{8,0},{10,2},{12,4},{14,6},{16,24},{18,... | collective-permute-start | bytes 196616 | tf_op jit(solution)/shard_map/ppermute | solution.py:116
  55.3 5.4 %collective-permute-start.8 = (bf16[2,128,128]{2,1,0:T(8,128)(2,1)}, bf16[2,128,128]{2,1,0:T(8,128)(2,1)S(1)}, u32[]{:S(2)}, u32[]{:S(2)}) collective-permute-start(bf16[2,128,128]{2,1,0:T(8,128)(2,1)} %get-tuple-element.27), channel_id=1, source_target_pairs={{0,16},{2,18},{4,20},{6,22},{8,24},{10,26},{12,28},{14,30},{16,0},... | collective-permute-start | bytes 196616 | tf_op jit(solution)/shard_map/ppermute | solution.py:116
  60.8 6.4 %collective-permute-start.11 = (bf16[4,128,128]{2,1,0:T(8,128)(2,1)S(1)}, bf16[4,128,128]{2,1,0:T(8,128)(2,1)S(1)}, u32[]{:S(2)}, u32[]{:S(2)}) collective-permute-start(bf16[4,128,128]{2,1,0:T(8,128)(2,1)S(1)} %get-tuple-element.30), channel_id=1, source_target_pairs={{0,4},{2,6},{4,0},{6,2},{8,12},{10,14},{12,8},{14,10},{16,20},{18,... | collective-permute-start | bytes 393224 | tf_op jit(solution)/shard_map/ppermute | solution.py:116
  61.9 5.4 %collective-permute-start.12 = (bf16[4,128,128]{2,1,0:T(8,128)(2,1)S(1)}, bf16[4,128,128]{2,1,0:T(8,128)(2,1)S(1)}, u32[]{:S(2)}, u32[]{:S(2)}) collective-permute-start(bf16[4,128,128]{2,1,0:T(8,128)(2,1)S(1)} %get-tuple-element.31), channel_id=1, source_target_pairs={{0,2},{2,0},{4,6},{6,4},{8,10},{10,8},{12,14},{14,12},{16,18},{18,... | collective-permute-start | bytes 393224 | tf_op jit(solution)/shard_map/ppermute | solution.py:116
  66.1 11.5 %copy-start.4 = (s32[64]{0:T(128)S(1)}, s32[64]{0:T(128)}, u32[]{:S(2)}) copy-start(s32[64]{0:T(128)} %table.1.table_ref) | copy-start | bytes 772
  66.1 11.5 %copy-start.5 = (s32[66]{0:T(128)S(1)}, s32[66]{0:T(128)}, u32[]{:S(2)}) copy-start(s32[66]{0:T(128)} %pad_add_fusion.meta_ref.place_ref) | copy-start | bytes 796
  67.3 6.7 %collective-permute-start.13 = (bf16[8,128,128]{2,1,0:T(8,128)(2,1)S(1)}, bf16[8,128,128]{2,1,0:T(8,128)(2,1)S(1)}, u32[]{:S(2)}, u32[]{:S(2)}) collective-permute-start(bf16[8,128,128]{2,1,0:T(8,128)(2,1)S(1)} %pad_maximum_fusion.2.refs_0_), channel_id=1, source_target_pairs={{0,2},{2,0},{4,6},{6,4},{8,10},{10,8},{12,14},{14,12},{16,18},{18,... | collective-permute-start | bytes 786440 | tf_op jit(solution)/shard_map/ppermute | solution.py:116
  68.8 6.4 %collective-permute-start.14 = (bf16[8,128,128]{2,1,0:T(8,128)(2,1)S(1)}, bf16[8,128,128]{2,1,0:T(8,128)(2,1)S(1)}, u32[]{:S(2)}, u32[]{:S(2)}) collective-permute-start(bf16[8,128,128]{2,1,0:T(8,128)(2,1)S(1)} %pad_maximum_fusion.3.refs_2_), channel_id=1, source_target_pairs={{0,4},{2,6},{4,0},{6,2},{8,12},{10,14},{12,8},{14,10},{16,20},{18,... | collective-permute-start | bytes 786440 | tf_op jit(solution)/shard_map/ppermute | solution.py:116
  69.8 5.9 %collective-permute-start.16 = (bf16[8,128,128]{2,1,0:T(8,128)(2,1)S(1)}, bf16[8,128,128]{2,1,0:T(8,128)(2,1)S(1)}, u32[]{:S(2)}, u32[]{:S(2)}) collective-permute-start(bf16[8,128,128]{2,1,0:T(8,128)(2,1)S(1)} %pad_maximum_fusion.2.refs_0_), channel_id=1, source_target_pairs={{0,1},{1,0},{2,3},{3,2},{4,5},{5,4},{6,7},{7,6},{8,9},{9,8},{10,11... | collective-permute-start | bytes 786440 | tf_op jit(solution)/shard_map/ppermute | solution.py:116
  69.8 5.9 %collective-permute-start.18 = (bf16[8,128,128]{2,1,0:T(8,128)(2,1)S(1)}, bf16[8,128,128]{2,1,0:T(8,128)(2,1)S(1)}, u32[]{:S(2)}, u32[]{:S(2)}) collective-permute-start(bf16[8,128,128]{2,1,0:T(8,128)(2,1)S(1)} %pad_maximum_fusion.3.refs_2_), channel_id=1, source_target_pairs={{0,1},{1,0},{2,3},{3,2},{4,5},{5,4},{6,7},{7,6},{8,9},{9,8},{10,11... | collective-permute-start | bytes 786440 | tf_op jit(solution)/shard_map/ppermute | solution.py:116
  75.2 2.3 %collective-permute-start.17 = (bf16[8,128,128]{2,1,0:T(8,128)(2,1)S(1)}, bf16[8,128,128]{2,1,0:T(8,128)(2,1)S(1)}, u32[]{:S(2)}, u32[]{:S(2)}) collective-permute-start(bf16[8,128,128]{2,1,0:T(8,128)(2,1)S(1)} %collective-permute-done.13.refs_1_), channel_id=1, source_target_pairs={{0,1},{1,0},{2,3},{3,2},{4,5},{5,4},{6,7},{7,6},{8,9},{9,8},{10,11... | collective-permute-start | bytes 786440 | tf_op jit(solution)/shard_map/ppermute | solution.py:116
  75.2 2.3 %collective-permute-start.19 = (bf16[8,128,128]{2,1,0:T(8,128)(2,1)S(1)}, bf16[8,128,128]{2,1,0:T(8,128)(2,1)S(1)}, u32[]{:S(2)}, u32[]{:S(2)}) collective-permute-start(bf16[8,128,128]{2,1,0:T(8,128)(2,1)S(1)} %collective-permute-done.14.refs_3_), channel_id=1, source_target_pairs={{0,1},{1,0},{2,3},{3,2},{4,5},{5,4},{6,7},{7,6},{8,9},{9,8},{10,11... | collective-permute-start | bytes 786440 | tf_op jit(solution)/shard_map/ppermute | solution.py:116
  75.7 1.8 %collective-permute-start.15 = (bf16[4,128,128]{2,1,0:T(8,128)(2,1)}, bf16[4,128,128]{2,1,0:T(8,128)(2,1)S(1)}, u32[]{:S(2)}, u32[]{:S(2)}) collective-permute-start(bf16[4,128,128]{2,1,0:T(8,128)(2,1)} %finish.1.own_ref), channel_id=1, source_target_pairs={{0,1},{1,0},{2,3},{3,2},{4,5},{5,4},{6,7},{7,6},{8,9},{9,8},{10,11... | collective-permute-start | bytes 393224 | tf_op jit(solution)/shard_map/ppermute | solution.py:116
  77.5 0.9 %copy-start.2 = (bf16[4,128,128]{2,1,0:T(8,128)(2,1)S(1)}, bf16[4,128,128]{2,1,0:T(8,128)(2,1)}, u32[]{:S(2)}) copy-start(bf16[4,128,128]{2,1,0:T(8,128)(2,1)} %finish.1.own_ref) | copy-start | bytes 393220

commit v4 on v3

--- a/solution.py
+++ b/solution.py
@@ -170,13 +170,6 @@
     return orders, offsets
 
 
-def tile_terms(block, col_tiles, kv_rows, f_ref):
-    tile = kv_rows.shape[0] // col_tiles
-    row = pl.multiple_of(block // col_tiles * tile, tile)
-    col = pl.multiple_of(block % col_tiles * tile, tile)
-    return dot(kv_rows[pl.ds(col, tile), :], f_ref[:, pl.ds(row, tile)], MM)
-
-
 def chunked(source, target, sems, first, count):
     rows = source.shape[0] // count
     return [
@@ -187,19 +180,22 @@
     ]
 
 
-def table_kernel(owners, capacity, meta_ref, table_ref, count, held):
+def table_kernel(owners, capacity, place_ref, owner_ref, kv_ref, *rest):
+    table_ref, own_rows, count, held = rest
+    own_rows[...] = kv_ref[...].T
+
     for o in range(owners):
         count[o] = 0
 
     def enter(b, carry):
-        o = meta_ref[2 + b]
+        o = owner_ref[b]
         s = count[o]
         count[o] = s + 1
         held[o * capacity + s] = b
         return carry
 
     lax.fori_loop(0, owners * capacity, enter, 0, unroll=8)
-    here, core = meta_ref[0], meta_ref[1]
+    here, core = place_ref[0], place_ref[1]
     offsets = stream_offsets(owners)[1]
     for side in range(2):
         first_slot = 2 * (core ^ side)
@@ -209,16 +205,19 @@
                 table_ref[entry] = held[(here ^ offsets[stream][p]) * capacity + first_slot + stream]
 
 
-def tiles_kernel(owners, col_tiles, first, table_ref, f_own, f_sib, kv_own, kv_sib, *rest):
-    out_a, out_b, own_rows, sib_rows = rest
-    own_rows[...] = kv_own[...].T
+def tiles_kernel(owners, first, table_ref, f_own, f_sib, own_rows, kv_sib, *rest):
+    out_a, out_b, sib_rows = rest
+    tile = out_a.shape[-1]
+    col_tiles = own_rows.shape[0] // tile
     sib_rows[...] = kv_sib[...].T
     for stream, out in enumerate((out_a, out_b)):
 
         def one(i, carry, stream=stream, out=out):
             block = table_ref[stream * owners + first + i]
-            out[i] = tile_terms(block, col_tiles, own_rows, f_own) + tile_terms(
-                block, col_tiles, sib_rows, f_sib
+            at = pl.ds(pl.multiple_of(block // col_tiles * tile, tile), tile)
+            cots = pl.ds(pl.multiple_of(block % col_tiles * tile, tile), tile)
+            out[i] = dot(own_rows[cots, :], f_own[:, at], MM) + dot(
+                sib_rows[cots, :], f_sib[:, at], MM
             )
             return carry
 
@@ -227,6 +226,7 @@
 
 SMEM = pl.BlockSpec(memory_space=pltpu.SMEM)
 HBM = pl.BlockSpec(memory_space=pltpu.HBM)
+VMEM = pl.BlockSpec(memory_space=pltpu.VMEM)
 
 
 def whole(shape):
@@ -237,7 +237,8 @@
     return [whole(a.shape) for a in arrays]
 
 
-BIG = pltpu.CompilerParams(vmem_limit_bytes=40 * 2**20)
+BIG = pltpu.CompilerParams(vmem_limit_bytes=24 * 2**20)
+SMALL = pltpu.CompilerParams(vmem_limit_bytes=12 * 2**20)
 
 
 def rotated_kernel(side_ref, m_ref, v_ref, l_ref, r_ref, ql_ref, qr_ref, *outs):
@@ -287,6 +288,7 @@
             in_specs=wholes(plain) + slots_of(*slotted),
             out_specs=tuple(wholes(outs)),
         ),
+        compiler_params=SMALL,
         cost_estimate=pl.CostEstimate(flops=flops, bytes_accessed=800_000, transcendentals=0),
         name=kernel.__name__.removesuffix("_kernel"),
     )(side, *plain, *slotted)
@@ -335,6 +337,7 @@
     return pl.pallas_call(
         kernel,
         out_shape=jax.ShapeDtypeStruct(values.shape, dtype),
+        compiler_params=SMALL,
         cost_estimate=pl.CostEstimate(
             flops=4 * 2 * count * 4 * 2 * tile**3, bytes_accessed=400_000, transcendentals=0
         ),
@@ -383,7 +386,7 @@
     col_tiles = width // tile
     here = lax.axis_index("dp")
     core = lax.axis_index("inner")
-    meta = jnp.concatenate([jnp.stack([here, core]).astype(jnp.int32), owner_of_block])
+    place = jnp.stack([here, core]).astype(jnp.int32)
     side = core.reshape(1).astype(jnp.int32)
     orders = stream_offsets(owners)[0]
     near = owners // 2
@@ -393,28 +396,32 @@
     flipped = pltpu.VMEM((width, rows), jnp.bfloat16)
     part = jax.ShapeDtypeStruct((near, tile, tile), jnp.float32)
     f32_pair = jax.ShapeDtypeStruct((2, tile, tile), jnp.float32)
-    table = pl.pallas_call(
+    table, own_rows = pl.pallas_call(
         functools.partial(table_kernel, owners, capacity),
-        out_shape=jax.ShapeDtypeStruct((4 * owners,), jnp.int32),
-        in_specs=[SMEM],
-        out_specs=SMEM,
+        out_shape=(
+            jax.ShapeDtypeStruct((4 * owners,), jnp.int32),
+            jax.ShapeDtypeStruct((width, rows), jnp.bfloat16),
+        ),
+        in_specs=[SMEM, SMEM, VMEM],
+        out_specs=(SMEM, VMEM),
+        compiler_params=SMALL,
         scratch_shapes=[
             pltpu.SMEM((owners,), jnp.int32),
             pltpu.SMEM((owners * capacity,), jnp.int32),
         ],
         cost_estimate=pl.CostEstimate(flops=0, bytes_accessed=1_000_000, transcendentals=0),
         name="table",
-    )(meta)
+    )(place, owner_of_block, kv_cotangent)
 
     def tiles_from(first):
-        inputs = (features, f_sib, kv_cotangent, kv_sib)
+        inputs = (features, f_sib, own_rows, kv_sib)
         return pl.pallas_call(
-            functools.partial(tiles_kernel, owners, col_tiles, first),
+            functools.partial(tiles_kernel, owners, first),
             out_shape=(part, part),
             grid=(1,),
             in_specs=[SMEM] + wholes(inputs),
             out_specs=(whole(part.shape), whole(part.shape)),
-            scratch_shapes=[flipped, flipped],
+            scratch_shapes=[flipped],
             compiler_params=BIG,
             cost_estimate=pl.CostEstimate(
                 flops=2 * owners * 2 * tile * tile * 2 * rows,
@@ -498,7 +505,7 @@
         ],
         compiler_params=BIG,
         name="placed",
-    )(table, meta, fresh, fresh_sib, *sources)
+    )(table, place, fresh, fresh_sib, *sources)
 
 
 def solution(mesh):

time: 82 us -> 75.5 us (0.921)
  Pallas kernels: 24.1 us -> 15.5 us
  waiting for transfers between devices: 26.6 us -> 32.2 us
  local copies, waits for them, and re-layouts: 5.21 us -> 2.88 us
  other arithmetic: 2.15 us -> 0.36 us
  starting transfers between devices: 22.7 us -> 23.6 us
    ppermute x20, waiting for transfers between devices: 26.6 us -> 32.2 us  [swap_along(): return lax.ppermute(values, axis, [(i, i ^ bit) for i in range(size)])]
    pallas_call x3, Pallas kernels: 8.18 us -> 2.91 us  [on_slots(): pl.pallas_call(kernel, out_shape=tuple(outs), grid_spec=pltpu.PrefetchSca...]
    pallas_call x2, Pallas kernels: 6.97 us -> 3.71 us  [sweeping(): pl.pallas_call(kernel, out_shape=jax.ShapeDtypeStruct(values.shape, dtype...]
    unnamed x14 -> x18, local copies, waits for them, and re-layouts: 4.39 us -> 2.86 us
    concatenate x1 -> x0, other arithmetic: 1.21 us -> none  [per_device_dealt(): jnp.concatenate([jnp.stack([here, core]).astype(jnp.int32), owner_of_block])]
    ppermute x20, starting transfers between devices: 22.7 us -> 23.6 us  [swap_along(): return lax.ppermute(values, axis, [(i, i ^ bit) for i in range(size)])]
  transfers between devices with their start and end apart: 20 -> 20, of which waited for: 11 -> 12; matrix products, arithmetic and copies ran while one was open for 3% -> 0% of each run, Pallas kernels for 20% -> 13%
where the time goes in v4:
time: 75.5 us; the launch traced here: 75.4 us
  waiting for transfers between devices  32.2 us (43%)
  starting transfers between devices  23.6 us (31%)
  Pallas kernels  15.5 us (21%)
  local copies, waits for them, and re-layouts  2.88 us (4%)
  between operations  0.85 us (1%)
    ppermute x20, waiting for transfers between devices, swap_along(): return lax.ppermute(values, axis, [(i, i ^ bit) for i in range(size)])  32.2 us
    ppermute x20, starting transfers between devices, swap_along(): return lax.ppermute(values, axis, [(i, i ^ bit) for i in range(size)])  23.6 us
    pallas_call x2, Pallas kernels, tiles_from(): pl.pallas_call(functools.partial(tiles_kernel, owners, first), out_shape=...  4.15 us
    pallas_call x2, Pallas kernels, sweeping(): pl.pallas_call(kernel, out_shape=jax.ShapeDtypeStruct(values.shape, dtype...  3.71 us
    pallas_call x1, Pallas kernels, per_device_dealt(): pl.pallas_call(functools.partial(place_kernel, col_tiles), out_shape=(jax...  3.12 us
    pallas_call x3, Pallas kernels, on_slots(): pl.pallas_call(kernel, out_shape=tuple(outs), grid_spec=pltpu.PrefetchSca...  2.91 us
    unnamed x18, local copies, waits for them, and re-layouts  2.86 us
    pallas_call x1, Pallas kernels, per_device_dealt(): pl.pallas_call(functools.partial(table_kernel, owners, capacity), out_sha...  1.65 us
  transfers between devices with their start and end apart: 20, of which 12 were waited for; matrix products, arithmetic and copies ran while one was open for 0% of the time, Pallas kernels for 13%

profile of v4, /device:TPU:0, one launch (start us, length us, event | category | flops | bytes accessed | tf_op | source)
XLA Modules:
  0.0 75.4 jit_solution(14050280234742411881)
XLA Ops:
  0.6 0.5 collective-permute-start
  1.1 0.1 collective-permute-start.1
  1.2 0.1 pad_add_fusion.place_ref
  1.3 0.9 %copy-done.7 = bf16[256,512]{1,0:T(8,128)(2,1)S(1)} copy-done((bf16[256,512]{1,0:T(8,128)(2,1)S(1)}, bf16[256,512]{1,0:T(8,128)(2,1)}, u32[]{:S(2)}) %copy-start.7) | copy-done | bytes 262168
  2.3 0.7 copy-done.8
  2.9 1.7 %table.1 = (s32[64]{0:T(128)S(1)}, bf16[512,256]{1,0:T(8,128)(2,1)S(1)}) custom-call(s32[2]{0:T(128)S(1)} %pad_add_fusion.place_ref, s32[64]{0:T(128)S(1)} %copy-done.8, bf16[256,512]{1,0:T(8,128)(2,1)S(1)} %copy-done.7), custom_call_target="tpu_custom_call" | custom-call | bytes 1000000 | tf_op jit(solution)/shard_map/table/pallas_call | solution.py:399
  4.6 0.0 copy-start
  4.6 1.2 %copy-done = bf16[256,2048]{1,0:T(8,128)(2,1)S(1)} copy-done((bf16[256,2048]{1,0:T(8,128)(2,1)S(1)}, bf16[256,2048]{1,0:T(8,128)(2,1)}, u32[]{:S(2)}) %copy-start) | copy-done | bytes 1048600
  5.8 2.1 %tiles.3 = (f32[8,128,128]{2,1,0:T(8,128)S(1)}, f32[8,128,128]{2,1,0:T(8,128)S(1)}) custom-call(s32[64]{0:T(128)S(1)} %get-tuple-element.23.table_ref, bf16[256,2048]{1,0:T(8,128)(2,1)S(1)} %copy-done, bf16[256,2048]{1,0:T(8,128)(2,1)S(1)} %collective-permute-done.f_sib, bf16[512,256]{1,0:T(8,128)(2,1)S(1)} %get-tuple-element.24.own_rows, ...), custom_call_target="tpu_custom_call" | custom-call | flops 536870912 | bytes 3500000 | tf_op jit(solution)/shard_map/tiles/pallas_call | solution.py:418
  7.9 3.0 %collective-permute-start.2 = (f32[8,128,128]{2,1,0:T(8,128)S(1)}, f32[8,128,128]{2,1,0:T(8,128)S(1)}, u32[]{:S(2)}, u32[]{:S(2)}) collective-permute-start(f32[8,128,128]{2,1,0:T(8,128)S(1)} %get-tuple-element.26), channel_id=1, source_target_pairs={{0,2},{2,0},{4,6},{6,4},{8,10},{10,8},{12,14},{14,12},{16,18},{18,... | collective-permute-start | bytes 1572872 | tf_op jit(solution)/shard_map/ppermute | solution.py:116
  10.9 1.5 %collective-permute-start.3 = (f32[8,128,128]{2,1,0:T(8,128)S(1)}, f32[8,128,128]{2,1,0:T(8,128)S(1)}, u32[]{:S(2)}, u32[]{:S(2)}) collective-permute-start(f32[8,128,128]{2,1,0:T(8,128)S(1)} %get-tuple-element.28), channel_id=1, source_target_pairs={{0,4},{2,6},{4,0},{6,2},{8,12},{10,14},{12,8},{14,10},{16,20},{18,... | collective-permute-start | bytes 1572872 | tf_op jit(solution)/shard_map/ppermute | solution.py:116
  12.4 2.1 %tiles.2 = (f32[8,128,128]{2,1,0:T(8,128)S(1)}, f32[8,128,128]{2,1,0:T(8,128)S(1)}) custom-call(s32[64]{0:T(128)S(1)} %get-tuple-element.23.table_ref, bf16[256,2048]{1,0:T(8,128)(2,1)S(1)} %copy-done, bf16[256,2048]{1,0:T(8,128)(2,1)S(1)} %collective-permute-done.f_sib, bf16[512,256]{1,0:T(8,128)(2,1)S(1)} %get-tuple-element.24.own_rows, ...), custom_call_target="tpu_custom_call" | custom-call | flops 536870912 | bytes 3500000 | tf_op jit(solution)/shard_map/tiles/pallas_call | solution.py:418
  14.5 8.6 %collective-permute-done.2 = f32[8,128,128]{2,1,0:T(8,128)S(1)} collective-permute-done((f32[8,128,128]{2,1,0:T(8,128)S(1)}, f32[8,128,128]{2,1,0:T(8,128)S(1)}, u32[]{:S(2)}, u32[]{:S(2)}) %collective-permute-start.2) | collective-permute-done | bytes 524320 | tf_op jit(solution)/shard_map/ppermute | solution.py:116
  23.1 0.1 fusion.5
  23.1 0.0 copy-start.1
  23.1 0.0 copy-start.3
  23.1 0.0 copy-start.4
  23.2 1.8 %collective-permute-start.4 = (f32[4,128,128]{2,1,0:T(8,128)S(1)}, f32[4,128,128]{2,1,0:T(8,128)S(1)}, u32[]{:S(2)}, u32[]{:S(2)}) collective-permute-start(f32[4,128,128]{2,1,0:T(8,128)S(1)} %get-tuple-element.46), channel_id=1, source_target_pairs={{0,4},{2,6},{4,0},{6,2},{8,12},{10,14},{12,8},{14,10},{16,20},{18,... | collective-permute-start | bytes 786440 | tf_op jit(solution)/shard_map/ppermute | solution.py:116
  25.0 0.1 fusion.4
  25.1 1.5 %collective-permute-start.5 = (f32[4,128,128]{2,1,0:T(8,128)S(1)}, f32[4,128,128]{2,1,0:T(8,128)S(1)}, u32[]{:S(2)}, u32[]{:S(2)}) collective-permute-start(f32[4,128,128]{2,1,0:T(8,128)S(1)} %get-tuple-element.48), channel_id=1, source_target_pairs={{0,2},{2,0},{4,6},{6,4},{8,10},{10,8},{12,14},{14,12},{16,18},{18,... | collective-permute-start | bytes 786440 | tf_op jit(solution)/shard_map/ppermute | solution.py:116
  26.6 4.4 %collective-permute-done.4 = f32[4,128,128]{2,1,0:T(8,128)S(1)} collective-permute-done((f32[4,128,128]{2,1,0:T(8,128)S(1)}, f32[4,128,128]{2,1,0:T(8,128)S(1)}, u32[]{:S(2)}, u32[]{:S(2)}) %collective-permute-start.4) | collective-permute-done | bytes 262176 | tf_op jit(solution)/shard_map/ppermute | solution.py:116
  31.0 1.3 %collective-permute-done.5 = f32[4,128,128]{2,1,0:T(8,128)S(1)} collective-permute-done((f32[4,128,128]{2,1,0:T(8,128)S(1)}, f32[4,128,128]{2,1,0:T(8,128)S(1)}, u32[]{:S(2)}, u32[]{:S(2)}) %collective-permute-start.5) | collective-permute-done | bytes 262176 | tf_op jit(solution)/shard_map/ppermute | solution.py:116
  32.3 0.1 fusion.1
  32.4 1.6 %collective-permute-start.6 = (f32[2,2,128,128]{3,2,1,0:T(8,128)S(1)}, f32[2,2,128,128]{3,2,1,0:T(8,128)S(1)}, u32[]{:S(2)}, u32[]{:S(2)}) collective-permute-start(f32[2,2,128,128]{3,2,1,0:T(8,128)S(1)} %get-tuple-element.44), channel_id=1, source_target_pairs={{0,8},{2,10},{4,12},{6,14},{8,0},{10,2},{12,4},{14,6},{16,24},{18,... | collective-permute-start | bytes 786440 | tf_op jit(solution)/shard_map/ppermute | solution.py:116
  34.0 4.8 %collective-permute-done.6 = f32[2,2,128,128]{3,2,1,0:T(8,128)S(1)} collective-permute-done((f32[2,2,128,128]{3,2,1,0:T(8,128)S(1)}, f32[2,2,128,128]{3,2,1,0:T(8,128)S(1)}, u32[]{:S(2)}, u32[]{:S(2)}) %collective-permute-start.6) | collective-permute-done | bytes 262176 | tf_op jit(solution)/shard_map/ppermute | solution.py:116
  38.9 3.1 %collective-permute-start.7 = (f32[2,128,128]{2,1,0:T(8,128)S(1)}, f32[2,128,128]{2,1,0:T(8,128)S(1)}, u32[]{:S(2)}, u32[]{:S(2)}) collective-permute-start(f32[2,128,128]{2,1,0:T(8,128)S(1)} %get-tuple-element.49), channel_id=1, source_target_pairs={{0,16},{2,18},{4,20},{6,22},{8,24},{10,26},{12,28},{14,30},{16,0},... | collective-permute-start | bytes 393224 | tf_op jit(solution)/shard_map/ppermute | solution.py:116
  42.0 0.5 rotated.1
  42.5 4.2 %collective-permute-done.7.b_ref = f32[2,128,128]{2,1,0:T(8,128)S(1)} collective-permute-done((f32[2,128,128]{2,1,0:T(8,128)S(1)}, f32[2,128,128]{2,1,0:T(8,128)S(1)}, u32[]{:S(2)}, u32[]{:S(2)}) %collective-permute-start.7) | collective-permute-done | bytes 131104 | tf_op jit(solution)/shard_map/ppermute | solution.py:116
  46.7 0.7 direction.1
  47.5 3.9 %collective-permute-start.10 = (bf16[2,128,128]{2,1,0:T(8,128)(2,1)S(1)}, bf16[2,128,128]{2,1,0:T(8,128)(2,1)S(1)}, u32[]{:S(2)}, u32[]{:S(2)}) collective-permute-start(bf16[2,128,128]{2,1,0:T(8,128)(2,1)S(1)} %get-tuple-element.31), channel_id=1, source_target_pairs={{0,24},{2,26},{4,28},{6,30},{8,16},{10,18},{12,20},{14,22},{16,8},... | collective-permute-start | bytes 196616 | tf_op jit(solution)/shard_map/ppermute | solution.py:116
  51.3 0.6 collective-permute-start.8
  52.0 1.7 %refresh.1.iter_ref = f32[4,128,128]{2,1,0:T(8,128)S(1)} custom-call(s32[1]{0:T(128)} %bitcast.1.side_ref, f32[2,128,128]{2,1,0:T(8,128)S(1)} %get-tuple-element.32.g_ref, f32[4,128,128]{2,1,0:T(8,128)S(1)} %get-tuple-element.33.power_ref, bf16[1,4,128,128]{3,2,1,0:T(8,128)(2,1)S(1)} %copy-done.1, bf16[1,4,128,128]{3,2,1,0:T(8,128)(2,1)S(1)} %copy-done.2), custom_call_target="tpu_custom_call" | custom-call | flops 671088640 | bytes 800000 | tf_op jit(solution)/shard_map/refresh/pallas_call | solution.py:282
  53.7 1.9 %collective-permute-done.9 = bf16[2,128,128]{2,1,0:T(8,128)(2,1)S(1)} collective-permute-done((bf16[2,128,128]{2,1,0:T(8,128)(2,1)S(1)}, bf16[2,128,128]{2,1,0:T(8,128)(2,1)S(1)}, u32[]{:S(2)}, u32[]{:S(2)}) %collective-permute-start.9) | collective-permute-done | bytes 65568 | tf_op jit(solution)/shard_map/ppermute | solution.py:116
  55.6 1.0 %collective-permute-done.8 = bf16[2,128,128]{2,1,0:T(8,128)(2,1)S(1)} collective-permute-done((bf16[2,128,128]{2,1,0:T(8,128)(2,1)S(1)}, bf16[2,128,128]{2,1,0:T(8,128)(2,1)S(1)}, u32[]{:S(2)}, u32[]{:S(2)}) %collective-permute-start.8) | collective-permute-done | bytes 65568 | tf_op jit(solution)/shard_map/ppermute | solution.py:116
  56.6 1.0 %collective-permute-start.11 = (bf16[4,128,128]{2,1,0:T(8,128)(2,1)S(1)}, bf16[4,128,128]{2,1,0:T(8,128)(2,1)S(1)}, u32[]{:S(2)}, u32[]{:S(2)}) collective-permute-start(bf16[4,128,128]{2,1,0:T(8,128)(2,1)S(1)} %get-tuple-element.34), channel_id=1, source_target_pairs={{0,4},{2,6},{4,0},{6,2},{8,12},{10,14},{12,8},{14,10},{16,20},{18,... | collective-permute-start | bytes 393224 | tf_op jit(solution)/shard_map/ppermute | solution.py:116
  57.6 1.1 %collective-permute-start.12 = (bf16[4,128,128]{2,1,0:T(8,128)(2,1)S(1)}, bf16[4,128,128]{2,1,0:T(8,128)(2,1)S(1)}, u32[]{:S(2)}, u32[]{:S(2)}) collective-permute-start(bf16[4,128,128]{2,1,0:T(8,128)(2,1)S(1)} %get-tuple-element.35), channel_id=1, source_target_pairs={{0,2},{2,0},{4,6},{6,4},{8,10},{10,8},{12,14},{14,12},{16,18},{18,... | collective-permute-start | bytes 393224 | tf_op jit(solution)/shard_map/ppermute | solution.py:116
  58.7 1.6 %middle.1.iter_ref = f32[4,128,128]{2,1,0:T(8,128)S(1)} custom-call(f32[4,128,128]{2,1,0:T(8,128)S(1)} %refresh.1.iter_ref), custom_call_target="tpu_custom_call" | custom-call | flops 536870912 | bytes 400000 | tf_op jit(solution)/shard_map/middle/pallas_call | solution.py:337
  60.3 2.0 %collective-permute-done.11 = bf16[4,128,128]{2,1,0:T(8,128)(2,1)S(1)} collective-permute-done((bf16[4,128,128]{2,1,0:T(8,128)(2,1)S(1)}, bf16[4,128,128]{2,1,0:T(8,128)(2,1)S(1)}, u32[]{:S(2)}, u32[]{:S(2)}) %collective-permute-start.11) | collective-permute-done | bytes 131104 | tf_op jit(solution)/shard_map/ppermute | solution.py:116
  62.4 0.2 collective-permute-done.12
  62.6 1.2 %collective-permute-start.13 = (bf16[8,128,128]{2,1,0:T(8,128)(2,1)S(1)}, bf16[8,128,128]{2,1,0:T(8,128)(2,1)S(1)}, u32[]{:S(2)}, u32[]{:S(2)}) collective-permute-start(bf16[8,128,128]{2,1,0:T(8,128)(2,1)S(1)} %pad_maximum_fusion.2.refs_0_), channel_id=1, source_target_pairs={{0,2},{2,0},{4,6},{6,4},{8,10},{10,8},{12,14},{14,12},{16,18},{18,... | collective-permute-start | bytes 786440 | tf_op jit(solution)/shard_map/ppermute | solution.py:116
  63.8 1.5 %collective-permute-start.14 = (bf16[8,128,128]{2,1,0:T(8,128)(2,1)S(1)}, bf16[8,128,128]{2,1,0:T(8,128)(2,1)S(1)}, u32[]{:S(2)}, u32[]{:S(2)}) collective-permute-start(bf16[8,128,128]{2,1,0:T(8,128)(2,1)S(1)} %pad_maximum_fusion.3.refs_2_), channel_id=1, source_target_pairs={{0,4},{2,6},{4,0},{6,2},{8,12},{10,14},{12,8},{14,10},{16,20},{18,... | collective-permute-start | bytes 786440 | tf_op jit(solution)/shard_map/ppermute | solution.py:116
  65.3 0.5 collective-permute-start.18
  65.8 2.1 %finish.1.own_ref = bf16[4,128,128]{2,1,0:T(8,128)(2,1)S(1)} custom-call(f32[4,128,128]{2,1,0:T(8,128)S(1)} %middle.1.iter_ref), custom_call_target="tpu_custom_call" | custom-call | flops 671088640 | bytes 400000 | tf_op jit(solution)/shard_map/finish/pallas_call | solution.py:337
  67.9 1.1 %collective-permute-done.13.refs_1_ = bf16[8,128,128]{2,1,0:T(8,128)(2,1)S(1)} collective-permute-done((bf16[8,128,128]{2,1,0:T(8,128)(2,1)S(1)}, bf16[8,128,128]{2,1,0:T(8,128)(2,1)S(1)}, u32[]{:S(2)}, u32[]{:S(2)}) %collective-permute-start.13) | collective-permute-done | bytes 262176 | tf_op jit(solution)/shard_map/ppermute | solution.py:116
  69.1 1.1 %collective-permute-done.14.refs_3_ = bf16[8,128,128]{2,1,0:T(8,128)(2,1)S(1)} collective-permute-done((bf16[8,128,128]{2,1,0:T(8,128)(2,1)S(1)}, bf16[8,128,128]{2,1,0:T(8,128)(2,1)S(1)}, u32[]{:S(2)}, u32[]{:S(2)}) %collective-permute-start.14) | collective-permute-done | bytes 262176 | tf_op jit(solution)/shard_map/ppermute | solution.py:116
  70.2 0.5 collective-permute-start.19
  70.7 1.6 %collective-permute-done.15.sib_ref = bf16[4,128,128]{2,1,0:T(8,128)(2,1)S(1)} collective-permute-done((bf16[4,128,128]{2,1,0:T(8,128)(2,1)S(1)}, bf16[4,128,128]{2,1,0:T(8,128)(2,1)S(1)}, u32[]{:S(2)}, u32[]{:S(2)}) %collective-permute-start.15) | collective-permute-done | bytes 131104 | tf_op jit(solution)/shard_map/ppermute | solution.py:116
  72.3 3.1 %placed.1 = (bf16[2048,512]{1,0:T(8,128)(2,1)}, bf16[1,4,128,128]{3,2,1,0:T(8,128)(2,1)}, bf16[1,4,128,128]{3,2,1,0:T(8,128)(2,1)}) custom-call(s32[64]{0:T(128)S(1)} %get-tuple-element.23.table_ref, s32[2]{0:T(128)S(1)} %pad_add_fusion.place_ref, bf16[4,128,128]{2,1,0:T(8,128)(2,1)S(1)} %finish.1.own_ref, ...), custom_call_target="tpu_custom_call" | custom-call | tf_op jit(solution)/shard_map/placed/pallas_call | solution.py:496
  (31 shorter events, 0.2 us)
Async XLA Ops:
  0.6 4.0 %collective-permute-start = (bf16[256,2048]{1,0:T(8,128)(2,1)}, bf16[256,2048]{1,0:T(8,128)(2,1)S(1)}, u32[]{:S(2)}, u32[]{:S(2)}) collective-permute-start(bf16[256,2048]{1,0:T(8,128)(2,1)} %f_own.3), channel_id=1, source_target_pairs={{0,1},{1,0},{2,3},{3,2},{4,5},{5,4},{6,7},{7,6},{8,9},{9,8},{10,11... | collective-permute-start | bytes 3145736 | tf_op jit(solution)/shard_map/ppermute | solution.py:116
  1.1 3.4 %collective-permute-start.1 = (bf16[256,512]{1,0:T(8,128)(2,1)}, bf16[256,512]{1,0:T(8,128)(2,1)S(1)}, u32[]{:S(2)}, u32[]{:S(2)}) collective-permute-start(bf16[256,512]{1,0:T(8,128)(2,1)} %kv_ref.1), channel_id=1, source_target_pairs={{0,1},{1,0},{2,3},{3,2},{4,5},{5,4},{6,7},{7,6},{8,9},{9,8},{10,11... | collective-permute-start | bytes 786440 | tf_op jit(solution)/shard_map/ppermute | solution.py:116
  1.3 0.9 %copy-start.7 = (bf16[256,512]{1,0:T(8,128)(2,1)S(1)}, bf16[256,512]{1,0:T(8,128)(2,1)}, u32[]{:S(2)}) copy-start(bf16[256,512]{1,0:T(8,128)(2,1)} %kv_ref.1) | copy-start | bytes 786436
  2.3 0.7 copy-start.8
  4.6 1.2 %copy-start = (bf16[256,2048]{1,0:T(8,128)(2,1)S(1)}, bf16[256,2048]{1,0:T(8,128)(2,1)}, u32[]{:S(2)}) copy-start(bf16[256,2048]{1,0:T(8,128)(2,1)} %f_own.3) | copy-start | bytes 3145732
  7.9 15.1 %collective-permute-start.2 = (f32[8,128,128]{2,1,0:T(8,128)S(1)}, f32[8,128,128]{2,1,0:T(8,128)S(1)}, u32[]{:S(2)}, u32[]{:S(2)}) collective-permute-start(f32[8,128,128]{2,1,0:T(8,128)S(1)} %get-tuple-element.26), channel_id=1, source_target_pairs={{0,2},{2,0},{4,6},{6,4},{8,10},{10,8},{12,14},{14,12},{16,18},{18,... | collective-permute-start | bytes 1572872 | tf_op jit(solution)/shard_map/ppermute | solution.py:116
  10.9 14.1 %collective-permute-start.3 = (f32[8,128,128]{2,1,0:T(8,128)S(1)}, f32[8,128,128]{2,1,0:T(8,128)S(1)}, u32[]{:S(2)}, u32[]{:S(2)}) collective-permute-start(f32[8,128,128]{2,1,0:T(8,128)S(1)} %get-tuple-element.28), channel_id=1, source_target_pairs={{0,4},{2,6},{4,0},{6,2},{8,12},{10,14},{12,8},{14,10},{16,20},{18,... | collective-permute-start | bytes 1572872 | tf_op jit(solution)/shard_map/ppermute | solution.py:116
  23.1 18.9 %copy-start.1 = (bf16[1,4,128,128]{3,2,1,0:T(8,128)(2,1)S(1)}, bf16[1,4,128,128]{3,2,1,0:T(8,128)(2,1)}, u32[]{:S(2)}) copy-start(bf16[1,4,128,128]{3,2,1,0:T(8,128)(2,1)} %ql_ref.5) | copy-start | bytes 393220
  23.1 18.9 %copy-start.2 = (bf16[1,4,128,128]{3,2,1,0:T(8,128)(2,1)S(1)}, bf16[1,4,128,128]{3,2,1,0:T(8,128)(2,1)}, u32[]{:S(2)}) copy-start(bf16[1,4,128,128]{3,2,1,0:T(8,128)(2,1)} %qr_ref.5) | copy-start | bytes 393220
  23.1 18.9 %copy-start.3 = (f32[1,4,128,128]{3,2,1,0:T(8,128)S(1)}, f32[1,4,128,128]{3,2,1,0:T(8,128)}, u32[]{:S(2)}) copy-start(f32[1,4,128,128]{3,2,1,0:T(8,128)} %m_ref.1) | copy-start | bytes 786436
  23.1 18.9 %copy-start.4 = (f32[1,4,128,128]{3,2,1,0:T(8,128)S(1)}, f32[1,4,128,128]{3,2,1,0:T(8,128)}, u32[]{:S(2)}) copy-start(f32[1,4,128,128]{3,2,1,0:T(8,128)} %v_ref.1) | copy-start | bytes 786436
  23.2 18.8 %copy-start.5 = (f32[1,4,128,128]{3,2,1,0:T(8,128)S(1)}, f32[1,4,128,128]{3,2,1,0:T(8,128)}, u32[]{:S(2)}) copy-start(f32[1,4,128,128]{3,2,1,0:T(8,128)} %l_ref.1) | copy-start | bytes 786436
  23.2 18.8 %copy-start.6 = (f32[1,4,128,128]{3,2,1,0:T(8,128)S(1)}, f32[1,4,128,128]{3,2,1,0:T(8,128)}, u32[]{:S(2)}) copy-start(f32[1,4,128,128]{3,2,1,0:T(8,128)} %r_ref.1) | copy-start | bytes 786436
  23.2 7.8 %collective-permute-start.4 = (f32[4,128,128]{2,1,0:T(8,128)S(1)}, f32[4,128,128]{2,1,0:T(8,128)S(1)}, u32[]{:S(2)}, u32[]{:S(2)}) collective-permute-start(f32[4,128,128]{2,1,0:T(8,128)S(1)} %get-tuple-element.46), channel_id=1, source_target_pairs={{0,4},{2,6},{4,0},{6,2},{8,12},{10,14},{12,8},{14,10},{16,20},{18,... | collective-permute-start | bytes 786440 | tf_op jit(solution)/shard_map/ppermute | solution.py:116
  25.1 7.2 %collective-permute-start.5 = (f32[4,128,128]{2,1,0:T(8,128)S(1)}, f32[4,128,128]{2,1,0:T(8,128)S(1)}, u32[]{:S(2)}, u32[]{:S(2)}) collective-permute-start(f32[4,128,128]{2,1,0:T(8,128)S(1)} %get-tuple-element.48), channel_id=1, source_target_pairs={{0,2},{2,0},{4,6},{6,4},{8,10},{10,8},{12,14},{14,12},{16,18},{18,... | collective-permute-start | bytes 786440 | tf_op jit(solution)/shard_map/ppermute | solution.py:116
  32.4 6.4 %collective-permute-start.6 = (f32[2,2,128,128]{3,2,1,0:T(8,128)S(1)}, f32[2,2,128,128]{3,2,1,0:T(8,128)S(1)}, u32[]{:S(2)}, u32[]{:S(2)}) collective-permute-start(f32[2,2,128,128]{3,2,1,0:T(8,128)S(1)} %get-tuple-element.44), channel_id=1, source_target_pairs={{0,8},{2,10},{4,12},{6,14},{8,0},{10,2},{12,4},{14,6},{16,24},{18,... | collective-permute-start | bytes 786440 | tf_op jit(solution)/shard_map/ppermute | solution.py:116
  38.9 7.9 %collective-permute-start.7 = (f32[2,128,128]{2,1,0:T(8,128)S(1)}, f32[2,128,128]{2,1,0:T(8,128)S(1)}, u32[]{:S(2)}, u32[]{:S(2)}) collective-permute-start(f32[2,128,128]{2,1,0:T(8,128)S(1)} %get-tuple-element.49), channel_id=1, source_target_pairs={{0,16},{2,18},{4,20},{6,22},{8,24},{10,26},{12,28},{14,30},{16,0},... | collective-permute-start | bytes 393224 | tf_op jit(solution)/shard_map/ppermute | solution.py:116
  47.5 6.3 %collective-permute-start.10 = (bf16[2,128,128]{2,1,0:T(8,128)(2,1)S(1)}, bf16[2,128,128]{2,1,0:T(8,128)(2,1)S(1)}, u32[]{:S(2)}, u32[]{:S(2)}) collective-permute-start(bf16[2,128,128]{2,1,0:T(8,128)(2,1)S(1)} %get-tuple-element.31), channel_id=1, source_target_pairs={{0,24},{2,26},{4,28},{6,30},{8,16},{10,18},{12,20},{14,22},{16,8},... | collective-permute-start | bytes 196616 | tf_op jit(solution)/shard_map/ppermute | solution.py:116
  51.3 4.3 %collective-permute-start.9 = (bf16[2,128,128]{2,1,0:T(8,128)(2,1)S(1)}, bf16[2,128,128]{2,1,0:T(8,128)(2,1)S(1)}, u32[]{:S(2)}, u32[]{:S(2)}) collective-permute-start(bf16[2,128,128]{2,1,0:T(8,128)(2,1)S(1)} %get-tuple-element.31), channel_id=1, source_target_pairs={{0,8},{2,10},{4,12},{6,14},{8,0},{10,2},{12,4},{14,6},{16,24},{18,... | collective-permute-start | bytes 196616 | tf_op jit(solution)/shard_map/ppermute | solution.py:116
  51.3 5.2 %collective-permute-start.8 = (bf16[2,128,128]{2,1,0:T(8,128)(2,1)S(1)}, bf16[2,128,128]{2,1,0:T(8,128)(2,1)S(1)}, u32[]{:S(2)}, u32[]{:S(2)}) collective-permute-start(bf16[2,128,128]{2,1,0:T(8,128)(2,1)S(1)} %get-tuple-element.31), channel_id=1, source_target_pairs={{0,16},{2,18},{4,20},{6,22},{8,24},{10,26},{12,28},{14,30},{16,0},... | collective-permute-start | bytes 196616 | tf_op jit(solution)/shard_map/ppermute | solution.py:116
  56.6 5.7 %collective-permute-start.11 = (bf16[4,128,128]{2,1,0:T(8,128)(2,1)S(1)}, bf16[4,128,128]{2,1,0:T(8,128)(2,1)S(1)}, u32[]{:S(2)}, u32[]{:S(2)}) collective-permute-start(bf16[4,128,128]{2,1,0:T(8,128)(2,1)S(1)} %get-tuple-element.34), channel_id=1, source_target_pairs={{0,4},{2,6},{4,0},{6,2},{8,12},{10,14},{12,8},{14,10},{16,20},{18,... | collective-permute-start | bytes 393224 | tf_op jit(solution)/shard_map/ppermute | solution.py:116
  57.6 5.0 %collective-permute-start.12 = (bf16[4,128,128]{2,1,0:T(8,128)(2,1)S(1)}, bf16[4,128,128]{2,1,0:T(8,128)(2,1)S(1)}, u32[]{:S(2)}, u32[]{:S(2)}) collective-permute-start(bf16[4,128,128]{2,1,0:T(8,128)(2,1)S(1)} %get-tuple-element.35), channel_id=1, source_target_pairs={{0,2},{2,0},{4,6},{6,4},{8,10},{10,8},{12,14},{14,12},{16,18},{18,... | collective-permute-start | bytes 393224 | tf_op jit(solution)/shard_map/ppermute | solution.py:116
  62.6 6.4 %collective-permute-start.13 = (bf16[8,128,128]{2,1,0:T(8,128)(2,1)S(1)}, bf16[8,128,128]{2,1,0:T(8,128)(2,1)S(1)}, u32[]{:S(2)}, u32[]{:S(2)}) collective-permute-start(bf16[8,128,128]{2,1,0:T(8,128)(2,1)S(1)} %pad_maximum_fusion.2.refs_0_), channel_id=1, source_target_pairs={{0,2},{2,0},{4,6},{6,4},{8,10},{10,8},{12,14},{14,12},{16,18},{18,... | collective-permute-start | bytes 786440 | tf_op jit(solution)/shard_map/ppermute | solution.py:116
  63.8 6.4 %collective-permute-start.14 = (bf16[8,128,128]{2,1,0:T(8,128)(2,1)S(1)}, bf16[8,128,128]{2,1,0:T(8,128)(2,1)S(1)}, u32[]{:S(2)}, u32[]{:S(2)}) collective-permute-start(bf16[8,128,128]{2,1,0:T(8,128)(2,1)S(1)} %pad_maximum_fusion.3.refs_2_), channel_id=1, source_target_pairs={{0,4},{2,6},{4,0},{6,2},{8,12},{10,14},{12,8},{14,10},{16,20},{18,... | collective-permute-start | bytes 786440 | tf_op jit(solution)/shard_map/ppermute | solution.py:116
  65.3 5.4 %collective-permute-start.16 = (bf16[8,128,128]{2,1,0:T(8,128)(2,1)S(1)}, bf16[8,128,128]{2,1,0:T(8,128)(2,1)S(1)}, u32[]{:S(2)}, u32[]{:S(2)}) collective-permute-start(bf16[8,128,128]{2,1,0:T(8,128)(2,1)S(1)} %pad_maximum_fusion.2.refs_0_), channel_id=1, source_target_pairs={{0,1},{1,0},{2,3},{3,2},{4,5},{5,4},{6,7},{7,6},{8,9},{9,8},{10,11... | collective-permute-start | bytes 786440 | tf_op jit(solution)/shard_map/ppermute | solution.py:116
  65.3 5.4 %collective-permute-start.18 = (bf16[8,128,128]{2,1,0:T(8,128)(2,1)S(1)}, bf16[8,128,128]{2,1,0:T(8,128)(2,1)S(1)}, u32[]{:S(2)}, u32[]{:S(2)}) collective-permute-start(bf16[8,128,128]{2,1,0:T(8,128)(2,1)S(1)} %pad_maximum_fusion.3.refs_2_), channel_id=1, source_target_pairs={{0,1},{1,0},{2,3},{3,2},{4,5},{5,4},{6,7},{7,6},{8,9},{9,8},{10,11... | collective-permute-start | bytes 786440 | tf_op jit(solution)/shard_map/ppermute | solution.py:116
  70.1 2.1 %collective-permute-start.17 = (bf16[8,128,128]{2,1,0:T(8,128)(2,1)S(1)}, bf16[8,128,128]{2,1,0:T(8,128)(2,1)S(1)}, u32[]{:S(2)}, u32[]{:S(2)}) collective-permute-start(bf16[8,128,128]{2,1,0:T(8,128)(2,1)S(1)} %collective-permute-done.13.refs_1_), channel_id=1, source_target_pairs={{0,1},{1,0},{2,3},{3,2},{4,5},{5,4},{6,7},{7,6},{8,9},{9,8},{10,11... | collective-permute-start | bytes 786440 | tf_op jit(solution)/shard_map/ppermute | solution.py:116
  70.2 2.1 %collective-permute-start.19 = (bf16[8,128,128]{2,1,0:T(8,128)(2,1)S(1)}, bf16[8,128,128]{2,1,0:T(8,128)(2,1)S(1)}, u32[]{:S(2)}, u32[]{:S(2)}) collective-permute-start(bf16[8,128,128]{2,1,0:T(8,128)(2,1)S(1)} %collective-permute-done.14.refs_3_), channel_id=1, source_target_pairs={{0,1},{1,0},{2,3},{3,2},{4,5},{5,4},{6,7},{7,6},{8,9},{9,8},{10,11... | collective-permute-start | bytes 786440 | tf_op jit(solution)/shard_map/ppermute | solution.py:116
  70.7 1.6 %collective-permute-start.15 = (bf16[4,128,128]{2,1,0:T(8,128)(2,1)S(1)}, bf16[4,128,128]{2,1,0:T(8,128)(2,1)S(1)}, u32[]{:S(2)}, u32[]{:S(2)}) collective-permute-start(bf16[4,128,128]{2,1,0:T(8,128)(2,1)S(1)} %finish.1.own_ref), channel_id=1, source_target_pairs={{0,1},{1,0},{2,3},{3,2},{4,5},{5,4},{6,7},{7,6},{8,9},{9,8},{10,11... | collective-permute-start | bytes 393224 | tf_op jit(solution)/shard_map/ppermute | solution.py:116

commit v5 on v4

--- a/solution.py
+++ b/solution.py
@@ -112,8 +112,16 @@
 TM = ((0,), (0,))
 
 
-def swap_along(values, axis, size, bit):
-    return lax.ppermute(values, axis, [(i, i ^ bit) for i in range(size)])
+BOTH = ("dp", "inner")
+
+
+def swap_cores(values):
+    return lax.ppermute(values, "inner", [(0, 1), (1, 0)])
+
+
+def swap_owners(values, owners, flips):
+    pairs = [(2 * o + c, 2 * (o ^ flips[c]) + c) for o in range(owners) for c in range(2)]
+    return lax.ppermute(values, BOTH, pairs)
 
 
 def dot(left, right, dims):
@@ -160,7 +168,7 @@
     return dot(beside(high, rest), above(low, low), MM)
 
 
-def stream_offsets(owners):
+def core_orders(owners):
     bits = owners.bit_length() - 1
     orders = ([0, 1] + list(range(2, bits)), [1, 0] + list(range(2, bits)))
     offsets = [
@@ -196,32 +204,31 @@
 
     lax.fori_loop(0, owners * capacity, enter, 0, unroll=8)
     here, core = place_ref[0], place_ref[1]
-    offsets = stream_offsets(owners)[1]
+    offsets = core_orders(owners)[1]
     for side in range(2):
-        first_slot = 2 * (core ^ side)
-        for stream in range(2):
-            for p in range(owners):
-                entry = (side * 2 + stream) * owners + p
-                table_ref[entry] = held[(here ^ offsets[stream][p]) * capacity + first_slot + stream]
-
-
-def tiles_kernel(owners, first, table_ref, f_own, f_sib, own_rows, kv_sib, *rest):
-    out_a, out_b, sib_rows = rest
-    tile = out_a.shape[-1]
+        at = core ^ side
+        for p in range(owners):
+            offset = offsets[0][p] + at * (offsets[1][p] - offsets[0][p])
+            first = (here ^ offset) * capacity + 2 * at
+            for k in range(2):
+                table_ref[(side * owners + p) * 2 + k] = held[first + k]
+
+
+def tiles_kernel(first, table_ref, f_own, f_sib, own_rows, kv_sib, out_ref, sib_rows):
+    tile = out_ref.shape[-1]
     col_tiles = own_rows.shape[0] // tile
     sib_rows[...] = kv_sib[...].T
-    for stream, out in enumerate((out_a, out_b)):
-
-        def one(i, carry, stream=stream, out=out):
-            block = table_ref[stream * owners + first + i]
-            at = pl.ds(pl.multiple_of(block // col_tiles * tile, tile), tile)
-            cots = pl.ds(pl.multiple_of(block % col_tiles * tile, tile), tile)
-            out[i] = dot(own_rows[cots, :], f_own[:, at], MM) + dot(
-                sib_rows[cots, :], f_sib[:, at], MM
-            )
-            return carry
-
-        lax.fori_loop(0, owners // 2, one, 0, unroll=4)
+
+    def one(i, carry):
+        block = table_ref[first + i]
+        at = pl.ds(pl.multiple_of(block // col_tiles * tile, tile), tile)
+        cots = pl.ds(pl.multiple_of(block % col_tiles * tile, tile), tile)
+        out_ref[i] = dot(own_rows[cots, :], f_own[:, at], MM) + dot(
+            sib_rows[cots, :], f_sib[:, at], MM
+        )
+        return carry
+
+    lax.fori_loop(0, out_ref.shape[0], one, 0, unroll=8)
 
 
 SMEM = pl.BlockSpec(memory_space=pltpu.SMEM)
@@ -388,13 +395,13 @@
     core = lax.axis_index("inner")
     place = jnp.stack([here, core]).astype(jnp.int32)
     side = core.reshape(1).astype(jnp.int32)
-    orders = stream_offsets(owners)[0]
-    near = owners // 2
-
-    f_sib = swap_along(features, "inner", 2, 1)
-    kv_sib = swap_along(kv_cotangent, "inner", 2, 1)
+    orders = core_orders(owners)[0]
+    bits = len(orders[0])
+
+    f_sib = swap_cores(features)
+    kv_sib = swap_cores(kv_cotangent)
     flipped = pltpu.VMEM((width, rows), jnp.bfloat16)
-    part = jax.ShapeDtypeStruct((near, tile, tile), jnp.float32)
+    part = jax.ShapeDtypeStruct((owners, tile, tile), jnp.float32)
     f32_pair = jax.ShapeDtypeStruct((2, tile, tile), jnp.float32)
     table, own_rows = pl.pallas_call(
         functools.partial(table_kernel, owners, capacity),
@@ -416,11 +423,11 @@
     def tiles_from(first):
         inputs = (features, f_sib, own_rows, kv_sib)
         return pl.pallas_call(
-            functools.partial(tiles_kernel, owners, first),
-            out_shape=(part, part),
+            functools.partial(tiles_kernel, first),
+            out_shape=part,
             grid=(1,),
             in_specs=[SMEM] + wholes(inputs),
-            out_specs=(whole(part.shape), whole(part.shape)),
+            out_specs=whole(part.shape),
             scratch_shapes=[flipped],
             compiler_params=BIG,
             cost_estimate=pl.CostEstimate(
@@ -431,10 +438,11 @@
             name="tiles",
         )(table, *inputs)
 
-    sent_a, sent_b = tiles_from(near)
-    got_a = swap_along(sent_a, "dp", owners, 1 << orders[0][0])
-    got_b = swap_along(sent_b, "dp", owners, 1 << orders[1][0])
-    kept_a, kept_b = tiles_from(0)
+    def exchanged(values, step):
+        return swap_owners(values, owners, [1 << order[step] for order in orders])
+
+    got = exchanged(tiles_from(owners), 0)
+    kept = tiles_from(0)
     quad = jax.ShapeDtypeStruct((4, tile, tile), jnp.float32)
     moment_rot, second, power = on_slots(
         rotated_kernel,
@@ -445,18 +453,11 @@
         16 * 2 * tile**3,
     )
 
-    half = near // 2
-    next_a = swap_along(kept_a[half:] + got_a[half:], "dp", owners, 1 << orders[0][1])
-    next_b = swap_along(kept_b[half:] + got_b[half:], "dp", owners, 1 << orders[1][1])
-    kept = jnp.stack([kept_a[:half] + got_a[:half], kept_b[:half] + got_b[:half]], axis=1)
-    got = jnp.stack([next_a, next_b], axis=1)
-    for bit in orders[0][2:]:
+    for step in range(1, bits):
         half = kept.shape[0] // 2
         sent = kept[half:] + got[half:]
         kept = kept[:half] + got[:half]
-        if half == 1:
-            sent, kept = sent[0], kept[0]
-        got = swap_along(sent, "dp", owners, 1 << bit)
+        got = exchanged(sent, step)
     direction, grads = on_slots(
         direction_kernel,
         side,
@@ -466,12 +467,10 @@
         16 * 2 * tile**3,
     )
 
-    bits = len(orders[0])
-    high = owners // 4
-    tiles = []
-    for p in range(high):
-        offset = sum(((p >> (bits - 3 - i)) & 1) << bit for i, bit in enumerate(orders[0][2:]))
-        tiles.append(swap_along(direction, "dp", owners, offset) if offset else direction)
+    mine = []
+    for p in range(owners // 4):
+        offset = core_orders(owners)[1][0][p]
+        mine.append(swap_owners(direction, owners, (offset, offset)) if p else direction)
     values = on_slots(
         refresh_kernel,
         side,
@@ -480,18 +479,17 @@
         (quad,),
         4 * (4 + 2 * STAGES[0]) * 4 * 2 * tile**3,
     )[0]
-    mine = [jnp.stack([t[stream] for t in tiles]) for stream in range(2)]
+    mine = jnp.concatenate(mine, axis=0)
     mine, values = lax.optimization_barrier((mine, values))
-    other = [swap_along(m, "dp", owners, 1 << order[1]) for m, order in zip(mine, orders)]
+    other = exchanged(mine, 1)
     values = sweeping(middle_kernel, values, jnp.float32, STAGES[1])
-    mine = [jnp.concatenate(both, axis=0) for both in zip(mine, other)]
+    mine = jnp.concatenate([mine, other], axis=0)
     mine, values = lax.optimization_barrier((mine, values))
-    other = [swap_along(m, "dp", owners, 1 << order[0]) for m, order in zip(mine, orders)]
+    other = exchanged(mine, 0)
     fresh = sweeping(finish_kernel, values, jnp.bfloat16, STAGES[2])
     other, fresh = lax.optimization_barrier((other, fresh))
-    fresh_sib = swap_along(fresh, "inner", 2, 1)
-    gathered = [part for both in zip(mine, other) for part in both]
-    sources = gathered + [swap_along(g, "inner", 2, 1) for g in gathered]
+    fresh_sib = swap_cores(fresh)
+    sources = [mine, other, swap_cores(mine), swap_cores(other)]
     basis = jax.ShapeDtypeStruct(left_basis.shape, left_basis.dtype)
     return pl.pallas_call(
         functools.partial(place_kernel, col_tiles),

time: 75.5 us -> 81.6 us (1.081)
  waiting for transfers between devices: 32.2 us -> 43.1 us
  starting transfers between devices: 23.6 us -> 19.4 us
    ppermute x20 -> x14, waiting for transfers between devices: 32.2 us -> 43.1 us  [the longest x9 41.5 us: swap_owners(): return lax.ppermute(values, BOTH, pairs)]
    ppermute x20 -> x14, starting transfers between devices: 23.6 us -> 19.4 us  [the longest x9 18.3 us: swap_owners(): return lax.ppermute(values, BOTH, pairs)]
  transfers between devices with their start and end apart: 20 -> 14, of which waited for: 12 -> 9; matrix products, arithmetic and copies ran while one was open for 0% -> 0% of each run, Pallas kernels for 13% -> 11%
where the time goes in v5:
time: 81.6 us; the launch traced here: 81.4 us
  waiting for transfers between devices  43.1 us (53%)
  starting transfers between devices  19.4 us (24%)
  Pallas kernels  14.8 us (18%)
  local copies, waits for them, and re-layouts  2.86 us (4%)
  between operations  0.82 us (1%)
    ppermute x9, waiting for transfers between devices, swap_owners(): return lax.ppermute(values, BOTH, pairs)  41.5 us
    ppermute x9, starting transfers between devices, swap_owners(): return lax.ppermute(values, BOTH, pairs)  18.3 us
    pallas_call x2, Pallas kernels, sweeping(): pl.pallas_call(kernel, out_shape=jax.ShapeDtypeStruct(values.shape, dtype...  3.7 us
    pallas_call x2, Pallas kernels, tiles_from(): pl.pallas_call(functools.partial(tiles_kernel, first), out_shape=part, gr...  3.45 us
    pallas_call x1, Pallas kernels, per_device_dealt(): pl.pallas_call(functools.partial(place_kernel, col_tiles), out_shape=(jax...  3.12 us
    pallas_call x3, Pallas kernels, on_slots(): pl.pallas_call(kernel, out_shape=tuple(outs), grid_spec=pltpu.PrefetchSca...  2.92 us
    unnamed x18, local copies, waits for them, and re-layouts  2.86 us
    pallas_call x1, Pallas kernels, per_device_dealt(): pl.pallas_call(functools.partial(table_kernel, owners, capacity), out_sha...  1.65 us
  transfers between devices with their start and end apart: 14, of which 9 were waited for; matrix products, arithmetic and copies ran while one was open for 0% of the time, Pallas kernels for 11%

profile of v5, /device:TPU:0, one launch (start us, length us, event | category | flops | bytes accessed | tf_op | source)
XLA Modules:
  0.0 81.4 jit_solution(12674321611877432216)
XLA Ops:
  0.6 0.5 collective-permute-start
  1.1 0.1 collective-permute-start.1
  1.2 0.1 pad_add_fusion.place_ref
  1.3 0.9 %copy-done.7 = bf16[256,512]{1,0:T(8,128)(2,1)S(1)} copy-done((bf16[256,512]{1,0:T(8,128)(2,1)S(1)}, bf16[256,512]{1,0:T(8,128)(2,1)}, u32[]{:S(2)}) %copy-start.7) | copy-done | bytes 262168
  2.3 0.7 copy-done.8
  2.9 1.6 %table.1 = (s32[64]{0:T(128)S(1)}, bf16[512,256]{1,0:T(8,128)(2,1)S(1)}) custom-call(s32[2]{0:T(128)S(1)} %pad_add_fusion.place_ref, s32[64]{0:T(128)S(1)} %copy-done.8, bf16[256,512]{1,0:T(8,128)(2,1)S(1)} %copy-done.7), custom_call_target="tpu_custom_call" | custom-call | bytes 1000000 | tf_op jit(solution)/shard_map/table/pallas_call | solution.py:406
  4.6 0.0 collective-permute-done.1.kv_sib
  4.6 0.0 collective-permute-done.f_sib
  4.6 0.0 copy-start
  4.6 1.2 %copy-done = bf16[256,2048]{1,0:T(8,128)(2,1)S(1)} copy-done((bf16[256,2048]{1,0:T(8,128)(2,1)S(1)}, bf16[256,2048]{1,0:T(8,128)(2,1)}, u32[]{:S(2)}) %copy-start) | copy-done | bytes 1048600
  5.8 1.7 %tiles.3 = f32[16,128,128]{2,1,0:T(8,128)S(1)} custom-call(s32[64]{0:T(128)S(1)} %get-tuple-element.16.table_ref, bf16[256,2048]{1,0:T(8,128)(2,1)S(1)} %copy-done, bf16[256,2048]{1,0:T(8,128)(2,1)S(1)} %collective-permute-done.f_sib, bf16[512,256]{1,0:T(8,128)(2,1)S(1)} %get-tuple-element.17.own_rows, bf16[256,512]{1,0:T(8,128)(2,1)S(1)} %collective-permute-done.1.kv_sib), custom_call_target="tpu_custom_call" | custom-call | flops 536870912 | bytes 3500000 | tf_op jit(solution)/shard_map/tiles/pallas_call | solution.py:425
  7.6 3.0 %collective-permute-start.2 = (f32[16,128,128]{2,1,0:T(8,128)S(1)}, f32[16,128,128]{2,1,0:T(8,128)S(1)}, u32[]{:S(2)}, u32[]{:S(2)}) collective-permute-start(f32[16,128,128]{2,1,0:T(8,128)S(1)} %tiles.3), channel_id=1, source_target_pairs={{0,2},{1,5},{2,0},{3,7},{4,6},{5,1},{6,4},{7,3},{8,10},{9,13},{10,... | collective-permute-start | bytes 3145736 | tf_op jit(solution)/shard_map/ppermute | solution.py:124
  10.5 1.7 %tiles.2 = f32[16,128,128]{2,1,0:T(8,128)S(1)} custom-call(s32[64]{0:T(128)S(1)} %get-tuple-element.16.table_ref, bf16[256,2048]{1,0:T(8,128)(2,1)S(1)} %copy-done, bf16[256,2048]{1,0:T(8,128)(2,1)S(1)} %collective-permute-done.f_sib, bf16[512,256]{1,0:T(8,128)(2,1)S(1)} %get-tuple-element.17.own_rows, bf16[256,512]{1,0:T(8,128)(2,1)S(1)} %collective-permute-done.1.kv_sib), custom_call_target="tpu_custom_call" | custom-call | flops 536870912 | bytes 3500000 | tf_op jit(solution)/shard_map/tiles/pallas_call | solution.py:425
  12.2 0.0 copy-start.1
  12.3 0.0 copy-start.2
  12.3 0.0 copy-start.3
  12.3 0.0 copy-start.4
  12.3 0.0 copy-start.5
  12.3 0.0 copy-start.6
  12.3 11.0 %collective-permute-done.2 = f32[16,128,128]{2,1,0:T(8,128)S(1)} collective-permute-done((f32[16,128,128]{2,1,0:T(8,128)S(1)}, f32[16,128,128]{2,1,0:T(8,128)S(1)}, u32[]{:S(2)}, u32[]{:S(2)}) %collective-permute-start.2) | collective-permute-done | bytes 1048608 | tf_op jit(solution)/shard_map/ppermute | solution.py:124
  23.3 0.1 slice_add_fusion.1
  23.4 2.1 %collective-permute-start.3 = (f32[8,128,128]{2,1,0:T(8,128)S(1)}, f32[8,128,128]{2,1,0:T(8,128)S(1)}, u32[]{:S(2)}, u32[]{:S(2)}) collective-permute-start(f32[8,128,128]{2,1,0:T(8,128)S(1)} %get-tuple-element.30), channel_id=1, source_target_pairs={{0,4},{1,3},{2,6},{3,1},{4,0},{5,7},{6,2},{7,5},{8,12},{9,11},{10,... | collective-permute-start | bytes 1572872 | tf_op jit(solution)/shard_map/ppermute | solution.py:124
  25.5 7.2 %collective-permute-done.3 = f32[8,128,128]{2,1,0:T(8,128)S(1)} collective-permute-done((f32[8,128,128]{2,1,0:T(8,128)S(1)}, f32[8,128,128]{2,1,0:T(8,128)S(1)}, u32[]{:S(2)}, u32[]{:S(2)}) %collective-permute-start.3) | collective-permute-done | bytes 524320 | tf_op jit(solution)/shard_map/ppermute | solution.py:124
  32.7 0.1 slice_add_fusion.3
  32.8 2.1 %collective-permute-start.4 = (f32[4,128,128]{2,1,0:T(8,128)S(1)}, f32[4,128,128]{2,1,0:T(8,128)S(1)}, u32[]{:S(2)}, u32[]{:S(2)}) collective-permute-start(f32[4,128,128]{2,1,0:T(8,128)S(1)} %get-tuple-element.32), channel_id=1, source_target_pairs={{0,8},{1,9},{2,10},{3,11},{4,12},{5,13},{6,14},{7,15},{8,0},{9,1},... | collective-permute-start | bytes 786440 | tf_op jit(solution)/shard_map/ppermute | solution.py:124
  34.9 4.8 %collective-permute-done.4 = f32[4,128,128]{2,1,0:T(8,128)S(1)} collective-permute-done((f32[4,128,128]{2,1,0:T(8,128)S(1)}, f32[4,128,128]{2,1,0:T(8,128)S(1)}, u32[]{:S(2)}, u32[]{:S(2)}) %collective-permute-start.4) | collective-permute-done | bytes 262176 | tf_op jit(solution)/shard_map/ppermute | solution.py:124
  39.8 2.8 %collective-permute-start.5 = (f32[2,128,128]{2,1,0:T(8,128)S(1)}, f32[2,128,128]{2,1,0:T(8,128)S(1)}, u32[]{:S(2)}, u32[]{:S(2)}) collective-permute-start(f32[2,128,128]{2,1,0:T(8,128)S(1)} %get-tuple-element.33), channel_id=1, source_target_pairs={{0,16},{1,17},{2,18},{3,19},{4,20},{5,21},{6,22},{7,23},{8,24},{9,... | collective-permute-start | bytes 393224 | tf_op jit(solution)/shard_map/ppermute | solution.py:124
  42.6 0.5 rotated.1
  43.1 4.0 %collective-permute-done.5.b_ref = f32[2,128,128]{2,1,0:T(8,128)S(1)} collective-permute-done((f32[2,128,128]{2,1,0:T(8,128)S(1)}, f32[2,128,128]{2,1,0:T(8,128)S(1)}, u32[]{:S(2)}, u32[]{:S(2)}) %collective-permute-start.5) | collective-permute-done | bytes 131104 | tf_op jit(solution)/shard_map/ppermute | solution.py:124
  47.1 0.7 direction.1
  47.8 4.5 %collective-permute-start.8 = (bf16[2,128,128]{2,1,0:T(8,128)(2,1)S(1)}, bf16[2,128,128]{2,1,0:T(8,128)(2,1)S(1)}, u32[]{:S(2)}, u32[]{:S(2)}) collective-permute-start(bf16[2,128,128]{2,1,0:T(8,128)(2,1)S(1)} %get-tuple-element.20), channel_id=1, source_target_pairs={{0,24},{1,25},{2,26},{3,27},{4,28},{5,29},{6,30},{7,31},{8,16},{9,... | collective-permute-start | bytes 196616 | tf_op jit(solution)/shard_map/ppermute | solution.py:124
  52.4 0.0 collective-permute-start.7
  52.4 0.6 collective-permute-start.6
  53.0 1.7 %refresh.1.iter_ref = f32[4,128,128]{2,1,0:T(8,128)S(1)} custom-call(s32[1]{0:T(128)} %bitcast.1.side_ref, f32[2,128,128]{2,1,0:T(8,128)S(1)} %get-tuple-element.21.g_ref, f32[4,128,128]{2,1,0:T(8,128)S(1)} %get-tuple-element.22.power_ref, bf16[1,4,128,128]{3,2,1,0:T(8,128)(2,1)S(1)} %copy-done.1, bf16[1,4,128,128]{3,2,1,0:T(8,128)(2,1)S(1)} %copy-done.2), custom_call_target="tpu_custom_call" | custom-call | flops 671088640 | bytes 800000 | tf_op jit(solution)/shard_map/refresh/pallas_call | solution.py:289
  54.7 0.0 collective-permute-done.8
  54.7 1.9 %collective-permute-done.7 = bf16[2,128,128]{2,1,0:T(8,128)(2,1)S(1)} collective-permute-done((bf16[2,128,128]{2,1,0:T(8,128)(2,1)S(1)}, bf16[2,128,128]{2,1,0:T(8,128)(2,1)S(1)}, u32[]{:S(2)}, u32[]{:S(2)}) %collective-permute-start.7) | collective-permute-done | bytes 65568 | tf_op jit(solution)/shard_map/ppermute | solution.py:124
  56.6 0.9 %collective-permute-done.6 = bf16[2,128,128]{2,1,0:T(8,128)(2,1)S(1)} collective-permute-done((bf16[2,128,128]{2,1,0:T(8,128)(2,1)S(1)}, bf16[2,128,128]{2,1,0:T(8,128)(2,1)S(1)}, u32[]{:S(2)}, u32[]{:S(2)}) %collective-permute-start.6) | collective-permute-done | bytes 65568 | tf_op jit(solution)/shard_map/ppermute | solution.py:124
  57.6 1.6 %collective-permute-start.9 = (bf16[8,128,128]{2,1,0:T(8,128)(2,1)S(1)}, bf16[8,128,128]{2,1,0:T(8,128)(2,1)S(1)}, u32[]{:S(2)}, u32[]{:S(2)}) collective-permute-start(bf16[8,128,128]{2,1,0:T(8,128)(2,1)S(1)} %pad_maximum_fusion.1), channel_id=1, source_target_pairs={{0,4},{1,3},{2,6},{3,1},{4,0},{5,7},{6,2},{7,5},{8,12},{9,11},{10,... | collective-permute-start | bytes 786440 | tf_op jit(solution)/shard_map/ppermute | solution.py:124
  59.2 1.6 %middle.1.iter_ref = f32[4,128,128]{2,1,0:T(8,128)S(1)} custom-call(f32[4,128,128]{2,1,0:T(8,128)S(1)} %refresh.1.iter_ref), custom_call_target="tpu_custom_call" | custom-call | flops 536870912 | bytes 400000 | tf_op jit(solution)/shard_map/middle/pallas_call | solution.py:344
  60.8 6.1 %collective-permute-done.9 = bf16[8,128,128]{2,1,0:T(8,128)(2,1)S(1)} collective-permute-done((bf16[8,128,128]{2,1,0:T(8,128)(2,1)S(1)}, bf16[8,128,128]{2,1,0:T(8,128)(2,1)S(1)}, u32[]{:S(2)}, u32[]{:S(2)}) %collective-permute-start.9) | collective-permute-done | bytes 262176 | tf_op jit(solution)/shard_map/ppermute | solution.py:124
  66.9 1.5 %collective-permute-start.10 = (bf16[16,128,128]{2,1,0:T(8,128)(2,1)S(1)}, bf16[16,128,128]{2,1,0:T(8,128)(2,1)S(1)}, u32[]{:S(2)}, u32[]{:S(2)}) collective-permute-start(bf16[16,128,128]{2,1,0:T(8,128)(2,1)S(1)} %pad_maximum_fusion.refs_0_), channel_id=1, source_target_pairs={{0,2},{1,5},{2,0},{3,7},{4,6},{5,1},{6,4},{7,3},{8,10},{9,13},{10,... | collective-permute-start | bytes 1572872 | tf_op jit(solution)/shard_map/ppermute | solution.py:124
  68.5 0.0 collective-permute-start.12
  68.5 2.1 %finish.1.own_ref = bf16[4,128,128]{2,1,0:T(8,128)(2,1)S(1)} custom-call(f32[4,128,128]{2,1,0:T(8,128)S(1)} %middle.1.iter_ref), custom_call_target="tpu_custom_call" | custom-call | flops 671088640 | bytes 400000 | tf_op jit(solution)/shard_map/finish/pallas_call | solution.py:344
  70.6 5.6 %collective-permute-done.10.refs_1_ = bf16[16,128,128]{2,1,0:T(8,128)(2,1)S(1)} collective-permute-done((bf16[16,128,128]{2,1,0:T(8,128)(2,1)S(1)}, bf16[16,128,128]{2,1,0:T(8,128)(2,1)S(1)}, u32[]{:S(2)}, u32[]{:S(2)}) %collective-permute-start.10) | collective-permute-done | bytes 524320 | tf_op jit(solution)/shard_map/ppermute | solution.py:124
  76.2 0.5 collective-permute-start.11
  76.7 0.0 collective-permute-done.12.refs_2_
  76.7 1.6 %collective-permute-done.11.sib_ref = bf16[4,128,128]{2,1,0:T(8,128)(2,1)S(1)} collective-permute-done((bf16[4,128,128]{2,1,0:T(8,128)(2,1)S(1)}, bf16[4,128,128]{2,1,0:T(8,128)(2,1)S(1)}, u32[]{:S(2)}, u32[]{:S(2)}) %collective-permute-start.11) | collective-permute-done | bytes 131104 | tf_op jit(solution)/shard_map/ppermute | solution.py:119
  78.3 3.1 %placed.1 = (bf16[2048,512]{1,0:T(8,128)(2,1)}, bf16[1,4,128,128]{3,2,1,0:T(8,128)(2,1)}, bf16[1,4,128,128]{3,2,1,0:T(8,128)(2,1)}) custom-call(s32[64]{0:T(128)S(1)} %get-tuple-element.16.table_ref, s32[2]{0:T(128)S(1)} %pad_add_fusion.place_ref, bf16[4,128,128]{2,1,0:T(8,128)(2,1)S(1)} %finish.1.own_ref, ...), custom_call_target="tpu_custom_call" | custom-call | tf_op jit(solution)/shard_map/placed/pallas_call | solution.py:494
  (13 shorter events, 0.1 us)
Async XLA Ops:
  0.6 3.9 %collective-permute-start = (bf16[256,2048]{1,0:T(8,128)(2,1)}, bf16[256,2048]{1,0:T(8,128)(2,1)S(1)}, u32[]{:S(2)}, u32[]{:S(2)}) collective-permute-start(bf16[256,2048]{1,0:T(8,128)(2,1)} %f_own.3), channel_id=1, source_target_pairs={{0,1},{1,0},{2,3},{3,2},{4,5},{5,4},{6,7},{7,6},{8,9},{9,8},{10,11... | collective-permute-start | bytes 3145736 | tf_op jit(solution)/shard_map/ppermute | solution.py:119
  1.1 3.4 %collective-permute-start.1 = (bf16[256,512]{1,0:T(8,128)(2,1)}, bf16[256,512]{1,0:T(8,128)(2,1)S(1)}, u32[]{:S(2)}, u32[]{:S(2)}) collective-permute-start(bf16[256,512]{1,0:T(8,128)(2,1)} %kv_ref.1), channel_id=1, source_target_pairs={{0,1},{1,0},{2,3},{3,2},{4,5},{5,4},{6,7},{7,6},{8,9},{9,8},{10,11... | collective-permute-start | bytes 786440 | tf_op jit(solution)/shard_map/ppermute | solution.py:119
  1.3 0.9 %copy-start.7 = (bf16[256,512]{1,0:T(8,128)(2,1)S(1)}, bf16[256,512]{1,0:T(8,128)(2,1)}, u32[]{:S(2)}) copy-start(bf16[256,512]{1,0:T(8,128)(2,1)} %kv_ref.1) | copy-start | bytes 786436
  2.3 0.7 copy-start.8
  4.6 1.2 %copy-start = (bf16[256,2048]{1,0:T(8,128)(2,1)S(1)}, bf16[256,2048]{1,0:T(8,128)(2,1)}, u32[]{:S(2)}) copy-start(bf16[256,2048]{1,0:T(8,128)(2,1)} %f_own.3) | copy-start | bytes 3145732
  7.6 15.7 %collective-permute-start.2 = (f32[16,128,128]{2,1,0:T(8,128)S(1)}, f32[16,128,128]{2,1,0:T(8,128)S(1)}, u32[]{:S(2)}, u32[]{:S(2)}) collective-permute-start(f32[16,128,128]{2,1,0:T(8,128)S(1)} %tiles.3), channel_id=1, source_target_pairs={{0,2},{1,5},{2,0},{3,7},{4,6},{5,1},{6,4},{7,3},{8,10},{9,13},{10,... | collective-permute-start | bytes 3145736 | tf_op jit(solution)/shard_map/ppermute | solution.py:124
  12.2 30.4 %copy-start.1 = (bf16[1,4,128,128]{3,2,1,0:T(8,128)(2,1)S(1)}, bf16[1,4,128,128]{3,2,1,0:T(8,128)(2,1)}, u32[]{:S(2)}) copy-start(bf16[1,4,128,128]{3,2,1,0:T(8,128)(2,1)} %ql_ref.5) | copy-start | bytes 393220
  12.3 30.3 %copy-start.2 = (bf16[1,4,128,128]{3,2,1,0:T(8,128)(2,1)S(1)}, bf16[1,4,128,128]{3,2,1,0:T(8,128)(2,1)}, u32[]{:S(2)}) copy-start(bf16[1,4,128,128]{3,2,1,0:T(8,128)(2,1)} %qr_ref.5) | copy-start | bytes 393220
  12.3 30.3 %copy-start.3 = (f32[1,4,128,128]{3,2,1,0:T(8,128)S(1)}, f32[1,4,128,128]{3,2,1,0:T(8,128)}, u32[]{:S(2)}) copy-start(f32[1,4,128,128]{3,2,1,0:T(8,128)} %m_ref.1) | copy-start | bytes 786436
  12.3 30.3 %copy-start.4 = (f32[1,4,128,128]{3,2,1,0:T(8,128)S(1)}, f32[1,4,128,128]{3,2,1,0:T(8,128)}, u32[]{:S(2)}) copy-start(f32[1,4,128,128]{3,2,1,0:T(8,128)} %v_ref.1) | copy-start | bytes 786436
  12.3 30.3 %copy-start.5 = (f32[1,4,128,128]{3,2,1,0:T(8,128)S(1)}, f32[1,4,128,128]{3,2,1,0:T(8,128)}, u32[]{:S(2)}) copy-start(f32[1,4,128,128]{3,2,1,0:T(8,128)} %l_ref.1) | copy-start | bytes 786436
  12.3 30.3 %copy-start.6 = (f32[1,4,128,128]{3,2,1,0:T(8,128)S(1)}, f32[1,4,128,128]{3,2,1,0:T(8,128)}, u32[]{:S(2)}) copy-start(f32[1,4,128,128]{3,2,1,0:T(8,128)} %r_ref.1) | copy-start | bytes 786436
  23.4 9.3 %collective-permute-start.3 = (f32[8,128,128]{2,1,0:T(8,128)S(1)}, f32[8,128,128]{2,1,0:T(8,128)S(1)}, u32[]{:S(2)}, u32[]{:S(2)}) collective-permute-start(f32[8,128,128]{2,1,0:T(8,128)S(1)} %get-tuple-element.30), channel_id=1, source_target_pairs={{0,4},{1,3},{2,6},{3,1},{4,0},{5,7},{6,2},{7,5},{8,12},{9,11},{10,... | collective-permute-start | bytes 1572872 | tf_op jit(solution)/shard_map/ppermute | solution.py:124
  32.8 7.0 %collective-permute-start.4 = (f32[4,128,128]{2,1,0:T(8,128)S(1)}, f32[4,128,128]{2,1,0:T(8,128)S(1)}, u32[]{:S(2)}, u32[]{:S(2)}) collective-permute-start(f32[4,128,128]{2,1,0:T(8,128)S(1)} %get-tuple-element.32), channel_id=1, source_target_pairs={{0,8},{1,9},{2,10},{3,11},{4,12},{5,13},{6,14},{7,15},{8,0},{9,1},... | collective-permute-start | bytes 786440 | tf_op jit(solution)/shard_map/ppermute | solution.py:124
  39.8 7.3 %collective-permute-start.5 = (f32[2,128,128]{2,1,0:T(8,128)S(1)}, f32[2,128,128]{2,1,0:T(8,128)S(1)}, u32[]{:S(2)}, u32[]{:S(2)}) collective-permute-start(f32[2,128,128]{2,1,0:T(8,128)S(1)} %get-tuple-element.33), channel_id=1, source_target_pairs={{0,16},{1,17},{2,18},{3,19},{4,20},{5,21},{6,22},{7,23},{8,24},{9,... | collective-permute-start | bytes 393224 | tf_op jit(solution)/shard_map/ppermute | solution.py:124
  47.8 6.9 %collective-permute-start.8 = (bf16[2,128,128]{2,1,0:T(8,128)(2,1)S(1)}, bf16[2,128,128]{2,1,0:T(8,128)(2,1)S(1)}, u32[]{:S(2)}, u32[]{:S(2)}) collective-permute-start(bf16[2,128,128]{2,1,0:T(8,128)(2,1)S(1)} %get-tuple-element.20), channel_id=1, source_target_pairs={{0,24},{1,25},{2,26},{3,27},{4,28},{5,29},{6,30},{7,31},{8,16},{9,... | collective-permute-start | bytes 196616 | tf_op jit(solution)/shard_map/ppermute | solution.py:124
  52.4 4.3 %collective-permute-start.7 = (bf16[2,128,128]{2,1,0:T(8,128)(2,1)S(1)}, bf16[2,128,128]{2,1,0:T(8,128)(2,1)S(1)}, u32[]{:S(2)}, u32[]{:S(2)}) collective-permute-start(bf16[2,128,128]{2,1,0:T(8,128)(2,1)S(1)} %get-tuple-element.20), channel_id=1, source_target_pairs={{0,8},{1,9},{2,10},{3,11},{4,12},{5,13},{6,14},{7,15},{8,0},{9,1},... | collective-permute-start | bytes 196616 | tf_op jit(solution)/shard_map/ppermute | solution.py:124
  52.4 5.2 %collective-permute-start.6 = (bf16[2,128,128]{2,1,0:T(8,128)(2,1)S(1)}, bf16[2,128,128]{2,1,0:T(8,128)(2,1)S(1)}, u32[]{:S(2)}, u32[]{:S(2)}) collective-permute-start(bf16[2,128,128]{2,1,0:T(8,128)(2,1)S(1)} %get-tuple-element.20), channel_id=1, source_target_pairs={{0,16},{1,17},{2,18},{3,19},{4,20},{5,21},{6,22},{7,23},{8,24},{9,... | collective-permute-start | bytes 196616 | tf_op jit(solution)/shard_map/ppermute | solution.py:124
  57.6 9.3 %collective-permute-start.9 = (bf16[8,128,128]{2,1,0:T(8,128)(2,1)S(1)}, bf16[8,128,128]{2,1,0:T(8,128)(2,1)S(1)}, u32[]{:S(2)}, u32[]{:S(2)}) collective-permute-start(bf16[8,128,128]{2,1,0:T(8,128)(2,1)S(1)} %pad_maximum_fusion.1), channel_id=1, source_target_pairs={{0,4},{1,3},{2,6},{3,1},{4,0},{5,7},{6,2},{7,5},{8,12},{9,11},{10,... | collective-permute-start | bytes 786440 | tf_op jit(solution)/shard_map/ppermute | solution.py:124
  66.9 9.2 %collective-permute-start.10 = (bf16[16,128,128]{2,1,0:T(8,128)(2,1)S(1)}, bf16[16,128,128]{2,1,0:T(8,128)(2,1)S(1)}, u32[]{:S(2)}, u32[]{:S(2)}) collective-permute-start(bf16[16,128,128]{2,1,0:T(8,128)(2,1)S(1)} %pad_maximum_fusion.refs_0_), channel_id=1, source_target_pairs={{0,2},{1,5},{2,0},{3,7},{4,6},{5,1},{6,4},{7,3},{8,10},{9,13},{10,... | collective-permute-start | bytes 1572872 | tf_op jit(solution)/shard_map/ppermute | solution.py:124
  68.5 8.2 %collective-permute-start.12 = (bf16[16,128,128]{2,1,0:T(8,128)(2,1)S(1)}, bf16[16,128,128]{2,1,0:T(8,128)(2,1)S(1)}, u32[]{:S(2)}, u32[]{:S(2)}) collective-permute-start(bf16[16,128,128]{2,1,0:T(8,128)(2,1)S(1)} %pad_maximum_fusion.refs_0_), channel_id=1, source_target_pairs={{0,1},{1,0},{2,3},{3,2},{4,5},{5,4},{6,7},{7,6},{8,9},{9,8},{10,11... | collective-permute-start | bytes 1572872 | tf_op jit(solution)/shard_map/ppermute | solution.py:119
  76.2 2.1 %collective-permute-start.13 = (bf16[16,128,128]{2,1,0:T(8,128)(2,1)S(1)}, bf16[16,128,128]{2,1,0:T(8,128)(2,1)S(1)}, u32[]{:S(2)}, u32[]{:S(2)}) collective-permute-start(bf16[16,128,128]{2,1,0:T(8,128)(2,1)S(1)} %collective-permute-done.10.refs_1_), channel_id=1, source_target_pairs={{0,1},{1,0},{2,3},{3,2},{4,5},{5,4},{6,7},{7,6},{8,9},{9,8},{10,11... | collective-permute-start | bytes 1572872 | tf_op jit(solution)/shard_map/ppermute | solution.py:119
  76.2 2.1 %collective-permute-start.11 = (bf16[4,128,128]{2,1,0:T(8,128)(2,1)S(1)}, bf16[4,128,128]{2,1,0:T(8,128)(2,1)S(1)}, u32[]{:S(2)}, u32[]{:S(2)}) collective-permute-start(bf16[4,128,128]{2,1,0:T(8,128)(2,1)S(1)} %finish.1.own_ref), channel_id=1, source_target_pairs={{0,1},{1,0},{2,3},{3,2},{4,5},{5,4},{6,7},{7,6},{8,9},{9,8},{10,11... | collective-permute-start | bytes 393224 | tf_op jit(solution)/shard_map/ppermute | solution.py:119

commit v6 on v4

--- a/solution.py
+++ b/solution.py
@@ -170,16 +170,6 @@
     return orders, offsets
 
 
-def chunked(source, target, sems, first, count):
-    rows = source.shape[0] // count
-    return [
-        pltpu.make_async_copy(
-            source.at[pl.ds(i * rows, rows)], target.at[pl.ds(i * rows, rows)], sems.at[first + i]
-        )
-        for i in range(count)
-    ]
-
-
 def table_kernel(owners, capacity, place_ref, owner_ref, kv_ref, *rest):
     table_ref, own_rows, count, held = rest
     own_rows[...] = kv_ref[...].T
@@ -221,7 +211,7 @@
             )
             return carry
 
-        lax.fori_loop(0, owners // 2, one, 0, unroll=4)
+        lax.fori_loop(0, owners // 2, one, 0, unroll=8)
 
 
 SMEM = pl.BlockSpec(memory_space=pltpu.SMEM)
@@ -306,7 +296,7 @@
     return lax.fori_loop(0, count, lambda i, v: sweep(v), tuple(values), unroll=2)
 
 
-STAGES = (3, 4, NS_STEPS - 7)
+STAGES = (5, NS_STEPS - 5)
 
 
 def refresh_kernel(side_ref, g_ref, power_ref, ql_ref, qr_ref, iter_ref):
@@ -322,13 +312,8 @@
         iter_ref[i] = y
 
 
-def middle_kernel(iter_ref, out_ref):
+def finish_kernel(iter_ref, out_ref):
     for i, y in enumerate(sweeps([iter_ref[i] for i in range(4)], STAGES[1])):
-        out_ref[i] = y
-
-
-def finish_kernel(iter_ref, out_ref):
-    for i, y in enumerate(sweeps([iter_ref[i] for i in range(4)], STAGES[2])):
         out_ref[i] = y.T.astype(out_ref.dtype)
 
 
@@ -345,26 +330,58 @@
     )(values)
 
 
-def place_kernel(col_tiles, table_ref, place_ref, own_ref, sib_ref, *refs):
-    sources = refs[:-5]
-    out_hbm, left_ref, right_ref, out, sems = refs[-5:]
-    half, tile = sources[0].shape[:2]
-    for number, source in enumerate(sources):
-        for i in range(half):
-            block = table_ref[number * half + i]
-            row = pl.multiple_of(block // col_tiles * tile, tile)
-            col = pl.multiple_of(block % col_tiles * tile, tile)
-            out[pl.ds(row, tile), pl.ds(col, tile)] = source[i]
-    copies = chunked(out, out_hbm, sems, 0, 8)
-    for copy in copies:
-        copy.start()
+def place_tiles(col_tiles, entries, table_ref, sources, out, sems):
+    tile = sources[0].shape[-1]
+    copies = []
+    for entry, source in zip(entries, sources):
+        for i in range(source.shape[0]):
+            block = table_ref[entry + i]
+            rows = pl.ds(pl.multiple_of(block // col_tiles * tile, tile), tile)
+            columns = pl.ds(pl.multiple_of(block % col_tiles * tile, tile), tile)
+            copies.append(
+                pltpu.make_async_copy(source.at[i], out.at[rows, columns], sems.at[len(copies)])
+            )
+            copies[-1].start()
+    return copies
+
+
+def begin_kernel(col_tiles, entries, table_ref, place_ref, own_ref, sib_ref, *refs):
+    sources = refs[:-4]
+    out, left, right, sems = refs[-4:]
+    copies = place_tiles(col_tiles, entries, table_ref, sources, out, sems)
     core = place_ref[1]
     for source, first in ((own_ref, 2 * core), (sib_ref, 2 - 2 * core)):
         for k in range(2):
-            left_ref[0, first + k] = source[2 * k]
-            right_ref[0, first + k] = source[2 * k + 1]
+            for i, target in enumerate((left, right)):
+                copies.append(
+                    pltpu.make_async_copy(
+                        source.at[2 * k + i], target.at[0, first + k], sems.at[len(copies)]
+                    )
+                )
+                copies[-1].start()
     for copy in copies:
         copy.wait()
+
+
+def more_kernel(col_tiles, entries, table_ref, *refs):
+    out, sems = refs[-2:]
+    for copy in place_tiles(col_tiles, entries, table_ref, refs[:-3], out, sems):
+        copy.wait()
+
+
+def place_more(update, table, col_tiles, entries, sources):
+    count = sum(x.shape[0] for x in sources)
+    return pl.pallas_call(
+        functools.partial(more_kernel, col_tiles, entries),
+        out_shape=jax.ShapeDtypeStruct(update.shape, update.dtype),
+        in_specs=[SMEM] + [VMEM] * len(sources) + [HBM],
+        out_specs=HBM,
+        scratch_shapes=[pltpu.SemaphoreType.DMA((count,))],
+        input_output_aliases={1 + len(sources): 0},
+        compiler_params=SMALL,
+        cost_estimate=pl.CostEstimate(flops=0, bytes_accessed=1_000_000, transcendentals=0),
+        name="more",
+    )(table, *sources, update)
 
 
 def per_device_dealt(
@@ -483,29 +500,32 @@
     mine = [jnp.stack([t[stream] for t in tiles]) for stream in range(2)]
     mine, values = lax.optimization_barrier((mine, values))
     other = [swap_along(m, "dp", owners, 1 << order[1]) for m, order in zip(mine, orders)]
-    values = sweeping(middle_kernel, values, jnp.float32, STAGES[1])
+    fresh = sweeping(finish_kernel, values, jnp.bfloat16, STAGES[1])
     mine = [jnp.concatenate(both, axis=0) for both in zip(mine, other)]
-    mine, values = lax.optimization_barrier((mine, values))
+    mine, fresh = lax.optimization_barrier((mine, fresh))
     other = [swap_along(m, "dp", owners, 1 << order[0]) for m, order in zip(mine, orders)]
-    fresh = sweeping(finish_kernel, values, jnp.bfloat16, STAGES[2])
-    other, fresh = lax.optimization_barrier((other, fresh))
     fresh_sib = swap_along(fresh, "inner", 2, 1)
-    gathered = [part for both in zip(mine, other) for part in both]
-    sources = gathered + [swap_along(g, "inner", 2, 1) for g in gathered]
+    mine_sib = [swap_along(m, "inner", 2, 1) for m in mine]
     basis = jax.ShapeDtypeStruct(left_basis.shape, left_basis.dtype)
-    return pl.pallas_call(
-        functools.partial(place_kernel, col_tiles),
+    update, new_left, new_right = pl.pallas_call(
+        functools.partial(
+            begin_kernel, col_tiles, (0, owners, 2 * owners, 3 * owners)
+        ),
         out_shape=(jax.ShapeDtypeStruct((d_win, width), jnp.bfloat16), basis, basis),
-        grid=(1,),
-        in_specs=[SMEM, SMEM] + wholes([fresh, fresh_sib] + sources),
-        out_specs=(HBM, whole(basis.shape), whole(basis.shape)),
-        scratch_shapes=[
-            pltpu.VMEM((d_win, width), jnp.bfloat16),
-            pltpu.SemaphoreType.DMA((8,)),
-        ],
-        compiler_params=BIG,
-        name="placed",
-    )(table, place, fresh, fresh_sib, *sources)
+        in_specs=[SMEM, SMEM] + [VMEM] * 6,
+        out_specs=(HBM, HBM, HBM),
+        scratch_shapes=[pltpu.SemaphoreType.DMA((4 * near + 8,))],
+        compiler_params=SMALL,
+        cost_estimate=pl.CostEstimate(flops=0, bytes_accessed=1_300_000, transcendentals=0),
+        name="begin",
+    )(table, place, fresh, fresh_sib, *mine, *mine_sib)
+    update, other = lax.optimization_barrier((update, other))
+    other_sib = [swap_along(o, "inner", 2, 1) for o in other]
+    update = place_more(update, table, col_tiles, (near, owners + near), other)
+    update = place_more(
+        update, table, col_tiles, (2 * owners + near, 3 * owners + near), other_sib
+    )
+    return update, new_left, new_right
 
 
 def solution(mesh):

time: 75.5 us -> 75.2 us (level)
  waiting for transfers between devices: 32.2 us -> 31.1 us
    pallas_call x1 -> x3, Pallas kernels: 3.12 us -> 4.88 us  [the longest x2 2.94 us: place_more(): pl.pallas_call(functools.partial(more_kernel, col_tiles, entries), out_sh...]
    pallas_call x2, Pallas kernels: 4.15 us -> 2.81 us  [tiles_from(): pl.pallas_call(functools.partial(tiles_kernel, owners, first), out_shape=...]
    pallas_call x3, Pallas kernels: 2.91 us -> 3.98 us  [on_slots(): pl.pallas_call(kernel, out_shape=tuple(outs), grid_spec=pltpu.PrefetchSca...]
    ppermute x20, waiting for transfers between devices: 32.2 us -> 31.1 us  [swap_along(): return lax.ppermute(values, axis, [(i, i ^ bit) for i in range(size)])]
    pallas_call x2 -> x1, Pallas kernels: 3.71 us -> 2.89 us  [sweeping(): pl.pallas_call(kernel, out_shape=jax.ShapeDtypeStruct(values.shape, dtype...]
  transfers between devices with their start and end apart: 20 -> 20, of which waited for: 12 -> 11; matrix products, arithmetic and copies ran while one was open for 0% -> 0% of each run, Pallas kernels for 13% -> 17%
where the time goes in v6:
time: 75.2 us; the launch traced here: 75.1 us
  waiting for transfers between devices  31.1 us (41%)
  starting transfers between devices  23.6 us (31%)
  Pallas kernels  16.2 us (22%)
  local copies, waits for them, and re-layouts  2.89 us (4%)
  between operations  0.88 us (1%)
    ppermute x20, waiting for transfers between devices, swap_along(): return lax.ppermute(values, axis, [(i, i ^ bit) for i in range(size)])  31.1 us
    ppermute x20, starting transfers between devices, swap_along(): return lax.ppermute(values, axis, [(i, i ^ bit) for i in range(size)])  23.6 us
    pallas_call x3, Pallas kernels, on_slots(): pl.pallas_call(kernel, out_shape=tuple(outs), grid_spec=pltpu.PrefetchSca...  3.98 us
    pallas_call x2, Pallas kernels, place_more(): pl.pallas_call(functools.partial(more_kernel, col_tiles, entries), out_sh...  2.94 us
    pallas_call x1, Pallas kernels, sweeping(): pl.pallas_call(kernel, out_shape=jax.ShapeDtypeStruct(values.shape, dtype...  2.89 us
    unnamed x18, local copies, waits for them, and re-layouts  2.86 us
    pallas_call x2, Pallas kernels, tiles_from(): pl.pallas_call(functools.partial(tiles_kernel, owners, first), out_shape=...  2.81 us
    pallas_call x1, Pallas kernels, per_device_dealt(): pl.pallas_call(functools.partial(begin_kernel, col_tiles, (0, owners, 2 *...  1.94 us
  transfers between devices with their start and end apart: 20, of which 11 were waited for; matrix products, arithmetic and copies ran while one was open for 0% of the time, Pallas kernels for 17%

profile of v6, /device:TPU:0, one launch (start us, length us, event | category | flops | bytes accessed | tf_op | source)
XLA Modules:
  0.0 75.1 jit_solution(5713029989818362346)
XLA Ops:
  0.6 0.5 collective-permute-start
  1.1 0.1 collective-permute-start.1
  1.2 0.1 pad_add_fusion.place_ref
  1.3 0.9 %copy-done.7 = bf16[256,512]{1,0:T(8,128)(2,1)S(1)} copy-done((bf16[256,512]{1,0:T(8,128)(2,1)S(1)}, bf16[256,512]{1,0:T(8,128)(2,1)}, u32[]{:S(2)}) %copy-start.7) | copy-done | bytes 262168
  2.3 0.7 copy-done.8
  2.9 1.7 %table.1 = (s32[64]{0:T(128)S(1)}, bf16[512,256]{1,0:T(8,128)(2,1)S(1)}) custom-call(s32[2]{0:T(128)S(1)} %pad_add_fusion.place_ref, s32[64]{0:T(128)S(1)} %copy-done.8, bf16[256,512]{1,0:T(8,128)(2,1)S(1)} %copy-done.7), custom_call_target="tpu_custom_call" | custom-call | bytes 1000000 | tf_op jit(solution)/shard_map/table/pallas_call | solution.py:416
  4.6 0.0 copy-start
  4.6 1.2 %copy-done = bf16[256,2048]{1,0:T(8,128)(2,1)S(1)} copy-done((bf16[256,2048]{1,0:T(8,128)(2,1)S(1)}, bf16[256,2048]{1,0:T(8,128)(2,1)}, u32[]{:S(2)}) %copy-start) | copy-done | bytes 1048600
  5.8 1.4 %tiles.3 = (f32[8,128,128]{2,1,0:T(8,128)S(1)}, f32[8,128,128]{2,1,0:T(8,128)S(1)}) custom-call(s32[64]{0:T(128)S(1)} %get-tuple-element.26.table_ref, bf16[256,2048]{1,0:T(8,128)(2,1)S(1)} %copy-done, bf16[256,2048]{1,0:T(8,128)(2,1)S(1)} %collective-permute-done.f_sib, bf16[512,256]{1,0:T(8,128)(2,1)S(1)} %get-tuple-element.27.own_rows, ...), custom_call_target="tpu_custom_call" | custom-call | flops 536870912 | bytes 3500000 | tf_op jit(solution)/shard_map/tiles/pallas_call | solution.py:435
  7.2 3.0 %collective-permute-start.2 = (f32[8,128,128]{2,1,0:T(8,128)S(1)}, f32[8,128,128]{2,1,0:T(8,128)S(1)}, u32[]{:S(2)}, u32[]{:S(2)}) collective-permute-start(f32[8,128,128]{2,1,0:T(8,128)S(1)} %get-tuple-element.29), channel_id=1, source_target_pairs={{0,2},{2,0},{4,6},{6,4},{8,10},{10,8},{12,14},{14,12},{16,18},{18,... | collective-permute-start | bytes 1572872 | tf_op jit(solution)/shard_map/ppermute | solution.py:116
  10.2 1.5 %collective-permute-start.3 = (f32[8,128,128]{2,1,0:T(8,128)S(1)}, f32[8,128,128]{2,1,0:T(8,128)S(1)}, u32[]{:S(2)}, u32[]{:S(2)}) collective-permute-start(f32[8,128,128]{2,1,0:T(8,128)S(1)} %get-tuple-element.31), channel_id=1, source_target_pairs={{0,4},{2,6},{4,0},{6,2},{8,12},{10,14},{12,8},{14,10},{16,20},{18,... | collective-permute-start | bytes 1572872 | tf_op jit(solution)/shard_map/ppermute | solution.py:116
  11.7 1.4 %tiles.2 = (f32[8,128,128]{2,1,0:T(8,128)S(1)}, f32[8,128,128]{2,1,0:T(8,128)S(1)}) custom-call(s32[64]{0:T(128)S(1)} %get-tuple-element.26.table_ref, bf16[256,2048]{1,0:T(8,128)(2,1)S(1)} %copy-done, bf16[256,2048]{1,0:T(8,128)(2,1)S(1)} %collective-permute-done.f_sib, bf16[512,256]{1,0:T(8,128)(2,1)S(1)} %get-tuple-element.27.own_rows, ...), custom_call_target="tpu_custom_call" | custom-call | flops 536870912 | bytes 3500000 | tf_op jit(solution)/shard_map/tiles/pallas_call | solution.py:435
  13.1 9.2 %collective-permute-done.2 = f32[8,128,128]{2,1,0:T(8,128)S(1)} collective-permute-done((f32[8,128,128]{2,1,0:T(8,128)S(1)}, f32[8,128,128]{2,1,0:T(8,128)S(1)}, u32[]{:S(2)}, u32[]{:S(2)}) %collective-permute-start.2) | collective-permute-done | bytes 524320 | tf_op jit(solution)/shard_map/ppermute | solution.py:116
  22.4 0.1 fusion.5
  22.5 0.0 copy-start.1
  22.5 0.0 copy-start.2
  22.5 1.8 %collective-permute-start.4 = (f32[4,128,128]{2,1,0:T(8,128)S(1)}, f32[4,128,128]{2,1,0:T(8,128)S(1)}, u32[]{:S(2)}, u32[]{:S(2)}) collective-permute-start(f32[4,128,128]{2,1,0:T(8,128)S(1)} %get-tuple-element.52), channel_id=1, source_target_pairs={{0,4},{2,6},{4,0},{6,2},{8,12},{10,14},{12,8},{14,10},{16,20},{18,... | collective-permute-start | bytes 786440 | tf_op jit(solution)/shard_map/ppermute | solution.py:116
  24.3 0.1 fusion.4
  24.4 1.6 %collective-permute-start.5 = (f32[4,128,128]{2,1,0:T(8,128)S(1)}, f32[4,128,128]{2,1,0:T(8,128)S(1)}, u32[]{:S(2)}, u32[]{:S(2)}) collective-permute-start(f32[4,128,128]{2,1,0:T(8,128)S(1)} %get-tuple-element.54), channel_id=1, source_target_pairs={{0,2},{2,0},{4,6},{6,4},{8,10},{10,8},{12,14},{14,12},{16,18},{18,... | collective-permute-start | bytes 786440 | tf_op jit(solution)/shard_map/ppermute | solution.py:116
  26.0 4.4 %collective-permute-done.4 = f32[4,128,128]{2,1,0:T(8,128)S(1)} collective-permute-done((f32[4,128,128]{2,1,0:T(8,128)S(1)}, f32[4,128,128]{2,1,0:T(8,128)S(1)}, u32[]{:S(2)}, u32[]{:S(2)}) %collective-permute-start.4) | collective-permute-done | bytes 262176 | tf_op jit(solution)/shard_map/ppermute | solution.py:116
  30.4 1.3 %collective-permute-done.5 = f32[4,128,128]{2,1,0:T(8,128)S(1)} collective-permute-done((f32[4,128,128]{2,1,0:T(8,128)S(1)}, f32[4,128,128]{2,1,0:T(8,128)S(1)}, u32[]{:S(2)}, u32[]{:S(2)}) %collective-permute-start.5) | collective-permute-done | bytes 262176 | tf_op jit(solution)/shard_map/ppermute | solution.py:116
  31.6 0.1 fusion.1
  31.7 1.6 %collective-permute-start.6 = (f32[2,2,128,128]{3,2,1,0:T(8,128)S(1)}, f32[2,2,128,128]{3,2,1,0:T(8,128)S(1)}, u32[]{:S(2)}, u32[]{:S(2)}) collective-permute-start(f32[2,2,128,128]{3,2,1,0:T(8,128)S(1)} %get-tuple-element.50), channel_id=1, source_target_pairs={{0,8},{2,10},{4,12},{6,14},{8,0},{10,2},{12,4},{14,6},{16,24},{18,... | collective-permute-start | bytes 786440 | tf_op jit(solution)/shard_map/ppermute | solution.py:116
  33.3 4.8 %collective-permute-done.6 = f32[2,2,128,128]{3,2,1,0:T(8,128)S(1)} collective-permute-done((f32[2,2,128,128]{3,2,1,0:T(8,128)S(1)}, f32[2,2,128,128]{3,2,1,0:T(8,128)S(1)}, u32[]{:S(2)}, u32[]{:S(2)}) %collective-permute-start.6) | collective-permute-done | bytes 262176 | tf_op jit(solution)/shard_map/ppermute | solution.py:116
  38.2 3.2 %collective-permute-start.7 = (f32[2,128,128]{2,1,0:T(8,128)S(1)}, f32[2,128,128]{2,1,0:T(8,128)S(1)}, u32[]{:S(2)}, u32[]{:S(2)}) collective-permute-start(f32[2,128,128]{2,1,0:T(8,128)S(1)} %get-tuple-element.55), channel_id=1, source_target_pairs={{0,16},{2,18},{4,20},{6,22},{8,24},{10,26},{12,28},{14,30},{16,0},... | collective-permute-start | bytes 393224 | tf_op jit(solution)/shard_map/ppermute | solution.py:116
  41.4 0.5 rotated.1
  41.9 4.2 %collective-permute-done.7.b_ref = f32[2,128,128]{2,1,0:T(8,128)S(1)} collective-permute-done((f32[2,128,128]{2,1,0:T(8,128)S(1)}, f32[2,128,128]{2,1,0:T(8,128)S(1)}, u32[]{:S(2)}, u32[]{:S(2)}) %collective-permute-start.7) | collective-permute-done | bytes 131104 | tf_op jit(solution)/shard_map/ppermute | solution.py:116
  46.1 0.7 direction.1
  46.8 3.8 %collective-permute-start.10 = (bf16[2,128,128]{2,1,0:T(8,128)(2,1)S(1)}, bf16[2,128,128]{2,1,0:T(8,128)(2,1)S(1)}, u32[]{:S(2)}, u32[]{:S(2)}) collective-permute-start(bf16[2,128,128]{2,1,0:T(8,128)(2,1)S(1)} %get-tuple-element.34), channel_id=1, source_target_pairs={{0,24},{2,26},{4,28},{6,30},{8,16},{10,18},{12,20},{14,22},{16,8},... | collective-permute-start | bytes 196616 | tf_op jit(solution)/shard_map/ppermute | solution.py:116
  50.7 0.6 collective-permute-start.8
  51.3 2.8 %refresh.1.iter_ref = f32[4,128,128]{2,1,0:T(8,128)S(1)} custom-call(s32[1]{0:T(128)} %bitcast.1.side_ref, f32[2,128,128]{2,1,0:T(8,128)S(1)} %get-tuple-element.35.g_ref, f32[4,128,128]{2,1,0:T(8,128)S(1)} %get-tuple-element.36.power_ref, bf16[1,4,128,128]{3,2,1,0:T(8,128)(2,1)S(1)} %copy-done.1, bf16[1,4,128,128]{3,2,1,0:T(8,128)(2,1)S(1)} %copy-done.2), custom_call_target="tpu_custom_call" | custom-call | flops 939524096 | bytes 800000 | tf_op jit(solution)/shard_map/refresh/pallas_call | solution.py:272
  54.1 0.8 %collective-permute-done.9 = bf16[2,128,128]{2,1,0:T(8,128)(2,1)S(1)} collective-permute-done((bf16[2,128,128]{2,1,0:T(8,128)(2,1)S(1)}, bf16[2,128,128]{2,1,0:T(8,128)(2,1)S(1)}, u32[]{:S(2)}, u32[]{:S(2)}) %collective-permute-start.9) | collective-permute-done | bytes 65568 | tf_op jit(solution)/shard_map/ppermute | solution.py:116
  54.9 0.9 %collective-permute-done.8 = bf16[2,128,128]{2,1,0:T(8,128)(2,1)S(1)} collective-permute-done((bf16[2,128,128]{2,1,0:T(8,128)(2,1)S(1)}, bf16[2,128,128]{2,1,0:T(8,128)(2,1)S(1)}, u32[]{:S(2)}, u32[]{:S(2)}) %collective-permute-start.8) | collective-permute-done | bytes 65568 | tf_op jit(solution)/shard_map/ppermute | solution.py:116
  55.9 1.0 %collective-permute-start.11 = (bf16[4,128,128]{2,1,0:T(8,128)(2,1)S(1)}, bf16[4,128,128]{2,1,0:T(8,128)(2,1)S(1)}, u32[]{:S(2)}, u32[]{:S(2)}) collective-permute-start(bf16[4,128,128]{2,1,0:T(8,128)(2,1)S(1)} %get-tuple-element.37), channel_id=1, source_target_pairs={{0,4},{2,6},{4,0},{6,2},{8,12},{10,14},{12,8},{14,10},{16,20},{18,... | collective-permute-start | bytes 393224 | tf_op jit(solution)/shard_map/ppermute | solution.py:116
  56.9 1.1 %collective-permute-start.12 = (bf16[4,128,128]{2,1,0:T(8,128)(2,1)S(1)}, bf16[4,128,128]{2,1,0:T(8,128)(2,1)S(1)}, u32[]{:S(2)}, u32[]{:S(2)}) collective-permute-start(bf16[4,128,128]{2,1,0:T(8,128)(2,1)S(1)} %get-tuple-element.38), channel_id=1, source_target_pairs={{0,2},{2,0},{4,6},{6,4},{8,10},{10,8},{12,14},{14,12},{16,18},{18,... | collective-permute-start | bytes 393224 | tf_op jit(solution)/shard_map/ppermute | solution.py:116
  58.0 2.9 %finish.1.own_ref = bf16[4,128,128]{2,1,0:T(8,128)(2,1)S(1)} custom-call(f32[4,128,128]{2,1,0:T(8,128)S(1)} %refresh.1.iter_ref), custom_call_target="tpu_custom_call" | custom-call | flops 939524096 | bytes 400000 | tf_op jit(solution)/shard_map/finish/pallas_call | solution.py:322
  61.0 0.9 %collective-permute-done.12 = bf16[4,128,128]{2,1,0:T(8,128)(2,1)S(1)} collective-permute-done((bf16[4,128,128]{2,1,0:T(8,128)(2,1)S(1)}, bf16[4,128,128]{2,1,0:T(8,128)(2,1)S(1)}, u32[]{:S(2)}, u32[]{:S(2)}) %collective-permute-start.12) | collective-permute-done | bytes 131104 | tf_op jit(solution)/shard_map/ppermute | solution.py:116
  61.9 0.1 collective-permute-start.14
  62.0 0.5 collective-permute-start.15
  62.5 1.1 %collective-permute-start.16 = (bf16[8,128,128]{2,1,0:T(8,128)(2,1)S(1)}, bf16[8,128,128]{2,1,0:T(8,128)(2,1)S(1)}, u32[]{:S(2)}, u32[]{:S(2)}) collective-permute-start(bf16[8,128,128]{2,1,0:T(8,128)(2,1)S(1)} %pad_maximum_fusion.2.refs_0_), channel_id=1, source_target_pairs={{0,2},{2,0},{4,6},{6,4},{8,10},{10,8},{12,14},{14,12},{16,18},{18,... | collective-permute-start | bytes 786440 | tf_op jit(solution)/shard_map/ppermute | solution.py:116
  63.6 1.5 %collective-permute-start.17 = (bf16[8,128,128]{2,1,0:T(8,128)(2,1)S(1)}, bf16[8,128,128]{2,1,0:T(8,128)(2,1)S(1)}, u32[]{:S(2)}, u32[]{:S(2)}) collective-permute-start(bf16[8,128,128]{2,1,0:T(8,128)(2,1)S(1)} %pad_maximum_fusion.3.refs_1_), channel_id=1, source_target_pairs={{0,4},{2,6},{4,0},{6,2},{8,12},{10,14},{12,8},{14,10},{16,20},{18,... | collective-permute-start | bytes 786440 | tf_op jit(solution)/shard_map/ppermute | solution.py:116
  65.1 1.3 %collective-permute-done.13.sib_ref = bf16[4,128,128]{2,1,0:T(8,128)(2,1)S(1)} collective-permute-done((bf16[4,128,128]{2,1,0:T(8,128)(2,1)S(1)}, bf16[4,128,128]{2,1,0:T(8,128)(2,1)S(1)}, u32[]{:S(2)}, u32[]{:S(2)}) %collective-permute-start.13) | collective-permute-done | bytes 131104 | tf_op jit(solution)/shard_map/ppermute | solution.py:116
  66.4 1.9 %begin.1 = (bf16[2048,512]{1,0:T(8,128)(2,1)}, bf16[1,4,128,128]{3,2,1,0:T(8,128)(2,1)}, bf16[1,4,128,128]{3,2,1,0:T(8,128)(2,1)}) custom-call(s32[64]{0:T(128)S(1)} %get-tuple-element.26.table_ref, s32[2]{0:T(128)S(1)} %pad_add_fusion.place_ref, bf16[4,128,128]{2,1,0:T(8,128)(2,1)S(1)} %finish.1.own_ref, ...), custom_call_target="tpu_custom_call" | custom-call | bytes 1300000 | tf_op jit(solution)/shard_map/begin/pallas_call | solution.py:510
  68.4 2.4 %collective-permute-done.16.refs_0_ = bf16[8,128,128]{2,1,0:T(8,128)(2,1)S(1)} collective-permute-done((bf16[8,128,128]{2,1,0:T(8,128)(2,1)S(1)}, bf16[8,128,128]{2,1,0:T(8,128)(2,1)S(1)}, u32[]{:S(2)}, u32[]{:S(2)}) %collective-permute-start.16) | collective-permute-done | bytes 262176 | tf_op jit(solution)/shard_map/ppermute | solution.py:116
  70.8 0.9 %collective-permute-done.17.refs_1_ = bf16[8,128,128]{2,1,0:T(8,128)(2,1)S(1)} collective-permute-done((bf16[8,128,128]{2,1,0:T(8,128)(2,1)S(1)}, bf16[8,128,128]{2,1,0:T(8,128)(2,1)S(1)}, u32[]{:S(2)}, u32[]{:S(2)}) %collective-permute-start.17) | collective-permute-done | bytes 262176 | tf_op jit(solution)/shard_map/ppermute | solution.py:116
  71.6 0.5 collective-permute-start.19
  72.1 1.5 %more.2.refs_2_ = bf16[2048,512]{1,0:T(8,128)(2,1)} custom-call(s32[64]{0:T(128)S(1)} %get-tuple-element.26.table_ref, bf16[8,128,128]{2,1,0:T(8,128)(2,1)S(1)} %collective-permute-done.16.refs_0_, bf16[8,128,128]{2,1,0:T(8,128)(2,1)S(1)} %collective-permute-done.17.refs_1_, bf16[2048,512]{1,0:T(8,128)(2,1)} %get-tuple-element.46.refs_2_), custom_call_target="tpu_custom_call", output_to_operand_aliasing={{}: (3, {})} | custom-call | bytes 1000000 | tf_op jit(solution)/shard_map/more/pallas_call | solution.py:374
  73.6 1.5 %more.3 = bf16[2048,512]{1,0:T(8,128)(2,1)} custom-call(s32[64]{0:T(128)S(1)} %get-tuple-element.26.table_ref, bf16[8,128,128]{2,1,0:T(8,128)(2,1)S(1)} %collective-permute-done.18.refs_0_, bf16[8,128,128]{2,1,0:T(8,128)(2,1)S(1)} %collective-permute-done.19.refs_1_, bf16[2048,512]{1,0:T(8,128)(2,1)} %more.2.refs_2_), custom_call_target="tpu_custom_call", output_to_operand_aliasing={{}: (3, {})} | custom-call | bytes 1000000 | tf_op jit(solution)/shard_map/more/pallas_call | solution.py:374
  (32 shorter events, 0.2 us)
Async XLA Ops:
  0.6 4.0 %collective-permute-start = (bf16[256,2048]{1,0:T(8,128)(2,1)}, bf16[256,2048]{1,0:T(8,128)(2,1)S(1)}, u32[]{:S(2)}, u32[]{:S(2)}) collective-permute-start(bf16[256,2048]{1,0:T(8,128)(2,1)} %f_own.3), channel_id=1, source_target_pairs={{0,1},{1,0},{2,3},{3,2},{4,5},{5,4},{6,7},{7,6},{8,9},{9,8},{10,11... | collective-permute-start | bytes 3145736 | tf_op jit(solution)/shard_map/ppermute | solution.py:116
  1.1 3.4 %collective-permute-start.1 = (bf16[256,512]{1,0:T(8,128)(2,1)}, bf16[256,512]{1,0:T(8,128)(2,1)S(1)}, u32[]{:S(2)}, u32[]{:S(2)}) collective-permute-start(bf16[256,512]{1,0:T(8,128)(2,1)} %kv_ref.1), channel_id=1, source_target_pairs={{0,1},{1,0},{2,3},{3,2},{4,5},{5,4},{6,7},{7,6},{8,9},{9,8},{10,11... | collective-permute-start | bytes 786440 | tf_op jit(solution)/shard_map/ppermute | solution.py:116
  1.3 0.9 %copy-start.7 = (bf16[256,512]{1,0:T(8,128)(2,1)S(1)}, bf16[256,512]{1,0:T(8,128)(2,1)}, u32[]{:S(2)}) copy-start(bf16[256,512]{1,0:T(8,128)(2,1)} %kv_ref.1) | copy-start | bytes 786436
  2.3 0.7 copy-start.8
  4.6 1.2 %copy-start = (bf16[256,2048]{1,0:T(8,128)(2,1)S(1)}, bf16[256,2048]{1,0:T(8,128)(2,1)}, u32[]{:S(2)}) copy-start(bf16[256,2048]{1,0:T(8,128)(2,1)} %f_own.3) | copy-start | bytes 3145732
  7.2 15.2 %collective-permute-start.2 = (f32[8,128,128]{2,1,0:T(8,128)S(1)}, f32[8,128,128]{2,1,0:T(8,128)S(1)}, u32[]{:S(2)}, u32[]{:S(2)}) collective-permute-start(f32[8,128,128]{2,1,0:T(8,128)S(1)} %get-tuple-element.29), channel_id=1, source_target_pairs={{0,2},{2,0},{4,6},{6,4},{8,10},{10,8},{12,14},{14,12},{16,18},{18,... | collective-permute-start | bytes 1572872 | tf_op jit(solution)/shard_map/ppermute | solution.py:116
  10.2 14.1 %collective-permute-start.3 = (f32[8,128,128]{2,1,0:T(8,128)S(1)}, f32[8,128,128]{2,1,0:T(8,128)S(1)}, u32[]{:S(2)}, u32[]{:S(2)}) collective-permute-start(f32[8,128,128]{2,1,0:T(8,128)S(1)} %get-tuple-element.31), channel_id=1, source_target_pairs={{0,4},{2,6},{4,0},{6,2},{8,12},{10,14},{12,8},{14,10},{16,20},{18,... | collective-permute-start | bytes 1572872 | tf_op jit(solution)/shard_map/ppermute | solution.py:116
  22.5 18.9 %copy-start.1 = (bf16[1,4,128,128]{3,2,1,0:T(8,128)(2,1)S(1)}, bf16[1,4,128,128]{3,2,1,0:T(8,128)(2,1)}, u32[]{:S(2)}) copy-start(bf16[1,4,128,128]{3,2,1,0:T(8,128)(2,1)} %ql_ref.5) | copy-start | bytes 393220
  22.5 18.9 %copy-start.2 = (bf16[1,4,128,128]{3,2,1,0:T(8,128)(2,1)S(1)}, bf16[1,4,128,128]{3,2,1,0:T(8,128)(2,1)}, u32[]{:S(2)}) copy-start(bf16[1,4,128,128]{3,2,1,0:T(8,128)(2,1)} %qr_ref.5) | copy-start | bytes 393220
  22.5 18.9 %copy-start.3 = (f32[1,4,128,128]{3,2,1,0:T(8,128)S(1)}, f32[1,4,128,128]{3,2,1,0:T(8,128)}, u32[]{:S(2)}) copy-start(f32[1,4,128,128]{3,2,1,0:T(8,128)} %m_ref.1) | copy-start | bytes 786436
  22.5 18.9 %copy-start.4 = (f32[1,4,128,128]{3,2,1,0:T(8,128)S(1)}, f32[1,4,128,128]{3,2,1,0:T(8,128)}, u32[]{:S(2)}) copy-start(f32[1,4,128,128]{3,2,1,0:T(8,128)} %v_ref.1) | copy-start | bytes 786436
  22.5 18.8 %copy-start.5 = (f32[1,4,128,128]{3,2,1,0:T(8,128)S(1)}, f32[1,4,128,128]{3,2,1,0:T(8,128)}, u32[]{:S(2)}) copy-start(f32[1,4,128,128]{3,2,1,0:T(8,128)} %l_ref.1) | copy-start | bytes 786436
  22.5 18.8 %copy-start.6 = (f32[1,4,128,128]{3,2,1,0:T(8,128)S(1)}, f32[1,4,128,128]{3,2,1,0:T(8,128)}, u32[]{:S(2)}) copy-start(f32[1,4,128,128]{3,2,1,0:T(8,128)} %r_ref.1) | copy-start | bytes 786436
  22.5 7.9 %collective-permute-start.4 = (f32[4,128,128]{2,1,0:T(8,128)S(1)}, f32[4,128,128]{2,1,0:T(8,128)S(1)}, u32[]{:S(2)}, u32[]{:S(2)}) collective-permute-start(f32[4,128,128]{2,1,0:T(8,128)S(1)} %get-tuple-element.52), channel_id=1, source_target_pairs={{0,4},{2,6},{4,0},{6,2},{8,12},{10,14},{12,8},{14,10},{16,20},{18,... | collective-permute-start | bytes 786440 | tf_op jit(solution)/shard_map/ppermute | solution.py:116
  24.4 7.2 %collective-permute-start.5 = (f32[4,128,128]{2,1,0:T(8,128)S(1)}, f32[4,128,128]{2,1,0:T(8,128)S(1)}, u32[]{:S(2)}, u32[]{:S(2)}) collective-permute-start(f32[4,128,128]{2,1,0:T(8,128)S(1)} %get-tuple-element.54), channel_id=1, source_target_pairs={{0,2},{2,0},{4,6},{6,4},{8,10},{10,8},{12,14},{14,12},{16,18},{18,... | collective-permute-start | bytes 786440 | tf_op jit(solution)/shard_map/ppermute | solution.py:116
  31.7 6.4 %collective-permute-start.6 = (f32[2,2,128,128]{3,2,1,0:T(8,128)S(1)}, f32[2,2,128,128]{3,2,1,0:T(8,128)S(1)}, u32[]{:S(2)}, u32[]{:S(2)}) collective-permute-start(f32[2,2,128,128]{3,2,1,0:T(8,128)S(1)} %get-tuple-element.50), channel_id=1, source_target_pairs={{0,8},{2,10},{4,12},{6,14},{8,0},{10,2},{12,4},{14,6},{16,24},{18,... | collective-permute-start | bytes 786440 | tf_op jit(solution)/shard_map/ppermute | solution.py:116
  38.2 7.9 %collective-permute-start.7 = (f32[2,128,128]{2,1,0:T(8,128)S(1)}, f32[2,128,128]{2,1,0:T(8,128)S(1)}, u32[]{:S(2)}, u32[]{:S(2)}) collective-permute-start(f32[2,128,128]{2,1,0:T(8,128)S(1)} %get-tuple-element.55), channel_id=1, source_target_pairs={{0,16},{2,18},{4,20},{6,22},{8,24},{10,26},{12,28},{14,30},{16,0},... | collective-permute-start | bytes 393224 | tf_op jit(solution)/shard_map/ppermute | solution.py:116
  46.8 7.3 %collective-permute-start.10 = (bf16[2,128,128]{2,1,0:T(8,128)(2,1)S(1)}, bf16[2,128,128]{2,1,0:T(8,128)(2,1)S(1)}, u32[]{:S(2)}, u32[]{:S(2)}) collective-permute-start(bf16[2,128,128]{2,1,0:T(8,128)(2,1)S(1)} %get-tuple-element.34), channel_id=1, source_target_pairs={{0,24},{2,26},{4,28},{6,30},{8,16},{10,18},{12,20},{14,22},{16,8},... | collective-permute-start | bytes 196616 | tf_op jit(solution)/shard_map/ppermute | solution.py:116
  50.7 4.3 %collective-permute-start.9 = (bf16[2,128,128]{2,1,0:T(8,128)(2,1)S(1)}, bf16[2,128,128]{2,1,0:T(8,128)(2,1)S(1)}, u32[]{:S(2)}, u32[]{:S(2)}) collective-permute-start(bf16[2,128,128]{2,1,0:T(8,128)(2,1)S(1)} %get-tuple-element.34), channel_id=1, source_target_pairs={{0,8},{2,10},{4,12},{6,14},{8,0},{10,2},{12,4},{14,6},{16,24},{18,... | collective-permute-start | bytes 196616 | tf_op jit(solution)/shard_map/ppermute | solution.py:116
  50.7 5.2 %collective-permute-start.8 = (bf16[2,128,128]{2,1,0:T(8,128)(2,1)S(1)}, bf16[2,128,128]{2,1,0:T(8,128)(2,1)S(1)}, u32[]{:S(2)}, u32[]{:S(2)}) collective-permute-start(bf16[2,128,128]{2,1,0:T(8,128)(2,1)S(1)} %get-tuple-element.34), channel_id=1, source_target_pairs={{0,16},{2,18},{4,20},{6,22},{8,24},{10,26},{12,28},{14,30},{16,0},... | collective-permute-start | bytes 196616 | tf_op jit(solution)/shard_map/ppermute | solution.py:116
  55.9 5.0 %collective-permute-start.11 = (bf16[4,128,128]{2,1,0:T(8,128)(2,1)S(1)}, bf16[4,128,128]{2,1,0:T(8,128)(2,1)S(1)}, u32[]{:S(2)}, u32[]{:S(2)}) collective-permute-start(bf16[4,128,128]{2,1,0:T(8,128)(2,1)S(1)} %get-tuple-element.37), channel_id=1, source_target_pairs={{0,4},{2,6},{4,0},{6,2},{8,12},{10,14},{12,8},{14,10},{16,20},{18,... | collective-permute-start | bytes 393224 | tf_op jit(solution)/shard_map/ppermute | solution.py:116
  56.9 5.0 %collective-permute-start.12 = (bf16[4,128,128]{2,1,0:T(8,128)(2,1)S(1)}, bf16[4,128,128]{2,1,0:T(8,128)(2,1)S(1)}, u32[]{:S(2)}, u32[]{:S(2)}) collective-permute-start(bf16[4,128,128]{2,1,0:T(8,128)(2,1)S(1)} %get-tuple-element.38), channel_id=1, source_target_pairs={{0,2},{2,0},{4,6},{6,4},{8,10},{10,8},{12,14},{14,12},{16,18},{18,... | collective-permute-start | bytes 393224 | tf_op jit(solution)/shard_map/ppermute | solution.py:116
  61.9 4.5 %collective-permute-start.14 = (bf16[8,128,128]{2,1,0:T(8,128)(2,1)S(1)}, bf16[8,128,128]{2,1,0:T(8,128)(2,1)S(1)}, u32[]{:S(2)}, u32[]{:S(2)}) collective-permute-start(bf16[8,128,128]{2,1,0:T(8,128)(2,1)S(1)} %pad_maximum_fusion.2.refs_0_), channel_id=1, source_target_pairs={{0,1},{1,0},{2,3},{3,2},{4,5},{5,4},{6,7},{7,6},{8,9},{9,8},{10,11... | collective-permute-start | bytes 786440 | tf_op jit(solution)/shard_map/ppermute | solution.py:116
  62.0 4.5 %collective-permute-start.15 = (bf16[8,128,128]{2,1,0:T(8,128)(2,1)S(1)}, bf16[8,128,128]{2,1,0:T(8,128)(2,1)S(1)}, u32[]{:S(2)}, u32[]{:S(2)}) collective-permute-start(bf16[8,128,128]{2,1,0:T(8,128)(2,1)S(1)} %pad_maximum_fusion.3.refs_1_), channel_id=1, source_target_pairs={{0,1},{1,0},{2,3},{3,2},{4,5},{5,4},{6,7},{7,6},{8,9},{9,8},{10,11... | collective-permute-start | bytes 786440 | tf_op jit(solution)/shard_map/ppermute | solution.py:116
  62.5 8.3 %collective-permute-start.16 = (bf16[8,128,128]{2,1,0:T(8,128)(2,1)S(1)}, bf16[8,128,128]{2,1,0:T(8,128)(2,1)S(1)}, u32[]{:S(2)}, u32[]{:S(2)}) collective-permute-start(bf16[8,128,128]{2,1,0:T(8,128)(2,1)S(1)} %pad_maximum_fusion.2.refs_0_), channel_id=1, source_target_pairs={{0,2},{2,0},{4,6},{6,4},{8,10},{10,8},{12,14},{14,12},{16,18},{18,... | collective-permute-start | bytes 786440 | tf_op jit(solution)/shard_map/ppermute | solution.py:116
  63.6 8.0 %collective-permute-start.17 = (bf16[8,128,128]{2,1,0:T(8,128)(2,1)S(1)}, bf16[8,128,128]{2,1,0:T(8,128)(2,1)S(1)}, u32[]{:S(2)}, u32[]{:S(2)}) collective-permute-start(bf16[8,128,128]{2,1,0:T(8,128)(2,1)S(1)} %pad_maximum_fusion.3.refs_1_), channel_id=1, source_target_pairs={{0,4},{2,6},{4,0},{6,2},{8,12},{10,14},{12,8},{14,10},{16,20},{18,... | collective-permute-start | bytes 786440 | tf_op jit(solution)/shard_map/ppermute | solution.py:116
  65.1 1.3 %collective-permute-start.13 = (bf16[4,128,128]{2,1,0:T(8,128)(2,1)S(1)}, bf16[4,128,128]{2,1,0:T(8,128)(2,1)S(1)}, u32[]{:S(2)}, u32[]{:S(2)}) collective-permute-start(bf16[4,128,128]{2,1,0:T(8,128)(2,1)S(1)} %finish.1.own_ref), channel_id=1, source_target_pairs={{0,1},{1,0},{2,3},{3,2},{4,5},{5,4},{6,7},{7,6},{8,9},{9,8},{10,11... | collective-permute-start | bytes 393224 | tf_op jit(solution)/shard_map/ppermute | solution.py:116
  71.6 2.0 %collective-permute-start.18 = (bf16[8,128,128]{2,1,0:T(8,128)(2,1)S(1)}, bf16[8,128,128]{2,1,0:T(8,128)(2,1)S(1)}, u32[]{:S(2)}, u32[]{:S(2)}) collective-permute-start(bf16[8,128,128]{2,1,0:T(8,128)(2,1)S(1)} %collective-permute-done.16.refs_0_), channel_id=1, source_target_pairs={{0,1},{1,0},{2,3},{3,2},{4,5},{5,4},{6,7},{7,6},{8,9},{9,8},{10,11... | collective-permute-start | bytes 786440 | tf_op jit(solution)/shard_map/ppermute | solution.py:116
  71.6 2.0 %collective-permute-start.19 = (bf16[8,128,128]{2,1,0:T(8,128)(2,1)S(1)}, bf16[8,128,128]{2,1,0:T(8,128)(2,1)S(1)}, u32[]{:S(2)}, u32[]{:S(2)}) collective-permute-start(bf16[8,128,128]{2,1,0:T(8,128)(2,1)S(1)} %collective-permute-done.17.refs_1_), channel_id=1, source_target_pairs={{0,1},{1,0},{2,3},{3,2},{4,5},{5,4},{6,7},{7,6},{8,9},{9,8},{10,11... | collective-permute-start | bytes 786440 | tf_op jit(solution)/shard_map/ppermute | solution.py:116

commit v7 on v6

--- a/solution.py
+++ b/solution.py
@@ -330,12 +330,16 @@
     )(values)
 
 
-def place_tiles(col_tiles, entries, table_ref, sources, out, sems):
+def far_order(high):
+    return [0] + sorted(range(1, high), key=lambda p: (p % 2, -(p // 2)))
+
+
+def place_tiles(col_tiles, high, entries, table_ref, sources, out, sems):
     tile = sources[0].shape[-1]
     copies = []
     for entry, source in zip(entries, sources):
         for i in range(source.shape[0]):
-            block = table_ref[entry + i]
+            block = table_ref[entry + i - i % high + far_order(high)[i % high]]
             rows = pl.ds(pl.multiple_of(block // col_tiles * tile, tile), tile)
             columns = pl.ds(pl.multiple_of(block % col_tiles * tile, tile), tile)
             copies.append(
@@ -345,10 +349,10 @@
     return copies
 
 
-def begin_kernel(col_tiles, entries, table_ref, place_ref, own_ref, sib_ref, *refs):
+def begin_kernel(col_tiles, high, entries, table_ref, place_ref, own_ref, sib_ref, *refs):
     sources = refs[:-4]
     out, left, right, sems = refs[-4:]
-    copies = place_tiles(col_tiles, entries, table_ref, sources, out, sems)
+    copies = place_tiles(col_tiles, high, entries, table_ref, sources, out, sems)
     core = place_ref[1]
     for source, first in ((own_ref, 2 * core), (sib_ref, 2 - 2 * core)):
         for k in range(2):
@@ -363,16 +367,16 @@
         copy.wait()
 
 
-def more_kernel(col_tiles, entries, table_ref, *refs):
+def more_kernel(col_tiles, high, entries, table_ref, *refs):
     out, sems = refs[-2:]
-    for copy in place_tiles(col_tiles, entries, table_ref, refs[:-3], out, sems):
+    for copy in place_tiles(col_tiles, high, entries, table_ref, refs[:-3], out, sems):
         copy.wait()
 
 
-def place_more(update, table, col_tiles, entries, sources):
+def place_more(update, table, col_tiles, high, entries, sources):
     count = sum(x.shape[0] for x in sources)
     return pl.pallas_call(
-        functools.partial(more_kernel, col_tiles, entries),
+        functools.partial(more_kernel, col_tiles, high, entries),
         out_shape=jax.ShapeDtypeStruct(update.shape, update.dtype),
         in_specs=[SMEM] + [VMEM] * len(sources) + [HBM],
         out_specs=HBM,
@@ -486,7 +490,7 @@
     bits = len(orders[0])
     high = owners // 4
     tiles = []
-    for p in range(high):
+    for p in far_order(high):
         offset = sum(((p >> (bits - 3 - i)) & 1) << bit for i, bit in enumerate(orders[0][2:]))
         tiles.append(swap_along(direction, "dp", owners, offset) if offset else direction)
     values = on_slots(
@@ -505,25 +509,30 @@
     mine, fresh = lax.optimization_barrier((mine, fresh))
     other = [swap_along(m, "dp", owners, 1 << order[0]) for m, order in zip(mine, orders)]
     fresh_sib = swap_along(fresh, "inner", 2, 1)
-    mine_sib = [swap_along(m, "inner", 2, 1) for m in mine]
     basis = jax.ShapeDtypeStruct(left_basis.shape, left_basis.dtype)
     update, new_left, new_right = pl.pallas_call(
-        functools.partial(
-            begin_kernel, col_tiles, (0, owners, 2 * owners, 3 * owners)
-        ),
+        functools.partial(begin_kernel, col_tiles, high, (0, owners)),
         out_shape=(jax.ShapeDtypeStruct((d_win, width), jnp.bfloat16), basis, basis),
-        in_specs=[SMEM, SMEM] + [VMEM] * 6,
+        in_specs=[SMEM, SMEM] + [VMEM] * 4,
         out_specs=(HBM, HBM, HBM),
-        scratch_shapes=[pltpu.SemaphoreType.DMA((4 * near + 8,))],
+        scratch_shapes=[pltpu.SemaphoreType.DMA((2 * near + 8,))],
         compiler_params=SMALL,
-        cost_estimate=pl.CostEstimate(flops=0, bytes_accessed=1_300_000, transcendentals=0),
+        cost_estimate=pl.CostEstimate(flops=0, bytes_accessed=800_000, transcendentals=0),
         name="begin",
-    )(table, place, fresh, fresh_sib, *mine, *mine_sib)
+    )(table, place, fresh, fresh_sib, *mine)
     update, other = lax.optimization_barrier((update, other))
+    mine_sib = [swap_along(m, "inner", 2, 1) for m in mine]
     other_sib = [swap_along(o, "inner", 2, 1) for o in other]
-    update = place_more(update, table, col_tiles, (near, owners + near), other)
     update = place_more(
-        update, table, col_tiles, (2 * owners + near, 3 * owners + near), other_sib
+        update,
+        table,
+        col_tiles,
+        high,
+        (2 * owners, 3 * owners, near, owners + near),
+        mine_sib + other,
+    )
+    update = place_more(
+        update, table, col_tiles, high, (2 * owners + near, 3 * owners + near), other_sib
     )
     return update, new_left, new_right
 

time: 75.2 us -> 74 us (0.984)
  waiting for transfers between devices: 31.1 us -> 28.6 us
  starting transfers between devices: 23.6 us -> 24.9 us
    ppermute x20, waiting for transfers between devices: 31.1 us -> 28.6 us  [swap_along(): return lax.ppermute(values, axis, [(i, i ^ bit) for i in range(size)])]
    ppermute x20, starting transfers between devices: 23.6 us -> 24.9 us  [swap_along(): return lax.ppermute(values, axis, [(i, i ^ bit) for i in range(size)])]
where the time goes in v7:
time: 74 us; the launch traced here: 73.8 us
  waiting for transfers between devices  28.6 us (39%)
  starting transfers between devices  24.9 us (34%)
  Pallas kernels  16.2 us (22%)
  local copies, waits for them, and re-layouts  2.89 us (4%)
  between operations  0.88 us (1%)
    ppermute x20, waiting for transfers between devices, swap_along(): return lax.ppermute(values, axis, [(i, i ^ bit) for i in range(size)])  28.6 us
    ppermute x20, starting transfers between devices, swap_along(): return lax.ppermute(values, axis, [(i, i ^ bit) for i in range(size)])  24.9 us
    pallas_call x3, Pallas kernels, on_slots(): pl.pallas_call(kernel, out_shape=tuple(outs), grid_spec=pltpu.PrefetchSca...  3.98 us
    pallas_call x2, Pallas kernels, place_more(): pl.pallas_call(functools.partial(more_kernel, col_tiles, high, entries),...  3.25 us
    pallas_call x1, Pallas kernels, sweeping(): pl.pallas_call(kernel, out_shape=jax.ShapeDtypeStruct(values.shape, dtype...  2.89 us
    unnamed x18, local copies, waits for them, and re-layouts  2.86 us
    pallas_call x2, Pallas kernels, tiles_from(): pl.pallas_call(functools.partial(tiles_kernel, owners, first), out_shape=...  2.81 us
    pallas_call x1, Pallas kernels, per_device_dealt(): pl.pallas_call(functools.partial(table_kernel, owners, capacity), out_sha...  1.65 us
  transfers between devices with their start and end apart: 20, of which 11 were waited for; matrix products, arithmetic and copies ran while one was open for 0% of the time, Pallas kernels for 17%

profile of v7, /device:TPU:0, one launch (start us, length us, event | category | flops | bytes accessed | tf_op | source)
XLA Modules:
  0.0 73.8 jit_solution(16370603998437310076)
XLA Ops:
  0.6 0.5 collective-permute-start
  1.1 0.1 collective-permute-start.1
  1.2 0.1 pad_add_fusion.place_ref
  1.3 0.9 %copy-done.7 = bf16[256,512]{1,0:T(8,128)(2,1)S(1)} copy-done((bf16[256,512]{1,0:T(8,128)(2,1)S(1)}, bf16[256,512]{1,0:T(8,128)(2,1)}, u32[]{:S(2)}) %copy-start.7) | copy-done | bytes 262168
  2.3 0.7 copy-done.8
  2.9 1.7 %table.1 = (s32[64]{0:T(128)S(1)}, bf16[512,256]{1,0:T(8,128)(2,1)S(1)}) custom-call(s32[2]{0:T(128)S(1)} %pad_add_fusion.place_ref, s32[64]{0:T(128)S(1)} %copy-done.8, bf16[256,512]{1,0:T(8,128)(2,1)S(1)} %copy-done.7), custom_call_target="tpu_custom_call" | custom-call | bytes 1000000 | tf_op jit(solution)/shard_map/table/pallas_call | solution.py:420
  4.6 1.2 %copy-done = bf16[256,2048]{1,0:T(8,128)(2,1)S(1)} copy-done((bf16[256,2048]{1,0:T(8,128)(2,1)S(1)}, bf16[256,2048]{1,0:T(8,128)(2,1)}, u32[]{:S(2)}) %copy-start) | copy-done | bytes 1048600
  5.8 1.4 %tiles.3 = (f32[8,128,128]{2,1,0:T(8,128)S(1)}, f32[8,128,128]{2,1,0:T(8,128)S(1)}) custom-call(s32[64]{0:T(128)S(1)} %get-tuple-element.26.table_ref, bf16[256,2048]{1,0:T(8,128)(2,1)S(1)} %copy-done, bf16[256,2048]{1,0:T(8,128)(2,1)S(1)} %collective-permute-done.f_sib, bf16[512,256]{1,0:T(8,128)(2,1)S(1)} %get-tuple-element.27.own_rows, ...), custom_call_target="tpu_custom_call" | custom-call | flops 536870912 | bytes 3500000 | tf_op jit(solution)/shard_map/tiles/pallas_call | solution.py:439
  7.2 3.0 %collective-permute-start.2 = (f32[8,128,128]{2,1,0:T(8,128)S(1)}, f32[8,128,128]{2,1,0:T(8,128)S(1)}, u32[]{:S(2)}, u32[]{:S(2)}) collective-permute-start(f32[8,128,128]{2,1,0:T(8,128)S(1)} %get-tuple-element.29), channel_id=1, source_target_pairs={{0,2},{2,0},{4,6},{6,4},{8,10},{10,8},{12,14},{14,12},{16,18},{18,... | collective-permute-start | bytes 1572872 | tf_op jit(solution)/shard_map/ppermute | solution.py:116
  10.2 1.5 %collective-permute-start.3 = (f32[8,128,128]{2,1,0:T(8,128)S(1)}, f32[8,128,128]{2,1,0:T(8,128)S(1)}, u32[]{:S(2)}, u32[]{:S(2)}) collective-permute-start(f32[8,128,128]{2,1,0:T(8,128)S(1)} %get-tuple-element.31), channel_id=1, source_target_pairs={{0,4},{2,6},{4,0},{6,2},{8,12},{10,14},{12,8},{14,10},{16,20},{18,... | collective-permute-start | bytes 1572872 | tf_op jit(solution)/shard_map/ppermute | solution.py:116
  11.7 1.4 %tiles.2 = (f32[8,128,128]{2,1,0:T(8,128)S(1)}, f32[8,128,128]{2,1,0:T(8,128)S(1)}) custom-call(s32[64]{0:T(128)S(1)} %get-tuple-element.26.table_ref, bf16[256,2048]{1,0:T(8,128)(2,1)S(1)} %copy-done, bf16[256,2048]{1,0:T(8,128)(2,1)S(1)} %collective-permute-done.f_sib, bf16[512,256]{1,0:T(8,128)(2,1)S(1)} %get-tuple-element.27.own_rows, ...), custom_call_target="tpu_custom_call" | custom-call | flops 536870912 | bytes 3500000 | tf_op jit(solution)/shard_map/tiles/pallas_call | solution.py:439
  13.1 9.2 %collective-permute-done.2 = f32[8,128,128]{2,1,0:T(8,128)S(1)} collective-permute-done((f32[8,128,128]{2,1,0:T(8,128)S(1)}, f32[8,128,128]{2,1,0:T(8,128)S(1)}, u32[]{:S(2)}, u32[]{:S(2)}) %collective-permute-start.2) | collective-permute-done | bytes 524320 | tf_op jit(solution)/shard_map/ppermute | solution.py:116
  22.4 0.1 fusion.5
  22.4 0.0 copy-start.1
  22.5 0.0 copy-start.4
  22.5 0.0 copy-start.5
  22.5 1.8 %collective-permute-start.4 = (f32[4,128,128]{2,1,0:T(8,128)S(1)}, f32[4,128,128]{2,1,0:T(8,128)S(1)}, u32[]{:S(2)}, u32[]{:S(2)}) collective-permute-start(f32[4,128,128]{2,1,0:T(8,128)S(1)} %get-tuple-element.52), channel_id=1, source_target_pairs={{0,4},{2,6},{4,0},{6,2},{8,12},{10,14},{12,8},{14,10},{16,20},{18,... | collective-permute-start | bytes 786440 | tf_op jit(solution)/shard_map/ppermute | solution.py:116
  24.3 0.1 fusion.4
  24.4 1.6 %collective-permute-start.5 = (f32[4,128,128]{2,1,0:T(8,128)S(1)}, f32[4,128,128]{2,1,0:T(8,128)S(1)}, u32[]{:S(2)}, u32[]{:S(2)}) collective-permute-start(f32[4,128,128]{2,1,0:T(8,128)S(1)} %get-tuple-element.54), channel_id=1, source_target_pairs={{0,2},{2,0},{4,6},{6,4},{8,10},{10,8},{12,14},{14,12},{16,18},{18,... | collective-permute-start | bytes 786440 | tf_op jit(solution)/shard_map/ppermute | solution.py:116
  26.0 4.4 %collective-permute-done.4 = f32[4,128,128]{2,1,0:T(8,128)S(1)} collective-permute-done((f32[4,128,128]{2,1,0:T(8,128)S(1)}, f32[4,128,128]{2,1,0:T(8,128)S(1)}, u32[]{:S(2)}, u32[]{:S(2)}) %collective-permute-start.4) | collective-permute-done | bytes 262176 | tf_op jit(solution)/shard_map/ppermute | solution.py:116
  30.4 1.3 %collective-permute-done.5 = f32[4,128,128]{2,1,0:T(8,128)S(1)} collective-permute-done((f32[4,128,128]{2,1,0:T(8,128)S(1)}, f32[4,128,128]{2,1,0:T(8,128)S(1)}, u32[]{:S(2)}, u32[]{:S(2)}) %collective-permute-start.5) | collective-permute-done | bytes 262176 | tf_op jit(solution)/shard_map/ppermute | solution.py:116
  31.6 0.1 fusion.1
  31.7 1.6 %collective-permute-start.6 = (f32[2,2,128,128]{3,2,1,0:T(8,128)S(1)}, f32[2,2,128,128]{3,2,1,0:T(8,128)S(1)}, u32[]{:S(2)}, u32[]{:S(2)}) collective-permute-start(f32[2,2,128,128]{3,2,1,0:T(8,128)S(1)} %get-tuple-element.50), channel_id=1, source_target_pairs={{0,8},{2,10},{4,12},{6,14},{8,0},{10,2},{12,4},{14,6},{16,24},{18,... | collective-permute-start | bytes 786440 | tf_op jit(solution)/shard_map/ppermute | solution.py:116
  33.3 4.8 %collective-permute-done.6 = f32[2,2,128,128]{3,2,1,0:T(8,128)S(1)} collective-permute-done((f32[2,2,128,128]{3,2,1,0:T(8,128)S(1)}, f32[2,2,128,128]{3,2,1,0:T(8,128)S(1)}, u32[]{:S(2)}, u32[]{:S(2)}) %collective-permute-start.6) | collective-permute-done | bytes 262176 | tf_op jit(solution)/shard_map/ppermute | solution.py:116
  38.2 3.1 %collective-permute-start.7 = (f32[2,128,128]{2,1,0:T(8,128)S(1)}, f32[2,128,128]{2,1,0:T(8,128)S(1)}, u32[]{:S(2)}, u32[]{:S(2)}) collective-permute-start(f32[2,128,128]{2,1,0:T(8,128)S(1)} %get-tuple-element.55), channel_id=1, source_target_pairs={{0,16},{2,18},{4,20},{6,22},{8,24},{10,26},{12,28},{14,30},{16,0},... | collective-permute-start | bytes 393224 | tf_op jit(solution)/shard_map/ppermute | solution.py:116
  41.3 0.5 rotated.1
  41.8 4.2 %collective-permute-done.7.b_ref = f32[2,128,128]{2,1,0:T(8,128)S(1)} collective-permute-done((f32[2,128,128]{2,1,0:T(8,128)S(1)}, f32[2,128,128]{2,1,0:T(8,128)S(1)}, u32[]{:S(2)}, u32[]{:S(2)}) %collective-permute-start.7) | collective-permute-done | bytes 131104 | tf_op jit(solution)/shard_map/ppermute | solution.py:116
  46.0 0.7 direction.1
  46.8 1.7 %collective-permute-start.10 = (bf16[2,128,128]{2,1,0:T(8,128)(2,1)S(1)}, bf16[2,128,128]{2,1,0:T(8,128)(2,1)S(1)}, u32[]{:S(2)}, u32[]{:S(2)}) collective-permute-start(bf16[2,128,128]{2,1,0:T(8,128)(2,1)S(1)} %get-tuple-element.34), channel_id=1, source_target_pairs={{0,16},{2,18},{4,20},{6,22},{8,24},{10,26},{12,28},{14,30},{16,0},... | collective-permute-start | bytes 196616 | tf_op jit(solution)/shard_map/ppermute | solution.py:116
  48.5 3.7 %collective-permute-start.9 = (bf16[2,128,128]{2,1,0:T(8,128)(2,1)S(1)}, bf16[2,128,128]{2,1,0:T(8,128)(2,1)S(1)}, u32[]{:S(2)}, u32[]{:S(2)}) collective-permute-start(bf16[2,128,128]{2,1,0:T(8,128)(2,1)S(1)} %get-tuple-element.34), channel_id=1, source_target_pairs={{0,24},{2,26},{4,28},{6,30},{8,16},{10,18},{12,20},{14,22},{16,8},... | collective-permute-start | bytes 196616 | tf_op jit(solution)/shard_map/ppermute | solution.py:116
  52.2 0.5 collective-permute-start.8
  52.7 2.8 %refresh.1.iter_ref = f32[4,128,128]{2,1,0:T(8,128)S(1)} custom-call(s32[1]{0:T(128)} %bitcast.1.side_ref, f32[2,128,128]{2,1,0:T(8,128)S(1)} %get-tuple-element.35.g_ref, f32[4,128,128]{2,1,0:T(8,128)S(1)} %get-tuple-element.36.power_ref, bf16[1,4,128,128]{3,2,1,0:T(8,128)(2,1)S(1)} %copy-done.1, bf16[1,4,128,128]{3,2,1,0:T(8,128)(2,1)S(1)} %copy-done.2), custom_call_target="tpu_custom_call" | custom-call | flops 939524096 | bytes 800000 | tf_op jit(solution)/shard_map/refresh/pallas_call | solution.py:272
  55.5 0.9 %collective-permute-done.8 = bf16[2,128,128]{2,1,0:T(8,128)(2,1)S(1)} collective-permute-done((bf16[2,128,128]{2,1,0:T(8,128)(2,1)S(1)}, bf16[2,128,128]{2,1,0:T(8,128)(2,1)S(1)}, u32[]{:S(2)}, u32[]{:S(2)}) %collective-permute-start.8) | collective-permute-done | bytes 65568 | tf_op jit(solution)/shard_map/ppermute | solution.py:116
  56.5 1.0 %collective-permute-start.11 = (bf16[4,128,128]{2,1,0:T(8,128)(2,1)S(1)}, bf16[4,128,128]{2,1,0:T(8,128)(2,1)S(1)}, u32[]{:S(2)}, u32[]{:S(2)}) collective-permute-start(bf16[4,128,128]{2,1,0:T(8,128)(2,1)S(1)} %get-tuple-element.37), channel_id=1, source_target_pairs={{0,4},{2,6},{4,0},{6,2},{8,12},{10,14},{12,8},{14,10},{16,20},{18,... | collective-permute-start | bytes 393224 | tf_op jit(solution)/shard_map/ppermute | solution.py:116
  57.6 1.0 %collective-permute-start.12 = (bf16[4,128,128]{2,1,0:T(8,128)(2,1)S(1)}, bf16[4,128,128]{2,1,0:T(8,128)(2,1)S(1)}, u32[]{:S(2)}, u32[]{:S(2)}) collective-permute-start(bf16[4,128,128]{2,1,0:T(8,128)(2,1)S(1)} %get-tuple-element.38), channel_id=1, source_target_pairs={{0,2},{2,0},{4,6},{6,4},{8,10},{10,8},{12,14},{14,12},{16,18},{18,... | collective-permute-start | bytes 393224 | tf_op jit(solution)/shard_map/ppermute | solution.py:116
  58.6 2.9 %finish.1.own_ref = bf16[4,128,128]{2,1,0:T(8,128)(2,1)S(1)} custom-call(f32[4,128,128]{2,1,0:T(8,128)S(1)} %refresh.1.iter_ref), custom_call_target="tpu_custom_call" | custom-call | flops 939524096 | bytes 400000 | tf_op jit(solution)/shard_map/finish/pallas_call | solution.py:322
  61.5 0.1 collective-permute-done.11
  61.6 1.0 %collective-permute-done.12 = bf16[4,128,128]{2,1,0:T(8,128)(2,1)S(1)} collective-permute-done((bf16[4,128,128]{2,1,0:T(8,128)(2,1)S(1)}, bf16[4,128,128]{2,1,0:T(8,128)(2,1)S(1)}, u32[]{:S(2)}, u32[]{:S(2)}) %collective-permute-start.12) | collective-permute-done | bytes 131104 | tf_op jit(solution)/shard_map/ppermute | solution.py:116
  62.6 1.1 %collective-permute-start.14 = (bf16[8,128,128]{2,1,0:T(8,128)(2,1)S(1)}, bf16[8,128,128]{2,1,0:T(8,128)(2,1)S(1)}, u32[]{:S(2)}, u32[]{:S(2)}) collective-permute-start(bf16[8,128,128]{2,1,0:T(8,128)(2,1)S(1)} %pad_maximum_fusion.2.refs_0_), channel_id=1, source_target_pairs={{0,2},{2,0},{4,6},{6,4},{8,10},{10,8},{12,14},{14,12},{16,18},{18,... | collective-permute-start | bytes 786440 | tf_op jit(solution)/shard_map/ppermute | solution.py:116
  63.6 1.5 %collective-permute-start.15 = (bf16[8,128,128]{2,1,0:T(8,128)(2,1)S(1)}, bf16[8,128,128]{2,1,0:T(8,128)(2,1)S(1)}, u32[]{:S(2)}, u32[]{:S(2)}) collective-permute-start(bf16[8,128,128]{2,1,0:T(8,128)(2,1)S(1)} %pad_maximum_fusion.3.refs_1_), channel_id=1, source_target_pairs={{0,4},{2,6},{4,0},{6,2},{8,12},{10,14},{12,8},{14,10},{16,20},{18,... | collective-permute-start | bytes 786440 | tf_op jit(solution)/shard_map/ppermute | solution.py:116
  65.2 0.5 collective-permute-start.18
  65.7 0.8 %collective-permute-done.13.sib_ref = bf16[4,128,128]{2,1,0:T(8,128)(2,1)S(1)} collective-permute-done((bf16[4,128,128]{2,1,0:T(8,128)(2,1)S(1)}, bf16[4,128,128]{2,1,0:T(8,128)(2,1)S(1)}, u32[]{:S(2)}, u32[]{:S(2)}) %collective-permute-start.13) | collective-permute-done | bytes 131104 | tf_op jit(solution)/shard_map/ppermute | solution.py:116
  66.5 1.6 %begin.1 = (bf16[2048,512]{1,0:T(8,128)(2,1)}, bf16[1,4,128,128]{3,2,1,0:T(8,128)(2,1)}, bf16[1,4,128,128]{3,2,1,0:T(8,128)(2,1)}) custom-call(s32[64]{0:T(128)S(1)} %get-tuple-element.26.table_ref, s32[2]{0:T(128)S(1)} %pad_add_fusion.place_ref, bf16[4,128,128]{2,1,0:T(8,128)(2,1)S(1)} %finish.1.own_ref, ...), custom_call_target="tpu_custom_call" | custom-call | bytes 800000 | tf_op jit(solution)/shard_map/begin/pallas_call | solution.py:513
  68.2 0.8 %collective-permute-done.14.refs_2_ = bf16[8,128,128]{2,1,0:T(8,128)(2,1)S(1)} collective-permute-done((bf16[8,128,128]{2,1,0:T(8,128)(2,1)S(1)}, bf16[8,128,128]{2,1,0:T(8,128)(2,1)S(1)}, u32[]{:S(2)}, u32[]{:S(2)}) %collective-permute-start.14) | collective-permute-done | bytes 262176 | tf_op jit(solution)/shard_map/ppermute | solution.py:116
  69.0 1.0 %collective-permute-done.15.refs_3_ = bf16[8,128,128]{2,1,0:T(8,128)(2,1)S(1)} collective-permute-done((bf16[8,128,128]{2,1,0:T(8,128)(2,1)S(1)}, bf16[8,128,128]{2,1,0:T(8,128)(2,1)S(1)}, u32[]{:S(2)}, u32[]{:S(2)}) %collective-permute-start.15) | collective-permute-done | bytes 262176 | tf_op jit(solution)/shard_map/ppermute | solution.py:116
  70.0 0.5 collective-permute-start.17
  70.5 1.8 %more.2.refs_2_ = bf16[2048,512]{1,0:T(8,128)(2,1)} custom-call(s32[64]{0:T(128)S(1)} %get-tuple-element.26.table_ref, bf16[8,128,128]{2,1,0:T(8,128)(2,1)S(1)} %collective-permute-done.18.refs_0_, bf16[8,128,128]{2,1,0:T(8,128)(2,1)S(1)} %collective-permute-done.19.refs_1_, ...), custom_call_target="tpu_custom_call", output_to_operand_aliasing={{}: (5, {})} | custom-call | bytes 1000000 | tf_op jit(solution)/shard_map/more/pallas_call | solution.py:378
  72.3 1.5 %more.3 = bf16[2048,512]{1,0:T(8,128)(2,1)} custom-call(s32[64]{0:T(128)S(1)} %get-tuple-element.26.table_ref, bf16[8,128,128]{2,1,0:T(8,128)(2,1)S(1)} %collective-permute-done.16.refs_0_, bf16[8,128,128]{2,1,0:T(8,128)(2,1)S(1)} %collective-permute-done.17.refs_1_, bf16[2048,512]{1,0:T(8,128)(2,1)} %more.2.refs_2_), custom_call_target="tpu_custom_call", output_to_operand_aliasing={{}: (3, {})} | custom-call | bytes 1000000 | tf_op jit(solution)/shard_map/more/pallas_call | solution.py:378
  (32 shorter events, 0.2 us)
Async XLA Ops:
  0.6 4.0 %collective-permute-start = (bf16[256,2048]{1,0:T(8,128)(2,1)}, bf16[256,2048]{1,0:T(8,128)(2,1)S(1)}, u32[]{:S(2)}, u32[]{:S(2)}) collective-permute-start(bf16[256,2048]{1,0:T(8,128)(2,1)} %f_own.3), channel_id=1, source_target_pairs={{0,1},{1,0},{2,3},{3,2},{4,5},{5,4},{6,7},{7,6},{8,9},{9,8},{10,11... | collective-permute-start | bytes 3145736 | tf_op jit(solution)/shard_map/ppermute | solution.py:116
  1.1 3.4 %collective-permute-start.1 = (bf16[256,512]{1,0:T(8,128)(2,1)}, bf16[256,512]{1,0:T(8,128)(2,1)S(1)}, u32[]{:S(2)}, u32[]{:S(2)}) collective-permute-start(bf16[256,512]{1,0:T(8,128)(2,1)} %kv_ref.1), channel_id=1, source_target_pairs={{0,1},{1,0},{2,3},{3,2},{4,5},{5,4},{6,7},{7,6},{8,9},{9,8},{10,11... | collective-permute-start | bytes 786440 | tf_op jit(solution)/shard_map/ppermute | solution.py:116
  1.3 0.9 %copy-start.7 = (bf16[256,512]{1,0:T(8,128)(2,1)S(1)}, bf16[256,512]{1,0:T(8,128)(2,1)}, u32[]{:S(2)}) copy-start(bf16[256,512]{1,0:T(8,128)(2,1)} %kv_ref.1) | copy-start | bytes 786436
  2.3 0.7 copy-start.8
  4.6 1.2 %copy-start = (bf16[256,2048]{1,0:T(8,128)(2,1)S(1)}, bf16[256,2048]{1,0:T(8,128)(2,1)}, u32[]{:S(2)}) copy-start(bf16[256,2048]{1,0:T(8,128)(2,1)} %f_own.3) | copy-start | bytes 3145732
  7.2 15.2 %collective-permute-start.2 = (f32[8,128,128]{2,1,0:T(8,128)S(1)}, f32[8,128,128]{2,1,0:T(8,128)S(1)}, u32[]{:S(2)}, u32[]{:S(2)}) collective-permute-start(f32[8,128,128]{2,1,0:T(8,128)S(1)} %get-tuple-element.29), channel_id=1, source_target_pairs={{0,2},{2,0},{4,6},{6,4},{8,10},{10,8},{12,14},{14,12},{16,18},{18,... | collective-permute-start | bytes 1572872 | tf_op jit(solution)/shard_map/ppermute | solution.py:116
  10.2 14.1 %collective-permute-start.3 = (f32[8,128,128]{2,1,0:T(8,128)S(1)}, f32[8,128,128]{2,1,0:T(8,128)S(1)}, u32[]{:S(2)}, u32[]{:S(2)}) collective-permute-start(f32[8,128,128]{2,1,0:T(8,128)S(1)} %get-tuple-element.31), channel_id=1, source_target_pairs={{0,4},{2,6},{4,0},{6,2},{8,12},{10,14},{12,8},{14,10},{16,20},{18,... | collective-permute-start | bytes 1572872 | tf_op jit(solution)/shard_map/ppermute | solution.py:116
  22.4 18.9 %copy-start.1 = (bf16[1,4,128,128]{3,2,1,0:T(8,128)(2,1)S(1)}, bf16[1,4,128,128]{3,2,1,0:T(8,128)(2,1)}, u32[]{:S(2)}) copy-start(bf16[1,4,128,128]{3,2,1,0:T(8,128)(2,1)} %ql_ref.5) | copy-start | bytes 393220
  22.5 18.9 %copy-start.2 = (bf16[1,4,128,128]{3,2,1,0:T(8,128)(2,1)S(1)}, bf16[1,4,128,128]{3,2,1,0:T(8,128)(2,1)}, u32[]{:S(2)}) copy-start(bf16[1,4,128,128]{3,2,1,0:T(8,128)(2,1)} %qr_ref.5) | copy-start | bytes 393220
  22.5 18.8 %copy-start.3 = (f32[1,4,128,128]{3,2,1,0:T(8,128)S(1)}, f32[1,4,128,128]{3,2,1,0:T(8,128)}, u32[]{:S(2)}) copy-start(f32[1,4,128,128]{3,2,1,0:T(8,128)} %m_ref.1) | copy-start | bytes 786436
  22.5 18.8 %copy-start.4 = (f32[1,4,128,128]{3,2,1,0:T(8,128)S(1)}, f32[1,4,128,128]{3,2,1,0:T(8,128)}, u32[]{:S(2)}) copy-start(f32[1,4,128,128]{3,2,1,0:T(8,128)} %v_ref.1) | copy-start | bytes 786436
  22.5 18.8 %copy-start.5 = (f32[1,4,128,128]{3,2,1,0:T(8,128)S(1)}, f32[1,4,128,128]{3,2,1,0:T(8,128)}, u32[]{:S(2)}) copy-start(f32[1,4,128,128]{3,2,1,0:T(8,128)} %l_ref.1) | copy-start | bytes 786436
  22.5 18.8 %copy-start.6 = (f32[1,4,128,128]{3,2,1,0:T(8,128)S(1)}, f32[1,4,128,128]{3,2,1,0:T(8,128)}, u32[]{:S(2)}) copy-start(f32[1,4,128,128]{3,2,1,0:T(8,128)} %r_ref.1) | copy-start | bytes 786436
  22.5 7.8 %collective-permute-start.4 = (f32[4,128,128]{2,1,0:T(8,128)S(1)}, f32[4,128,128]{2,1,0:T(8,128)S(1)}, u32[]{:S(2)}, u32[]{:S(2)}) collective-permute-start(f32[4,128,128]{2,1,0:T(8,128)S(1)} %get-tuple-element.52), channel_id=1, source_target_pairs={{0,4},{2,6},{4,0},{6,2},{8,12},{10,14},{12,8},{14,10},{16,20},{18,... | collective-permute-start | bytes 786440 | tf_op jit(solution)/shard_map/ppermute | solution.py:116
  24.4 7.2 %collective-permute-start.5 = (f32[4,128,128]{2,1,0:T(8,128)S(1)}, f32[4,128,128]{2,1,0:T(8,128)S(1)}, u32[]{:S(2)}, u32[]{:S(2)}) collective-permute-start(f32[4,128,128]{2,1,0:T(8,128)S(1)} %get-tuple-element.54), channel_id=1, source_target_pairs={{0,2},{2,0},{4,6},{6,4},{8,10},{10,8},{12,14},{14,12},{16,18},{18,... | collective-permute-start | bytes 786440 | tf_op jit(solution)/shard_map/ppermute | solution.py:116
  31.7 6.4 %collective-permute-start.6 = (f32[2,2,128,128]{3,2,1,0:T(8,128)S(1)}, f32[2,2,128,128]{3,2,1,0:T(8,128)S(1)}, u32[]{:S(2)}, u32[]{:S(2)}) collective-permute-start(f32[2,2,128,128]{3,2,1,0:T(8,128)S(1)} %get-tuple-element.50), channel_id=1, source_target_pairs={{0,8},{2,10},{4,12},{6,14},{8,0},{10,2},{12,4},{14,6},{16,24},{18,... | collective-permute-start | bytes 786440 | tf_op jit(solution)/shard_map/ppermute | solution.py:116
  38.2 7.9 %collective-permute-start.7 = (f32[2,128,128]{2,1,0:T(8,128)S(1)}, f32[2,128,128]{2,1,0:T(8,128)S(1)}, u32[]{:S(2)}, u32[]{:S(2)}) collective-permute-start(f32[2,128,128]{2,1,0:T(8,128)S(1)} %get-tuple-element.55), channel_id=1, source_target_pairs={{0,16},{2,18},{4,20},{6,22},{8,24},{10,26},{12,28},{14,30},{16,0},... | collective-permute-start | bytes 393224 | tf_op jit(solution)/shard_map/ppermute | solution.py:116
  46.8 8.7 %collective-permute-start.10 = (bf16[2,128,128]{2,1,0:T(8,128)(2,1)S(1)}, bf16[2,128,128]{2,1,0:T(8,128)(2,1)S(1)}, u32[]{:S(2)}, u32[]{:S(2)}) collective-permute-start(bf16[2,128,128]{2,1,0:T(8,128)(2,1)S(1)} %get-tuple-element.34), channel_id=1, source_target_pairs={{0,16},{2,18},{4,20},{6,22},{8,24},{10,26},{12,28},{14,30},{16,0},... | collective-permute-start | bytes 196616 | tf_op jit(solution)/shard_map/ppermute | solution.py:116
  48.5 7.0 %collective-permute-start.9 = (bf16[2,128,128]{2,1,0:T(8,128)(2,1)S(1)}, bf16[2,128,128]{2,1,0:T(8,128)(2,1)S(1)}, u32[]{:S(2)}, u32[]{:S(2)}) collective-permute-start(bf16[2,128,128]{2,1,0:T(8,128)(2,1)S(1)} %get-tuple-element.34), channel_id=1, source_target_pairs={{0,24},{2,26},{4,28},{6,30},{8,16},{10,18},{12,20},{14,22},{16,8},... | collective-permute-start | bytes 196616 | tf_op jit(solution)/shard_map/ppermute | solution.py:116
  52.2 4.3 %collective-permute-start.8 = (bf16[2,128,128]{2,1,0:T(8,128)(2,1)S(1)}, bf16[2,128,128]{2,1,0:T(8,128)(2,1)S(1)}, u32[]{:S(2)}, u32[]{:S(2)}) collective-permute-start(bf16[2,128,128]{2,1,0:T(8,128)(2,1)S(1)} %get-tuple-element.34), channel_id=1, source_target_pairs={{0,8},{2,10},{4,12},{6,14},{8,0},{10,2},{12,4},{14,6},{16,24},{18,... | collective-permute-start | bytes 196616 | tf_op jit(solution)/shard_map/ppermute | solution.py:116
  56.5 5.0 %collective-permute-start.11 = (bf16[4,128,128]{2,1,0:T(8,128)(2,1)S(1)}, bf16[4,128,128]{2,1,0:T(8,128)(2,1)S(1)}, u32[]{:S(2)}, u32[]{:S(2)}) collective-permute-start(bf16[4,128,128]{2,1,0:T(8,128)(2,1)S(1)} %get-tuple-element.37), channel_id=1, source_target_pairs={{0,4},{2,6},{4,0},{6,2},{8,12},{10,14},{12,8},{14,10},{16,20},{18,... | collective-permute-start | bytes 393224 | tf_op jit(solution)/shard_map/ppermute | solution.py:116
  57.6 5.0 %collective-permute-start.12 = (bf16[4,128,128]{2,1,0:T(8,128)(2,1)S(1)}, bf16[4,128,128]{2,1,0:T(8,128)(2,1)S(1)}, u32[]{:S(2)}, u32[]{:S(2)}) collective-permute-start(bf16[4,128,128]{2,1,0:T(8,128)(2,1)S(1)} %get-tuple-element.38), channel_id=1, source_target_pairs={{0,2},{2,0},{4,6},{6,4},{8,10},{10,8},{12,14},{14,12},{16,18},{18,... | collective-permute-start | bytes 393224 | tf_op jit(solution)/shard_map/ppermute | solution.py:116
  62.6 6.4 %collective-permute-start.14 = (bf16[8,128,128]{2,1,0:T(8,128)(2,1)S(1)}, bf16[8,128,128]{2,1,0:T(8,128)(2,1)S(1)}, u32[]{:S(2)}, u32[]{:S(2)}) collective-permute-start(bf16[8,128,128]{2,1,0:T(8,128)(2,1)S(1)} %pad_maximum_fusion.2.refs_0_), channel_id=1, source_target_pairs={{0,2},{2,0},{4,6},{6,4},{8,10},{10,8},{12,14},{14,12},{16,18},{18,... | collective-permute-start | bytes 786440 | tf_op jit(solution)/shard_map/ppermute | solution.py:116
  63.6 6.4 %collective-permute-start.15 = (bf16[8,128,128]{2,1,0:T(8,128)(2,1)S(1)}, bf16[8,128,128]{2,1,0:T(8,128)(2,1)S(1)}, u32[]{:S(2)}, u32[]{:S(2)}) collective-permute-start(bf16[8,128,128]{2,1,0:T(8,128)(2,1)S(1)} %pad_maximum_fusion.3.refs_1_), channel_id=1, source_target_pairs={{0,4},{2,6},{4,0},{6,2},{8,12},{10,14},{12,8},{14,10},{16,20},{18,... | collective-permute-start | bytes 786440 | tf_op jit(solution)/shard_map/ppermute | solution.py:116
  65.2 1.3 %collective-permute-start.13 = (bf16[4,128,128]{2,1,0:T(8,128)(2,1)S(1)}, bf16[4,128,128]{2,1,0:T(8,128)(2,1)S(1)}, u32[]{:S(2)}, u32[]{:S(2)}) collective-permute-start(bf16[4,128,128]{2,1,0:T(8,128)(2,1)S(1)} %finish.1.own_ref), channel_id=1, source_target_pairs={{0,1},{1,0},{2,3},{3,2},{4,5},{5,4},{6,7},{7,6},{8,9},{9,8},{10,11... | collective-permute-start | bytes 393224 | tf_op jit(solution)/shard_map/ppermute | solution.py:116
  65.2 5.3 %collective-permute-start.18 = (bf16[8,128,128]{2,1,0:T(8,128)(2,1)S(1)}, bf16[8,128,128]{2,1,0:T(8,128)(2,1)S(1)}, u32[]{:S(2)}, u32[]{:S(2)}) collective-permute-start(bf16[8,128,128]{2,1,0:T(8,128)(2,1)S(1)} %pad_maximum_fusion.2.refs_0_), channel_id=1, source_target_pairs={{0,1},{1,0},{2,3},{3,2},{4,5},{5,4},{6,7},{7,6},{8,9},{9,8},{10,11... | collective-permute-start | bytes 786440 | tf_op jit(solution)/shard_map/ppermute | solution.py:116
  65.7 4.8 %collective-permute-start.19 = (bf16[8,128,128]{2,1,0:T(8,128)(2,1)S(1)}, bf16[8,128,128]{2,1,0:T(8,128)(2,1)S(1)}, u32[]{:S(2)}, u32[]{:S(2)}) collective-permute-start(bf16[8,128,128]{2,1,0:T(8,128)(2,1)S(1)} %pad_maximum_fusion.3.refs_1_), channel_id=1, source_target_pairs={{0,1},{1,0},{2,3},{3,2},{4,5},{5,4},{6,7},{7,6},{8,9},{9,8},{10,11... | collective-permute-start | bytes 786440 | tf_op jit(solution)/shard_map/ppermute | solution.py:116
  70.0 2.3 %collective-permute-start.16 = (bf16[8,128,128]{2,1,0:T(8,128)(2,1)S(1)}, bf16[8,128,128]{2,1,0:T(8,128)(2,1)S(1)}, u32[]{:S(2)}, u32[]{:S(2)}) collective-permute-start(bf16[8,128,128]{2,1,0:T(8,128)(2,1)S(1)} %collective-permute-done.14.refs_2_), channel_id=1, source_target_pairs={{0,1},{1,0},{2,3},{3,2},{4,5},{5,4},{6,7},{7,6},{8,9},{9,8},{10,11... | collective-permute-start | bytes 786440 | tf_op jit(solution)/shard_map/ppermute | solution.py:116
  70.0 2.3 %collective-permute-start.17 = (bf16[8,128,128]{2,1,0:T(8,128)(2,1)S(1)}, bf16[8,128,128]{2,1,0:T(8,128)(2,1)S(1)}, u32[]{:S(2)}, u32[]{:S(2)}) collective-permute-start(bf16[8,128,128]{2,1,0:T(8,128)(2,1)S(1)} %collective-permute-done.15.refs_3_), channel_id=1, source_target_pairs={{0,1},{1,0},{2,3},{3,2},{4,5},{5,4},{6,7},{7,6},{8,9},{9,8},{10,11... | collective-permute-start | bytes 786440 | tf_op jit(solution)/shard_map/ppermute | solution.py:116

commit v8 on v6

--- a/solution.py
+++ b/solution.py
@@ -162,7 +162,8 @@
 
 def stream_offsets(owners):
     bits = owners.bit_length() - 1
-    orders = ([0, 1] + list(range(2, bits)), [1, 0] + list(range(2, bits)))
+    highs = list(range(2, bits))
+    orders = ([0, 1] + highs, [1, 0] + highs, highs + [0, 1])
     offsets = [
         [sum(((p >> (bits - 1 - i)) & 1) << bit for i, bit in enumerate(order)) for p in range(owners)]
         for order in orders
@@ -195,23 +196,40 @@
                 table_ref[entry] = held[(here ^ offsets[stream][p]) * capacity + first_slot + stream]
 
 
+EDGE = 16
+
+
 def tiles_kernel(owners, first, table_ref, f_own, f_sib, own_rows, kv_sib, *rest):
-    out_a, out_b, sib_rows = rest
+    sib_rows = rest[-1]
+    out_a, out_b = rest[-5:-3] if first == 0 else rest[:2]
     tile = out_a.shape[-1]
+    body = tile - EDGE
+    near = owners // 2
     col_tiles = own_rows.shape[0] // tile
+    offsets = stream_offsets(owners)[1]
     sib_rows[...] = kv_sib[...].T
     for stream, out in enumerate((out_a, out_b)):
-
-        def one(i, carry, stream=stream, out=out):
+        for i in range(near):
             block = table_ref[stream * owners + first + i]
             at = pl.ds(pl.multiple_of(block // col_tiles * tile, tile), tile)
             cots = pl.ds(pl.multiple_of(block % col_tiles * tile, tile), tile)
-            out[i] = dot(own_rows[cots, :], f_own[:, at], MM) + dot(
+            total = dot(own_rows[cots, :], f_own[:, at], MM) + dot(
                 sib_rows[cots, :], f_sib[:, at], MM
             )
-            return carry
-
-        lax.fori_loop(0, owners // 2, one, 0, unroll=8)
+            out[i] = total[:body]
+            place = 2 * offsets[2].index(offsets[stream][first + i]) + stream
+            if first:
+                rest[2][place] = total[body:]
+            elif place < owners:
+                rest[-3][place] = total[body:]
+            else:
+                rest[-2][place - owners] = total[body:]
+            if first == 0:
+                place = 2 * offsets[2].index(offsets[stream][near + i]) + stream
+                if place < owners:
+                    rest[-3][place] = rest[0][place]
+                else:
+                    rest[-2][place - owners] = rest[0][place]
 
 
 SMEM = pl.BlockSpec(memory_space=pltpu.SMEM)
@@ -243,12 +261,13 @@
         power_ref[2 * k + 1] = 0.95 * times_low(r_ref[0, k], right)
 
 
-def direction_kernel(side_ref, a_ref, b_ref, m_ref, v_ref, ql_ref, qr_ref, dir_ref, grad_ref):
+def direction_kernel(side_ref, a_ref, b_ref, c_ref, d_ref, m_ref, v_ref, *rest):
+    ql_ref, qr_ref, dir_ref, grad_ref = rest
     pair = range(2)
     lefts = [ql_ref[0, k] for k in pair]
     rights = [qr_ref[0, k] for k in pair]
     turned = [right.T for right in rights]
-    grads = [a_ref[k] + b_ref[k] for k in pair]
+    grads = [above(a_ref[k] + b_ref[k], c_ref[k] + d_ref[k]) for k in pair]
     rots = [times_low(grads[k], lefts[k]) for k in pair]
     rots = [low_times(turned[k], rots[k], MM) for k in pair]
     scaled = []
@@ -407,11 +426,14 @@
     side = core.reshape(1).astype(jnp.int32)
     orders = stream_offsets(owners)[0]
     near = owners // 2
+    bits = len(orders[0])
 
     f_sib = swap_along(features, "inner", 2, 1)
     kv_sib = swap_along(kv_cotangent, "inner", 2, 1)
     flipped = pltpu.VMEM((width, rows), jnp.bfloat16)
-    part = jax.ShapeDtypeStruct((near, tile, tile), jnp.float32)
+    part = jax.ShapeDtypeStruct((near, tile - EDGE, tile), jnp.float32)
+    edge = jax.ShapeDtypeStruct((owners, EDGE, tile), jnp.float32)
+    edges = jax.ShapeDtypeStruct((2 * owners, EDGE, tile), jnp.float32)
     f32_pair = jax.ShapeDtypeStruct((2, tile, tile), jnp.float32)
     table, own_rows = pl.pallas_call(
         functools.partial(table_kernel, owners, capacity),
@@ -430,14 +452,14 @@
         name="table",
     )(place, owner_of_block, kv_cotangent)
 
-    def tiles_from(first):
-        inputs = (features, f_sib, own_rows, kv_sib)
+    def tiles_from(first, outs, *more):
+        inputs = (features, f_sib, own_rows, kv_sib, *more)
         return pl.pallas_call(
             functools.partial(tiles_kernel, owners, first),
-            out_shape=(part, part),
+            out_shape=outs,
             grid=(1,),
             in_specs=[SMEM] + wholes(inputs),
-            out_specs=(whole(part.shape), whole(part.shape)),
+            out_specs=tuple(wholes(outs)),
             scratch_shapes=[flipped],
             compiler_params=BIG,
             cost_estimate=pl.CostEstimate(
@@ -448,10 +470,11 @@
             name="tiles",
         )(table, *inputs)
 
-    sent_a, sent_b = tiles_from(near)
+    sent_a, sent_b, early = tiles_from(near, (part, part, edges))
     got_a = swap_along(sent_a, "dp", owners, 1 << orders[0][0])
     got_b = swap_along(sent_b, "dp", owners, 1 << orders[1][0])
-    kept_a, kept_b = tiles_from(0)
+    kept_a, kept_b, kept_c, sent_c = tiles_from(0, (part, part, edge, edge), early)
+    got_c = swap_along(sent_c, "dp", owners, 1 << orders[2][0])
     quad = jax.ShapeDtypeStruct((4, tile, tile), jnp.float32)
     moment_rot, second, power = on_slots(
         rotated_kernel,
@@ -462,28 +485,41 @@
         16 * 2 * tile**3,
     )
 
-    half = near // 2
-    next_a = swap_along(kept_a[half:] + got_a[half:], "dp", owners, 1 << orders[0][1])
-    next_b = swap_along(kept_b[half:] + got_b[half:], "dp", owners, 1 << orders[1][1])
-    kept = jnp.stack([kept_a[:half] + got_a[:half], kept_b[:half] + got_b[:half]], axis=1)
-    got = jnp.stack([next_a, next_b], axis=1)
-    for bit in orders[0][2:]:
+    def halved(kept, got):
         half = kept.shape[0] // 2
-        sent = kept[half:] + got[half:]
-        kept = kept[:half] + got[:half]
-        if half == 1:
+        return kept[:half] + got[:half], kept[half:] + got[half:]
+
+    def after(values, *needed):
+        return lax.optimization_barrier((values, *needed))[0]
+
+    def edges_on(step, kept, got):
+        kept, sent = halved(kept, got)
+        return kept, sent, swap_along(sent, "dp", owners, 1 << orders[2][step])
+
+    kept_c, sent_c, got_c = edges_on(1, kept_c, got_c)
+    kept_a, sent_a = halved(kept_a, got_a)
+    kept_b, sent_b = halved(kept_b, got_b)
+    got_a = swap_along(sent_a, "dp", owners, 1 << orders[0][1])
+    got_b = swap_along(sent_b, "dp", owners, 1 << orders[1][1])
+    kept = jnp.stack([kept_a, kept_b], axis=1)
+    got = jnp.stack([got_a, got_b], axis=1)
+    for step in range(2, bits):
+        due = got_c
+        kept_c, sent_c, got_c = edges_on(step, kept_c, got_c)
+        kept, sent = halved(kept, got)
+        sent = after(sent, due)
+        if step == bits - 1:
             sent, kept = sent[0], kept[0]
-        got = swap_along(sent, "dp", owners, 1 << bit)
+        got = swap_along(sent, "dp", owners, 1 << orders[0][step])
     direction, grads = on_slots(
         direction_kernel,
         side,
-        (kept, got, moment_rot, second),
+        (kept, got, kept_c, got_c, moment_rot, second),
         (left_basis, right_basis),
         (jax.ShapeDtypeStruct(f32_pair.shape, jnp.bfloat16), f32_pair),
         16 * 2 * tile**3,
     )
 
-    bits = len(orders[0])
     high = owners // 4
     tiles = []
     for p in range(high):
@@ -505,23 +541,27 @@
     mine, fresh = lax.optimization_barrier((mine, fresh))
     other = [swap_along(m, "dp", owners, 1 << order[0]) for m, order in zip(mine, orders)]
     fresh_sib = swap_along(fresh, "inner", 2, 1)
-    mine_sib = [swap_along(m, "inner", 2, 1) for m in mine]
     basis = jax.ShapeDtypeStruct(left_basis.shape, left_basis.dtype)
     update, new_left, new_right = pl.pallas_call(
-        functools.partial(
-            begin_kernel, col_tiles, (0, owners, 2 * owners, 3 * owners)
-        ),
+        functools.partial(begin_kernel, col_tiles, (0, owners)),
         out_shape=(jax.ShapeDtypeStruct((d_win, width), jnp.bfloat16), basis, basis),
-        in_specs=[SMEM, SMEM] + [VMEM] * 6,
+        in_specs=[SMEM, SMEM] + [VMEM] * 4,
         out_specs=(HBM, HBM, HBM),
-        scratch_shapes=[pltpu.SemaphoreType.DMA((4 * near + 8,))],
+        scratch_shapes=[pltpu.SemaphoreType.DMA((2 * near + 8,))],
         compiler_params=SMALL,
-        cost_estimate=pl.CostEstimate(flops=0, bytes_accessed=1_300_000, transcendentals=0),
+        cost_estimate=pl.CostEstimate(flops=0, bytes_accessed=800_000, transcendentals=0),
         name="begin",
-    )(table, place, fresh, fresh_sib, *mine, *mine_sib)
+    )(table, place, fresh, fresh_sib, *mine)
     update, other = lax.optimization_barrier((update, other))
+    mine_sib = [swap_along(m, "inner", 2, 1) for m in mine]
     other_sib = [swap_along(o, "inner", 2, 1) for o in other]
-    update = place_more(update, table, col_tiles, (near, owners + near), other)
+    update = place_more(
+        update,
+        table,
+        col_tiles,
+        (2 * owners, 3 * owners, near, owners + near),
+        mine_sib + other,
+    )
     update = place_more(
         update, table, col_tiles, (2 * owners + near, 3 * owners + near), other_sib
     )

time: 75.2 us -> 71.5 us (0.951)
  waiting for transfers between devices: 31.1 us -> 21.1 us
  starting transfers between devices: 23.6 us -> 29.9 us
    ppermute x20 -> x24, waiting for transfers between devices: 31.1 us -> 21.1 us  [swap_along(): return lax.ppermute(values, axis, [(i, i ^ bit) for i in range(size)])]
    ppermute x20 -> x24, starting transfers between devices: 23.6 us -> 29.9 us  [swap_along(): return lax.ppermute(values, axis, [(i, i ^ bit) for i in range(size)])]
  transfers between devices with their start and end apart: 20 -> 24, of which waited for: 11 -> 14; matrix products, arithmetic and copies ran while one was open for 0% -> 0% of each run, Pallas kernels for 17% -> 18%
where the time goes in v8:
time: 71.5 us; the launch traced here: 71.3 us
  starting transfers between devices  29.9 us (42%)
  waiting for transfers between devices  21.1 us (30%)
  Pallas kernels  16.2 us (23%)
  local copies, waits for them, and re-layouts  2.89 us (4%)
  between operations  0.88 us (1%)
    ppermute x24, starting transfers between devices, swap_along(): return lax.ppermute(values, axis, [(i, i ^ bit) for i in range(size)])  29.9 us
    ppermute x24, waiting for transfers between devices, swap_along(): return lax.ppermute(values, axis, [(i, i ^ bit) for i in range(size)])  21.1 us
    pallas_call x3, Pallas kernels, on_slots(): pl.pallas_call(kernel, out_shape=tuple(outs), grid_spec=pltpu.PrefetchSca...  3.98 us
    pallas_call x2, Pallas kernels, place_more(): pl.pallas_call(functools.partial(more_kernel, col_tiles, entries), out_sh...  3.25 us
    pallas_call x1, Pallas kernels, sweeping(): pl.pallas_call(kernel, out_shape=jax.ShapeDtypeStruct(values.shape, dtype...  2.9 us
    unnamed x18, local copies, waits for them, and re-layouts  2.86 us
    pallas_call x2, Pallas kernels, tiles_from(): pl.pallas_call(functools.partial(tiles_kernel, owners, first), out_shape=...  2.8 us
    pallas_call x1, Pallas kernels, per_device_dealt(): pl.pallas_call(functools.partial(table_kernel, owners, capacity), out_sha...  1.65 us
  transfers between devices with their start and end apart: 24, of which 14 were waited for; matrix products, arithmetic and copies ran while one was open for 0% of the time, Pallas kernels for 18%

profile of v8, /device:TPU:0, one launch (start us, length us, event | category | flops | bytes accessed | tf_op | source)
XLA Modules:
  0.0 71.3 jit_solution(16452777888826677707)
XLA Ops:
  0.6 0.5 collective-permute-start
  1.1 0.1 collective-permute-start.1
  1.2 0.1 pad_add_fusion.place_ref
  1.3 0.9 %copy-done.7 = bf16[256,512]{1,0:T(8,128)(2,1)S(1)} copy-done((bf16[256,512]{1,0:T(8,128)(2,1)S(1)}, bf16[256,512]{1,0:T(8,128)(2,1)}, u32[]{:S(2)}) %copy-start.7) | copy-done | bytes 262168
  2.3 0.7 copy-done.8
  2.9 1.7 %table.1 = (s32[64]{0:T(128)S(1)}, bf16[512,256]{1,0:T(8,128)(2,1)S(1)}) custom-call(s32[2]{0:T(128)S(1)} %pad_add_fusion.place_ref, s32[64]{0:T(128)S(1)} %copy-done.8, bf16[256,512]{1,0:T(8,128)(2,1)S(1)} %copy-done.7), custom_call_target="tpu_custom_call" | custom-call | bytes 1000000 | tf_op jit(solution)/shard_map/table/pallas_call | solution.py:438
  4.6 1.2 %copy-done = bf16[256,2048]{1,0:T(8,128)(2,1)S(1)} copy-done((bf16[256,2048]{1,0:T(8,128)(2,1)S(1)}, bf16[256,2048]{1,0:T(8,128)(2,1)}, u32[]{:S(2)}) %copy-start) | copy-done | bytes 1048600
  5.8 1.4 %tiles.2 = (f32[8,112,128]{2,1,0:T(8,128)S(1)}, f32[8,112,128]{2,1,0:T(8,128)S(1)}, f32[32,16,128]{2,1,0:T(8,128)S(1)}) custom-call(s32[64]{0:T(128)S(1)} %get-tuple-element.31.table_ref, bf16[256,2048]{1,0:T(8,128)(2,1)S(1)} %copy-done, bf16[256,2048]{1,0:T(8,128)(2,1)S(1)} %collective-permute-done.f_sib, bf16[512,256]{1,0:T(8,128)(2,1)S(1)} %get-tuple-element.32.own_rows, ...), custom_call_target="tpu_custom_call" | custom-call | flops 536870912 | bytes 3500000 | tf_op jit(solution)/shard_map/tiles/pallas_call | solution.py:457
  7.2 3.0 %collective-permute-start.2 = (f32[8,112,128]{2,1,0:T(8,128)S(1)}, f32[8,112,128]{2,1,0:T(8,128)S(1)}, u32[]{:S(2)}, u32[]{:S(2)}) collective-permute-start(f32[8,112,128]{2,1,0:T(8,128)S(1)} %get-tuple-element.35), channel_id=1, source_target_pairs={{0,2},{2,0},{4,6},{6,4},{8,10},{10,8},{12,14},{14,12},{16,18},{18,... | collective-permute-start | bytes 1376264 | tf_op jit(solution)/shard_map/ppermute | solution.py:116
  10.2 1.5 %collective-permute-start.3 = (f32[8,112,128]{2,1,0:T(8,128)S(1)}, f32[8,112,128]{2,1,0:T(8,128)S(1)}, u32[]{:S(2)}, u32[]{:S(2)}) collective-permute-start(f32[8,112,128]{2,1,0:T(8,128)S(1)} %get-tuple-element.37), channel_id=1, source_target_pairs={{0,4},{2,6},{4,0},{6,2},{8,12},{10,14},{12,8},{14,10},{16,20},{18,... | collective-permute-start | bytes 1376264 | tf_op jit(solution)/shard_map/ppermute | solution.py:116
  11.7 1.4 %tiles.3 = (f32[8,112,128]{2,1,0:T(8,128)S(1)}, f32[8,112,128]{2,1,0:T(8,128)S(1)}, f32[16,16,128]{2,1,0:T(8,128)S(1)}, f32[16,16,128]{2,1,0:T(8,128)S(1)}) custom-call(s32[64]{0:T(128)S(1)} %get-tuple-element.31.table_ref, bf16[256,2048]{1,0:T(8,128)(2,1)S(1)} %copy-done, bf16[256,2048]{1,0:T(8,128)(2,1)S(1)} %collective-permute-done.f_sib, ...), custom_call_target="tpu_custom_call" | custom-call | flops 536870912 | bytes 3500000 | tf_op jit(solution)/shard_map/tiles/pallas_call | solution.py:457
  13.1 1.6 %collective-permute-start.6 = (f32[16,16,128]{2,1,0:T(8,128)S(1)}, f32[16,16,128]{2,1,0:T(8,128)S(1)}, u32[]{:S(2)}, u32[]{:S(2)}) collective-permute-start(f32[16,16,128]{2,1,0:T(8,128)S(1)} %get-tuple-element.39), channel_id=1, source_target_pairs={{0,8},{2,10},{4,12},{6,14},{8,0},{10,2},{12,4},{14,6},{16,24},{18,... | collective-permute-start | bytes 393224 | tf_op jit(solution)/shard_map/ppermute | solution.py:116
  14.8 6.2 %collective-permute-done.2 = f32[8,112,128]{2,1,0:T(8,128)S(1)} collective-permute-done((f32[8,112,128]{2,1,0:T(8,128)S(1)}, f32[8,112,128]{2,1,0:T(8,128)S(1)}, u32[]{:S(2)}, u32[]{:S(2)}) %collective-permute-start.2) | collective-permute-done | bytes 458784 | tf_op jit(solution)/shard_map/ppermute | solution.py:116
  21.1 1.8 %collective-permute-start.4 = (f32[4,112,128]{2,1,0:T(8,128)S(1)}, f32[4,112,128]{2,1,0:T(8,128)S(1)}, u32[]{:S(2)}, u32[]{:S(2)}) collective-permute-start(f32[4,112,128]{2,1,0:T(8,128)S(1)} %get-tuple-element.62), channel_id=1, source_target_pairs={{0,4},{2,6},{4,0},{6,2},{8,12},{10,14},{12,8},{14,10},{16,20},{18,... | collective-permute-start | bytes 688136 | tf_op jit(solution)/shard_map/ppermute | solution.py:116
  23.0 1.6 %collective-permute-start.5 = (f32[4,112,128]{2,1,0:T(8,128)S(1)}, f32[4,112,128]{2,1,0:T(8,128)S(1)}, u32[]{:S(2)}, u32[]{:S(2)}) collective-permute-start(f32[4,112,128]{2,1,0:T(8,128)S(1)} %get-tuple-element.64), channel_id=1, source_target_pairs={{0,2},{2,0},{4,6},{6,4},{8,10},{10,8},{12,14},{14,12},{16,18},{18,... | collective-permute-start | bytes 688136 | tf_op jit(solution)/shard_map/ppermute | solution.py:116
  24.6 2.7 %collective-permute-start.7 = (f32[8,16,128]{2,1,0:T(8,128)S(1)}, f32[8,16,128]{2,1,0:T(8,128)S(1)}, u32[]{:S(2)}, u32[]{:S(2)}) collective-permute-start(f32[8,16,128]{2,1,0:T(8,128)S(1)} %get-tuple-element.68), channel_id=1, source_target_pairs={{0,16},{2,18},{4,20},{6,22},{8,24},{10,26},{12,28},{14,30},{16,0},... | collective-permute-start | bytes 196616 | tf_op jit(solution)/shard_map/ppermute | solution.py:116
  27.2 1.0 %collective-permute-done.4 = f32[4,112,128]{2,1,0:T(8,128)S(1)} collective-permute-done((f32[4,112,128]{2,1,0:T(8,128)S(1)}, f32[4,112,128]{2,1,0:T(8,128)S(1)}, u32[]{:S(2)}, u32[]{:S(2)}) %collective-permute-start.4) | collective-permute-done | bytes 229408 | tf_op jit(solution)/shard_map/ppermute | solution.py:116
  28.2 1.3 %collective-permute-done.5 = f32[4,112,128]{2,1,0:T(8,128)S(1)} collective-permute-done((f32[4,112,128]{2,1,0:T(8,128)S(1)}, f32[4,112,128]{2,1,0:T(8,128)S(1)}, u32[]{:S(2)}, u32[]{:S(2)}) %collective-permute-start.5) | collective-permute-done | bytes 229408 | tf_op jit(solution)/shard_map/ppermute | solution.py:116
  29.6 0.2 collective-permute-done.7
  29.8 1.6 %collective-permute-start.8 = (f32[2,2,112,128]{3,2,1,0:T(8,128)S(1)}, f32[2,2,112,128]{3,2,1,0:T(8,128)S(1)}, u32[]{:S(2)}, u32[]{:S(2)}) collective-permute-start(f32[2,2,112,128]{3,2,1,0:T(8,128)S(1)} %get-tuple-element.40), channel_id=1, source_target_pairs={{0,8},{2,10},{4,12},{6,14},{8,0},{10,2},{12,4},{14,6},{16,24},{18,... | collective-permute-start | bytes 688136 | tf_op jit(solution)/shard_map/ppermute | solution.py:116
  31.4 1.4 %collective-permute-start.9 = (f32[4,16,128]{2,1,0:T(8,128)S(1)}, f32[4,16,128]{2,1,0:T(8,128)S(1)}, u32[]{:S(2)}, u32[]{:S(2)}) collective-permute-start(f32[4,16,128]{2,1,0:T(8,128)S(1)} %get-tuple-element.70), channel_id=1, source_target_pairs={{0,2},{2,0},{4,6},{6,4},{8,10},{10,8},{12,14},{14,12},{16,18},{18,... | collective-permute-start | bytes 98312 | tf_op jit(solution)/shard_map/ppermute | solution.py:116
  32.8 3.0 %collective-permute-done.8 = f32[2,2,112,128]{3,2,1,0:T(8,128)S(1)} collective-permute-done((f32[2,2,112,128]{3,2,1,0:T(8,128)S(1)}, f32[2,2,112,128]{3,2,1,0:T(8,128)S(1)}, u32[]{:S(2)}, u32[]{:S(2)}) %collective-permute-start.8) | collective-permute-done | bytes 229408 | tf_op jit(solution)/shard_map/ppermute | solution.py:116
  35.9 3.3 %collective-permute-start.10 = (f32[2,112,128]{2,1,0:T(8,128)S(1)}, f32[2,112,128]{2,1,0:T(8,128)S(1)}, u32[]{:S(2)}, u32[]{:S(2)}) collective-permute-start(f32[2,112,128]{2,1,0:T(8,128)S(1)} %bitcast.17), channel_id=1, source_target_pairs={{0,16},{2,18},{4,20},{6,22},{8,24},{10,26},{12,28},{14,30},{16,0},... | collective-permute-start | bytes 344072 | tf_op jit(solution)/shard_map/ppermute | solution.py:116
  39.2 0.6 collective-permute-start.11
  39.9 0.5 rotated.1
  40.4 2.6 %collective-permute-done.11.d_ref = f32[2,16,128]{2,1,0:T(8,128)S(1)} collective-permute-done((f32[2,16,128]{2,1,0:T(8,128)S(1)}, f32[2,16,128]{2,1,0:T(8,128)S(1)}, u32[]{:S(2)}, u32[]{:S(2)}) %collective-permute-start.11) | collective-permute-done | bytes 16416 | tf_op jit(solution)/shard_map/ppermute | solution.py:116
  43.0 0.4 collective-permute-done.10.b_ref
  43.4 0.7 %direction.1 = (bf16[2,128,128]{2,1,0:T(8,128)(2,1)S(1)}, f32[2,128,128]{2,1,0:T(8,128)S(1)}) custom-call(s32[1]{0:T(128)} %bitcast.1.side_ref, f32[2,112,128]{2,1,0:T(8,128)S(1)} %get-tuple-element.66.a_ref, f32[2,112,128]{2,1,0:T(8,128)S(1)} %collective-permute-done.10.b_ref, f32[2,16,128]{2,1,0:T(8,128)S(1)} %get-tuple-element.80.c_ref, ...), custom_call_target="tpu_custom_call" | custom-call | flops 67108864 | bytes 800000 | tf_op jit(solution)/shard_map/direction/pallas_call | solution.py:291
  44.1 4.9 %collective-permute-start.14 = (bf16[2,128,128]{2,1,0:T(8,128)(2,1)S(1)}, bf16[2,128,128]{2,1,0:T(8,128)(2,1)S(1)}, u32[]{:S(2)}, u32[]{:S(2)}) collective-permute-start(bf16[2,128,128]{2,1,0:T(8,128)(2,1)S(1)} %get-tuple-element.44), channel_id=1, source_target_pairs={{0,24},{2,26},{4,28},{6,30},{8,16},{10,18},{12,20},{14,22},{16,8},... | collective-permute-start | bytes 196616 | tf_op jit(solution)/shard_map/ppermute | solution.py:116
  49.0 0.6 collective-permute-start.12
  49.7 2.8 %refresh.1.iter_ref = f32[4,128,128]{2,1,0:T(8,128)S(1)} custom-call(s32[1]{0:T(128)} %bitcast.1.side_ref, f32[2,128,128]{2,1,0:T(8,128)S(1)} %get-tuple-element.45.g_ref, f32[4,128,128]{2,1,0:T(8,128)S(1)} %get-tuple-element.46.power_ref, bf16[1,4,128,128]{3,2,1,0:T(8,128)(2,1)S(1)} %copy-done.1, bf16[1,4,128,128]{3,2,1,0:T(8,128)(2,1)S(1)} %copy-done.2), custom_call_target="tpu_custom_call" | custom-call | flops 939524096 | bytes 800000 | tf_op jit(solution)/shard_map/refresh/pallas_call | solution.py:291
  52.5 0.8 %collective-permute-done.13 = bf16[2,128,128]{2,1,0:T(8,128)(2,1)S(1)} collective-permute-done((bf16[2,128,128]{2,1,0:T(8,128)(2,1)S(1)}, bf16[2,128,128]{2,1,0:T(8,128)(2,1)S(1)}, u32[]{:S(2)}, u32[]{:S(2)}) %collective-permute-start.13) | collective-permute-done | bytes 65568 | tf_op jit(solution)/shard_map/ppermute | solution.py:116
  53.3 0.9 %collective-permute-done.12 = bf16[2,128,128]{2,1,0:T(8,128)(2,1)S(1)} collective-permute-done((bf16[2,128,128]{2,1,0:T(8,128)(2,1)S(1)}, bf16[2,128,128]{2,1,0:T(8,128)(2,1)S(1)}, u32[]{:S(2)}, u32[]{:S(2)}) %collective-permute-start.12) | collective-permute-done | bytes 65568 | tf_op jit(solution)/shard_map/ppermute | solution.py:116
  54.2 0.8 %collective-permute-start.15 = (bf16[4,128,128]{2,1,0:T(8,128)(2,1)S(1)}, bf16[4,128,128]{2,1,0:T(8,128)(2,1)S(1)}, u32[]{:S(2)}, u32[]{:S(2)}) collective-permute-start(bf16[4,128,128]{2,1,0:T(8,128)(2,1)S(1)} %get-tuple-element.47), channel_id=1, source_target_pairs={{0,4},{2,6},{4,0},{6,2},{8,12},{10,14},{12,8},{14,10},{16,20},{18,... | collective-permute-start | bytes 393224 | tf_op jit(solution)/shard_map/ppermute | solution.py:116
  55.0 1.1 %collective-permute-start.16 = (bf16[4,128,128]{2,1,0:T(8,128)(2,1)S(1)}, bf16[4,128,128]{2,1,0:T(8,128)(2,1)S(1)}, u32[]{:S(2)}, u32[]{:S(2)}) collective-permute-start(bf16[4,128,128]{2,1,0:T(8,128)(2,1)S(1)} %get-tuple-element.48), channel_id=1, source_target_pairs={{0,2},{2,0},{4,6},{6,4},{8,10},{10,8},{12,14},{14,12},{16,18},{18,... | collective-permute-start | bytes 393224 | tf_op jit(solution)/shard_map/ppermute | solution.py:116
  56.1 2.9 %finish.1.own_ref = bf16[4,128,128]{2,1,0:T(8,128)(2,1)S(1)} custom-call(f32[4,128,128]{2,1,0:T(8,128)S(1)} %refresh.1.iter_ref), custom_call_target="tpu_custom_call" | custom-call | flops 939524096 | bytes 400000 | tf_op jit(solution)/shard_map/finish/pallas_call | solution.py:341
  59.0 0.3 collective-permute-done.15
  59.3 0.7 %collective-permute-done.16 = bf16[4,128,128]{2,1,0:T(8,128)(2,1)S(1)} collective-permute-done((bf16[4,128,128]{2,1,0:T(8,128)(2,1)S(1)}, bf16[4,128,128]{2,1,0:T(8,128)(2,1)S(1)}, u32[]{:S(2)}, u32[]{:S(2)}) %collective-permute-start.16) | collective-permute-done | bytes 131104 | tf_op jit(solution)/shard_map/ppermute | solution.py:116
  60.0 1.1 %collective-permute-start.18 = (bf16[8,128,128]{2,1,0:T(8,128)(2,1)S(1)}, bf16[8,128,128]{2,1,0:T(8,128)(2,1)S(1)}, u32[]{:S(2)}, u32[]{:S(2)}) collective-permute-start(bf16[8,128,128]{2,1,0:T(8,128)(2,1)S(1)} %pad_maximum_fusion.refs_0_), channel_id=1, source_target_pairs={{0,2},{2,0},{4,6},{6,4},{8,10},{10,8},{12,14},{14,12},{16,18},{18,... | collective-permute-start | bytes 786440 | tf_op jit(solution)/shard_map/ppermute | solution.py:116
  61.1 0.5 collective-permute-start.19
  61.7 0.5 collective-permute-start.22
  62.2 0.8 %collective-permute-done.17.sib_ref = bf16[4,128,128]{2,1,0:T(8,128)(2,1)S(1)} collective-permute-done((bf16[4,128,128]{2,1,0:T(8,128)(2,1)S(1)}, bf16[4,128,128]{2,1,0:T(8,128)(2,1)S(1)}, u32[]{:S(2)}, u32[]{:S(2)}) %collective-permute-start.17) | collective-permute-done | bytes 131104 | tf_op jit(solution)/shard_map/ppermute | solution.py:116
  63.0 1.6 %begin.1 = (bf16[2048,512]{1,0:T(8,128)(2,1)}, bf16[1,4,128,128]{3,2,1,0:T(8,128)(2,1)}, bf16[1,4,128,128]{3,2,1,0:T(8,128)(2,1)}) custom-call(s32[64]{0:T(128)S(1)} %get-tuple-element.31.table_ref, s32[2]{0:T(128)S(1)} %pad_add_fusion.place_ref, bf16[4,128,128]{2,1,0:T(8,128)(2,1)S(1)} %finish.1.own_ref, ...), custom_call_target="tpu_custom_call" | custom-call | bytes 800000 | tf_op jit(solution)/shard_map/begin/pallas_call | solution.py:545
  64.7 1.8 %collective-permute-done.18.refs_2_ = bf16[8,128,128]{2,1,0:T(8,128)(2,1)S(1)} collective-permute-done((bf16[8,128,128]{2,1,0:T(8,128)(2,1)S(1)}, bf16[8,128,128]{2,1,0:T(8,128)(2,1)S(1)}, u32[]{:S(2)}, u32[]{:S(2)}) %collective-permute-start.18) | collective-permute-done | bytes 262176 | tf_op jit(solution)/shard_map/ppermute | solution.py:116
  66.5 1.1 %collective-permute-done.19.refs_3_ = bf16[8,128,128]{2,1,0:T(8,128)(2,1)S(1)} collective-permute-done((bf16[8,128,128]{2,1,0:T(8,128)(2,1)S(1)}, bf16[8,128,128]{2,1,0:T(8,128)(2,1)S(1)}, u32[]{:S(2)}, u32[]{:S(2)}) %collective-permute-start.19) | collective-permute-done | bytes 262176 | tf_op jit(solution)/shard_map/ppermute | solution.py:116
  67.5 0.5 collective-permute-start.21
  68.0 1.8 %more.2.refs_2_ = bf16[2048,512]{1,0:T(8,128)(2,1)} custom-call(s32[64]{0:T(128)S(1)} %get-tuple-element.31.table_ref, bf16[8,128,128]{2,1,0:T(8,128)(2,1)S(1)} %collective-permute-done.22.refs_0_, bf16[8,128,128]{2,1,0:T(8,128)(2,1)S(1)} %collective-permute-done.23.refs_1_, ...), custom_call_target="tpu_custom_call", output_to_operand_aliasing={{}: (5, {})} | custom-call | bytes 1000000 | tf_op jit(solution)/shard_map/more/pallas_call | solution.py:393
  69.8 1.5 %more.3 = bf16[2048,512]{1,0:T(8,128)(2,1)} custom-call(s32[64]{0:T(128)S(1)} %get-tuple-element.31.table_ref, bf16[8,128,128]{2,1,0:T(8,128)(2,1)S(1)} %collective-permute-done.20.refs_0_, bf16[8,128,128]{2,1,0:T(8,128)(2,1)S(1)} %collective-permute-done.21.refs_1_, bf16[2048,512]{1,0:T(8,128)(2,1)} %more.2.refs_2_), custom_call_target="tpu_custom_call", output_to_operand_aliasing={{}: (3, {})} | custom-call | bytes 1000000 | tf_op jit(solution)/shard_map/more/pallas_call | solution.py:393
  (43 shorter events, 0.4 us)
Async XLA Ops:
  0.6 4.0 %collective-permute-start = (bf16[256,2048]{1,0:T(8,128)(2,1)}, bf16[256,2048]{1,0:T(8,128)(2,1)S(1)}, u32[]{:S(2)}, u32[]{:S(2)}) collective-permute-start(bf16[256,2048]{1,0:T(8,128)(2,1)} %f_own.3), channel_id=1, source_target_pairs={{0,1},{1,0},{2,3},{3,2},{4,5},{5,4},{6,7},{7,6},{8,9},{9,8},{10,11... | collective-permute-start | bytes 3145736 | tf_op jit(solution)/shard_map/ppermute | solution.py:116
  1.1 3.4 %collective-permute-start.1 = (bf16[256,512]{1,0:T(8,128)(2,1)}, bf16[256,512]{1,0:T(8,128)(2,1)S(1)}, u32[]{:S(2)}, u32[]{:S(2)}) collective-permute-start(bf16[256,512]{1,0:T(8,128)(2,1)} %kv_ref.1), channel_id=1, source_target_pairs={{0,1},{1,0},{2,3},{3,2},{4,5},{5,4},{6,7},{7,6},{8,9},{9,8},{10,11... | collective-permute-start | bytes 786440 | tf_op jit(solution)/shard_map/ppermute | solution.py:116
  1.3 0.9 %copy-start.7 = (bf16[256,512]{1,0:T(8,128)(2,1)S(1)}, bf16[256,512]{1,0:T(8,128)(2,1)}, u32[]{:S(2)}) copy-start(bf16[256,512]{1,0:T(8,128)(2,1)} %kv_ref.1) | copy-start | bytes 786436
  2.3 0.7 copy-start.8
  4.6 1.2 %copy-start = (bf16[256,2048]{1,0:T(8,128)(2,1)S(1)}, bf16[256,2048]{1,0:T(8,128)(2,1)}, u32[]{:S(2)}) copy-start(bf16[256,2048]{1,0:T(8,128)(2,1)} %f_own.3) | copy-start | bytes 3145732
  7.2 13.8 %collective-permute-start.2 = (f32[8,112,128]{2,1,0:T(8,128)S(1)}, f32[8,112,128]{2,1,0:T(8,128)S(1)}, u32[]{:S(2)}, u32[]{:S(2)}) collective-permute-start(f32[8,112,128]{2,1,0:T(8,128)S(1)} %get-tuple-element.35), channel_id=1, source_target_pairs={{0,2},{2,0},{4,6},{6,4},{8,10},{10,8},{12,14},{14,12},{16,18},{18,... | collective-permute-start | bytes 1376264 | tf_op jit(solution)/shard_map/ppermute | solution.py:116
  10.2 12.7 %collective-permute-start.3 = (f32[8,112,128]{2,1,0:T(8,128)S(1)}, f32[8,112,128]{2,1,0:T(8,128)S(1)}, u32[]{:S(2)}, u32[]{:S(2)}) collective-permute-start(f32[8,112,128]{2,1,0:T(8,128)S(1)} %get-tuple-element.37), channel_id=1, source_target_pairs={{0,4},{2,6},{4,0},{6,2},{8,12},{10,14},{12,8},{14,10},{16,20},{18,... | collective-permute-start | bytes 1376264 | tf_op jit(solution)/shard_map/ppermute | solution.py:116
  13.1 11.4 %collective-permute-start.6 = (f32[16,16,128]{2,1,0:T(8,128)S(1)}, f32[16,16,128]{2,1,0:T(8,128)S(1)}, u32[]{:S(2)}, u32[]{:S(2)}) collective-permute-start(f32[16,16,128]{2,1,0:T(8,128)S(1)} %get-tuple-element.39), channel_id=1, source_target_pairs={{0,8},{2,10},{4,12},{6,14},{8,0},{10,2},{12,4},{14,6},{16,24},{18,... | collective-permute-start | bytes 393224 | tf_op jit(solution)/shard_map/ppermute | solution.py:116
  21.0 18.8 %copy-start.1 = (bf16[1,4,128,128]{3,2,1,0:T(8,128)(2,1)S(1)}, bf16[1,4,128,128]{3,2,1,0:T(8,128)(2,1)}, u32[]{:S(2)}) copy-start(bf16[1,4,128,128]{3,2,1,0:T(8,128)(2,1)} %ql_ref.3) | copy-start | bytes 393220
  21.0 18.8 %copy-start.2 = (bf16[1,4,128,128]{3,2,1,0:T(8,128)(2,1)S(1)}, bf16[1,4,128,128]{3,2,1,0:T(8,128)(2,1)}, u32[]{:S(2)}) copy-start(bf16[1,4,128,128]{3,2,1,0:T(8,128)(2,1)} %qr_ref.3) | copy-start | bytes 393220
  21.1 18.8 %copy-start.3 = (f32[1,4,128,128]{3,2,1,0:T(8,128)S(1)}, f32[1,4,128,128]{3,2,1,0:T(8,128)}, u32[]{:S(2)}) copy-start(f32[1,4,128,128]{3,2,1,0:T(8,128)} %m_ref.1) | copy-start | bytes 786436
  21.1 18.8 %copy-start.4 = (f32[1,4,128,128]{3,2,1,0:T(8,128)S(1)}, f32[1,4,128,128]{3,2,1,0:T(8,128)}, u32[]{:S(2)}) copy-start(f32[1,4,128,128]{3,2,1,0:T(8,128)} %v_ref.1) | copy-start | bytes 786436
  21.1 18.8 %copy-start.5 = (f32[1,4,128,128]{3,2,1,0:T(8,128)S(1)}, f32[1,4,128,128]{3,2,1,0:T(8,128)}, u32[]{:S(2)}) copy-start(f32[1,4,128,128]{3,2,1,0:T(8,128)} %l_ref.1) | copy-start | bytes 786436
  21.1 18.8 %copy-start.6 = (f32[1,4,128,128]{3,2,1,0:T(8,128)S(1)}, f32[1,4,128,128]{3,2,1,0:T(8,128)}, u32[]{:S(2)}) copy-start(f32[1,4,128,128]{3,2,1,0:T(8,128)} %r_ref.1) | copy-start | bytes 786436
  21.1 7.1 %collective-permute-start.4 = (f32[4,112,128]{2,1,0:T(8,128)S(1)}, f32[4,112,128]{2,1,0:T(8,128)S(1)}, u32[]{:S(2)}, u32[]{:S(2)}) collective-permute-start(f32[4,112,128]{2,1,0:T(8,128)S(1)} %get-tuple-element.62), channel_id=1, source_target_pairs={{0,4},{2,6},{4,0},{6,2},{8,12},{10,14},{12,8},{14,10},{16,20},{18,... | collective-permute-start | bytes 688136 | tf_op jit(solution)/shard_map/ppermute | solution.py:116
  23.0 6.5 %collective-permute-start.5 = (f32[4,112,128]{2,1,0:T(8,128)S(1)}, f32[4,112,128]{2,1,0:T(8,128)S(1)}, u32[]{:S(2)}, u32[]{:S(2)}) collective-permute-start(f32[4,112,128]{2,1,0:T(8,128)S(1)} %get-tuple-element.64), channel_id=1, source_target_pairs={{0,2},{2,0},{4,6},{6,4},{8,10},{10,8},{12,14},{14,12},{16,18},{18,... | collective-permute-start | bytes 688136 | tf_op jit(solution)/shard_map/ppermute | solution.py:116
  24.6 5.2 %collective-permute-start.7 = (f32[8,16,128]{2,1,0:T(8,128)S(1)}, f32[8,16,128]{2,1,0:T(8,128)S(1)}, u32[]{:S(2)}, u32[]{:S(2)}) collective-permute-start(f32[8,16,128]{2,1,0:T(8,128)S(1)} %get-tuple-element.68), channel_id=1, source_target_pairs={{0,16},{2,18},{4,20},{6,22},{8,24},{10,26},{12,28},{14,30},{16,0},... | collective-permute-start | bytes 196616 | tf_op jit(solution)/shard_map/ppermute | solution.py:116
  29.8 6.0 %collective-permute-start.8 = (f32[2,2,112,128]{3,2,1,0:T(8,128)S(1)}, f32[2,2,112,128]{3,2,1,0:T(8,128)S(1)}, u32[]{:S(2)}, u32[]{:S(2)}) collective-permute-start(f32[2,2,112,128]{3,2,1,0:T(8,128)S(1)} %get-tuple-element.40), channel_id=1, source_target_pairs={{0,8},{2,10},{4,12},{6,14},{8,0},{10,2},{12,4},{14,6},{16,24},{18,... | collective-permute-start | bytes 688136 | tf_op jit(solution)/shard_map/ppermute | solution.py:116
  31.4 4.5 %collective-permute-start.9 = (f32[4,16,128]{2,1,0:T(8,128)S(1)}, f32[4,16,128]{2,1,0:T(8,128)S(1)}, u32[]{:S(2)}, u32[]{:S(2)}) collective-permute-start(f32[4,16,128]{2,1,0:T(8,128)S(1)} %get-tuple-element.70), channel_id=1, source_target_pairs={{0,2},{2,0},{4,6},{6,4},{8,10},{10,8},{12,14},{14,12},{16,18},{18,... | collective-permute-start | bytes 98312 | tf_op jit(solution)/shard_map/ppermute | solution.py:116
  35.9 7.5 %collective-permute-start.10 = (f32[2,112,128]{2,1,0:T(8,128)S(1)}, f32[2,112,128]{2,1,0:T(8,128)S(1)}, u32[]{:S(2)}, u32[]{:S(2)}) collective-permute-start(f32[2,112,128]{2,1,0:T(8,128)S(1)} %bitcast.17), channel_id=1, source_target_pairs={{0,16},{2,18},{4,20},{6,22},{8,24},{10,26},{12,28},{14,30},{16,0},... | collective-permute-start | bytes 344072 | tf_op jit(solution)/shard_map/ppermute | solution.py:116
  39.2 3.7 %collective-permute-start.11 = (f32[2,16,128]{2,1,0:T(8,128)S(1)}, f32[2,16,128]{2,1,0:T(8,128)S(1)}, u32[]{:S(2)}, u32[]{:S(2)}) collective-permute-start(f32[2,16,128]{2,1,0:T(8,128)S(1)} %get-tuple-element.79), channel_id=1, source_target_pairs={{0,4},{2,6},{4,0},{6,2},{8,12},{10,14},{12,8},{14,10},{16,20},{18,... | collective-permute-start | bytes 49160 | tf_op jit(solution)/shard_map/ppermute | solution.py:116
  44.1 8.3 %collective-permute-start.14 = (bf16[2,128,128]{2,1,0:T(8,128)(2,1)S(1)}, bf16[2,128,128]{2,1,0:T(8,128)(2,1)S(1)}, u32[]{:S(2)}, u32[]{:S(2)}) collective-permute-start(bf16[2,128,128]{2,1,0:T(8,128)(2,1)S(1)} %get-tuple-element.44), channel_id=1, source_target_pairs={{0,24},{2,26},{4,28},{6,30},{8,16},{10,18},{12,20},{14,22},{16,8},... | collective-permute-start | bytes 196616 | tf_op jit(solution)/shard_map/ppermute | solution.py:116
  49.0 4.3 %collective-permute-start.13 = (bf16[2,128,128]{2,1,0:T(8,128)(2,1)S(1)}, bf16[2,128,128]{2,1,0:T(8,128)(2,1)S(1)}, u32[]{:S(2)}, u32[]{:S(2)}) collective-permute-start(bf16[2,128,128]{2,1,0:T(8,128)(2,1)S(1)} %get-tuple-element.44), channel_id=1, source_target_pairs={{0,8},{2,10},{4,12},{6,14},{8,0},{10,2},{12,4},{14,6},{16,24},{18,... | collective-permute-start | bytes 196616 | tf_op jit(solution)/shard_map/ppermute | solution.py:116
  49.0 5.2 %collective-permute-start.12 = (bf16[2,128,128]{2,1,0:T(8,128)(2,1)S(1)}, bf16[2,128,128]{2,1,0:T(8,128)(2,1)S(1)}, u32[]{:S(2)}, u32[]{:S(2)}) collective-permute-start(bf16[2,128,128]{2,1,0:T(8,128)(2,1)S(1)} %get-tuple-element.44), channel_id=1, source_target_pairs={{0,16},{2,18},{4,20},{6,22},{8,24},{10,26},{12,28},{14,30},{16,0},... | collective-permute-start | bytes 196616 | tf_op jit(solution)/shard_map/ppermute | solution.py:116
  54.2 5.0 %collective-permute-start.15 = (bf16[4,128,128]{2,1,0:T(8,128)(2,1)S(1)}, bf16[4,128,128]{2,1,0:T(8,128)(2,1)S(1)}, u32[]{:S(2)}, u32[]{:S(2)}) collective-permute-start(bf16[4,128,128]{2,1,0:T(8,128)(2,1)S(1)} %get-tuple-element.47), channel_id=1, source_target_pairs={{0,4},{2,6},{4,0},{6,2},{8,12},{10,14},{12,8},{14,10},{16,20},{18,... | collective-permute-start | bytes 393224 | tf_op jit(solution)/shard_map/ppermute | solution.py:116
  55.0 5.0 %collective-permute-start.16 = (bf16[4,128,128]{2,1,0:T(8,128)(2,1)S(1)}, bf16[4,128,128]{2,1,0:T(8,128)(2,1)S(1)}, u32[]{:S(2)}, u32[]{:S(2)}) collective-permute-start(bf16[4,128,128]{2,1,0:T(8,128)(2,1)S(1)} %get-tuple-element.48), channel_id=1, source_target_pairs={{0,2},{2,0},{4,6},{6,4},{8,10},{10,8},{12,14},{14,12},{16,18},{18,... | collective-permute-start | bytes 393224 | tf_op jit(solution)/shard_map/ppermute | solution.py:116
  60.0 6.4 %collective-permute-start.18 = (bf16[8,128,128]{2,1,0:T(8,128)(2,1)S(1)}, bf16[8,128,128]{2,1,0:T(8,128)(2,1)S(1)}, u32[]{:S(2)}, u32[]{:S(2)}) collective-permute-start(bf16[8,128,128]{2,1,0:T(8,128)(2,1)S(1)} %pad_maximum_fusion.refs_0_), channel_id=1, source_target_pairs={{0,2},{2,0},{4,6},{6,4},{8,10},{10,8},{12,14},{14,12},{16,18},{18,... | collective-permute-start | bytes 786440 | tf_op jit(solution)/shard_map/ppermute | solution.py:116
  61.1 6.4 %collective-permute-start.19 = (bf16[8,128,128]{2,1,0:T(8,128)(2,1)S(1)}, bf16[8,128,128]{2,1,0:T(8,128)(2,1)S(1)}, u32[]{:S(2)}, u32[]{:S(2)}) collective-permute-start(bf16[8,128,128]{2,1,0:T(8,128)(2,1)S(1)} %pad_maximum_fusion.1.refs_1_), channel_id=1, source_target_pairs={{0,4},{2,6},{4,0},{6,2},{8,12},{10,14},{12,8},{14,10},{16,20},{18,... | collective-permute-start | bytes 786440 | tf_op jit(solution)/shard_map/ppermute | solution.py:116
  61.7 1.3 %collective-permute-start.17 = (bf16[4,128,128]{2,1,0:T(8,128)(2,1)S(1)}, bf16[4,128,128]{2,1,0:T(8,128)(2,1)S(1)}, u32[]{:S(2)}, u32[]{:S(2)}) collective-permute-start(bf16[4,128,128]{2,1,0:T(8,128)(2,1)S(1)} %finish.1.own_ref), channel_id=1, source_target_pairs={{0,1},{1,0},{2,3},{3,2},{4,5},{5,4},{6,7},{7,6},{8,9},{9,8},{10,11... | collective-permute-start | bytes 393224 | tf_op jit(solution)/shard_map/ppermute | solution.py:116
  61.7 6.3 %collective-permute-start.22 = (bf16[8,128,128]{2,1,0:T(8,128)(2,1)S(1)}, bf16[8,128,128]{2,1,0:T(8,128)(2,1)S(1)}, u32[]{:S(2)}, u32[]{:S(2)}) collective-permute-start(bf16[8,128,128]{2,1,0:T(8,128)(2,1)S(1)} %pad_maximum_fusion.refs_0_), channel_id=1, source_target_pairs={{0,1},{1,0},{2,3},{3,2},{4,5},{5,4},{6,7},{7,6},{8,9},{9,8},{10,11... | collective-permute-start | bytes 786440 | tf_op jit(solution)/shard_map/ppermute | solution.py:116
  62.2 5.8 %collective-permute-start.23 = (bf16[8,128,128]{2,1,0:T(8,128)(2,1)S(1)}, bf16[8,128,128]{2,1,0:T(8,128)(2,1)S(1)}, u32[]{:S(2)}, u32[]{:S(2)}) collective-permute-start(bf16[8,128,128]{2,1,0:T(8,128)(2,1)S(1)} %pad_maximum_fusion.1.refs_1_), channel_id=1, source_target_pairs={{0,1},{1,0},{2,3},{3,2},{4,5},{5,4},{6,7},{7,6},{8,9},{9,8},{10,11... | collective-permute-start | bytes 786440 | tf_op jit(solution)/shard_map/ppermute | solution.py:116
  67.5 2.3 %collective-permute-start.20 = (bf16[8,128,128]{2,1,0:T(8,128)(2,1)S(1)}, bf16[8,128,128]{2,1,0:T(8,128)(2,1)S(1)}, u32[]{:S(2)}, u32[]{:S(2)}) collective-permute-start(bf16[8,128,128]{2,1,0:T(8,128)(2,1)S(1)} %collective-permute-done.18.refs_2_), channel_id=1, source_target_pairs={{0,1},{1,0},{2,3},{3,2},{4,5},{5,4},{6,7},{7,6},{8,9},{9,8},{10,11... | collective-permute-start | bytes 786440 | tf_op jit(solution)/shard_map/ppermute | solution.py:116
  67.5 2.3 %collective-permute-start.21 = (bf16[8,128,128]{2,1,0:T(8,128)(2,1)S(1)}, bf16[8,128,128]{2,1,0:T(8,128)(2,1)S(1)}, u32[]{:S(2)}, u32[]{:S(2)}) collective-permute-start(bf16[8,128,128]{2,1,0:T(8,128)(2,1)S(1)} %collective-permute-done.19.refs_3_), channel_id=1, source_target_pairs={{0,1},{1,0},{2,3},{3,2},{4,5},{5,4},{6,7},{7,6},{8,9},{9,8},{10,11... | collective-permute-start | bytes 786440 | tf_op jit(solution)/shard_map/ppermute | solution.py:116

commit v9 on v8

--- a/solution.py
+++ b/solution.py
@@ -196,7 +196,7 @@
                 table_ref[entry] = held[(here ^ offsets[stream][p]) * capacity + first_slot + stream]
 
 
-EDGE = 16
+EDGE = 24
 
 
 def tiles_kernel(owners, first, table_ref, f_own, f_sib, own_rows, kv_sib, *rest):
@@ -504,13 +504,14 @@
     kept = jnp.stack([kept_a, kept_b], axis=1)
     got = jnp.stack([got_a, got_b], axis=1)
     for step in range(2, bits):
-        due = got_c
-        kept_c, sent_c, got_c = edges_on(step, kept_c, got_c)
         kept, sent = halved(kept, got)
-        sent = after(sent, due)
+        if step > 2:
+            sent = after(sent, got_c)
+            kept_c, sent_c, got_c = edges_on(step - 1, kept_c, got_c)
         if step == bits - 1:
             sent, kept = sent[0], kept[0]
         got = swap_along(sent, "dp", owners, 1 << orders[0][step])
+    kept_c, sent_c, got_c = edges_on(bits - 1, kept_c, got_c)
     direction, grads = on_slots(
         direction_kernel,
         side,

time: 71.5 us -> 69 us (0.965)
  waiting for transfers between devices: 21.1 us -> 18.2 us
    ppermute x24, waiting for transfers between devices: 21.1 us -> 18.2 us  [swap_along(): return lax.ppermute(values, axis, [(i, i ^ bit) for i in range(size)])]
  transfers between devices with their start and end apart: 24 -> 24, of which waited for: 14 -> 13; matrix products, arithmetic and copies ran while one was open for 0% -> 0% of each run, Pallas kernels for 18% -> 18%
where the time goes in v9:
time: 69 us; the launch traced here: 68.8 us
  starting transfers between devices  30.3 us (44%)
  waiting for transfers between devices  18.2 us (26%)
  Pallas kernels  16.2 us (23%)
  local copies, waits for them, and re-layouts  2.88 us (4%)
  between operations  0.87 us (1%)
    ppermute x24, starting transfers between devices, swap_along(): return lax.ppermute(values, axis, [(i, i ^ bit) for i in range(size)])  30.3 us
    ppermute x24, waiting for transfers between devices, swap_along(): return lax.ppermute(values, axis, [(i, i ^ bit) for i in range(size)])  18.2 us
    pallas_call x3, Pallas kernels, on_slots(): pl.pallas_call(kernel, out_shape=tuple(outs), grid_spec=pltpu.PrefetchSca...  3.99 us
    pallas_call x2, Pallas kernels, place_more(): pl.pallas_call(functools.partial(more_kernel, col_tiles, entries), out_sh...  3.25 us
    pallas_call x1, Pallas kernels, sweeping(): pl.pallas_call(kernel, out_shape=jax.ShapeDtypeStruct(values.shape, dtype...  2.9 us
    unnamed x18, local copies, waits for them, and re-layouts  2.85 us
    pallas_call x2, Pallas kernels, tiles_from(): pl.pallas_call(functools.partial(tiles_kernel, owners, first), out_shape=...  2.82 us
    pallas_call x1, Pallas kernels, per_device_dealt(): pl.pallas_call(functools.partial(table_kernel, owners, capacity), out_sha...  1.65 us
  transfers between devices with their start and end apart: 24, of which 13 were waited for; matrix products, arithmetic and copies ran while one was open for 0% of the time, Pallas kernels for 18%

profile of v9, /device:TPU:0, one launch (start us, length us, event | category | flops | bytes accessed | tf_op | source)
XLA Modules:
  0.0 68.8 jit_solution(1781302593440385585)
XLA Ops:
  0.6 0.5 collective-permute-start
  1.1 0.1 collective-permute-start.1
  1.2 0.1 pad_add_fusion.place_ref
  1.3 0.9 %copy-done.7 = bf16[256,512]{1,0:T(8,128)(2,1)S(1)} copy-done((bf16[256,512]{1,0:T(8,128)(2,1)S(1)}, bf16[256,512]{1,0:T(8,128)(2,1)}, u32[]{:S(2)}) %copy-start.7) | copy-done | bytes 262168
  2.3 0.7 copy-done.8
  2.9 1.7 %table.1 = (s32[64]{0:T(128)S(1)}, bf16[512,256]{1,0:T(8,128)(2,1)S(1)}) custom-call(s32[2]{0:T(128)S(1)} %pad_add_fusion.place_ref, s32[64]{0:T(128)S(1)} %copy-done.8, bf16[256,512]{1,0:T(8,128)(2,1)S(1)} %copy-done.7), custom_call_target="tpu_custom_call" | custom-call | bytes 1000000 | tf_op jit(solution)/shard_map/table/pallas_call | solution.py:438
  4.6 1.2 %copy-done = bf16[256,2048]{1,0:T(8,128)(2,1)S(1)} copy-done((bf16[256,2048]{1,0:T(8,128)(2,1)S(1)}, bf16[256,2048]{1,0:T(8,128)(2,1)}, u32[]{:S(2)}) %copy-start) | copy-done | bytes 1048600
  5.8 1.4 %tiles.2 = (f32[8,104,128]{2,1,0:T(8,128)S(1)}, f32[8,104,128]{2,1,0:T(8,128)S(1)}, f32[32,24,128]{2,1,0:T(8,128)S(1)}) custom-call(s32[64]{0:T(128)S(1)} %get-tuple-element.30.table_ref, bf16[256,2048]{1,0:T(8,128)(2,1)S(1)} %copy-done, bf16[256,2048]{1,0:T(8,128)(2,1)S(1)} %collective-permute-done.f_sib, bf16[512,256]{1,0:T(8,128)(2,1)S(1)} %get-tuple-element.31.own_rows, ...), custom_call_target="tpu_custom_call" | custom-call | flops 536870912 | bytes 3500000 | tf_op jit(solution)/shard_map/tiles/pallas_call | solution.py:457
  7.2 3.0 %collective-permute-start.2 = (f32[8,104,128]{2,1,0:T(8,128)S(1)}, f32[8,104,128]{2,1,0:T(8,128)S(1)}, u32[]{:S(2)}, u32[]{:S(2)}) collective-permute-start(f32[8,104,128]{2,1,0:T(8,128)S(1)} %get-tuple-element.34), channel_id=1, source_target_pairs={{0,2},{2,0},{4,6},{6,4},{8,10},{10,8},{12,14},{14,12},{16,18},{18,... | collective-permute-start | bytes 1277960 | tf_op jit(solution)/shard_map/ppermute | solution.py:116
  10.2 1.5 %collective-permute-start.3 = (f32[8,104,128]{2,1,0:T(8,128)S(1)}, f32[8,104,128]{2,1,0:T(8,128)S(1)}, u32[]{:S(2)}, u32[]{:S(2)}) collective-permute-start(f32[8,104,128]{2,1,0:T(8,128)S(1)} %get-tuple-element.36), channel_id=1, source_target_pairs={{0,4},{2,6},{4,0},{6,2},{8,12},{10,14},{12,8},{14,10},{16,20},{18,... | collective-permute-start | bytes 1277960 | tf_op jit(solution)/shard_map/ppermute | solution.py:116
  11.7 1.4 %tiles.3 = (f32[8,104,128]{2,1,0:T(8,128)S(1)}, f32[8,104,128]{2,1,0:T(8,128)S(1)}, f32[16,24,128]{2,1,0:T(8,128)S(1)}, f32[16,24,128]{2,1,0:T(8,128)S(1)}) custom-call(s32[64]{0:T(128)S(1)} %get-tuple-element.30.table_ref, bf16[256,2048]{1,0:T(8,128)(2,1)S(1)} %copy-done, bf16[256,2048]{1,0:T(8,128)(2,1)S(1)} %collective-permute-done.f_sib, ...), custom_call_target="tpu_custom_call" | custom-call | flops 536870912 | bytes 3500000 | tf_op jit(solution)/shard_map/tiles/pallas_call | solution.py:457
  13.1 1.6 %collective-permute-start.7 = (f32[16,24,128]{2,1,0:T(8,128)S(1)}, f32[16,24,128]{2,1,0:T(8,128)S(1)}, u32[]{:S(2)}, u32[]{:S(2)}) collective-permute-start(f32[16,24,128]{2,1,0:T(8,128)S(1)} %get-tuple-element.38), channel_id=1, source_target_pairs={{0,8},{2,10},{4,12},{6,14},{8,0},{10,2},{12,4},{14,6},{16,24},{18,... | collective-permute-start | bytes 589832 | tf_op jit(solution)/shard_map/ppermute | solution.py:116
  14.8 5.5 %collective-permute-done.2 = f32[8,104,128]{2,1,0:T(8,128)S(1)} collective-permute-done((f32[8,104,128]{2,1,0:T(8,128)S(1)}, f32[8,104,128]{2,1,0:T(8,128)S(1)}, u32[]{:S(2)}, u32[]{:S(2)}) %collective-permute-start.2) | collective-permute-done | bytes 426016 | tf_op jit(solution)/shard_map/ppermute | solution.py:116
  20.3 1.8 %collective-permute-start.4 = (f32[4,104,128]{2,1,0:T(8,128)S(1)}, f32[4,104,128]{2,1,0:T(8,128)S(1)}, u32[]{:S(2)}, u32[]{:S(2)}) collective-permute-start(f32[4,104,128]{2,1,0:T(8,128)S(1)} %get-tuple-element.60), channel_id=1, source_target_pairs={{0,4},{2,6},{4,0},{6,2},{8,12},{10,14},{12,8},{14,10},{16,20},{18,... | collective-permute-start | bytes 638984 | tf_op jit(solution)/shard_map/ppermute | solution.py:116
  22.2 0.0 copy-start.4
  22.3 1.6 %collective-permute-start.5 = (f32[4,104,128]{2,1,0:T(8,128)S(1)}, f32[4,104,128]{2,1,0:T(8,128)S(1)}, u32[]{:S(2)}, u32[]{:S(2)}) collective-permute-start(f32[4,104,128]{2,1,0:T(8,128)S(1)} %get-tuple-element.62), channel_id=1, source_target_pairs={{0,2},{2,0},{4,6},{6,4},{8,10},{10,8},{12,14},{14,12},{16,18},{18,... | collective-permute-start | bytes 638984 | tf_op jit(solution)/shard_map/ppermute | solution.py:116
  23.9 2.6 %collective-permute-start.8 = (f32[8,24,128]{2,1,0:T(8,128)S(1)}, f32[8,24,128]{2,1,0:T(8,128)S(1)}, u32[]{:S(2)}, u32[]{:S(2)}) collective-permute-start(f32[8,24,128]{2,1,0:T(8,128)S(1)} %get-tuple-element.66), channel_id=1, source_target_pairs={{0,16},{2,18},{4,20},{6,22},{8,24},{10,26},{12,28},{14,30},{16,0},... | collective-permute-start | bytes 294920 | tf_op jit(solution)/shard_map/ppermute | solution.py:116
  26.5 0.6 collective-permute-done.4
  27.1 1.4 %collective-permute-done.5 = f32[4,104,128]{2,1,0:T(8,128)S(1)} collective-permute-done((f32[4,104,128]{2,1,0:T(8,128)S(1)}, f32[4,104,128]{2,1,0:T(8,128)S(1)}, u32[]{:S(2)}, u32[]{:S(2)}) %collective-permute-start.5) | collective-permute-done | bytes 213024 | tf_op jit(solution)/shard_map/ppermute | solution.py:116
  28.5 1.6 %collective-permute-start.6 = (f32[2,2,104,128]{3,2,1,0:T(8,128)S(1)}, f32[2,2,104,128]{3,2,1,0:T(8,128)S(1)}, u32[]{:S(2)}, u32[]{:S(2)}) collective-permute-start(f32[2,2,104,128]{3,2,1,0:T(8,128)S(1)} %get-tuple-element.58), channel_id=1, source_target_pairs={{0,8},{2,10},{4,12},{6,14},{8,0},{10,2},{12,4},{14,6},{16,24},{18,... | collective-permute-start | bytes 638984 | tf_op jit(solution)/shard_map/ppermute | solution.py:116
  30.2 1.5 %collective-permute-start.10 = (f32[4,24,128]{2,1,0:T(8,128)S(1)}, f32[4,24,128]{2,1,0:T(8,128)S(1)}, u32[]{:S(2)}, u32[]{:S(2)}) collective-permute-start(f32[4,24,128]{2,1,0:T(8,128)S(1)} %get-tuple-element.68), channel_id=1, source_target_pairs={{0,2},{2,0},{4,6},{6,4},{8,10},{10,8},{12,14},{14,12},{16,18},{18,... | collective-permute-start | bytes 147464 | tf_op jit(solution)/shard_map/ppermute | solution.py:116
  31.7 2.7 %collective-permute-done.6 = f32[2,2,104,128]{3,2,1,0:T(8,128)S(1)} collective-permute-done((f32[2,2,104,128]{3,2,1,0:T(8,128)S(1)}, f32[2,2,104,128]{3,2,1,0:T(8,128)S(1)}, u32[]{:S(2)}, u32[]{:S(2)}) %collective-permute-start.6) | collective-permute-done | bytes 213024 | tf_op jit(solution)/shard_map/ppermute | solution.py:116
  34.5 2.6 %collective-permute-start.9 = (f32[2,104,128]{2,1,0:T(8,128)S(1)}, f32[2,104,128]{2,1,0:T(8,128)S(1)}, u32[]{:S(2)}, u32[]{:S(2)}) collective-permute-start(f32[2,104,128]{2,1,0:T(8,128)S(1)} %bitcast.17), channel_id=1, source_target_pairs={{0,16},{2,18},{4,20},{6,22},{8,24},{10,26},{12,28},{14,30},{16,0},... | collective-permute-start | bytes 319496 | tf_op jit(solution)/shard_map/ppermute | solution.py:116
  37.1 1.1 %collective-permute-start.11 = (f32[2,24,128]{2,1,0:T(8,128)S(1)}, f32[2,24,128]{2,1,0:T(8,128)S(1)}, u32[]{:S(2)}, u32[]{:S(2)}) collective-permute-start(f32[2,24,128]{2,1,0:T(8,128)S(1)} %get-tuple-element.69), channel_id=1, source_target_pairs={{0,4},{2,6},{4,0},{6,2},{8,12},{10,14},{12,8},{14,10},{16,20},{18,... | collective-permute-start | bytes 73736 | tf_op jit(solution)/shard_map/ppermute | solution.py:116
  38.2 0.5 rotated.1
  38.7 2.3 %collective-permute-done.11.d_ref = f32[2,24,128]{2,1,0:T(8,128)S(1)} collective-permute-done((f32[2,24,128]{2,1,0:T(8,128)S(1)}, f32[2,24,128]{2,1,0:T(8,128)S(1)}, u32[]{:S(2)}, u32[]{:S(2)}) %collective-permute-start.11) | collective-permute-done | bytes 24608 | tf_op jit(solution)/shard_map/ppermute | solution.py:116
  41.0 0.3 collective-permute-done.9.b_ref
  41.3 0.7 %direction.1 = (bf16[2,128,128]{2,1,0:T(8,128)(2,1)S(1)}, f32[2,128,128]{2,1,0:T(8,128)S(1)}) custom-call(s32[1]{0:T(128)} %bitcast.1.side_ref, f32[2,104,128]{2,1,0:T(8,128)S(1)} %get-tuple-element.64.a_ref, f32[2,104,128]{2,1,0:T(8,128)S(1)} %collective-permute-done.9.b_ref, f32[2,24,128]{2,1,0:T(8,128)S(1)} %get-tuple-element.70.c_ref, ...), custom_call_target="tpu_custom_call" | custom-call | flops 67108864 | bytes 800000 | tf_op jit(solution)/shard_map/direction/pallas_call | solution.py:291
  42.0 4.3 %collective-permute-start.14 = (bf16[2,128,128]{2,1,0:T(8,128)(2,1)S(1)}, bf16[2,128,128]{2,1,0:T(8,128)(2,1)S(1)}, u32[]{:S(2)}, u32[]{:S(2)}) collective-permute-start(bf16[2,128,128]{2,1,0:T(8,128)(2,1)S(1)} %get-tuple-element.42), channel_id=1, source_target_pairs={{0,24},{2,26},{4,28},{6,30},{8,16},{10,18},{12,20},{14,22},{16,8},... | collective-permute-start | bytes 196616 | tf_op jit(solution)/shard_map/ppermute | solution.py:116
  46.4 0.6 collective-permute-start.12
  47.0 2.8 %refresh.1.iter_ref = f32[4,128,128]{2,1,0:T(8,128)S(1)} custom-call(s32[1]{0:T(128)} %bitcast.1.side_ref, f32[2,128,128]{2,1,0:T(8,128)S(1)} %get-tuple-element.43.g_ref, f32[4,128,128]{2,1,0:T(8,128)S(1)} %get-tuple-element.44.power_ref, bf16[1,4,128,128]{3,2,1,0:T(8,128)(2,1)S(1)} %copy-done.1, bf16[1,4,128,128]{3,2,1,0:T(8,128)(2,1)S(1)} %copy-done.2), custom_call_target="tpu_custom_call" | custom-call | flops 939524096 | bytes 800000 | tf_op jit(solution)/shard_map/refresh/pallas_call | solution.py:291
  49.8 0.8 %collective-permute-done.13 = bf16[2,128,128]{2,1,0:T(8,128)(2,1)S(1)} collective-permute-done((bf16[2,128,128]{2,1,0:T(8,128)(2,1)S(1)}, bf16[2,128,128]{2,1,0:T(8,128)(2,1)S(1)}, u32[]{:S(2)}, u32[]{:S(2)}) %collective-permute-start.13) | collective-permute-done | bytes 65568 | tf_op jit(solution)/shard_map/ppermute | solution.py:116
  50.6 0.9 %collective-permute-done.12 = bf16[2,128,128]{2,1,0:T(8,128)(2,1)S(1)} collective-permute-done((bf16[2,128,128]{2,1,0:T(8,128)(2,1)S(1)}, bf16[2,128,128]{2,1,0:T(8,128)(2,1)S(1)}, u32[]{:S(2)}, u32[]{:S(2)}) %collective-permute-start.12) | collective-permute-done | bytes 65568 | tf_op jit(solution)/shard_map/ppermute | solution.py:116
  51.6 1.1 %collective-permute-start.15 = (bf16[4,128,128]{2,1,0:T(8,128)(2,1)S(1)}, bf16[4,128,128]{2,1,0:T(8,128)(2,1)S(1)}, u32[]{:S(2)}, u32[]{:S(2)}) collective-permute-start(bf16[4,128,128]{2,1,0:T(8,128)(2,1)S(1)} %get-tuple-element.45), channel_id=1, source_target_pairs={{0,4},{2,6},{4,0},{6,2},{8,12},{10,14},{12,8},{14,10},{16,20},{18,... | collective-permute-start | bytes 393224 | tf_op jit(solution)/shard_map/ppermute | solution.py:116
  52.7 0.9 %collective-permute-start.16 = (bf16[4,128,128]{2,1,0:T(8,128)(2,1)S(1)}, bf16[4,128,128]{2,1,0:T(8,128)(2,1)S(1)}, u32[]{:S(2)}, u32[]{:S(2)}) collective-permute-start(bf16[4,128,128]{2,1,0:T(8,128)(2,1)S(1)} %get-tuple-element.46), channel_id=1, source_target_pairs={{0,2},{2,0},{4,6},{6,4},{8,10},{10,8},{12,14},{14,12},{16,18},{18,... | collective-permute-start | bytes 393224 | tf_op jit(solution)/shard_map/ppermute | solution.py:116
  53.6 2.9 %finish.1.own_ref = bf16[4,128,128]{2,1,0:T(8,128)(2,1)S(1)} custom-call(f32[4,128,128]{2,1,0:T(8,128)S(1)} %refresh.1.iter_ref), custom_call_target="tpu_custom_call" | custom-call | flops 939524096 | bytes 400000 | tf_op jit(solution)/shard_map/finish/pallas_call | solution.py:341
  56.5 1.0 %collective-permute-done.15 = bf16[4,128,128]{2,1,0:T(8,128)(2,1)S(1)} collective-permute-done((bf16[4,128,128]{2,1,0:T(8,128)(2,1)S(1)}, bf16[4,128,128]{2,1,0:T(8,128)(2,1)S(1)}, u32[]{:S(2)}, u32[]{:S(2)}) %collective-permute-start.15) | collective-permute-done | bytes 131104 | tf_op jit(solution)/shard_map/ppermute | solution.py:116
  57.5 0.1 collective-permute-done.16
  57.7 1.0 %collective-permute-start.18 = (bf16[8,128,128]{2,1,0:T(8,128)(2,1)S(1)}, bf16[8,128,128]{2,1,0:T(8,128)(2,1)S(1)}, u32[]{:S(2)}, u32[]{:S(2)}) collective-permute-start(bf16[8,128,128]{2,1,0:T(8,128)(2,1)S(1)} %pad_maximum_fusion.refs_0_), channel_id=1, source_target_pairs={{0,2},{2,0},{4,6},{6,4},{8,10},{10,8},{12,14},{14,12},{16,18},{18,... | collective-permute-start | bytes 786440 | tf_op jit(solution)/shard_map/ppermute | solution.py:116
  58.7 1.6 %collective-permute-start.19 = (bf16[8,128,128]{2,1,0:T(8,128)(2,1)S(1)}, bf16[8,128,128]{2,1,0:T(8,128)(2,1)S(1)}, u32[]{:S(2)}, u32[]{:S(2)}) collective-permute-start(bf16[8,128,128]{2,1,0:T(8,128)(2,1)S(1)} %pad_maximum_fusion.1.refs_1_), channel_id=1, source_target_pairs={{0,4},{2,6},{4,0},{6,2},{8,12},{10,14},{12,8},{14,10},{16,20},{18,... | collective-permute-start | bytes 786440 | tf_op jit(solution)/shard_map/ppermute | solution.py:116
  60.2 0.5 collective-permute-start.22
  60.7 0.8 %collective-permute-done.17.sib_ref = bf16[4,128,128]{2,1,0:T(8,128)(2,1)S(1)} collective-permute-done((bf16[4,128,128]{2,1,0:T(8,128)(2,1)S(1)}, bf16[4,128,128]{2,1,0:T(8,128)(2,1)S(1)}, u32[]{:S(2)}, u32[]{:S(2)}) %collective-permute-start.17) | collective-permute-done | bytes 131104 | tf_op jit(solution)/shard_map/ppermute | solution.py:116
  61.6 1.6 %begin.1 = (bf16[2048,512]{1,0:T(8,128)(2,1)}, bf16[1,4,128,128]{3,2,1,0:T(8,128)(2,1)}, bf16[1,4,128,128]{3,2,1,0:T(8,128)(2,1)}) custom-call(s32[64]{0:T(128)S(1)} %get-tuple-element.30.table_ref, s32[2]{0:T(128)S(1)} %pad_add_fusion.place_ref, bf16[4,128,128]{2,1,0:T(8,128)(2,1)S(1)} %finish.1.own_ref, ...), custom_call_target="tpu_custom_call" | custom-call | bytes 800000 | tf_op jit(solution)/shard_map/begin/pallas_call | solution.py:546
  63.2 0.9 %collective-permute-done.18.refs_2_ = bf16[8,128,128]{2,1,0:T(8,128)(2,1)S(1)} collective-permute-done((bf16[8,128,128]{2,1,0:T(8,128)(2,1)S(1)}, bf16[8,128,128]{2,1,0:T(8,128)(2,1)S(1)}, u32[]{:S(2)}, u32[]{:S(2)}) %collective-permute-start.18) | collective-permute-done | bytes 262176 | tf_op jit(solution)/shard_map/ppermute | solution.py:116
  64.1 0.9 %collective-permute-done.19.refs_3_ = bf16[8,128,128]{2,1,0:T(8,128)(2,1)S(1)} collective-permute-done((bf16[8,128,128]{2,1,0:T(8,128)(2,1)S(1)}, bf16[8,128,128]{2,1,0:T(8,128)(2,1)S(1)}, u32[]{:S(2)}, u32[]{:S(2)}) %collective-permute-start.19) | collective-permute-done | bytes 262176 | tf_op jit(solution)/shard_map/ppermute | solution.py:116
  65.0 0.5 collective-permute-start.21
  65.5 1.8 %more.2.refs_2_ = bf16[2048,512]{1,0:T(8,128)(2,1)} custom-call(s32[64]{0:T(128)S(1)} %get-tuple-element.30.table_ref, bf16[8,128,128]{2,1,0:T(8,128)(2,1)S(1)} %collective-permute-done.22.refs_0_, bf16[8,128,128]{2,1,0:T(8,128)(2,1)S(1)} %collective-permute-done.23.refs_1_, ...), custom_call_target="tpu_custom_call", output_to_operand_aliasing={{}: (5, {})} | custom-call | bytes 1000000 | tf_op jit(solution)/shard_map/more/pallas_call | solution.py:393
  67.4 1.5 %more.3 = bf16[2048,512]{1,0:T(8,128)(2,1)} custom-call(s32[64]{0:T(128)S(1)} %get-tuple-element.30.table_ref, bf16[8,128,128]{2,1,0:T(8,128)(2,1)S(1)} %collective-permute-done.20.refs_0_, bf16[8,128,128]{2,1,0:T(8,128)(2,1)S(1)} %collective-permute-done.21.refs_1_, bf16[2048,512]{1,0:T(8,128)(2,1)} %more.2.refs_2_), custom_call_target="tpu_custom_call", output_to_operand_aliasing={{}: (3, {})} | custom-call | bytes 1000000 | tf_op jit(solution)/shard_map/more/pallas_call | solution.py:393
  (43 shorter events, 0.4 us)
Async XLA Ops:
  0.6 4.0 %collective-permute-start = (bf16[256,2048]{1,0:T(8,128)(2,1)}, bf16[256,2048]{1,0:T(8,128)(2,1)S(1)}, u32[]{:S(2)}, u32[]{:S(2)}) collective-permute-start(bf16[256,2048]{1,0:T(8,128)(2,1)} %f_own.3), channel_id=1, source_target_pairs={{0,1},{1,0},{2,3},{3,2},{4,5},{5,4},{6,7},{7,6},{8,9},{9,8},{10,11... | collective-permute-start | bytes 3145736 | tf_op jit(solution)/shard_map/ppermute | solution.py:116
  1.1 3.4 %collective-permute-start.1 = (bf16[256,512]{1,0:T(8,128)(2,1)}, bf16[256,512]{1,0:T(8,128)(2,1)S(1)}, u32[]{:S(2)}, u32[]{:S(2)}) collective-permute-start(bf16[256,512]{1,0:T(8,128)(2,1)} %kv_ref.1), channel_id=1, source_target_pairs={{0,1},{1,0},{2,3},{3,2},{4,5},{5,4},{6,7},{7,6},{8,9},{9,8},{10,11... | collective-permute-start | bytes 786440 | tf_op jit(solution)/shard_map/ppermute | solution.py:116
  1.3 0.9 %copy-start.7 = (bf16[256,512]{1,0:T(8,128)(2,1)S(1)}, bf16[256,512]{1,0:T(8,128)(2,1)}, u32[]{:S(2)}) copy-start(bf16[256,512]{1,0:T(8,128)(2,1)} %kv_ref.1) | copy-start | bytes 786436
  2.3 0.7 copy-start.8
  4.6 1.2 %copy-start = (bf16[256,2048]{1,0:T(8,128)(2,1)S(1)}, bf16[256,2048]{1,0:T(8,128)(2,1)}, u32[]{:S(2)}) copy-start(bf16[256,2048]{1,0:T(8,128)(2,1)} %f_own.3) | copy-start | bytes 3145732
  7.2 13.0 %collective-permute-start.2 = (f32[8,104,128]{2,1,0:T(8,128)S(1)}, f32[8,104,128]{2,1,0:T(8,128)S(1)}, u32[]{:S(2)}, u32[]{:S(2)}) collective-permute-start(f32[8,104,128]{2,1,0:T(8,128)S(1)} %get-tuple-element.34), channel_id=1, source_target_pairs={{0,2},{2,0},{4,6},{6,4},{8,10},{10,8},{12,14},{14,12},{16,18},{18,... | collective-permute-start | bytes 1277960 | tf_op jit(solution)/shard_map/ppermute | solution.py:116
  10.2 11.9 %collective-permute-start.3 = (f32[8,104,128]{2,1,0:T(8,128)S(1)}, f32[8,104,128]{2,1,0:T(8,128)S(1)}, u32[]{:S(2)}, u32[]{:S(2)}) collective-permute-start(f32[8,104,128]{2,1,0:T(8,128)S(1)} %get-tuple-element.36), channel_id=1, source_target_pairs={{0,4},{2,6},{4,0},{6,2},{8,12},{10,14},{12,8},{14,10},{16,20},{18,... | collective-permute-start | bytes 1277960 | tf_op jit(solution)/shard_map/ppermute | solution.py:116
  13.1 10.7 %collective-permute-start.7 = (f32[16,24,128]{2,1,0:T(8,128)S(1)}, f32[16,24,128]{2,1,0:T(8,128)S(1)}, u32[]{:S(2)}, u32[]{:S(2)}) collective-permute-start(f32[16,24,128]{2,1,0:T(8,128)S(1)} %get-tuple-element.38), channel_id=1, source_target_pairs={{0,8},{2,10},{4,12},{6,14},{8,0},{10,2},{12,4},{14,6},{16,24},{18,... | collective-permute-start | bytes 589832 | tf_op jit(solution)/shard_map/ppermute | solution.py:116
  20.3 6.8 %collective-permute-start.4 = (f32[4,104,128]{2,1,0:T(8,128)S(1)}, f32[4,104,128]{2,1,0:T(8,128)S(1)}, u32[]{:S(2)}, u32[]{:S(2)}) collective-permute-start(f32[4,104,128]{2,1,0:T(8,128)S(1)} %get-tuple-element.60), channel_id=1, source_target_pairs={{0,4},{2,6},{4,0},{6,2},{8,12},{10,14},{12,8},{14,10},{16,20},{18,... | collective-permute-start | bytes 638984 | tf_op jit(solution)/shard_map/ppermute | solution.py:116
  22.2 16.0 %copy-start.1 = (bf16[1,4,128,128]{3,2,1,0:T(8,128)(2,1)S(1)}, bf16[1,4,128,128]{3,2,1,0:T(8,128)(2,1)}, u32[]{:S(2)}) copy-start(bf16[1,4,128,128]{3,2,1,0:T(8,128)(2,1)} %ql_ref.3) | copy-start | bytes 393220
  22.2 16.0 %copy-start.2 = (bf16[1,4,128,128]{3,2,1,0:T(8,128)(2,1)S(1)}, bf16[1,4,128,128]{3,2,1,0:T(8,128)(2,1)}, u32[]{:S(2)}) copy-start(bf16[1,4,128,128]{3,2,1,0:T(8,128)(2,1)} %qr_ref.3) | copy-start | bytes 393220
  22.2 16.0 %copy-start.3 = (f32[1,4,128,128]{3,2,1,0:T(8,128)S(1)}, f32[1,4,128,128]{3,2,1,0:T(8,128)}, u32[]{:S(2)}) copy-start(f32[1,4,128,128]{3,2,1,0:T(8,128)} %m_ref.1) | copy-start | bytes 786436
  22.2 16.0 %copy-start.4 = (f32[1,4,128,128]{3,2,1,0:T(8,128)S(1)}, f32[1,4,128,128]{3,2,1,0:T(8,128)}, u32[]{:S(2)}) copy-start(f32[1,4,128,128]{3,2,1,0:T(8,128)} %v_ref.1) | copy-start | bytes 786436
  22.2 16.0 %copy-start.5 = (f32[1,4,128,128]{3,2,1,0:T(8,128)S(1)}, f32[1,4,128,128]{3,2,1,0:T(8,128)}, u32[]{:S(2)}) copy-start(f32[1,4,128,128]{3,2,1,0:T(8,128)} %l_ref.1) | copy-start | bytes 786436
  22.2 16.0 %copy-start.6 = (f32[1,4,128,128]{3,2,1,0:T(8,128)S(1)}, f32[1,4,128,128]{3,2,1,0:T(8,128)}, u32[]{:S(2)}) copy-start(f32[1,4,128,128]{3,2,1,0:T(8,128)} %r_ref.1) | copy-start | bytes 786436
  22.3 6.2 %collective-permute-start.5 = (f32[4,104,128]{2,1,0:T(8,128)S(1)}, f32[4,104,128]{2,1,0:T(8,128)S(1)}, u32[]{:S(2)}, u32[]{:S(2)}) collective-permute-start(f32[4,104,128]{2,1,0:T(8,128)S(1)} %get-tuple-element.62), channel_id=1, source_target_pairs={{0,2},{2,0},{4,6},{6,4},{8,10},{10,8},{12,14},{14,12},{16,18},{18,... | collective-permute-start | bytes 638984 | tf_op jit(solution)/shard_map/ppermute | solution.py:116
  23.9 6.3 %collective-permute-start.8 = (f32[8,24,128]{2,1,0:T(8,128)S(1)}, f32[8,24,128]{2,1,0:T(8,128)S(1)}, u32[]{:S(2)}, u32[]{:S(2)}) collective-permute-start(f32[8,24,128]{2,1,0:T(8,128)S(1)} %get-tuple-element.66), channel_id=1, source_target_pairs={{0,16},{2,18},{4,20},{6,22},{8,24},{10,26},{12,28},{14,30},{16,0},... | collective-permute-start | bytes 294920 | tf_op jit(solution)/shard_map/ppermute | solution.py:116
  28.5 5.9 %collective-permute-start.6 = (f32[2,2,104,128]{3,2,1,0:T(8,128)S(1)}, f32[2,2,104,128]{3,2,1,0:T(8,128)S(1)}, u32[]{:S(2)}, u32[]{:S(2)}) collective-permute-start(f32[2,2,104,128]{3,2,1,0:T(8,128)S(1)} %get-tuple-element.58), channel_id=1, source_target_pairs={{0,8},{2,10},{4,12},{6,14},{8,0},{10,2},{12,4},{14,6},{16,24},{18,... | collective-permute-start | bytes 638984 | tf_op jit(solution)/shard_map/ppermute | solution.py:116
  30.2 6.9 %collective-permute-start.10 = (f32[4,24,128]{2,1,0:T(8,128)S(1)}, f32[4,24,128]{2,1,0:T(8,128)S(1)}, u32[]{:S(2)}, u32[]{:S(2)}) collective-permute-start(f32[4,24,128]{2,1,0:T(8,128)S(1)} %get-tuple-element.68), channel_id=1, source_target_pairs={{0,2},{2,0},{4,6},{6,4},{8,10},{10,8},{12,14},{14,12},{16,18},{18,... | collective-permute-start | bytes 147464 | tf_op jit(solution)/shard_map/ppermute | solution.py:116
  34.5 6.8 %collective-permute-start.9 = (f32[2,104,128]{2,1,0:T(8,128)S(1)}, f32[2,104,128]{2,1,0:T(8,128)S(1)}, u32[]{:S(2)}, u32[]{:S(2)}) collective-permute-start(f32[2,104,128]{2,1,0:T(8,128)S(1)} %bitcast.17), channel_id=1, source_target_pairs={{0,16},{2,18},{4,20},{6,22},{8,24},{10,26},{12,28},{14,30},{16,0},... | collective-permute-start | bytes 319496 | tf_op jit(solution)/shard_map/ppermute | solution.py:116
  37.1 3.9 %collective-permute-start.11 = (f32[2,24,128]{2,1,0:T(8,128)S(1)}, f32[2,24,128]{2,1,0:T(8,128)S(1)}, u32[]{:S(2)}, u32[]{:S(2)}) collective-permute-start(f32[2,24,128]{2,1,0:T(8,128)S(1)} %get-tuple-element.69), channel_id=1, source_target_pairs={{0,4},{2,6},{4,0},{6,2},{8,12},{10,14},{12,8},{14,10},{16,20},{18,... | collective-permute-start | bytes 73736 | tf_op jit(solution)/shard_map/ppermute | solution.py:116
  42.0 7.8 %collective-permute-start.14 = (bf16[2,128,128]{2,1,0:T(8,128)(2,1)S(1)}, bf16[2,128,128]{2,1,0:T(8,128)(2,1)S(1)}, u32[]{:S(2)}, u32[]{:S(2)}) collective-permute-start(bf16[2,128,128]{2,1,0:T(8,128)(2,1)S(1)} %get-tuple-element.42), channel_id=1, source_target_pairs={{0,24},{2,26},{4,28},{6,30},{8,16},{10,18},{12,20},{14,22},{16,8},... | collective-permute-start | bytes 196616 | tf_op jit(solution)/shard_map/ppermute | solution.py:116
  46.4 4.3 %collective-permute-start.13 = (bf16[2,128,128]{2,1,0:T(8,128)(2,1)S(1)}, bf16[2,128,128]{2,1,0:T(8,128)(2,1)S(1)}, u32[]{:S(2)}, u32[]{:S(2)}) collective-permute-start(bf16[2,128,128]{2,1,0:T(8,128)(2,1)S(1)} %get-tuple-element.42), channel_id=1, source_target_pairs={{0,8},{2,10},{4,12},{6,14},{8,0},{10,2},{12,4},{14,6},{16,24},{18,... | collective-permute-start | bytes 196616 | tf_op jit(solution)/shard_map/ppermute | solution.py:116
  46.4 5.2 %collective-permute-start.12 = (bf16[2,128,128]{2,1,0:T(8,128)(2,1)S(1)}, bf16[2,128,128]{2,1,0:T(8,128)(2,1)S(1)}, u32[]{:S(2)}, u32[]{:S(2)}) collective-permute-start(bf16[2,128,128]{2,1,0:T(8,128)(2,1)S(1)} %get-tuple-element.42), channel_id=1, source_target_pairs={{0,16},{2,18},{4,20},{6,22},{8,24},{10,26},{12,28},{14,30},{16,0},... | collective-permute-start | bytes 196616 | tf_op jit(solution)/shard_map/ppermute | solution.py:116
  51.6 5.9 %collective-permute-start.15 = (bf16[4,128,128]{2,1,0:T(8,128)(2,1)S(1)}, bf16[4,128,128]{2,1,0:T(8,128)(2,1)S(1)}, u32[]{:S(2)}, u32[]{:S(2)}) collective-permute-start(bf16[4,128,128]{2,1,0:T(8,128)(2,1)S(1)} %get-tuple-element.45), channel_id=1, source_target_pairs={{0,4},{2,6},{4,0},{6,2},{8,12},{10,14},{12,8},{14,10},{16,20},{18,... | collective-permute-start | bytes 393224 | tf_op jit(solution)/shard_map/ppermute | solution.py:116
  52.7 5.0 %collective-permute-start.16 = (bf16[4,128,128]{2,1,0:T(8,128)(2,1)S(1)}, bf16[4,128,128]{2,1,0:T(8,128)(2,1)S(1)}, u32[]{:S(2)}, u32[]{:S(2)}) collective-permute-start(bf16[4,128,128]{2,1,0:T(8,128)(2,1)S(1)} %get-tuple-element.46), channel_id=1, source_target_pairs={{0,2},{2,0},{4,6},{6,4},{8,10},{10,8},{12,14},{14,12},{16,18},{18,... | collective-permute-start | bytes 393224 | tf_op jit(solution)/shard_map/ppermute | solution.py:116
  57.7 6.4 %collective-permute-start.18 = (bf16[8,128,128]{2,1,0:T(8,128)(2,1)S(1)}, bf16[8,128,128]{2,1,0:T(8,128)(2,1)S(1)}, u32[]{:S(2)}, u32[]{:S(2)}) collective-permute-start(bf16[8,128,128]{2,1,0:T(8,128)(2,1)S(1)} %pad_maximum_fusion.refs_0_), channel_id=1, source_target_pairs={{0,2},{2,0},{4,6},{6,4},{8,10},{10,8},{12,14},{14,12},{16,18},{18,... | collective-permute-start | bytes 786440 | tf_op jit(solution)/shard_map/ppermute | solution.py:116
  58.7 6.4 %collective-permute-start.19 = (bf16[8,128,128]{2,1,0:T(8,128)(2,1)S(1)}, bf16[8,128,128]{2,1,0:T(8,128)(2,1)S(1)}, u32[]{:S(2)}, u32[]{:S(2)}) collective-permute-start(bf16[8,128,128]{2,1,0:T(8,128)(2,1)S(1)} %pad_maximum_fusion.1.refs_1_), channel_id=1, source_target_pairs={{0,4},{2,6},{4,0},{6,2},{8,12},{10,14},{12,8},{14,10},{16,20},{18,... | collective-permute-start | bytes 786440 | tf_op jit(solution)/shard_map/ppermute | solution.py:116
  60.2 1.3 %collective-permute-start.17 = (bf16[4,128,128]{2,1,0:T(8,128)(2,1)S(1)}, bf16[4,128,128]{2,1,0:T(8,128)(2,1)S(1)}, u32[]{:S(2)}, u32[]{:S(2)}) collective-permute-start(bf16[4,128,128]{2,1,0:T(8,128)(2,1)S(1)} %finish.1.own_ref), channel_id=1, source_target_pairs={{0,1},{1,0},{2,3},{3,2},{4,5},{5,4},{6,7},{7,6},{8,9},{9,8},{10,11... | collective-permute-start | bytes 393224 | tf_op jit(solution)/shard_map/ppermute | solution.py:116
  60.2 5.3 %collective-permute-start.22 = (bf16[8,128,128]{2,1,0:T(8,128)(2,1)S(1)}, bf16[8,128,128]{2,1,0:T(8,128)(2,1)S(1)}, u32[]{:S(2)}, u32[]{:S(2)}) collective-permute-start(bf16[8,128,128]{2,1,0:T(8,128)(2,1)S(1)} %pad_maximum_fusion.refs_0_), channel_id=1, source_target_pairs={{0,1},{1,0},{2,3},{3,2},{4,5},{5,4},{6,7},{7,6},{8,9},{9,8},{10,11... | collective-permute-start | bytes 786440 | tf_op jit(solution)/shard_map/ppermute | solution.py:116
  60.7 4.8 %collective-permute-start.23 = (bf16[8,128,128]{2,1,0:T(8,128)(2,1)S(1)}, bf16[8,128,128]{2,1,0:T(8,128)(2,1)S(1)}, u32[]{:S(2)}, u32[]{:S(2)}) collective-permute-start(bf16[8,128,128]{2,1,0:T(8,128)(2,1)S(1)} %pad_maximum_fusion.1.refs_1_), channel_id=1, source_target_pairs={{0,1},{1,0},{2,3},{3,2},{4,5},{5,4},{6,7},{7,6},{8,9},{9,8},{10,11... | collective-permute-start | bytes 786440 | tf_op jit(solution)/shard_map/ppermute | solution.py:116
  65.0 2.3 %collective-permute-start.20 = (bf16[8,128,128]{2,1,0:T(8,128)(2,1)S(1)}, bf16[8,128,128]{2,1,0:T(8,128)(2,1)S(1)}, u32[]{:S(2)}, u32[]{:S(2)}) collective-permute-start(bf16[8,128,128]{2,1,0:T(8,128)(2,1)S(1)} %collective-permute-done.18.refs_2_), channel_id=1, source_target_pairs={{0,1},{1,0},{2,3},{3,2},{4,5},{5,4},{6,7},{7,6},{8,9},{9,8},{10,11... | collective-permute-start | bytes 786440 | tf_op jit(solution)/shard_map/ppermute | solution.py:116
  65.0 2.3 %collective-permute-start.21 = (bf16[8,128,128]{2,1,0:T(8,128)(2,1)S(1)}, bf16[8,128,128]{2,1,0:T(8,128)(2,1)S(1)}, u32[]{:S(2)}, u32[]{:S(2)}) collective-permute-start(bf16[8,128,128]{2,1,0:T(8,128)(2,1)S(1)} %collective-permute-done.19.refs_3_), channel_id=1, source_target_pairs={{0,1},{1,0},{2,3},{3,2},{4,5},{5,4},{6,7},{7,6},{8,9},{9,8},{10,11... | collective-permute-start | bytes 786440 | tf_op jit(solution)/shard_map/ppermute | solution.py:116

commit v10 on v9

--- a/solution.py
+++ b/solution.py
@@ -196,40 +196,46 @@
                 table_ref[entry] = held[(here ^ offsets[stream][p]) * capacity + first_slot + stream]
 
 
-EDGE = 24
-
-
-def tiles_kernel(owners, first, table_ref, f_own, f_sib, own_rows, kv_sib, *rest):
-    sib_rows = rest[-1]
-    out_a, out_b = rest[-5:-3] if first == 0 else rest[:2]
-    tile = out_a.shape[-1]
-    body = tile - EDGE
+EDGE = 32
+
+
+def tile_of(block, f_own, f_sib, own_rows, sib_rows, tile):
+    col_tiles = own_rows.shape[0] // tile
+    at = pl.ds(pl.multiple_of(block // col_tiles * tile, tile), tile)
+    cots = pl.ds(pl.multiple_of(block % col_tiles * tile, tile), tile)
+    return dot(own_rows[cots, :], f_own[:, at], MM) + dot(sib_rows[cots, :], f_sib[:, at], MM)
+
+
+def sent_kernel(owners, stream, table_ref, f_own, f_sib, own_rows, cots_sib, out, edge, *flipped):
+    sib_rows = cots_sib
+    if flipped:
+        sib_rows = flipped[0]
+        sib_rows[...] = cots_sib[...].T
     near = owners // 2
-    col_tiles = own_rows.shape[0] // tile
+    body, tile = out.shape[1:]
+    for i in range(near):
+        block = table_ref[stream * owners + near + i]
+        total = tile_of(block, f_own, f_sib, own_rows, sib_rows, tile)
+        out[i] = total[:body]
+        edge[i] = total[body:]
+
+
+def kept_kernel(owners, table_ref, f_own, f_sib, own_rows, sib_rows, *rest):
+    early, outs, edges = rest[:2], rest[2:4], rest[4:]
+    near = owners // 2
+    body, tile = outs[0].shape[1:]
     offsets = stream_offsets(owners)[1]
-    sib_rows[...] = kv_sib[...].T
-    for stream, out in enumerate((out_a, out_b)):
-        for i in range(near):
-            block = table_ref[stream * owners + first + i]
-            at = pl.ds(pl.multiple_of(block // col_tiles * tile, tile), tile)
-            cots = pl.ds(pl.multiple_of(block % col_tiles * tile, tile), tile)
-            total = dot(own_rows[cots, :], f_own[:, at], MM) + dot(
-                sib_rows[cots, :], f_sib[:, at], MM
-            )
-            out[i] = total[:body]
-            place = 2 * offsets[2].index(offsets[stream][first + i]) + stream
-            if first:
-                rest[2][place] = total[body:]
-            elif place < owners:
-                rest[-3][place] = total[body:]
+    for stream, out in enumerate(outs):
+        for p in range(owners):
+            place = 2 * offsets[2].index(offsets[stream][p]) + stream
+            target, at = edges[place // owners], place % owners
+            if p < near:
+                block = table_ref[stream * owners + p]
+                total = tile_of(block, f_own, f_sib, own_rows, sib_rows, tile)
+                out[p] = total[:body]
+                target[at] = total[body:]
             else:
-                rest[-2][place - owners] = total[body:]
-            if first == 0:
-                place = 2 * offsets[2].index(offsets[stream][near + i]) + stream
-                if place < owners:
-                    rest[-3][place] = rest[0][place]
-                else:
-                    rest[-2][place - owners] = rest[0][place]
+                target[at] = early[stream][p - near]
 
 
 SMEM = pl.BlockSpec(memory_space=pltpu.SMEM)
@@ -430,10 +436,9 @@
 
     f_sib = swap_along(features, "inner", 2, 1)
     kv_sib = swap_along(kv_cotangent, "inner", 2, 1)
-    flipped = pltpu.VMEM((width, rows), jnp.bfloat16)
     part = jax.ShapeDtypeStruct((near, tile - EDGE, tile), jnp.float32)
     edge = jax.ShapeDtypeStruct((owners, EDGE, tile), jnp.float32)
-    edges = jax.ShapeDtypeStruct((2 * owners, EDGE, tile), jnp.float32)
+    early = jax.ShapeDtypeStruct((near, EDGE, tile), jnp.float32)
     f32_pair = jax.ShapeDtypeStruct((2, tile, tile), jnp.float32)
     table, own_rows = pl.pallas_call(
         functools.partial(table_kernel, owners, capacity),
@@ -452,28 +457,42 @@
         name="table",
     )(place, owner_of_block, kv_cotangent)
 
-    def tiles_from(first, outs, *more):
-        inputs = (features, f_sib, own_rows, kv_sib, *more)
+    def tiles(kernel, outs, inputs, share):
         return pl.pallas_call(
-            functools.partial(tiles_kernel, owners, first),
+            kernel,
             out_shape=outs,
             grid=(1,),
             in_specs=[SMEM] + wholes(inputs),
             out_specs=tuple(wholes(outs)),
-            scratch_shapes=[flipped],
             compiler_params=BIG,
             cost_estimate=pl.CostEstimate(
-                flops=2 * owners * 2 * tile * tile * 2 * rows,
-                bytes_accessed=3_500_000,
+                flops=share * owners * 2 * tile * tile * 2 * rows,
+                bytes_accessed=share * 1_700_000,
                 transcendentals=0,
             ),
             name="tiles",
         )(table, *inputs)
 
-    sent_a, sent_b, early = tiles_from(near, (part, part, edges))
+    sent_a, early_a, sib_rows = tiles(
+        functools.partial(sent_kernel, owners, 0),
+        (part, early, jax.ShapeDtypeStruct((width, rows), jnp.bfloat16)),
+        (features, f_sib, own_rows, kv_sib),
+        1,
+    )
     got_a = swap_along(sent_a, "dp", owners, 1 << orders[0][0])
+    sent_b, early_b = tiles(
+        functools.partial(sent_kernel, owners, 1),
+        (part, early),
+        (features, f_sib, own_rows, sib_rows),
+        1,
+    )
     got_b = swap_along(sent_b, "dp", owners, 1 << orders[1][0])
-    kept_a, kept_b, kept_c, sent_c = tiles_from(0, (part, part, edge, edge), early)
+    kept_a, kept_b, kept_c, sent_c = tiles(
+        functools.partial(kept_kernel, owners),
+        (part, part, edge, edge),
+        (features, f_sib, own_rows, sib_rows, early_a, early_b),
+        2,
+    )
     got_c = swap_along(sent_c, "dp", owners, 1 << orders[2][0])
     quad = jax.ShapeDtypeStruct((4, tile, tile), jnp.float32)
     moment_rot, second, power = on_slots(

time: 69 us -> 68.7 us (level)
  starting transfers between devices: 30.3 us -> 28 us
  waiting for transfers between devices: 18.2 us -> 19.5 us
  Pallas kernels: 16.2 us -> 17 us
    ppermute x24, starting transfers between devices: 30.3 us -> 28 us  [swap_along(): return lax.ppermute(values, axis, [(i, i ^ bit) for i in range(size)])]
    ppermute x24, waiting for transfers between devices: 18.2 us -> 19.5 us  [swap_along(): return lax.ppermute(values, axis, [(i, i ^ bit) for i in range(size)])]
    pallas_call x2 -> x3, Pallas kernels: 2.82 us -> 3.57 us  [tiles(): pl.pallas_call(kernel, out_shape=outs, grid=(1,), in_specs=[SMEM] + whole...]
  transfers between devices with their start and end apart: 24 -> 24, of which waited for: 13 -> 14; matrix products, arithmetic and copies ran while one was open for 0% -> 0% of each run, Pallas kernels for 18% -> 20%
where the time goes in v10:
time: 68.7 us; the launch traced here: 68.6 us
  starting transfers between devices  28 us (41%)
  waiting for transfers between devices  19.5 us (28%)
  Pallas kernels  17 us (25%)
  local copies, waits for them, and re-layouts  2.88 us (4%)
  between operations  0.86 us (1%)
    ppermute x24, starting transfers between devices, swap_along(): return lax.ppermute(values, axis, [(i, i ^ bit) for i in range(size)])  28 us
    ppermute x24, waiting for transfers between devices, swap_along(): return lax.ppermute(values, axis, [(i, i ^ bit) for i in range(size)])  19.5 us
    pallas_call x3, Pallas kernels, on_slots(): pl.pallas_call(kernel, out_shape=tuple(outs), grid_spec=pltpu.PrefetchSca...  3.98 us
    pallas_call x3, Pallas kernels, tiles(): pl.pallas_call(kernel, out_shape=outs, grid=(1,), in_specs=[SMEM] + whole...  3.57 us
    pallas_call x2, Pallas kernels, place_more(): pl.pallas_call(functools.partial(more_kernel, col_tiles, entries), out_sh...  3.25 us
    pallas_call x1, Pallas kernels, sweeping(): pl.pallas_call(kernel, out_shape=jax.ShapeDtypeStruct(values.shape, dtype...  2.89 us
    unnamed x18, local copies, waits for them, and re-layouts  2.85 us
    pallas_call x1, Pallas kernels, per_device_dealt(): pl.pallas_call(functools.partial(table_kernel, owners, capacity), out_sha...  1.65 us
  transfers between devices with their start and end apart: 24, of which 14 were waited for; matrix products, arithmetic and copies ran while one was open for 0% of the time, Pallas kernels for 20%

profile of v10, /device:TPU:0, one launch (start us, length us, event | category | flops | bytes accessed | tf_op | source)
XLA Modules:
  0.0 68.6 jit_solution(2903986258241526882)
XLA Ops:
  0.6 0.5 collective-permute-start
  1.1 0.1 collective-permute-start.1
  1.3 0.9 %copy-done.7 = bf16[256,512]{1,0:T(8,128)(2,1)S(1)} copy-done((bf16[256,512]{1,0:T(8,128)(2,1)S(1)}, bf16[256,512]{1,0:T(8,128)(2,1)}, u32[]{:S(2)}) %copy-start.7) | copy-done | bytes 262168
  2.3 0.7 copy-done.8
  2.9 1.7 %table.1 = (s32[64]{0:T(128)S(1)}, bf16[512,256]{1,0:T(8,128)(2,1)S(1)}) custom-call(s32[2]{0:T(128)S(1)} %pad_add_fusion.place_ref, s32[64]{0:T(128)S(1)} %copy-done.8, bf16[256,512]{1,0:T(8,128)(2,1)S(1)} %copy-done.7), custom_call_target="tpu_custom_call" | custom-call | bytes 1000000 | tf_op jit(solution)/shard_map/table/pallas_call | solution.py:443
  4.6 1.2 %copy-done = bf16[256,2048]{1,0:T(8,128)(2,1)S(1)} copy-done((bf16[256,2048]{1,0:T(8,128)(2,1)S(1)}, bf16[256,2048]{1,0:T(8,128)(2,1)}, u32[]{:S(2)}) %copy-start) | copy-done | bytes 1048600
  5.8 1.1 %tiles.3 = (f32[8,96,128]{2,1,0:T(8,128)S(1)}, f32[8,32,128]{2,1,0:T(8,128)S(1)}, bf16[512,256]{1,0:T(8,128)(2,1)S(1)}) custom-call(s32[64]{0:T(128)S(1)} %get-tuple-element.32.table_ref, bf16[256,2048]{1,0:T(8,128)(2,1)S(1)} %copy-done, bf16[256,2048]{1,0:T(8,128)(2,1)S(1)} %collective-permute-done.f_sib, bf16[512,256]{1,0:T(8,128)(2,1)S(1)} %get-tuple-element.33.own_rows, ...), custom_call_target="tpu_custom_call" | custom-call | flops 268435456 | bytes 1700000 | tf_op jit(solution)/shard_map/tiles/pallas_call | solution.py:461
  6.9 3.0 %collective-permute-start.2 = (f32[8,96,128]{2,1,0:T(8,128)S(1)}, f32[8,96,128]{2,1,0:T(8,128)S(1)}, u32[]{:S(2)}, u32[]{:S(2)}) collective-permute-start(f32[8,96,128]{2,1,0:T(8,128)S(1)} %get-tuple-element.38), channel_id=1, source_target_pairs={{0,2},{2,0},{4,6},{6,4},{8,10},{10,8},{12,14},{14,12},{16,18},{18,... | collective-permute-start | bytes 1179656 | tf_op jit(solution)/shard_map/ppermute | solution.py:116
  9.9 1.1 %tiles.4 = (f32[8,96,128]{2,1,0:T(8,128)S(1)}, f32[8,32,128]{2,1,0:T(8,128)S(1)}) custom-call(s32[64]{0:T(128)S(1)} %get-tuple-element.32.table_ref, bf16[256,2048]{1,0:T(8,128)(2,1)S(1)} %copy-done, bf16[256,2048]{1,0:T(8,128)(2,1)S(1)} %collective-permute-done.f_sib, bf16[512,256]{1,0:T(8,128)(2,1)S(1)} %get-tuple-element.33.own_rows, ...), custom_call_target="tpu_custom_call" | custom-call | flops 268435456 | bytes 1700000 | tf_op jit(solution)/shard_map/tiles/pallas_call | solution.py:461
  11.0 1.6 %collective-permute-start.3 = (f32[8,96,128]{2,1,0:T(8,128)S(1)}, f32[8,96,128]{2,1,0:T(8,128)S(1)}, u32[]{:S(2)}, u32[]{:S(2)}) collective-permute-start(f32[8,96,128]{2,1,0:T(8,128)S(1)} %get-tuple-element.40), channel_id=1, source_target_pairs={{0,4},{2,6},{4,0},{6,2},{8,12},{10,14},{12,8},{14,10},{16,20},{18,... | collective-permute-start | bytes 1179656 | tf_op jit(solution)/shard_map/ppermute | solution.py:116
  12.6 1.4 %tiles.5 = (f32[8,96,128]{2,1,0:T(8,128)S(1)}, f32[8,96,128]{2,1,0:T(8,128)S(1)}, f32[16,32,128]{2,1,0:T(8,128)S(1)}, f32[16,32,128]{2,1,0:T(8,128)S(1)}) custom-call(s32[64]{0:T(128)S(1)} %get-tuple-element.32.table_ref, bf16[256,2048]{1,0:T(8,128)(2,1)S(1)} %copy-done, bf16[256,2048]{1,0:T(8,128)(2,1)S(1)} %collective-permute-done.f_sib, ...), custom_call_target="tpu_custom_call" | custom-call | flops 536870912 | bytes 3400000 | tf_op jit(solution)/shard_map/tiles/pallas_call | solution.py:461
  14.0 1.6 %collective-permute-start.7 = (f32[16,32,128]{2,1,0:T(8,128)S(1)}, f32[16,32,128]{2,1,0:T(8,128)S(1)}, u32[]{:S(2)}, u32[]{:S(2)}) collective-permute-start(f32[16,32,128]{2,1,0:T(8,128)S(1)} %get-tuple-element.42), channel_id=1, source_target_pairs={{0,8},{2,10},{4,12},{6,14},{8,0},{10,2},{12,4},{14,6},{16,24},{18,... | collective-permute-start | bytes 786440 | tf_op jit(solution)/shard_map/ppermute | solution.py:116
  15.6 3.6 %collective-permute-done.2 = f32[8,96,128]{2,1,0:T(8,128)S(1)} collective-permute-done((f32[8,96,128]{2,1,0:T(8,128)S(1)}, f32[8,96,128]{2,1,0:T(8,128)S(1)}, u32[]{:S(2)}, u32[]{:S(2)}) %collective-permute-start.2) | collective-permute-done | bytes 393248 | tf_op jit(solution)/shard_map/ppermute | solution.py:116
  19.3 1.8 %collective-permute-start.4 = (f32[4,96,128]{2,1,0:T(8,128)S(1)}, f32[4,96,128]{2,1,0:T(8,128)S(1)}, u32[]{:S(2)}, u32[]{:S(2)}) collective-permute-start(f32[4,96,128]{2,1,0:T(8,128)S(1)} %get-tuple-element.64), channel_id=1, source_target_pairs={{0,4},{2,6},{4,0},{6,2},{8,12},{10,14},{12,8},{14,10},{16,20},{18,... | collective-permute-start | bytes 589832 | tf_op jit(solution)/shard_map/ppermute | solution.py:116
  21.1 1.0 %collective-permute-done.3 = f32[8,96,128]{2,1,0:T(8,128)S(1)} collective-permute-done((f32[8,96,128]{2,1,0:T(8,128)S(1)}, f32[8,96,128]{2,1,0:T(8,128)S(1)}, u32[]{:S(2)}, u32[]{:S(2)}) %collective-permute-start.3) | collective-permute-done | bytes 393248 | tf_op jit(solution)/shard_map/ppermute | solution.py:116
  22.2 0.6 collective-permute-start.5
  22.8 2.7 %collective-permute-start.8 = (f32[8,32,128]{2,1,0:T(8,128)S(1)}, f32[8,32,128]{2,1,0:T(8,128)S(1)}, u32[]{:S(2)}, u32[]{:S(2)}) collective-permute-start(f32[8,32,128]{2,1,0:T(8,128)S(1)} %get-tuple-element.68), channel_id=1, source_target_pairs={{0,16},{2,18},{4,20},{6,22},{8,24},{10,26},{12,28},{14,30},{16,0},... | collective-permute-start | bytes 393224 | tf_op jit(solution)/shard_map/ppermute | solution.py:116
  25.5 0.6 collective-permute-done.4
  26.1 1.9 %collective-permute-done.5 = f32[4,96,128]{2,1,0:T(8,128)S(1)} collective-permute-done((f32[4,96,128]{2,1,0:T(8,128)S(1)}, f32[4,96,128]{2,1,0:T(8,128)S(1)}, u32[]{:S(2)}, u32[]{:S(2)}) %collective-permute-start.5) | collective-permute-done | bytes 196640 | tf_op jit(solution)/shard_map/ppermute | solution.py:116
  28.0 1.7 %collective-permute-start.6 = (f32[2,2,96,128]{3,2,1,0:T(8,128)S(1)}, f32[2,2,96,128]{3,2,1,0:T(8,128)S(1)}, u32[]{:S(2)}, u32[]{:S(2)}) collective-permute-start(f32[2,2,96,128]{3,2,1,0:T(8,128)S(1)} %get-tuple-element.62), channel_id=1, source_target_pairs={{0,8},{2,10},{4,12},{6,14},{8,0},{10,2},{12,4},{14,6},{16,24},{18,... | collective-permute-start | bytes 589832 | tf_op jit(solution)/shard_map/ppermute | solution.py:116
  29.7 1.1 %collective-permute-done.8 = f32[8,32,128]{2,1,0:T(8,128)S(1)} collective-permute-done((f32[8,32,128]{2,1,0:T(8,128)S(1)}, f32[8,32,128]{2,1,0:T(8,128)S(1)}, u32[]{:S(2)}, u32[]{:S(2)}) %collective-permute-start.8) | collective-permute-done | bytes 131104 | tf_op jit(solution)/shard_map/ppermute | solution.py:116
  30.8 1.3 %collective-permute-start.10 = (f32[4,32,128]{2,1,0:T(8,128)S(1)}, f32[4,32,128]{2,1,0:T(8,128)S(1)}, u32[]{:S(2)}, u32[]{:S(2)}) collective-permute-start(f32[4,32,128]{2,1,0:T(8,128)S(1)} %get-tuple-element.72), channel_id=1, source_target_pairs={{0,2},{2,0},{4,6},{6,4},{8,10},{10,8},{12,14},{14,12},{16,18},{18,... | collective-permute-start | bytes 196616 | tf_op jit(solution)/shard_map/ppermute | solution.py:116
  32.1 1.6 %collective-permute-done.6 = f32[2,2,96,128]{3,2,1,0:T(8,128)S(1)} collective-permute-done((f32[2,2,96,128]{3,2,1,0:T(8,128)S(1)}, f32[2,2,96,128]{3,2,1,0:T(8,128)S(1)}, u32[]{:S(2)}, u32[]{:S(2)}) %collective-permute-start.6) | collective-permute-done | bytes 196640 | tf_op jit(solution)/shard_map/ppermute | solution.py:116
  33.8 2.7 %collective-permute-start.9 = (f32[2,96,128]{2,1,0:T(8,128)S(1)}, f32[2,96,128]{2,1,0:T(8,128)S(1)}, u32[]{:S(2)}, u32[]{:S(2)}) collective-permute-start(f32[2,96,128]{2,1,0:T(8,128)S(1)} %bitcast.17), channel_id=1, source_target_pairs={{0,16},{2,18},{4,20},{6,22},{8,24},{10,26},{12,28},{14,30},{16,0},... | collective-permute-start | bytes 294920 | tf_op jit(solution)/shard_map/ppermute | solution.py:116
  36.5 1.6 %collective-permute-start.11 = (f32[2,32,128]{2,1,0:T(8,128)S(1)}, f32[2,32,128]{2,1,0:T(8,128)S(1)}, u32[]{:S(2)}, u32[]{:S(2)}) collective-permute-start(f32[2,32,128]{2,1,0:T(8,128)S(1)} %get-tuple-element.73), channel_id=1, source_target_pairs={{0,4},{2,6},{4,0},{6,2},{8,12},{10,14},{12,8},{14,10},{16,20},{18,... | collective-permute-start | bytes 98312 | tf_op jit(solution)/shard_map/ppermute | solution.py:116
  38.1 0.5 rotated.1
  38.6 1.9 %collective-permute-done.11.d_ref = f32[2,32,128]{2,1,0:T(8,128)S(1)} collective-permute-done((f32[2,32,128]{2,1,0:T(8,128)S(1)}, f32[2,32,128]{2,1,0:T(8,128)S(1)}, u32[]{:S(2)}, u32[]{:S(2)}) %collective-permute-start.11) | collective-permute-done | bytes 32800 | tf_op jit(solution)/shard_map/ppermute | solution.py:116
  40.5 0.7 %direction.1 = (bf16[2,128,128]{2,1,0:T(8,128)(2,1)S(1)}, f32[2,128,128]{2,1,0:T(8,128)S(1)}) custom-call(s32[1]{0:T(128)} %bitcast.1.side_ref, f32[2,96,128]{2,1,0:T(8,128)S(1)} %get-tuple-element.70.a_ref, f32[2,96,128]{2,1,0:T(8,128)S(1)} %collective-permute-done.9.b_ref, f32[2,32,128]{2,1,0:T(8,128)S(1)} %get-tuple-element.74.c_ref, ...), custom_call_target="tpu_custom_call" | custom-call | flops 67108864 | bytes 800000 | tf_op jit(solution)/shard_map/direction/pallas_call | solution.py:297
  41.2 3.6 %collective-permute-start.14 = (bf16[2,128,128]{2,1,0:T(8,128)(2,1)S(1)}, bf16[2,128,128]{2,1,0:T(8,128)(2,1)S(1)}, u32[]{:S(2)}, u32[]{:S(2)}) collective-permute-start(bf16[2,128,128]{2,1,0:T(8,128)(2,1)S(1)} %get-tuple-element.46), channel_id=1, source_target_pairs={{0,24},{2,26},{4,28},{6,30},{8,16},{10,18},{12,20},{14,22},{16,8},... | collective-permute-start | bytes 196616 | tf_op jit(solution)/shard_map/ppermute | solution.py:116
  44.8 0.9 %collective-permute-start.12 = (bf16[2,128,128]{2,1,0:T(8,128)(2,1)S(1)}, bf16[2,128,128]{2,1,0:T(8,128)(2,1)S(1)}, u32[]{:S(2)}, u32[]{:S(2)}) collective-permute-start(bf16[2,128,128]{2,1,0:T(8,128)(2,1)S(1)} %get-tuple-element.46), channel_id=1, source_target_pairs={{0,16},{2,18},{4,20},{6,22},{8,24},{10,26},{12,28},{14,30},{16,0},... | collective-permute-start | bytes 196616 | tf_op jit(solution)/shard_map/ppermute | solution.py:116
  45.7 2.8 %refresh.1.iter_ref = f32[4,128,128]{2,1,0:T(8,128)S(1)} custom-call(s32[1]{0:T(128)} %bitcast.1.side_ref, f32[2,128,128]{2,1,0:T(8,128)S(1)} %get-tuple-element.47.g_ref, f32[4,128,128]{2,1,0:T(8,128)S(1)} %get-tuple-element.48.power_ref, bf16[1,4,128,128]{3,2,1,0:T(8,128)(2,1)S(1)} %copy-done.1, bf16[1,4,128,128]{3,2,1,0:T(8,128)(2,1)S(1)} %copy-done.2), custom_call_target="tpu_custom_call" | custom-call | flops 939524096 | bytes 800000 | tf_op jit(solution)/shard_map/refresh/pallas_call | solution.py:297
  48.5 0.6 collective-permute-done.13
  49.1 0.9 %collective-permute-done.12 = bf16[2,128,128]{2,1,0:T(8,128)(2,1)S(1)} collective-permute-done((bf16[2,128,128]{2,1,0:T(8,128)(2,1)S(1)}, bf16[2,128,128]{2,1,0:T(8,128)(2,1)S(1)}, u32[]{:S(2)}, u32[]{:S(2)}) %collective-permute-start.12) | collective-permute-done | bytes 65568 | tf_op jit(solution)/shard_map/ppermute | solution.py:116
  50.0 1.7 %collective-permute-start.15 = (bf16[4,128,128]{2,1,0:T(8,128)(2,1)S(1)}, bf16[4,128,128]{2,1,0:T(8,128)(2,1)S(1)}, u32[]{:S(2)}, u32[]{:S(2)}) collective-permute-start(bf16[4,128,128]{2,1,0:T(8,128)(2,1)S(1)} %get-tuple-element.49), channel_id=1, source_target_pairs={{0,4},{2,6},{4,0},{6,2},{8,12},{10,14},{12,8},{14,10},{16,20},{18,... | collective-permute-start | bytes 393224 | tf_op jit(solution)/shard_map/ppermute | solution.py:116
  51.7 0.2 collective-permute-start.16
  51.9 2.9 %finish.1.own_ref = bf16[4,128,128]{2,1,0:T(8,128)(2,1)S(1)} custom-call(f32[4,128,128]{2,1,0:T(8,128)S(1)} %refresh.1.iter_ref), custom_call_target="tpu_custom_call" | custom-call | flops 939524096 | bytes 400000 | tf_op jit(solution)/shard_map/finish/pallas_call | solution.py:347
  54.8 1.3 %collective-permute-done.15 = bf16[4,128,128]{2,1,0:T(8,128)(2,1)S(1)} collective-permute-done((bf16[4,128,128]{2,1,0:T(8,128)(2,1)S(1)}, bf16[4,128,128]{2,1,0:T(8,128)(2,1)S(1)}, u32[]{:S(2)}, u32[]{:S(2)}) %collective-permute-start.15) | collective-permute-done | bytes 131104 | tf_op jit(solution)/shard_map/ppermute | solution.py:116
  56.2 1.5 %collective-permute-done.16 = bf16[4,128,128]{2,1,0:T(8,128)(2,1)S(1)} collective-permute-done((bf16[4,128,128]{2,1,0:T(8,128)(2,1)S(1)}, bf16[4,128,128]{2,1,0:T(8,128)(2,1)S(1)}, u32[]{:S(2)}, u32[]{:S(2)}) %collective-permute-start.16) | collective-permute-done | bytes 131104 | tf_op jit(solution)/shard_map/ppermute | solution.py:116
  57.7 0.7 %collective-permute-start.18 = (bf16[8,128,128]{2,1,0:T(8,128)(2,1)S(1)}, bf16[8,128,128]{2,1,0:T(8,128)(2,1)S(1)}, u32[]{:S(2)}, u32[]{:S(2)}) collective-permute-start(bf16[8,128,128]{2,1,0:T(8,128)(2,1)S(1)} %pad_maximum_fusion.refs_0_), channel_id=1, source_target_pairs={{0,2},{2,0},{4,6},{6,4},{8,10},{10,8},{12,14},{14,12},{16,18},{18,... | collective-permute-start | bytes 786440 | tf_op jit(solution)/shard_map/ppermute | solution.py:116
  58.4 0.7 %collective-permute-start.19 = (bf16[8,128,128]{2,1,0:T(8,128)(2,1)S(1)}, bf16[8,128,128]{2,1,0:T(8,128)(2,1)S(1)}, u32[]{:S(2)}, u32[]{:S(2)}) collective-permute-start(bf16[8,128,128]{2,1,0:T(8,128)(2,1)S(1)} %pad_maximum_fusion.1.refs_1_), channel_id=1, source_target_pairs={{0,4},{2,6},{4,0},{6,2},{8,12},{10,14},{12,8},{14,10},{16,20},{18,... | collective-permute-start | bytes 786440 | tf_op jit(solution)/shard_map/ppermute | solution.py:116
  59.1 0.5 collective-permute-start.22
  59.6 0.8 %collective-permute-done.17.sib_ref = bf16[4,128,128]{2,1,0:T(8,128)(2,1)S(1)} collective-permute-done((bf16[4,128,128]{2,1,0:T(8,128)(2,1)S(1)}, bf16[4,128,128]{2,1,0:T(8,128)(2,1)S(1)}, u32[]{:S(2)}, u32[]{:S(2)}) %collective-permute-start.17) | collective-permute-done | bytes 131104 | tf_op jit(solution)/shard_map/ppermute | solution.py:116
  60.5 1.6 %begin.1 = (bf16[2048,512]{1,0:T(8,128)(2,1)}, bf16[1,4,128,128]{3,2,1,0:T(8,128)(2,1)}, bf16[1,4,128,128]{3,2,1,0:T(8,128)(2,1)}) custom-call(s32[64]{0:T(128)S(1)} %get-tuple-element.32.table_ref, s32[2]{0:T(128)S(1)} %pad_add_fusion.place_ref, bf16[4,128,128]{2,1,0:T(8,128)(2,1)S(1)} %finish.1.own_ref, ...), custom_call_target="tpu_custom_call" | custom-call | bytes 800000 | tf_op jit(solution)/shard_map/begin/pallas_call | solution.py:565
  62.1 2.0 %collective-permute-done.18.refs_2_ = bf16[8,128,128]{2,1,0:T(8,128)(2,1)S(1)} collective-permute-done((bf16[8,128,128]{2,1,0:T(8,128)(2,1)S(1)}, bf16[8,128,128]{2,1,0:T(8,128)(2,1)S(1)}, u32[]{:S(2)}, u32[]{:S(2)}) %collective-permute-start.18) | collective-permute-done | bytes 262176 | tf_op jit(solution)/shard_map/ppermute | solution.py:116
  64.1 0.7 collective-permute-done.19.refs_3_
  64.8 0.5 collective-permute-start.21
  65.3 1.8 %more.2.refs_2_ = bf16[2048,512]{1,0:T(8,128)(2,1)} custom-call(s32[64]{0:T(128)S(1)} %get-tuple-element.32.table_ref, bf16[8,128,128]{2,1,0:T(8,128)(2,1)S(1)} %collective-permute-done.22.refs_0_, bf16[8,128,128]{2,1,0:T(8,128)(2,1)S(1)} %collective-permute-done.23.refs_1_, ...), custom_call_target="tpu_custom_call", output_to_operand_aliasing={{}: (5, {})} | custom-call | bytes 1000000 | tf_op jit(solution)/shard_map/more/pallas_call | solution.py:399
  67.1 1.5 %more.3 = bf16[2048,512]{1,0:T(8,128)(2,1)} custom-call(s32[64]{0:T(128)S(1)} %get-tuple-element.32.table_ref, bf16[8,128,128]{2,1,0:T(8,128)(2,1)S(1)} %collective-permute-done.20.refs_0_, bf16[8,128,128]{2,1,0:T(8,128)(2,1)S(1)} %collective-permute-done.21.refs_1_, bf16[2048,512]{1,0:T(8,128)(2,1)} %more.2.refs_2_), custom_call_target="tpu_custom_call", output_to_operand_aliasing={{}: (3, {})} | custom-call | bytes 1000000 | tf_op jit(solution)/shard_map/more/pallas_call | solution.py:399
  (44 shorter events, 0.5 us)
Async XLA Ops:
  0.6 4.0 %collective-permute-start = (bf16[256,2048]{1,0:T(8,128)(2,1)}, bf16[256,2048]{1,0:T(8,128)(2,1)S(1)}, u32[]{:S(2)}, u32[]{:S(2)}) collective-permute-start(bf16[256,2048]{1,0:T(8,128)(2,1)} %f_own.5), channel_id=1, source_target_pairs={{0,1},{1,0},{2,3},{3,2},{4,5},{5,4},{6,7},{7,6},{8,9},{9,8},{10,11... | collective-permute-start | bytes 3145736 | tf_op jit(solution)/shard_map/ppermute | solution.py:116
  1.1 3.4 %collective-permute-start.1 = (bf16[256,512]{1,0:T(8,128)(2,1)}, bf16[256,512]{1,0:T(8,128)(2,1)S(1)}, u32[]{:S(2)}, u32[]{:S(2)}) collective-permute-start(bf16[256,512]{1,0:T(8,128)(2,1)} %kv_ref.1), channel_id=1, source_target_pairs={{0,1},{1,0},{2,3},{3,2},{4,5},{5,4},{6,7},{7,6},{8,9},{9,8},{10,11... | collective-permute-start | bytes 786440 | tf_op jit(solution)/shard_map/ppermute | solution.py:116
  1.3 0.9 %copy-start.7 = (bf16[256,512]{1,0:T(8,128)(2,1)S(1)}, bf16[256,512]{1,0:T(8,128)(2,1)}, u32[]{:S(2)}) copy-start(bf16[256,512]{1,0:T(8,128)(2,1)} %kv_ref.1) | copy-start | bytes 786436
  2.3 0.7 copy-start.8
  4.6 1.2 %copy-start = (bf16[256,2048]{1,0:T(8,128)(2,1)S(1)}, bf16[256,2048]{1,0:T(8,128)(2,1)}, u32[]{:S(2)}) copy-start(bf16[256,2048]{1,0:T(8,128)(2,1)} %f_own.5) | copy-start | bytes 3145732
  6.9 12.3 %collective-permute-start.2 = (f32[8,96,128]{2,1,0:T(8,128)S(1)}, f32[8,96,128]{2,1,0:T(8,128)S(1)}, u32[]{:S(2)}, u32[]{:S(2)}) collective-permute-start(f32[8,96,128]{2,1,0:T(8,128)S(1)} %get-tuple-element.38), channel_id=1, source_target_pairs={{0,2},{2,0},{4,6},{6,4},{8,10},{10,8},{12,14},{14,12},{16,18},{18,... | collective-permute-start | bytes 1179656 | tf_op jit(solution)/shard_map/ppermute | solution.py:116
  11.0 11.2 %collective-permute-start.3 = (f32[8,96,128]{2,1,0:T(8,128)S(1)}, f32[8,96,128]{2,1,0:T(8,128)S(1)}, u32[]{:S(2)}, u32[]{:S(2)}) collective-permute-start(f32[8,96,128]{2,1,0:T(8,128)S(1)} %get-tuple-element.40), channel_id=1, source_target_pairs={{0,4},{2,6},{4,0},{6,2},{8,12},{10,14},{12,8},{14,10},{16,20},{18,... | collective-permute-start | bytes 1179656 | tf_op jit(solution)/shard_map/ppermute | solution.py:116
  14.0 8.8 %collective-permute-start.7 = (f32[16,32,128]{2,1,0:T(8,128)S(1)}, f32[16,32,128]{2,1,0:T(8,128)S(1)}, u32[]{:S(2)}, u32[]{:S(2)}) collective-permute-start(f32[16,32,128]{2,1,0:T(8,128)S(1)} %get-tuple-element.42), channel_id=1, source_target_pairs={{0,8},{2,10},{4,12},{6,14},{8,0},{10,2},{12,4},{14,6},{16,24},{18,... | collective-permute-start | bytes 786440 | tf_op jit(solution)/shard_map/ppermute | solution.py:116
  19.3 6.8 %collective-permute-start.4 = (f32[4,96,128]{2,1,0:T(8,128)S(1)}, f32[4,96,128]{2,1,0:T(8,128)S(1)}, u32[]{:S(2)}, u32[]{:S(2)}) collective-permute-start(f32[4,96,128]{2,1,0:T(8,128)S(1)} %get-tuple-element.64), channel_id=1, source_target_pairs={{0,4},{2,6},{4,0},{6,2},{8,12},{10,14},{12,8},{14,10},{16,20},{18,... | collective-permute-start | bytes 589832 | tf_op jit(solution)/shard_map/ppermute | solution.py:116
  22.1 16.0 %copy-start.1 = (bf16[1,4,128,128]{3,2,1,0:T(8,128)(2,1)S(1)}, bf16[1,4,128,128]{3,2,1,0:T(8,128)(2,1)}, u32[]{:S(2)}) copy-start(bf16[1,4,128,128]{3,2,1,0:T(8,128)(2,1)} %ql_ref.3) | copy-start | bytes 393220
  22.1 16.0 %copy-start.2 = (bf16[1,4,128,128]{3,2,1,0:T(8,128)(2,1)S(1)}, bf16[1,4,128,128]{3,2,1,0:T(8,128)(2,1)}, u32[]{:S(2)}) copy-start(bf16[1,4,128,128]{3,2,1,0:T(8,128)(2,1)} %qr_ref.3) | copy-start | bytes 393220
  22.1 16.0 %copy-start.3 = (f32[1,4,128,128]{3,2,1,0:T(8,128)S(1)}, f32[1,4,128,128]{3,2,1,0:T(8,128)}, u32[]{:S(2)}) copy-start(f32[1,4,128,128]{3,2,1,0:T(8,128)} %m_ref.1) | copy-start | bytes 786436
  22.1 16.0 %copy-start.4 = (f32[1,4,128,128]{3,2,1,0:T(8,128)S(1)}, f32[1,4,128,128]{3,2,1,0:T(8,128)}, u32[]{:S(2)}) copy-start(f32[1,4,128,128]{3,2,1,0:T(8,128)} %v_ref.1) | copy-start | bytes 786436
  22.2 16.0 %copy-start.5 = (f32[1,4,128,128]{3,2,1,0:T(8,128)S(1)}, f32[1,4,128,128]{3,2,1,0:T(8,128)}, u32[]{:S(2)}) copy-start(f32[1,4,128,128]{3,2,1,0:T(8,128)} %l_ref.1) | copy-start | bytes 786436
  22.2 16.0 %copy-start.6 = (f32[1,4,128,128]{3,2,1,0:T(8,128)S(1)}, f32[1,4,128,128]{3,2,1,0:T(8,128)}, u32[]{:S(2)}) copy-start(f32[1,4,128,128]{3,2,1,0:T(8,128)} %r_ref.1) | copy-start | bytes 786436
  22.2 5.7 %collective-permute-start.5 = (f32[4,96,128]{2,1,0:T(8,128)S(1)}, f32[4,96,128]{2,1,0:T(8,128)S(1)}, u32[]{:S(2)}, u32[]{:S(2)}) collective-permute-start(f32[4,96,128]{2,1,0:T(8,128)S(1)} %get-tuple-element.66), channel_id=1, source_target_pairs={{0,2},{2,0},{4,6},{6,4},{8,10},{10,8},{12,14},{14,12},{16,18},{18,... | collective-permute-start | bytes 589832 | tf_op jit(solution)/shard_map/ppermute | solution.py:116
  22.8 8.0 %collective-permute-start.8 = (f32[8,32,128]{2,1,0:T(8,128)S(1)}, f32[8,32,128]{2,1,0:T(8,128)S(1)}, u32[]{:S(2)}, u32[]{:S(2)}) collective-permute-start(f32[8,32,128]{2,1,0:T(8,128)S(1)} %get-tuple-element.68), channel_id=1, source_target_pairs={{0,16},{2,18},{4,20},{6,22},{8,24},{10,26},{12,28},{14,30},{16,0},... | collective-permute-start | bytes 393224 | tf_op jit(solution)/shard_map/ppermute | solution.py:116
  28.0 5.7 %collective-permute-start.6 = (f32[2,2,96,128]{3,2,1,0:T(8,128)S(1)}, f32[2,2,96,128]{3,2,1,0:T(8,128)S(1)}, u32[]{:S(2)}, u32[]{:S(2)}) collective-permute-start(f32[2,2,96,128]{3,2,1,0:T(8,128)S(1)} %get-tuple-element.62), channel_id=1, source_target_pairs={{0,8},{2,10},{4,12},{6,14},{8,0},{10,2},{12,4},{14,6},{16,24},{18,... | collective-permute-start | bytes 589832 | tf_op jit(solution)/shard_map/ppermute | solution.py:116
  30.8 5.7 %collective-permute-start.10 = (f32[4,32,128]{2,1,0:T(8,128)S(1)}, f32[4,32,128]{2,1,0:T(8,128)S(1)}, u32[]{:S(2)}, u32[]{:S(2)}) collective-permute-start(f32[4,32,128]{2,1,0:T(8,128)S(1)} %get-tuple-element.72), channel_id=1, source_target_pairs={{0,2},{2,0},{4,6},{6,4},{8,10},{10,8},{12,14},{14,12},{16,18},{18,... | collective-permute-start | bytes 196616 | tf_op jit(solution)/shard_map/ppermute | solution.py:116
  33.8 6.7 %collective-permute-start.9 = (f32[2,96,128]{2,1,0:T(8,128)S(1)}, f32[2,96,128]{2,1,0:T(8,128)S(1)}, u32[]{:S(2)}, u32[]{:S(2)}) collective-permute-start(f32[2,96,128]{2,1,0:T(8,128)S(1)} %bitcast.17), channel_id=1, source_target_pairs={{0,16},{2,18},{4,20},{6,22},{8,24},{10,26},{12,28},{14,30},{16,0},... | collective-permute-start | bytes 294920 | tf_op jit(solution)/shard_map/ppermute | solution.py:116
  36.5 4.0 %collective-permute-start.11 = (f32[2,32,128]{2,1,0:T(8,128)S(1)}, f32[2,32,128]{2,1,0:T(8,128)S(1)}, u32[]{:S(2)}, u32[]{:S(2)}) collective-permute-start(f32[2,32,128]{2,1,0:T(8,128)S(1)} %get-tuple-element.73), channel_id=1, source_target_pairs={{0,4},{2,6},{4,0},{6,2},{8,12},{10,14},{12,8},{14,10},{16,20},{18,... | collective-permute-start | bytes 98312 | tf_op jit(solution)/shard_map/ppermute | solution.py:116
  41.2 7.2 %collective-permute-start.14 = (bf16[2,128,128]{2,1,0:T(8,128)(2,1)S(1)}, bf16[2,128,128]{2,1,0:T(8,128)(2,1)S(1)}, u32[]{:S(2)}, u32[]{:S(2)}) collective-permute-start(bf16[2,128,128]{2,1,0:T(8,128)(2,1)S(1)} %get-tuple-element.46), channel_id=1, source_target_pairs={{0,24},{2,26},{4,28},{6,30},{8,16},{10,18},{12,20},{14,22},{16,8},... | collective-permute-start | bytes 196616 | tf_op jit(solution)/shard_map/ppermute | solution.py:116
  44.8 4.3 %collective-permute-start.13 = (bf16[2,128,128]{2,1,0:T(8,128)(2,1)S(1)}, bf16[2,128,128]{2,1,0:T(8,128)(2,1)S(1)}, u32[]{:S(2)}, u32[]{:S(2)}) collective-permute-start(bf16[2,128,128]{2,1,0:T(8,128)(2,1)S(1)} %get-tuple-element.46), channel_id=1, source_target_pairs={{0,8},{2,10},{4,12},{6,14},{8,0},{10,2},{12,4},{14,6},{16,24},{18,... | collective-permute-start | bytes 196616 | tf_op jit(solution)/shard_map/ppermute | solution.py:116
  44.8 5.2 %collective-permute-start.12 = (bf16[2,128,128]{2,1,0:T(8,128)(2,1)S(1)}, bf16[2,128,128]{2,1,0:T(8,128)(2,1)S(1)}, u32[]{:S(2)}, u32[]{:S(2)}) collective-permute-start(bf16[2,128,128]{2,1,0:T(8,128)(2,1)S(1)} %get-tuple-element.46), channel_id=1, source_target_pairs={{0,16},{2,18},{4,20},{6,22},{8,24},{10,26},{12,28},{14,30},{16,0},... | collective-permute-start | bytes 196616 | tf_op jit(solution)/shard_map/ppermute | solution.py:116
  50.0 6.1 %collective-permute-start.15 = (bf16[4,128,128]{2,1,0:T(8,128)(2,1)S(1)}, bf16[4,128,128]{2,1,0:T(8,128)(2,1)S(1)}, u32[]{:S(2)}, u32[]{:S(2)}) collective-permute-start(bf16[4,128,128]{2,1,0:T(8,128)(2,1)S(1)} %get-tuple-element.49), channel_id=1, source_target_pairs={{0,4},{2,6},{4,0},{6,2},{8,12},{10,14},{12,8},{14,10},{16,20},{18,... | collective-permute-start | bytes 393224 | tf_op jit(solution)/shard_map/ppermute | solution.py:116
  51.7 5.9 %collective-permute-start.16 = (bf16[4,128,128]{2,1,0:T(8,128)(2,1)S(1)}, bf16[4,128,128]{2,1,0:T(8,128)(2,1)S(1)}, u32[]{:S(2)}, u32[]{:S(2)}) collective-permute-start(bf16[4,128,128]{2,1,0:T(8,128)(2,1)S(1)} %get-tuple-element.50), channel_id=1, source_target_pairs={{0,2},{2,0},{4,6},{6,4},{8,10},{10,8},{12,14},{14,12},{16,18},{18,... | collective-permute-start | bytes 393224 | tf_op jit(solution)/shard_map/ppermute | solution.py:116
  57.7 6.4 %collective-permute-start.18 = (bf16[8,128,128]{2,1,0:T(8,128)(2,1)S(1)}, bf16[8,128,128]{2,1,0:T(8,128)(2,1)S(1)}, u32[]{:S(2)}, u32[]{:S(2)}) collective-permute-start(bf16[8,128,128]{2,1,0:T(8,128)(2,1)S(1)} %pad_maximum_fusion.refs_0_), channel_id=1, source_target_pairs={{0,2},{2,0},{4,6},{6,4},{8,10},{10,8},{12,14},{14,12},{16,18},{18,... | collective-permute-start | bytes 786440 | tf_op jit(solution)/shard_map/ppermute | solution.py:116
  58.4 6.4 %collective-permute-start.19 = (bf16[8,128,128]{2,1,0:T(8,128)(2,1)S(1)}, bf16[8,128,128]{2,1,0:T(8,128)(2,1)S(1)}, u32[]{:S(2)}, u32[]{:S(2)}) collective-permute-start(bf16[8,128,128]{2,1,0:T(8,128)(2,1)S(1)} %pad_maximum_fusion.1.refs_1_), channel_id=1, source_target_pairs={{0,4},{2,6},{4,0},{6,2},{8,12},{10,14},{12,8},{14,10},{16,20},{18,... | collective-permute-start | bytes 786440 | tf_op jit(solution)/shard_map/ppermute | solution.py:116
  59.1 1.3 %collective-permute-start.17 = (bf16[4,128,128]{2,1,0:T(8,128)(2,1)S(1)}, bf16[4,128,128]{2,1,0:T(8,128)(2,1)S(1)}, u32[]{:S(2)}, u32[]{:S(2)}) collective-permute-start(bf16[4,128,128]{2,1,0:T(8,128)(2,1)S(1)} %finish.1.own_ref), channel_id=1, source_target_pairs={{0,1},{1,0},{2,3},{3,2},{4,5},{5,4},{6,7},{7,6},{8,9},{9,8},{10,11... | collective-permute-start | bytes 393224 | tf_op jit(solution)/shard_map/ppermute | solution.py:116
  59.1 6.1 %collective-permute-start.22 = (bf16[8,128,128]{2,1,0:T(8,128)(2,1)S(1)}, bf16[8,128,128]{2,1,0:T(8,128)(2,1)S(1)}, u32[]{:S(2)}, u32[]{:S(2)}) collective-permute-start(bf16[8,128,128]{2,1,0:T(8,128)(2,1)S(1)} %pad_maximum_fusion.refs_0_), channel_id=1, source_target_pairs={{0,1},{1,0},{2,3},{3,2},{4,5},{5,4},{6,7},{7,6},{8,9},{9,8},{10,11... | collective-permute-start | bytes 786440 | tf_op jit(solution)/shard_map/ppermute | solution.py:116
  59.6 5.6 %collective-permute-start.23 = (bf16[8,128,128]{2,1,0:T(8,128)(2,1)S(1)}, bf16[8,128,128]{2,1,0:T(8,128)(2,1)S(1)}, u32[]{:S(2)}, u32[]{:S(2)}) collective-permute-start(bf16[8,128,128]{2,1,0:T(8,128)(2,1)S(1)} %pad_maximum_fusion.1.refs_1_), channel_id=1, source_target_pairs={{0,1},{1,0},{2,3},{3,2},{4,5},{5,4},{6,7},{7,6},{8,9},{9,8},{10,11... | collective-permute-start | bytes 786440 | tf_op jit(solution)/shard_map/ppermute | solution.py:116
  64.8 2.3 %collective-permute-start.20 = (bf16[8,128,128]{2,1,0:T(8,128)(2,1)S(1)}, bf16[8,128,128]{2,1,0:T(8,128)(2,1)S(1)}, u32[]{:S(2)}, u32[]{:S(2)}) collective-permute-start(bf16[8,128,128]{2,1,0:T(8,128)(2,1)S(1)} %collective-permute-done.18.refs_2_), channel_id=1, source_target_pairs={{0,1},{1,0},{2,3},{3,2},{4,5},{5,4},{6,7},{7,6},{8,9},{9,8},{10,11... | collective-permute-start | bytes 786440 | tf_op jit(solution)/shard_map/ppermute | solution.py:116
  64.8 2.3 %collective-permute-start.21 = (bf16[8,128,128]{2,1,0:T(8,128)(2,1)S(1)}, bf16[8,128,128]{2,1,0:T(8,128)(2,1)S(1)}, u32[]{:S(2)}, u32[]{:S(2)}) collective-permute-start(bf16[8,128,128]{2,1,0:T(8,128)(2,1)S(1)} %collective-permute-done.19.refs_3_), channel_id=1, source_target_pairs={{0,1},{1,0},{2,3},{3,2},{4,5},{5,4},{6,7},{7,6},{8,9},{9,8},{10,11... | collective-permute-start | bytes 786440 | tf_op jit(solution)/shard_map/ppermute | solution.py:116

commit v11 on v9

--- a/solution.py
+++ b/solution.py
@@ -196,7 +196,7 @@
                 table_ref[entry] = held[(here ^ offsets[stream][p]) * capacity + first_slot + stream]
 
 
-EDGE = 24
+EDGE = 32
 
 
 def tiles_kernel(owners, first, table_ref, f_own, f_sib, own_rows, kv_sib, *rest):

time: 69 us -> 68.3 us (0.990)
  starting transfers between devices: 30.3 us -> 28.2 us
  waiting for transfers between devices: 18.2 us -> 19.5 us
    ppermute x24, starting transfers between devices: 30.3 us -> 28.2 us  [swap_along(): return lax.ppermute(values, axis, [(i, i ^ bit) for i in range(size)])]
    ppermute x24, waiting for transfers between devices: 18.2 us -> 19.5 us  [swap_along(): return lax.ppermute(values, axis, [(i, i ^ bit) for i in range(size)])]
  transfers between devices with their start and end apart: 24 -> 24, of which waited for: 13 -> 13; matrix products, arithmetic and copies ran while one was open for 0% -> 1% of each run, Pallas kernels for 18% -> 19%
where the time goes in v11:
time: 68.3 us; the launch traced here: 68.1 us
  starting transfers between devices  28.2 us (41%)
  waiting for transfers between devices  19.5 us (29%)
  Pallas kernels  16.2 us (24%)
  local copies, waits for them, and re-layouts  2.88 us (4%)
  between operations  0.88 us (1%)
    ppermute x24, starting transfers between devices, swap_along(): return lax.ppermute(values, axis, [(i, i ^ bit) for i in range(size)])  28.2 us
    ppermute x24, waiting for transfers between devices, swap_along(): return lax.ppermute(values, axis, [(i, i ^ bit) for i in range(size)])  19.5 us
    pallas_call x3, Pallas kernels, on_slots(): pl.pallas_call(kernel, out_shape=tuple(outs), grid_spec=pltpu.PrefetchSca...  3.98 us
    pallas_call x2, Pallas kernels, place_more(): pl.pallas_call(functools.partial(more_kernel, col_tiles, entries), out_sh...  3.25 us
    pallas_call x1, Pallas kernels, sweeping(): pl.pallas_call(kernel, out_shape=jax.ShapeDtypeStruct(values.shape, dtype...  2.9 us
    unnamed x18, local copies, waits for them, and re-layouts  2.85 us
    pallas_call x2, Pallas kernels, tiles_from(): pl.pallas_call(functools.partial(tiles_kernel, owners, first), out_shape=...  2.82 us
    pallas_call x1, Pallas kernels, per_device_dealt(): pl.pallas_call(functools.partial(table_kernel, owners, capacity), out_sha...  1.65 us
  transfers between devices with their start and end apart: 24, of which 13 were waited for; matrix products, arithmetic and copies ran while one was open for 1% of the time, Pallas kernels for 19%

profile of v11, /device:TPU:0, one launch (start us, length us, event | category | flops | bytes accessed | tf_op | source)
XLA Modules:
  0.0 68.1 jit_solution(12874944435160644143)
XLA Ops:
  0.6 0.5 collective-permute-start
  1.1 0.1 collective-permute-start.1
  1.2 0.1 pad_add_fusion.place_ref
  1.3 0.9 %copy-done.7 = bf16[256,512]{1,0:T(8,128)(2,1)S(1)} copy-done((bf16[256,512]{1,0:T(8,128)(2,1)S(1)}, bf16[256,512]{1,0:T(8,128)(2,1)}, u32[]{:S(2)}) %copy-start.7) | copy-done | bytes 262168
  2.3 0.7 copy-done.8
  2.9 1.7 %table.1 = (s32[64]{0:T(128)S(1)}, bf16[512,256]{1,0:T(8,128)(2,1)S(1)}) custom-call(s32[2]{0:T(128)S(1)} %pad_add_fusion.place_ref, s32[64]{0:T(128)S(1)} %copy-done.8, bf16[256,512]{1,0:T(8,128)(2,1)S(1)} %copy-done.7), custom_call_target="tpu_custom_call" | custom-call | bytes 1000000 | tf_op jit(solution)/shard_map/table/pallas_call | solution.py:438
  4.6 1.2 %copy-done = bf16[256,2048]{1,0:T(8,128)(2,1)S(1)} copy-done((bf16[256,2048]{1,0:T(8,128)(2,1)S(1)}, bf16[256,2048]{1,0:T(8,128)(2,1)}, u32[]{:S(2)}) %copy-start) | copy-done | bytes 1048600
  5.8 1.4 %tiles.2 = (f32[8,96,128]{2,1,0:T(8,128)S(1)}, f32[8,96,128]{2,1,0:T(8,128)S(1)}, f32[32,32,128]{2,1,0:T(8,128)S(1)}) custom-call(s32[64]{0:T(128)S(1)} %get-tuple-element.30.table_ref, bf16[256,2048]{1,0:T(8,128)(2,1)S(1)} %copy-done, bf16[256,2048]{1,0:T(8,128)(2,1)S(1)} %collective-permute-done.f_sib, bf16[512,256]{1,0:T(8,128)(2,1)S(1)} %get-tuple-element.31.own_rows, ...), custom_call_target="tpu_custom_call" | custom-call | flops 536870912 | bytes 3500000 | tf_op jit(solution)/shard_map/tiles/pallas_call | solution.py:457
  7.2 3.0 %collective-permute-start.2 = (f32[8,96,128]{2,1,0:T(8,128)S(1)}, f32[8,96,128]{2,1,0:T(8,128)S(1)}, u32[]{:S(2)}, u32[]{:S(2)}) collective-permute-start(f32[8,96,128]{2,1,0:T(8,128)S(1)} %get-tuple-element.34), channel_id=1, source_target_pairs={{0,2},{2,0},{4,6},{6,4},{8,10},{10,8},{12,14},{14,12},{16,18},{18,... | collective-permute-start | bytes 1179656 | tf_op jit(solution)/shard_map/ppermute | solution.py:116
  10.2 1.5 %collective-permute-start.3 = (f32[8,96,128]{2,1,0:T(8,128)S(1)}, f32[8,96,128]{2,1,0:T(8,128)S(1)}, u32[]{:S(2)}, u32[]{:S(2)}) collective-permute-start(f32[8,96,128]{2,1,0:T(8,128)S(1)} %get-tuple-element.36), channel_id=1, source_target_pairs={{0,4},{2,6},{4,0},{6,2},{8,12},{10,14},{12,8},{14,10},{16,20},{18,... | collective-permute-start | bytes 1179656 | tf_op jit(solution)/shard_map/ppermute | solution.py:116
  11.7 1.4 %tiles.3 = (f32[8,96,128]{2,1,0:T(8,128)S(1)}, f32[8,96,128]{2,1,0:T(8,128)S(1)}, f32[16,32,128]{2,1,0:T(8,128)S(1)}, f32[16,32,128]{2,1,0:T(8,128)S(1)}) custom-call(s32[64]{0:T(128)S(1)} %get-tuple-element.30.table_ref, bf16[256,2048]{1,0:T(8,128)(2,1)S(1)} %copy-done, bf16[256,2048]{1,0:T(8,128)(2,1)S(1)} %collective-permute-done.f_sib, ...), custom_call_target="tpu_custom_call" | custom-call | flops 536870912 | bytes 3500000 | tf_op jit(solution)/shard_map/tiles/pallas_call | solution.py:457
  13.1 1.6 %collective-permute-start.7 = (f32[16,32,128]{2,1,0:T(8,128)S(1)}, f32[16,32,128]{2,1,0:T(8,128)S(1)}, u32[]{:S(2)}, u32[]{:S(2)}) collective-permute-start(f32[16,32,128]{2,1,0:T(8,128)S(1)} %get-tuple-element.38), channel_id=1, source_target_pairs={{0,8},{2,10},{4,12},{6,14},{8,0},{10,2},{12,4},{14,6},{16,24},{18,... | collective-permute-start | bytes 786440 | tf_op jit(solution)/shard_map/ppermute | solution.py:116
  14.8 4.8 %collective-permute-done.2 = f32[8,96,128]{2,1,0:T(8,128)S(1)} collective-permute-done((f32[8,96,128]{2,1,0:T(8,128)S(1)}, f32[8,96,128]{2,1,0:T(8,128)S(1)}, u32[]{:S(2)}, u32[]{:S(2)}) %collective-permute-start.2) | collective-permute-done | bytes 393248 | tf_op jit(solution)/shard_map/ppermute | solution.py:116
  19.6 1.8 %collective-permute-start.4 = (f32[4,96,128]{2,1,0:T(8,128)S(1)}, f32[4,96,128]{2,1,0:T(8,128)S(1)}, u32[]{:S(2)}, u32[]{:S(2)}) collective-permute-start(f32[4,96,128]{2,1,0:T(8,128)S(1)} %get-tuple-element.60), channel_id=1, source_target_pairs={{0,4},{2,6},{4,0},{6,2},{8,12},{10,14},{12,8},{14,10},{16,20},{18,... | collective-permute-start | bytes 589832 | tf_op jit(solution)/shard_map/ppermute | solution.py:116
  21.5 1.6 %collective-permute-start.5 = (f32[4,96,128]{2,1,0:T(8,128)S(1)}, f32[4,96,128]{2,1,0:T(8,128)S(1)}, u32[]{:S(2)}, u32[]{:S(2)}) collective-permute-start(f32[4,96,128]{2,1,0:T(8,128)S(1)} %get-tuple-element.62), channel_id=1, source_target_pairs={{0,2},{2,0},{4,6},{6,4},{8,10},{10,8},{12,14},{14,12},{16,18},{18,... | collective-permute-start | bytes 589832 | tf_op jit(solution)/shard_map/ppermute | solution.py:116
  23.2 2.7 %collective-permute-start.8 = (f32[8,32,128]{2,1,0:T(8,128)S(1)}, f32[8,32,128]{2,1,0:T(8,128)S(1)}, u32[]{:S(2)}, u32[]{:S(2)}) collective-permute-start(f32[8,32,128]{2,1,0:T(8,128)S(1)} %get-tuple-element.64), channel_id=1, source_target_pairs={{0,16},{2,18},{4,20},{6,22},{8,24},{10,26},{12,28},{14,30},{16,0},... | collective-permute-start | bytes 393224 | tf_op jit(solution)/shard_map/ppermute | solution.py:116
  25.8 0.2 collective-permute-done.4
  26.1 1.3 %collective-permute-done.5 = f32[4,96,128]{2,1,0:T(8,128)S(1)} collective-permute-done((f32[4,96,128]{2,1,0:T(8,128)S(1)}, f32[4,96,128]{2,1,0:T(8,128)S(1)}, u32[]{:S(2)}, u32[]{:S(2)}) %collective-permute-start.5) | collective-permute-done | bytes 196640 | tf_op jit(solution)/shard_map/ppermute | solution.py:116
  27.4 0.1 fusion.1
  27.4 1.7 %collective-permute-start.6 = (f32[2,2,96,128]{3,2,1,0:T(8,128)S(1)}, f32[2,2,96,128]{3,2,1,0:T(8,128)S(1)}, u32[]{:S(2)}, u32[]{:S(2)}) collective-permute-start(f32[2,2,96,128]{3,2,1,0:T(8,128)S(1)} %get-tuple-element.58), channel_id=1, source_target_pairs={{0,8},{2,10},{4,12},{6,14},{8,0},{10,2},{12,4},{14,6},{16,24},{18,... | collective-permute-start | bytes 589832 | tf_op jit(solution)/shard_map/ppermute | solution.py:116
  29.1 2.0 %collective-permute-done.8 = f32[8,32,128]{2,1,0:T(8,128)S(1)} collective-permute-done((f32[8,32,128]{2,1,0:T(8,128)S(1)}, f32[8,32,128]{2,1,0:T(8,128)S(1)}, u32[]{:S(2)}, u32[]{:S(2)}) %collective-permute-start.8) | collective-permute-done | bytes 131104 | tf_op jit(solution)/shard_map/ppermute | solution.py:116
  31.1 0.6 collective-permute-start.10
  31.7 2.1 %collective-permute-done.6 = f32[2,2,96,128]{3,2,1,0:T(8,128)S(1)} collective-permute-done((f32[2,2,96,128]{3,2,1,0:T(8,128)S(1)}, f32[2,2,96,128]{3,2,1,0:T(8,128)S(1)}, u32[]{:S(2)}, u32[]{:S(2)}) %collective-permute-start.6) | collective-permute-done | bytes 196640 | tf_op jit(solution)/shard_map/ppermute | solution.py:116
  33.9 2.1 %collective-permute-start.9 = (f32[2,96,128]{2,1,0:T(8,128)S(1)}, f32[2,96,128]{2,1,0:T(8,128)S(1)}, u32[]{:S(2)}, u32[]{:S(2)}) collective-permute-start(f32[2,96,128]{2,1,0:T(8,128)S(1)} %bitcast.17), channel_id=1, source_target_pairs={{0,16},{2,18},{4,20},{6,22},{8,24},{10,26},{12,28},{14,30},{16,0},... | collective-permute-start | bytes 294920 | tf_op jit(solution)/shard_map/ppermute | solution.py:116
  35.9 1.1 %collective-permute-start.11 = (f32[2,32,128]{2,1,0:T(8,128)S(1)}, f32[2,32,128]{2,1,0:T(8,128)S(1)}, u32[]{:S(2)}, u32[]{:S(2)}) collective-permute-start(f32[2,32,128]{2,1,0:T(8,128)S(1)} %get-tuple-element.69), channel_id=1, source_target_pairs={{0,4},{2,6},{4,0},{6,2},{8,12},{10,14},{12,8},{14,10},{16,20},{18,... | collective-permute-start | bytes 98312 | tf_op jit(solution)/shard_map/ppermute | solution.py:116
  37.1 0.5 rotated.1
  37.6 2.3 %collective-permute-done.11.d_ref = f32[2,32,128]{2,1,0:T(8,128)S(1)} collective-permute-done((f32[2,32,128]{2,1,0:T(8,128)S(1)}, f32[2,32,128]{2,1,0:T(8,128)S(1)}, u32[]{:S(2)}, u32[]{:S(2)}) %collective-permute-start.11) | collective-permute-done | bytes 32800 | tf_op jit(solution)/shard_map/ppermute | solution.py:116
  39.9 0.9 %collective-permute-done.9.b_ref = f32[2,96,128]{2,1,0:T(8,128)S(1)} collective-permute-done((f32[2,96,128]{2,1,0:T(8,128)S(1)}, f32[2,96,128]{2,1,0:T(8,128)S(1)}, u32[]{:S(2)}, u32[]{:S(2)}) %collective-permute-start.9) | collective-permute-done | bytes 98336 | tf_op jit(solution)/shard_map/ppermute | solution.py:116
  40.8 0.7 %direction.1 = (bf16[2,128,128]{2,1,0:T(8,128)(2,1)S(1)}, f32[2,128,128]{2,1,0:T(8,128)S(1)}) custom-call(s32[1]{0:T(128)} %bitcast.1.side_ref, f32[2,96,128]{2,1,0:T(8,128)S(1)} %get-tuple-element.66.a_ref, f32[2,96,128]{2,1,0:T(8,128)S(1)} %collective-permute-done.9.b_ref, f32[2,32,128]{2,1,0:T(8,128)S(1)} %get-tuple-element.70.c_ref, ...), custom_call_target="tpu_custom_call" | custom-call | flops 67108864 | bytes 800000 | tf_op jit(solution)/shard_map/direction/pallas_call | solution.py:291
  41.5 2.7 %collective-permute-start.14 = (bf16[2,128,128]{2,1,0:T(8,128)(2,1)S(1)}, bf16[2,128,128]{2,1,0:T(8,128)(2,1)S(1)}, u32[]{:S(2)}, u32[]{:S(2)}) collective-permute-start(bf16[2,128,128]{2,1,0:T(8,128)(2,1)S(1)} %get-tuple-element.42), channel_id=1, source_target_pairs={{0,24},{2,26},{4,28},{6,30},{8,16},{10,18},{12,20},{14,22},{16,8},... | collective-permute-start | bytes 196616 | tf_op jit(solution)/shard_map/ppermute | solution.py:116
  44.3 1.7 %collective-permute-start.12 = (bf16[2,128,128]{2,1,0:T(8,128)(2,1)S(1)}, bf16[2,128,128]{2,1,0:T(8,128)(2,1)S(1)}, u32[]{:S(2)}, u32[]{:S(2)}) collective-permute-start(bf16[2,128,128]{2,1,0:T(8,128)(2,1)S(1)} %get-tuple-element.42), channel_id=1, source_target_pairs={{0,16},{2,18},{4,20},{6,22},{8,24},{10,26},{12,28},{14,30},{16,0},... | collective-permute-start | bytes 196616 | tf_op jit(solution)/shard_map/ppermute | solution.py:116
  46.0 2.8 %refresh.1.iter_ref = f32[4,128,128]{2,1,0:T(8,128)S(1)} custom-call(s32[1]{0:T(128)} %bitcast.1.side_ref, f32[2,128,128]{2,1,0:T(8,128)S(1)} %get-tuple-element.43.g_ref, f32[4,128,128]{2,1,0:T(8,128)S(1)} %get-tuple-element.44.power_ref, bf16[1,4,128,128]{3,2,1,0:T(8,128)(2,1)S(1)} %copy-done.1, bf16[1,4,128,128]{3,2,1,0:T(8,128)(2,1)S(1)} %copy-done.2), custom_call_target="tpu_custom_call" | custom-call | flops 939524096 | bytes 800000 | tf_op jit(solution)/shard_map/refresh/pallas_call | solution.py:291
  48.8 0.6 collective-permute-done.12
  49.5 1.1 %collective-permute-start.15 = (bf16[4,128,128]{2,1,0:T(8,128)(2,1)S(1)}, bf16[4,128,128]{2,1,0:T(8,128)(2,1)S(1)}, u32[]{:S(2)}, u32[]{:S(2)}) collective-permute-start(bf16[4,128,128]{2,1,0:T(8,128)(2,1)S(1)} %get-tuple-element.45), channel_id=1, source_target_pairs={{0,4},{2,6},{4,0},{6,2},{8,12},{10,14},{12,8},{14,10},{16,20},{18,... | collective-permute-start | bytes 393224 | tf_op jit(solution)/shard_map/ppermute | solution.py:116
  50.5 1.0 %collective-permute-start.16 = (bf16[4,128,128]{2,1,0:T(8,128)(2,1)S(1)}, bf16[4,128,128]{2,1,0:T(8,128)(2,1)S(1)}, u32[]{:S(2)}, u32[]{:S(2)}) collective-permute-start(bf16[4,128,128]{2,1,0:T(8,128)(2,1)S(1)} %get-tuple-element.46), channel_id=1, source_target_pairs={{0,2},{2,0},{4,6},{6,4},{8,10},{10,8},{12,14},{14,12},{16,18},{18,... | collective-permute-start | bytes 393224 | tf_op jit(solution)/shard_map/ppermute | solution.py:116
  51.5 2.9 %finish.1.own_ref = bf16[4,128,128]{2,1,0:T(8,128)(2,1)S(1)} custom-call(f32[4,128,128]{2,1,0:T(8,128)S(1)} %refresh.1.iter_ref), custom_call_target="tpu_custom_call" | custom-call | flops 939524096 | bytes 400000 | tf_op jit(solution)/shard_map/finish/pallas_call | solution.py:341
  54.4 0.9 %collective-permute-done.15 = bf16[4,128,128]{2,1,0:T(8,128)(2,1)S(1)} collective-permute-done((bf16[4,128,128]{2,1,0:T(8,128)(2,1)S(1)}, bf16[4,128,128]{2,1,0:T(8,128)(2,1)S(1)}, u32[]{:S(2)}, u32[]{:S(2)}) %collective-permute-start.15) | collective-permute-done | bytes 131104 | tf_op jit(solution)/shard_map/ppermute | solution.py:116
  55.3 1.6 %collective-permute-done.16 = bf16[4,128,128]{2,1,0:T(8,128)(2,1)S(1)} collective-permute-done((bf16[4,128,128]{2,1,0:T(8,128)(2,1)S(1)}, bf16[4,128,128]{2,1,0:T(8,128)(2,1)S(1)}, u32[]{:S(2)}, u32[]{:S(2)}) %collective-permute-start.16) | collective-permute-done | bytes 131104 | tf_op jit(solution)/shard_map/ppermute | solution.py:116
  56.9 1.0 %collective-permute-start.18 = (bf16[8,128,128]{2,1,0:T(8,128)(2,1)S(1)}, bf16[8,128,128]{2,1,0:T(8,128)(2,1)S(1)}, u32[]{:S(2)}, u32[]{:S(2)}) collective-permute-start(bf16[8,128,128]{2,1,0:T(8,128)(2,1)S(1)} %pad_maximum_fusion.refs_0_), channel_id=1, source_target_pairs={{0,2},{2,0},{4,6},{6,4},{8,10},{10,8},{12,14},{14,12},{16,18},{18,... | collective-permute-start | bytes 786440 | tf_op jit(solution)/shard_map/ppermute | solution.py:116
  58.0 1.5 %collective-permute-start.19 = (bf16[8,128,128]{2,1,0:T(8,128)(2,1)S(1)}, bf16[8,128,128]{2,1,0:T(8,128)(2,1)S(1)}, u32[]{:S(2)}, u32[]{:S(2)}) collective-permute-start(bf16[8,128,128]{2,1,0:T(8,128)(2,1)S(1)} %pad_maximum_fusion.1.refs_1_), channel_id=1, source_target_pairs={{0,4},{2,6},{4,0},{6,2},{8,12},{10,14},{12,8},{14,10},{16,20},{18,... | collective-permute-start | bytes 786440 | tf_op jit(solution)/shard_map/ppermute | solution.py:116
  59.5 0.5 collective-permute-start.22
  60.0 0.8 %collective-permute-done.17.sib_ref = bf16[4,128,128]{2,1,0:T(8,128)(2,1)S(1)} collective-permute-done((bf16[4,128,128]{2,1,0:T(8,128)(2,1)S(1)}, bf16[4,128,128]{2,1,0:T(8,128)(2,1)S(1)}, u32[]{:S(2)}, u32[]{:S(2)}) %collective-permute-start.17) | collective-permute-done | bytes 131104 | tf_op jit(solution)/shard_map/ppermute | solution.py:116
  60.8 1.6 %begin.1 = (bf16[2048,512]{1,0:T(8,128)(2,1)}, bf16[1,4,128,128]{3,2,1,0:T(8,128)(2,1)}, bf16[1,4,128,128]{3,2,1,0:T(8,128)(2,1)}) custom-call(s32[64]{0:T(128)S(1)} %get-tuple-element.30.table_ref, s32[2]{0:T(128)S(1)} %pad_add_fusion.place_ref, bf16[4,128,128]{2,1,0:T(8,128)(2,1)S(1)} %finish.1.own_ref, ...), custom_call_target="tpu_custom_call" | custom-call | bytes 800000 | tf_op jit(solution)/shard_map/begin/pallas_call | solution.py:546
  62.5 0.9 %collective-permute-done.18.refs_2_ = bf16[8,128,128]{2,1,0:T(8,128)(2,1)S(1)} collective-permute-done((bf16[8,128,128]{2,1,0:T(8,128)(2,1)S(1)}, bf16[8,128,128]{2,1,0:T(8,128)(2,1)S(1)}, u32[]{:S(2)}, u32[]{:S(2)}) %collective-permute-start.18) | collective-permute-done | bytes 262176 | tf_op jit(solution)/shard_map/ppermute | solution.py:116
  63.4 1.0 %collective-permute-done.19.refs_3_ = bf16[8,128,128]{2,1,0:T(8,128)(2,1)S(1)} collective-permute-done((bf16[8,128,128]{2,1,0:T(8,128)(2,1)S(1)}, bf16[8,128,128]{2,1,0:T(8,128)(2,1)S(1)}, u32[]{:S(2)}, u32[]{:S(2)}) %collective-permute-start.19) | collective-permute-done | bytes 262176 | tf_op jit(solution)/shard_map/ppermute | solution.py:116
  64.3 0.5 collective-permute-start.21
  64.9 1.8 %more.2.refs_2_ = bf16[2048,512]{1,0:T(8,128)(2,1)} custom-call(s32[64]{0:T(128)S(1)} %get-tuple-element.30.table_ref, bf16[8,128,128]{2,1,0:T(8,128)(2,1)S(1)} %collective-permute-done.22.refs_0_, bf16[8,128,128]{2,1,0:T(8,128)(2,1)S(1)} %collective-permute-done.23.refs_1_, ...), custom_call_target="tpu_custom_call", output_to_operand_aliasing={{}: (5, {})} | custom-call | bytes 1000000 | tf_op jit(solution)/shard_map/more/pallas_call | solution.py:393
  66.7 1.5 %more.3 = bf16[2048,512]{1,0:T(8,128)(2,1)} custom-call(s32[64]{0:T(128)S(1)} %get-tuple-element.30.table_ref, bf16[8,128,128]{2,1,0:T(8,128)(2,1)S(1)} %collective-permute-done.20.refs_0_, bf16[8,128,128]{2,1,0:T(8,128)(2,1)S(1)} %collective-permute-done.21.refs_1_, bf16[2048,512]{1,0:T(8,128)(2,1)} %more.2.refs_2_), custom_call_target="tpu_custom_call", output_to_operand_aliasing={{}: (3, {})} | custom-call | bytes 1000000 | tf_op jit(solution)/shard_map/more/pallas_call | solution.py:393
  (43 shorter events, 0.4 us)
Async XLA Ops:
  0.6 4.0 %collective-permute-start = (bf16[256,2048]{1,0:T(8,128)(2,1)}, bf16[256,2048]{1,0:T(8,128)(2,1)S(1)}, u32[]{:S(2)}, u32[]{:S(2)}) collective-permute-start(bf16[256,2048]{1,0:T(8,128)(2,1)} %f_own.3), channel_id=1, source_target_pairs={{0,1},{1,0},{2,3},{3,2},{4,5},{5,4},{6,7},{7,6},{8,9},{9,8},{10,11... | collective-permute-start | bytes 3145736 | tf_op jit(solution)/shard_map/ppermute | solution.py:116
  1.1 3.4 %collective-permute-start.1 = (bf16[256,512]{1,0:T(8,128)(2,1)}, bf16[256,512]{1,0:T(8,128)(2,1)S(1)}, u32[]{:S(2)}, u32[]{:S(2)}) collective-permute-start(bf16[256,512]{1,0:T(8,128)(2,1)} %kv_ref.1), channel_id=1, source_target_pairs={{0,1},{1,0},{2,3},{3,2},{4,5},{5,4},{6,7},{7,6},{8,9},{9,8},{10,11... | collective-permute-start | bytes 786440 | tf_op jit(solution)/shard_map/ppermute | solution.py:116
  1.3 0.9 %copy-start.7 = (bf16[256,512]{1,0:T(8,128)(2,1)S(1)}, bf16[256,512]{1,0:T(8,128)(2,1)}, u32[]{:S(2)}) copy-start(bf16[256,512]{1,0:T(8,128)(2,1)} %kv_ref.1) | copy-start | bytes 786436
  2.3 0.7 copy-start.8
  4.6 1.2 %copy-start = (bf16[256,2048]{1,0:T(8,128)(2,1)S(1)}, bf16[256,2048]{1,0:T(8,128)(2,1)}, u32[]{:S(2)}) copy-start(bf16[256,2048]{1,0:T(8,128)(2,1)} %f_own.3) | copy-start | bytes 3145732
  7.2 12.4 %collective-permute-start.2 = (f32[8,96,128]{2,1,0:T(8,128)S(1)}, f32[8,96,128]{2,1,0:T(8,128)S(1)}, u32[]{:S(2)}, u32[]{:S(2)}) collective-permute-start(f32[8,96,128]{2,1,0:T(8,128)S(1)} %get-tuple-element.34), channel_id=1, source_target_pairs={{0,2},{2,0},{4,6},{6,4},{8,10},{10,8},{12,14},{14,12},{16,18},{18,... | collective-permute-start | bytes 1179656 | tf_op jit(solution)/shard_map/ppermute | solution.py:116
  10.2 11.2 %collective-permute-start.3 = (f32[8,96,128]{2,1,0:T(8,128)S(1)}, f32[8,96,128]{2,1,0:T(8,128)S(1)}, u32[]{:S(2)}, u32[]{:S(2)}) collective-permute-start(f32[8,96,128]{2,1,0:T(8,128)S(1)} %get-tuple-element.36), channel_id=1, source_target_pairs={{0,4},{2,6},{4,0},{6,2},{8,12},{10,14},{12,8},{14,10},{16,20},{18,... | collective-permute-start | bytes 1179656 | tf_op jit(solution)/shard_map/ppermute | solution.py:116
  13.1 10.0 %collective-permute-start.7 = (f32[16,32,128]{2,1,0:T(8,128)S(1)}, f32[16,32,128]{2,1,0:T(8,128)S(1)}, u32[]{:S(2)}, u32[]{:S(2)}) collective-permute-start(f32[16,32,128]{2,1,0:T(8,128)S(1)} %get-tuple-element.38), channel_id=1, source_target_pairs={{0,8},{2,10},{4,12},{6,14},{8,0},{10,2},{12,4},{14,6},{16,24},{18,... | collective-permute-start | bytes 786440 | tf_op jit(solution)/shard_map/ppermute | solution.py:116
  19.6 6.4 %collective-permute-start.4 = (f32[4,96,128]{2,1,0:T(8,128)S(1)}, f32[4,96,128]{2,1,0:T(8,128)S(1)}, u32[]{:S(2)}, u32[]{:S(2)}) collective-permute-start(f32[4,96,128]{2,1,0:T(8,128)S(1)} %get-tuple-element.60), channel_id=1, source_target_pairs={{0,4},{2,6},{4,0},{6,2},{8,12},{10,14},{12,8},{14,10},{16,20},{18,... | collective-permute-start | bytes 589832 | tf_op jit(solution)/shard_map/ppermute | solution.py:116
  21.4 15.6 %copy-start.1 = (bf16[1,4,128,128]{3,2,1,0:T(8,128)(2,1)S(1)}, bf16[1,4,128,128]{3,2,1,0:T(8,128)(2,1)}, u32[]{:S(2)}) copy-start(bf16[1,4,128,128]{3,2,1,0:T(8,128)(2,1)} %ql_ref.3) | copy-start | bytes 393220
  21.4 15.6 %copy-start.2 = (bf16[1,4,128,128]{3,2,1,0:T(8,128)(2,1)S(1)}, bf16[1,4,128,128]{3,2,1,0:T(8,128)(2,1)}, u32[]{:S(2)}) copy-start(bf16[1,4,128,128]{3,2,1,0:T(8,128)(2,1)} %qr_ref.3) | copy-start | bytes 393220
  21.4 15.6 %copy-start.3 = (f32[1,4,128,128]{3,2,1,0:T(8,128)S(1)}, f32[1,4,128,128]{3,2,1,0:T(8,128)}, u32[]{:S(2)}) copy-start(f32[1,4,128,128]{3,2,1,0:T(8,128)} %m_ref.1) | copy-start | bytes 786436
  21.5 15.6 %copy-start.4 = (f32[1,4,128,128]{3,2,1,0:T(8,128)S(1)}, f32[1,4,128,128]{3,2,1,0:T(8,128)}, u32[]{:S(2)}) copy-start(f32[1,4,128,128]{3,2,1,0:T(8,128)} %v_ref.1) | copy-start | bytes 786436
  21.5 15.6 %copy-start.5 = (f32[1,4,128,128]{3,2,1,0:T(8,128)S(1)}, f32[1,4,128,128]{3,2,1,0:T(8,128)}, u32[]{:S(2)}) copy-start(f32[1,4,128,128]{3,2,1,0:T(8,128)} %l_ref.1) | copy-start | bytes 786436
  21.5 15.6 %copy-start.6 = (f32[1,4,128,128]{3,2,1,0:T(8,128)S(1)}, f32[1,4,128,128]{3,2,1,0:T(8,128)}, u32[]{:S(2)}) copy-start(f32[1,4,128,128]{3,2,1,0:T(8,128)} %r_ref.1) | copy-start | bytes 786436
  21.5 5.8 %collective-permute-start.5 = (f32[4,96,128]{2,1,0:T(8,128)S(1)}, f32[4,96,128]{2,1,0:T(8,128)S(1)}, u32[]{:S(2)}, u32[]{:S(2)}) collective-permute-start(f32[4,96,128]{2,1,0:T(8,128)S(1)} %get-tuple-element.62), channel_id=1, source_target_pairs={{0,2},{2,0},{4,6},{6,4},{8,10},{10,8},{12,14},{14,12},{16,18},{18,... | collective-permute-start | bytes 589832 | tf_op jit(solution)/shard_map/ppermute | solution.py:116
  23.2 8.0 %collective-permute-start.8 = (f32[8,32,128]{2,1,0:T(8,128)S(1)}, f32[8,32,128]{2,1,0:T(8,128)S(1)}, u32[]{:S(2)}, u32[]{:S(2)}) collective-permute-start(f32[8,32,128]{2,1,0:T(8,128)S(1)} %get-tuple-element.64), channel_id=1, source_target_pairs={{0,16},{2,18},{4,20},{6,22},{8,24},{10,26},{12,28},{14,30},{16,0},... | collective-permute-start | bytes 393224 | tf_op jit(solution)/shard_map/ppermute | solution.py:116
  27.4 6.4 %collective-permute-start.6 = (f32[2,2,96,128]{3,2,1,0:T(8,128)S(1)}, f32[2,2,96,128]{3,2,1,0:T(8,128)S(1)}, u32[]{:S(2)}, u32[]{:S(2)}) collective-permute-start(f32[2,2,96,128]{3,2,1,0:T(8,128)S(1)} %get-tuple-element.58), channel_id=1, source_target_pairs={{0,8},{2,10},{4,12},{6,14},{8,0},{10,2},{12,4},{14,6},{16,24},{18,... | collective-permute-start | bytes 589832 | tf_op jit(solution)/shard_map/ppermute | solution.py:116
  31.1 4.8 %collective-permute-start.10 = (f32[4,32,128]{2,1,0:T(8,128)S(1)}, f32[4,32,128]{2,1,0:T(8,128)S(1)}, u32[]{:S(2)}, u32[]{:S(2)}) collective-permute-start(f32[4,32,128]{2,1,0:T(8,128)S(1)} %get-tuple-element.68), channel_id=1, source_target_pairs={{0,2},{2,0},{4,6},{6,4},{8,10},{10,8},{12,14},{14,12},{16,18},{18,... | collective-permute-start | bytes 196616 | tf_op jit(solution)/shard_map/ppermute | solution.py:116
  33.9 6.9 %collective-permute-start.9 = (f32[2,96,128]{2,1,0:T(8,128)S(1)}, f32[2,96,128]{2,1,0:T(8,128)S(1)}, u32[]{:S(2)}, u32[]{:S(2)}) collective-permute-start(f32[2,96,128]{2,1,0:T(8,128)S(1)} %bitcast.17), channel_id=1, source_target_pairs={{0,16},{2,18},{4,20},{6,22},{8,24},{10,26},{12,28},{14,30},{16,0},... | collective-permute-start | bytes 294920 | tf_op jit(solution)/shard_map/ppermute | solution.py:116
  35.9 4.0 %collective-permute-start.11 = (f32[2,32,128]{2,1,0:T(8,128)S(1)}, f32[2,32,128]{2,1,0:T(8,128)S(1)}, u32[]{:S(2)}, u32[]{:S(2)}) collective-permute-start(f32[2,32,128]{2,1,0:T(8,128)S(1)} %get-tuple-element.69), channel_id=1, source_target_pairs={{0,4},{2,6},{4,0},{6,2},{8,12},{10,14},{12,8},{14,10},{16,20},{18,... | collective-permute-start | bytes 98312 | tf_op jit(solution)/shard_map/ppermute | solution.py:116
  41.5 7.2 %collective-permute-start.14 = (bf16[2,128,128]{2,1,0:T(8,128)(2,1)S(1)}, bf16[2,128,128]{2,1,0:T(8,128)(2,1)S(1)}, u32[]{:S(2)}, u32[]{:S(2)}) collective-permute-start(bf16[2,128,128]{2,1,0:T(8,128)(2,1)S(1)} %get-tuple-element.42), channel_id=1, source_target_pairs={{0,24},{2,26},{4,28},{6,30},{8,16},{10,18},{12,20},{14,22},{16,8},... | collective-permute-start | bytes 196616 | tf_op jit(solution)/shard_map/ppermute | solution.py:116
  44.3 4.5 %collective-permute-start.13 = (bf16[2,128,128]{2,1,0:T(8,128)(2,1)S(1)}, bf16[2,128,128]{2,1,0:T(8,128)(2,1)S(1)}, u32[]{:S(2)}, u32[]{:S(2)}) collective-permute-start(bf16[2,128,128]{2,1,0:T(8,128)(2,1)S(1)} %get-tuple-element.42), channel_id=1, source_target_pairs={{0,8},{2,10},{4,12},{6,14},{8,0},{10,2},{12,4},{14,6},{16,24},{18,... | collective-permute-start | bytes 196616 | tf_op jit(solution)/shard_map/ppermute | solution.py:116
  44.3 5.2 %collective-permute-start.12 = (bf16[2,128,128]{2,1,0:T(8,128)(2,1)S(1)}, bf16[2,128,128]{2,1,0:T(8,128)(2,1)S(1)}, u32[]{:S(2)}, u32[]{:S(2)}) collective-permute-start(bf16[2,128,128]{2,1,0:T(8,128)(2,1)S(1)} %get-tuple-element.42), channel_id=1, source_target_pairs={{0,16},{2,18},{4,20},{6,22},{8,24},{10,26},{12,28},{14,30},{16,0},... | collective-permute-start | bytes 196616 | tf_op jit(solution)/shard_map/ppermute | solution.py:116
  49.5 5.8 %collective-permute-start.15 = (bf16[4,128,128]{2,1,0:T(8,128)(2,1)S(1)}, bf16[4,128,128]{2,1,0:T(8,128)(2,1)S(1)}, u32[]{:S(2)}, u32[]{:S(2)}) collective-permute-start(bf16[4,128,128]{2,1,0:T(8,128)(2,1)S(1)} %get-tuple-element.45), channel_id=1, source_target_pairs={{0,4},{2,6},{4,0},{6,2},{8,12},{10,14},{12,8},{14,10},{16,20},{18,... | collective-permute-start | bytes 393224 | tf_op jit(solution)/shard_map/ppermute | solution.py:116
  50.5 6.4 %collective-permute-start.16 = (bf16[4,128,128]{2,1,0:T(8,128)(2,1)S(1)}, bf16[4,128,128]{2,1,0:T(8,128)(2,1)S(1)}, u32[]{:S(2)}, u32[]{:S(2)}) collective-permute-start(bf16[4,128,128]{2,1,0:T(8,128)(2,1)S(1)} %get-tuple-element.46), channel_id=1, source_target_pairs={{0,2},{2,0},{4,6},{6,4},{8,10},{10,8},{12,14},{14,12},{16,18},{18,... | collective-permute-start | bytes 393224 | tf_op jit(solution)/shard_map/ppermute | solution.py:116
  56.9 6.4 %collective-permute-start.18 = (bf16[8,128,128]{2,1,0:T(8,128)(2,1)S(1)}, bf16[8,128,128]{2,1,0:T(8,128)(2,1)S(1)}, u32[]{:S(2)}, u32[]{:S(2)}) collective-permute-start(bf16[8,128,128]{2,1,0:T(8,128)(2,1)S(1)} %pad_maximum_fusion.refs_0_), channel_id=1, source_target_pairs={{0,2},{2,0},{4,6},{6,4},{8,10},{10,8},{12,14},{14,12},{16,18},{18,... | collective-permute-start | bytes 786440 | tf_op jit(solution)/shard_map/ppermute | solution.py:116
  58.0 6.4 %collective-permute-start.19 = (bf16[8,128,128]{2,1,0:T(8,128)(2,1)S(1)}, bf16[8,128,128]{2,1,0:T(8,128)(2,1)S(1)}, u32[]{:S(2)}, u32[]{:S(2)}) collective-permute-start(bf16[8,128,128]{2,1,0:T(8,128)(2,1)S(1)} %pad_maximum_fusion.1.refs_1_), channel_id=1, source_target_pairs={{0,4},{2,6},{4,0},{6,2},{8,12},{10,14},{12,8},{14,10},{16,20},{18,... | collective-permute-start | bytes 786440 | tf_op jit(solution)/shard_map/ppermute | solution.py:116
  59.5 1.3 %collective-permute-start.17 = (bf16[4,128,128]{2,1,0:T(8,128)(2,1)S(1)}, bf16[4,128,128]{2,1,0:T(8,128)(2,1)S(1)}, u32[]{:S(2)}, u32[]{:S(2)}) collective-permute-start(bf16[4,128,128]{2,1,0:T(8,128)(2,1)S(1)} %finish.1.own_ref), channel_id=1, source_target_pairs={{0,1},{1,0},{2,3},{3,2},{4,5},{5,4},{6,7},{7,6},{8,9},{9,8},{10,11... | collective-permute-start | bytes 393224 | tf_op jit(solution)/shard_map/ppermute | solution.py:116
  59.5 5.4 %collective-permute-start.22 = (bf16[8,128,128]{2,1,0:T(8,128)(2,1)S(1)}, bf16[8,128,128]{2,1,0:T(8,128)(2,1)S(1)}, u32[]{:S(2)}, u32[]{:S(2)}) collective-permute-start(bf16[8,128,128]{2,1,0:T(8,128)(2,1)S(1)} %pad_maximum_fusion.refs_0_), channel_id=1, source_target_pairs={{0,1},{1,0},{2,3},{3,2},{4,5},{5,4},{6,7},{7,6},{8,9},{9,8},{10,11... | collective-permute-start | bytes 786440 | tf_op jit(solution)/shard_map/ppermute | solution.py:116
  60.0 4.9 %collective-permute-start.23 = (bf16[8,128,128]{2,1,0:T(8,128)(2,1)S(1)}, bf16[8,128,128]{2,1,0:T(8,128)(2,1)S(1)}, u32[]{:S(2)}, u32[]{:S(2)}) collective-permute-start(bf16[8,128,128]{2,1,0:T(8,128)(2,1)S(1)} %pad_maximum_fusion.1.refs_1_), channel_id=1, source_target_pairs={{0,1},{1,0},{2,3},{3,2},{4,5},{5,4},{6,7},{7,6},{8,9},{9,8},{10,11... | collective-permute-start | bytes 786440 | tf_op jit(solution)/shard_map/ppermute | solution.py:116
  64.3 2.3 %collective-permute-start.20 = (bf16[8,128,128]{2,1,0:T(8,128)(2,1)S(1)}, bf16[8,128,128]{2,1,0:T(8,128)(2,1)S(1)}, u32[]{:S(2)}, u32[]{:S(2)}) collective-permute-start(bf16[8,128,128]{2,1,0:T(8,128)(2,1)S(1)} %collective-permute-done.18.refs_2_), channel_id=1, source_target_pairs={{0,1},{1,0},{2,3},{3,2},{4,5},{5,4},{6,7},{7,6},{8,9},{9,8},{10,11... | collective-permute-start | bytes 786440 | tf_op jit(solution)/shard_map/ppermute | solution.py:116
  64.3 2.3 %collective-permute-start.21 = (bf16[8,128,128]{2,1,0:T(8,128)(2,1)S(1)}, bf16[8,128,128]{2,1,0:T(8,128)(2,1)S(1)}, u32[]{:S(2)}, u32[]{:S(2)}) collective-permute-start(bf16[8,128,128]{2,1,0:T(8,128)(2,1)S(1)} %collective-permute-done.19.refs_3_), channel_id=1, source_target_pairs={{0,1},{1,0},{2,3},{3,2},{4,5},{5,4},{6,7},{7,6},{8,9},{9,8},{10,11... | collective-permute-start | bytes 786440 | tf_op jit(solution)/shard_map/ppermute | solution.py:116

commit v12 on v11

--- a/solution.py
+++ b/solution.py
@@ -172,20 +172,23 @@
 
 
 def table_kernel(owners, capacity, place_ref, owner_ref, kv_ref, *rest):
-    table_ref, own_rows, count, held = rest
+    table_ref, own_rows, held = rest
     own_rows[...] = kv_ref[...].T
 
-    for o in range(owners):
-        count[o] = 0
-
-    def enter(b, carry):
+
+    def enter(b, counts):
         o = owner_ref[b]
-        s = count[o]
-        count[o] = s + 1
+        shift = 4 * (o & 7)
+        low = o < 8
+        s = (jnp.where(low, counts[0], counts[1]) >> shift) & 15
         held[o * capacity + s] = b
-        return carry
-
-    lax.fori_loop(0, owners * capacity, enter, 0, unroll=8)
+        one = jnp.int32(1) << shift
+        return (
+            counts[0] + jnp.where(low, one, 0),
+            counts[1] + jnp.where(low, 0, one),
+        )
+
+    lax.fori_loop(0, owners * capacity, enter, (jnp.int32(0), jnp.int32(0)), unroll=16)
     here, core = place_ref[0], place_ref[1]
     offsets = stream_offsets(owners)[1]
     for side in range(2):
@@ -445,7 +448,6 @@
         out_specs=(SMEM, VMEM),
         compiler_params=SMALL,
         scratch_shapes=[
-            pltpu.SMEM((owners,), jnp.int32),
             pltpu.SMEM((owners * capacity,), jnp.int32),
         ],
         cost_estimate=pl.CostEstimate(flops=0, bytes_accessed=1_000_000, transcendentals=0),
@@ -576,7 +578,7 @@
     def per_device(*args):
         capacity = args[-1].shape[1]
         full = args[2].shape[0] == owners * capacity
-        if full and inner == 2 and capacity == 4 and owners >= 8 and owners & (owners - 1) == 0:
+        if full and inner == 2 and capacity == 4 and 8 <= owners <= 16 and owners & (owners - 1) == 0:
             return per_device_dealt(owners, *args)
         return per_device_plain(*args)
 

time: 68.3 us -> 68.3 us (level)
  no operation moved by 1% of the time
where the time goes in v12:
time: 68.3 us; the launch traced here: 68.1 us
  starting transfers between devices  28.3 us (41%)
  waiting for transfers between devices  19.4 us (28%)
  Pallas kernels  16.3 us (24%)
  local copies, waits for them, and re-layouts  2.88 us (4%)
  between operations  0.88 us (1%)
    ppermute x24, starting transfers between devices, swap_along(): return lax.ppermute(values, axis, [(i, i ^ bit) for i in range(size)])  28.3 us
    ppermute x24, waiting for transfers between devices, swap_along(): return lax.ppermute(values, axis, [(i, i ^ bit) for i in range(size)])  19.4 us
    pallas_call x3, Pallas kernels, on_slots(): pl.pallas_call(kernel, out_shape=tuple(outs), grid_spec=pltpu.PrefetchSca...  3.99 us
    pallas_call x2, Pallas kernels, place_more(): pl.pallas_call(functools.partial(more_kernel, col_tiles, entries), out_sh...  3.25 us
    pallas_call x1, Pallas kernels, sweeping(): pl.pallas_call(kernel, out_shape=jax.ShapeDtypeStruct(values.shape, dtype...  2.89 us
    unnamed x18, local copies, waits for them, and re-layouts  2.85 us
    pallas_call x2, Pallas kernels, tiles_from(): pl.pallas_call(functools.partial(tiles_kernel, owners, first), out_shape=...  2.83 us
    pallas_call x1, Pallas kernels, per_device_dealt(): pl.pallas_call(functools.partial(table_kernel, owners, capacity), out_sha...  1.67 us
  transfers between devices with their start and end apart: 24, of which 13 were waited for; matrix products, arithmetic and copies ran while one was open for 1% of the time, Pallas kernels for 19%

profile of v12, /device:TPU:0, one launch (start us, length us, event | category | flops | bytes accessed | tf_op | source)
XLA Modules:
  0.0 68.1 jit_solution(18320993884962805737)
XLA Ops:
  0.6 0.5 collective-permute-start
  1.1 0.1 collective-permute-start.1
  1.2 0.1 pad_add_fusion.place_ref
  1.3 0.9 %copy-done.7 = bf16[256,512]{1,0:T(8,128)(2,1)S(1)} copy-done((bf16[256,512]{1,0:T(8,128)(2,1)S(1)}, bf16[256,512]{1,0:T(8,128)(2,1)}, u32[]{:S(2)}) %copy-start.7) | copy-done | bytes 262168
  2.3 0.7 copy-done.8
  2.9 1.7 %table.1 = (s32[64]{0:T(128)S(1)}, bf16[512,256]{1,0:T(8,128)(2,1)S(1)}) custom-call(s32[2]{0:T(128)S(1)} %pad_add_fusion.place_ref, s32[64]{0:T(128)S(1)} %copy-done.8, bf16[256,512]{1,0:T(8,128)(2,1)S(1)} %copy-done.7), custom_call_target="tpu_custom_call" | custom-call | bytes 1000000 | tf_op jit(solution)/shard_map/table/pallas_call | solution.py:441
  4.6 1.2 %copy-done = bf16[256,2048]{1,0:T(8,128)(2,1)S(1)} copy-done((bf16[256,2048]{1,0:T(8,128)(2,1)S(1)}, bf16[256,2048]{1,0:T(8,128)(2,1)}, u32[]{:S(2)}) %copy-start) | copy-done | bytes 1048600
  5.8 1.4 %tiles.2 = (f32[8,96,128]{2,1,0:T(8,128)S(1)}, f32[8,96,128]{2,1,0:T(8,128)S(1)}, f32[32,32,128]{2,1,0:T(8,128)S(1)}) custom-call(s32[64]{0:T(128)S(1)} %get-tuple-element.30.table_ref, bf16[256,2048]{1,0:T(8,128)(2,1)S(1)} %copy-done, bf16[256,2048]{1,0:T(8,128)(2,1)S(1)} %collective-permute-done.f_sib, bf16[512,256]{1,0:T(8,128)(2,1)S(1)} %get-tuple-element.31.own_rows, ...), custom_call_target="tpu_custom_call" | custom-call | flops 536870912 | bytes 3500000 | tf_op jit(solution)/shard_map/tiles/pallas_call | solution.py:459
  7.2 3.0 %collective-permute-start.2 = (f32[8,96,128]{2,1,0:T(8,128)S(1)}, f32[8,96,128]{2,1,0:T(8,128)S(1)}, u32[]{:S(2)}, u32[]{:S(2)}) collective-permute-start(f32[8,96,128]{2,1,0:T(8,128)S(1)} %get-tuple-element.34), channel_id=1, source_target_pairs={{0,2},{2,0},{4,6},{6,4},{8,10},{10,8},{12,14},{14,12},{16,18},{18,... | collective-permute-start | bytes 1179656 | tf_op jit(solution)/shard_map/ppermute | solution.py:116
  10.2 1.5 %collective-permute-start.3 = (f32[8,96,128]{2,1,0:T(8,128)S(1)}, f32[8,96,128]{2,1,0:T(8,128)S(1)}, u32[]{:S(2)}, u32[]{:S(2)}) collective-permute-start(f32[8,96,128]{2,1,0:T(8,128)S(1)} %get-tuple-element.36), channel_id=1, source_target_pairs={{0,4},{2,6},{4,0},{6,2},{8,12},{10,14},{12,8},{14,10},{16,20},{18,... | collective-permute-start | bytes 1179656 | tf_op jit(solution)/shard_map/ppermute | solution.py:116
  11.7 1.4 %tiles.3 = (f32[8,96,128]{2,1,0:T(8,128)S(1)}, f32[8,96,128]{2,1,0:T(8,128)S(1)}, f32[16,32,128]{2,1,0:T(8,128)S(1)}, f32[16,32,128]{2,1,0:T(8,128)S(1)}) custom-call(s32[64]{0:T(128)S(1)} %get-tuple-element.30.table_ref, bf16[256,2048]{1,0:T(8,128)(2,1)S(1)} %copy-done, bf16[256,2048]{1,0:T(8,128)(2,1)S(1)} %collective-permute-done.f_sib, ...), custom_call_target="tpu_custom_call" | custom-call | flops 536870912 | bytes 3500000 | tf_op jit(solution)/shard_map/tiles/pallas_call | solution.py:459
  13.2 1.6 %collective-permute-start.7 = (f32[16,32,128]{2,1,0:T(8,128)S(1)}, f32[16,32,128]{2,1,0:T(8,128)S(1)}, u32[]{:S(2)}, u32[]{:S(2)}) collective-permute-start(f32[16,32,128]{2,1,0:T(8,128)S(1)} %get-tuple-element.38), channel_id=1, source_target_pairs={{0,8},{2,10},{4,12},{6,14},{8,0},{10,2},{12,4},{14,6},{16,24},{18,... | collective-permute-start | bytes 786440 | tf_op jit(solution)/shard_map/ppermute | solution.py:116
  14.8 4.8 %collective-permute-done.2 = f32[8,96,128]{2,1,0:T(8,128)S(1)} collective-permute-done((f32[8,96,128]{2,1,0:T(8,128)S(1)}, f32[8,96,128]{2,1,0:T(8,128)S(1)}, u32[]{:S(2)}, u32[]{:S(2)}) %collective-permute-start.2) | collective-permute-done | bytes 393248 | tf_op jit(solution)/shard_map/ppermute | solution.py:116
  19.6 1.8 %collective-permute-start.4 = (f32[4,96,128]{2,1,0:T(8,128)S(1)}, f32[4,96,128]{2,1,0:T(8,128)S(1)}, u32[]{:S(2)}, u32[]{:S(2)}) collective-permute-start(f32[4,96,128]{2,1,0:T(8,128)S(1)} %get-tuple-element.60), channel_id=1, source_target_pairs={{0,4},{2,6},{4,0},{6,2},{8,12},{10,14},{12,8},{14,10},{16,20},{18,... | collective-permute-start | bytes 589832 | tf_op jit(solution)/shard_map/ppermute | solution.py:116
  21.6 1.6 %collective-permute-start.5 = (f32[4,96,128]{2,1,0:T(8,128)S(1)}, f32[4,96,128]{2,1,0:T(8,128)S(1)}, u32[]{:S(2)}, u32[]{:S(2)}) collective-permute-start(f32[4,96,128]{2,1,0:T(8,128)S(1)} %get-tuple-element.62), channel_id=1, source_target_pairs={{0,2},{2,0},{4,6},{6,4},{8,10},{10,8},{12,14},{14,12},{16,18},{18,... | collective-permute-start | bytes 589832 | tf_op jit(solution)/shard_map/ppermute | solution.py:116
  23.2 2.7 %collective-permute-start.8 = (f32[8,32,128]{2,1,0:T(8,128)S(1)}, f32[8,32,128]{2,1,0:T(8,128)S(1)}, u32[]{:S(2)}, u32[]{:S(2)}) collective-permute-start(f32[8,32,128]{2,1,0:T(8,128)S(1)} %get-tuple-element.64), channel_id=1, source_target_pairs={{0,16},{2,18},{4,20},{6,22},{8,24},{10,26},{12,28},{14,30},{16,0},... | collective-permute-start | bytes 393224 | tf_op jit(solution)/shard_map/ppermute | solution.py:116
  25.8 0.2 collective-permute-done.4
  26.1 1.4 %collective-permute-done.5 = f32[4,96,128]{2,1,0:T(8,128)S(1)} collective-permute-done((f32[4,96,128]{2,1,0:T(8,128)S(1)}, f32[4,96,128]{2,1,0:T(8,128)S(1)}, u32[]{:S(2)}, u32[]{:S(2)}) %collective-permute-start.5) | collective-permute-done | bytes 196640 | tf_op jit(solution)/shard_map/ppermute | solution.py:116
  27.4 0.1 fusion.1
  27.5 1.6 %collective-permute-start.6 = (f32[2,2,96,128]{3,2,1,0:T(8,128)S(1)}, f32[2,2,96,128]{3,2,1,0:T(8,128)S(1)}, u32[]{:S(2)}, u32[]{:S(2)}) collective-permute-start(f32[2,2,96,128]{3,2,1,0:T(8,128)S(1)} %get-tuple-element.58), channel_id=1, source_target_pairs={{0,8},{2,10},{4,12},{6,14},{8,0},{10,2},{12,4},{14,6},{16,24},{18,... | collective-permute-start | bytes 589832 | tf_op jit(solution)/shard_map/ppermute | solution.py:116
  29.1 2.0 %collective-permute-done.8 = f32[8,32,128]{2,1,0:T(8,128)S(1)} collective-permute-done((f32[8,32,128]{2,1,0:T(8,128)S(1)}, f32[8,32,128]{2,1,0:T(8,128)S(1)}, u32[]{:S(2)}, u32[]{:S(2)}) %collective-permute-start.8) | collective-permute-done | bytes 131104 | tf_op jit(solution)/shard_map/ppermute | solution.py:116
  31.2 0.6 collective-permute-start.10
  31.8 2.1 %collective-permute-done.6 = f32[2,2,96,128]{3,2,1,0:T(8,128)S(1)} collective-permute-done((f32[2,2,96,128]{3,2,1,0:T(8,128)S(1)}, f32[2,2,96,128]{3,2,1,0:T(8,128)S(1)}, u32[]{:S(2)}, u32[]{:S(2)}) %collective-permute-start.6) | collective-permute-done | bytes 196640 | tf_op jit(solution)/shard_map/ppermute | solution.py:116
  33.9 2.1 %collective-permute-start.9 = (f32[2,96,128]{2,1,0:T(8,128)S(1)}, f32[2,96,128]{2,1,0:T(8,128)S(1)}, u32[]{:S(2)}, u32[]{:S(2)}) collective-permute-start(f32[2,96,128]{2,1,0:T(8,128)S(1)} %bitcast.17), channel_id=1, source_target_pairs={{0,16},{2,18},{4,20},{6,22},{8,24},{10,26},{12,28},{14,30},{16,0},... | collective-permute-start | bytes 294920 | tf_op jit(solution)/shard_map/ppermute | solution.py:116
  36.0 1.1 %collective-permute-start.11 = (f32[2,32,128]{2,1,0:T(8,128)S(1)}, f32[2,32,128]{2,1,0:T(8,128)S(1)}, u32[]{:S(2)}, u32[]{:S(2)}) collective-permute-start(f32[2,32,128]{2,1,0:T(8,128)S(1)} %get-tuple-element.69), channel_id=1, source_target_pairs={{0,4},{2,6},{4,0},{6,2},{8,12},{10,14},{12,8},{14,10},{16,20},{18,... | collective-permute-start | bytes 98312 | tf_op jit(solution)/shard_map/ppermute | solution.py:116
  37.1 0.5 rotated.1
  37.6 2.4 %collective-permute-done.11.d_ref = f32[2,32,128]{2,1,0:T(8,128)S(1)} collective-permute-done((f32[2,32,128]{2,1,0:T(8,128)S(1)}, f32[2,32,128]{2,1,0:T(8,128)S(1)}, u32[]{:S(2)}, u32[]{:S(2)}) %collective-permute-start.11) | collective-permute-done | bytes 32800 | tf_op jit(solution)/shard_map/ppermute | solution.py:116
  40.0 0.8 %collective-permute-done.9.b_ref = f32[2,96,128]{2,1,0:T(8,128)S(1)} collective-permute-done((f32[2,96,128]{2,1,0:T(8,128)S(1)}, f32[2,96,128]{2,1,0:T(8,128)S(1)}, u32[]{:S(2)}, u32[]{:S(2)}) %collective-permute-start.9) | collective-permute-done | bytes 98336 | tf_op jit(solution)/shard_map/ppermute | solution.py:116
  40.8 0.7 %direction.1 = (bf16[2,128,128]{2,1,0:T(8,128)(2,1)S(1)}, f32[2,128,128]{2,1,0:T(8,128)S(1)}) custom-call(s32[1]{0:T(128)} %bitcast.1.side_ref, f32[2,96,128]{2,1,0:T(8,128)S(1)} %get-tuple-element.66.a_ref, f32[2,96,128]{2,1,0:T(8,128)S(1)} %collective-permute-done.9.b_ref, f32[2,32,128]{2,1,0:T(8,128)S(1)} %get-tuple-element.70.c_ref, ...), custom_call_target="tpu_custom_call" | custom-call | flops 67108864 | bytes 800000 | tf_op jit(solution)/shard_map/direction/pallas_call | solution.py:294
  41.5 2.7 %collective-permute-start.14 = (bf16[2,128,128]{2,1,0:T(8,128)(2,1)S(1)}, bf16[2,128,128]{2,1,0:T(8,128)(2,1)S(1)}, u32[]{:S(2)}, u32[]{:S(2)}) collective-permute-start(bf16[2,128,128]{2,1,0:T(8,128)(2,1)S(1)} %get-tuple-element.42), channel_id=1, source_target_pairs={{0,24},{2,26},{4,28},{6,30},{8,16},{10,18},{12,20},{14,22},{16,8},... | collective-permute-start | bytes 196616 | tf_op jit(solution)/shard_map/ppermute | solution.py:116
  44.3 1.7 %collective-permute-start.12 = (bf16[2,128,128]{2,1,0:T(8,128)(2,1)S(1)}, bf16[2,128,128]{2,1,0:T(8,128)(2,1)S(1)}, u32[]{:S(2)}, u32[]{:S(2)}) collective-permute-start(bf16[2,128,128]{2,1,0:T(8,128)(2,1)S(1)} %get-tuple-element.42), channel_id=1, source_target_pairs={{0,16},{2,18},{4,20},{6,22},{8,24},{10,26},{12,28},{14,30},{16,0},... | collective-permute-start | bytes 196616 | tf_op jit(solution)/shard_map/ppermute | solution.py:116
  46.0 2.8 %refresh.1.iter_ref = f32[4,128,128]{2,1,0:T(8,128)S(1)} custom-call(s32[1]{0:T(128)} %bitcast.1.side_ref, f32[2,128,128]{2,1,0:T(8,128)S(1)} %get-tuple-element.43.g_ref, f32[4,128,128]{2,1,0:T(8,128)S(1)} %get-tuple-element.44.power_ref, bf16[1,4,128,128]{3,2,1,0:T(8,128)(2,1)S(1)} %copy-done.1, bf16[1,4,128,128]{3,2,1,0:T(8,128)(2,1)S(1)} %copy-done.2), custom_call_target="tpu_custom_call" | custom-call | flops 939524096 | bytes 800000 | tf_op jit(solution)/shard_map/refresh/pallas_call | solution.py:294
  48.8 0.6 collective-permute-done.12
  49.5 1.1 %collective-permute-start.15 = (bf16[4,128,128]{2,1,0:T(8,128)(2,1)S(1)}, bf16[4,128,128]{2,1,0:T(8,128)(2,1)S(1)}, u32[]{:S(2)}, u32[]{:S(2)}) collective-permute-start(bf16[4,128,128]{2,1,0:T(8,128)(2,1)S(1)} %get-tuple-element.45), channel_id=1, source_target_pairs={{0,4},{2,6},{4,0},{6,2},{8,12},{10,14},{12,8},{14,10},{16,20},{18,... | collective-permute-start | bytes 393224 | tf_op jit(solution)/shard_map/ppermute | solution.py:116
  50.5 0.9 %collective-permute-start.16 = (bf16[4,128,128]{2,1,0:T(8,128)(2,1)S(1)}, bf16[4,128,128]{2,1,0:T(8,128)(2,1)S(1)}, u32[]{:S(2)}, u32[]{:S(2)}) collective-permute-start(bf16[4,128,128]{2,1,0:T(8,128)(2,1)S(1)} %get-tuple-element.46), channel_id=1, source_target_pairs={{0,2},{2,0},{4,6},{6,4},{8,10},{10,8},{12,14},{14,12},{16,18},{18,... | collective-permute-start | bytes 393224 | tf_op jit(solution)/shard_map/ppermute | solution.py:116
  51.5 2.9 %finish.1.own_ref = bf16[4,128,128]{2,1,0:T(8,128)(2,1)S(1)} custom-call(f32[4,128,128]{2,1,0:T(8,128)S(1)} %refresh.1.iter_ref), custom_call_target="tpu_custom_call" | custom-call | flops 939524096 | bytes 400000 | tf_op jit(solution)/shard_map/finish/pallas_call | solution.py:344
  54.3 1.0 %collective-permute-done.15 = bf16[4,128,128]{2,1,0:T(8,128)(2,1)S(1)} collective-permute-done((bf16[4,128,128]{2,1,0:T(8,128)(2,1)S(1)}, bf16[4,128,128]{2,1,0:T(8,128)(2,1)S(1)}, u32[]{:S(2)}, u32[]{:S(2)}) %collective-permute-start.15) | collective-permute-done | bytes 131104 | tf_op jit(solution)/shard_map/ppermute | solution.py:116
  55.4 1.5 %collective-permute-done.16 = bf16[4,128,128]{2,1,0:T(8,128)(2,1)S(1)} collective-permute-done((bf16[4,128,128]{2,1,0:T(8,128)(2,1)S(1)}, bf16[4,128,128]{2,1,0:T(8,128)(2,1)S(1)}, u32[]{:S(2)}, u32[]{:S(2)}) %collective-permute-start.16) | collective-permute-done | bytes 131104 | tf_op jit(solution)/shard_map/ppermute | solution.py:116
  56.9 1.0 %collective-permute-start.18 = (bf16[8,128,128]{2,1,0:T(8,128)(2,1)S(1)}, bf16[8,128,128]{2,1,0:T(8,128)(2,1)S(1)}, u32[]{:S(2)}, u32[]{:S(2)}) collective-permute-start(bf16[8,128,128]{2,1,0:T(8,128)(2,1)S(1)} %pad_maximum_fusion.refs_0_), channel_id=1, source_target_pairs={{0,2},{2,0},{4,6},{6,4},{8,10},{10,8},{12,14},{14,12},{16,18},{18,... | collective-permute-start | bytes 786440 | tf_op jit(solution)/shard_map/ppermute | solution.py:116
  57.9 1.7 %collective-permute-start.19 = (bf16[8,128,128]{2,1,0:T(8,128)(2,1)S(1)}, bf16[8,128,128]{2,1,0:T(8,128)(2,1)S(1)}, u32[]{:S(2)}, u32[]{:S(2)}) collective-permute-start(bf16[8,128,128]{2,1,0:T(8,128)(2,1)S(1)} %pad_maximum_fusion.1.refs_1_), channel_id=1, source_target_pairs={{0,4},{2,6},{4,0},{6,2},{8,12},{10,14},{12,8},{14,10},{16,20},{18,... | collective-permute-start | bytes 786440 | tf_op jit(solution)/shard_map/ppermute | solution.py:116
  59.6 0.5 collective-permute-start.22
  60.1 0.8 %collective-permute-done.17.sib_ref = bf16[4,128,128]{2,1,0:T(8,128)(2,1)S(1)} collective-permute-done((bf16[4,128,128]{2,1,0:T(8,128)(2,1)S(1)}, bf16[4,128,128]{2,1,0:T(8,128)(2,1)S(1)}, u32[]{:S(2)}, u32[]{:S(2)}) %collective-permute-start.17) | collective-permute-done | bytes 131104 | tf_op jit(solution)/shard_map/ppermute | solution.py:116
  60.9 1.6 %begin.1 = (bf16[2048,512]{1,0:T(8,128)(2,1)}, bf16[1,4,128,128]{3,2,1,0:T(8,128)(2,1)}, bf16[1,4,128,128]{3,2,1,0:T(8,128)(2,1)}) custom-call(s32[64]{0:T(128)S(1)} %get-tuple-element.30.table_ref, s32[2]{0:T(128)S(1)} %pad_add_fusion.place_ref, bf16[4,128,128]{2,1,0:T(8,128)(2,1)S(1)} %finish.1.own_ref, ...), custom_call_target="tpu_custom_call" | custom-call | bytes 800000 | tf_op jit(solution)/shard_map/begin/pallas_call | solution.py:548
  62.6 0.8 %collective-permute-done.18.refs_2_ = bf16[8,128,128]{2,1,0:T(8,128)(2,1)S(1)} collective-permute-done((bf16[8,128,128]{2,1,0:T(8,128)(2,1)S(1)}, bf16[8,128,128]{2,1,0:T(8,128)(2,1)S(1)}, u32[]{:S(2)}, u32[]{:S(2)}) %collective-permute-start.18) | collective-permute-done | bytes 262176 | tf_op jit(solution)/shard_map/ppermute | solution.py:116
  63.4 0.9 %collective-permute-done.19.refs_3_ = bf16[8,128,128]{2,1,0:T(8,128)(2,1)S(1)} collective-permute-done((bf16[8,128,128]{2,1,0:T(8,128)(2,1)S(1)}, bf16[8,128,128]{2,1,0:T(8,128)(2,1)S(1)}, u32[]{:S(2)}, u32[]{:S(2)}) %collective-permute-start.19) | collective-permute-done | bytes 262176 | tf_op jit(solution)/shard_map/ppermute | solution.py:116
  64.3 0.5 collective-permute-start.21
  64.8 1.8 %more.2.refs_2_ = bf16[2048,512]{1,0:T(8,128)(2,1)} custom-call(s32[64]{0:T(128)S(1)} %get-tuple-element.30.table_ref, bf16[8,128,128]{2,1,0:T(8,128)(2,1)S(1)} %collective-permute-done.22.refs_0_, bf16[8,128,128]{2,1,0:T(8,128)(2,1)S(1)} %collective-permute-done.23.refs_1_, ...), custom_call_target="tpu_custom_call", output_to_operand_aliasing={{}: (5, {})} | custom-call | bytes 1000000 | tf_op jit(solution)/shard_map/more/pallas_call | solution.py:396
  66.6 1.5 %more.3 = bf16[2048,512]{1,0:T(8,128)(2,1)} custom-call(s32[64]{0:T(128)S(1)} %get-tuple-element.30.table_ref, bf16[8,128,128]{2,1,0:T(8,128)(2,1)S(1)} %collective-permute-done.20.refs_0_, bf16[8,128,128]{2,1,0:T(8,128)(2,1)S(1)} %collective-permute-done.21.refs_1_, bf16[2048,512]{1,0:T(8,128)(2,1)} %more.2.refs_2_), custom_call_target="tpu_custom_call", output_to_operand_aliasing={{}: (3, {})} | custom-call | bytes 1000000 | tf_op jit(solution)/shard_map/more/pallas_call | solution.py:396
  (43 shorter events, 0.4 us)
Async XLA Ops:
  0.6 4.0 %collective-permute-start = (bf16[256,2048]{1,0:T(8,128)(2,1)}, bf16[256,2048]{1,0:T(8,128)(2,1)S(1)}, u32[]{:S(2)}, u32[]{:S(2)}) collective-permute-start(bf16[256,2048]{1,0:T(8,128)(2,1)} %f_own.3), channel_id=1, source_target_pairs={{0,1},{1,0},{2,3},{3,2},{4,5},{5,4},{6,7},{7,6},{8,9},{9,8},{10,11... | collective-permute-start | bytes 3145736 | tf_op jit(solution)/shard_map/ppermute | solution.py:116
  1.1 3.4 %collective-permute-start.1 = (bf16[256,512]{1,0:T(8,128)(2,1)}, bf16[256,512]{1,0:T(8,128)(2,1)S(1)}, u32[]{:S(2)}, u32[]{:S(2)}) collective-permute-start(bf16[256,512]{1,0:T(8,128)(2,1)} %kv_ref.1), channel_id=1, source_target_pairs={{0,1},{1,0},{2,3},{3,2},{4,5},{5,4},{6,7},{7,6},{8,9},{9,8},{10,11... | collective-permute-start | bytes 786440 | tf_op jit(solution)/shard_map/ppermute | solution.py:116
  1.3 0.9 %copy-start.7 = (bf16[256,512]{1,0:T(8,128)(2,1)S(1)}, bf16[256,512]{1,0:T(8,128)(2,1)}, u32[]{:S(2)}) copy-start(bf16[256,512]{1,0:T(8,128)(2,1)} %kv_ref.1) | copy-start | bytes 786436
  2.3 0.7 copy-start.8
  4.6 1.2 %copy-start = (bf16[256,2048]{1,0:T(8,128)(2,1)S(1)}, bf16[256,2048]{1,0:T(8,128)(2,1)}, u32[]{:S(2)}) copy-start(bf16[256,2048]{1,0:T(8,128)(2,1)} %f_own.3) | copy-start | bytes 3145732
  7.2 12.3 %collective-permute-start.2 = (f32[8,96,128]{2,1,0:T(8,128)S(1)}, f32[8,96,128]{2,1,0:T(8,128)S(1)}, u32[]{:S(2)}, u32[]{:S(2)}) collective-permute-start(f32[8,96,128]{2,1,0:T(8,128)S(1)} %get-tuple-element.34), channel_id=1, source_target_pairs={{0,2},{2,0},{4,6},{6,4},{8,10},{10,8},{12,14},{14,12},{16,18},{18,... | collective-permute-start | bytes 1179656 | tf_op jit(solution)/shard_map/ppermute | solution.py:116
  10.2 11.3 %collective-permute-start.3 = (f32[8,96,128]{2,1,0:T(8,128)S(1)}, f32[8,96,128]{2,1,0:T(8,128)S(1)}, u32[]{:S(2)}, u32[]{:S(2)}) collective-permute-start(f32[8,96,128]{2,1,0:T(8,128)S(1)} %get-tuple-element.36), channel_id=1, source_target_pairs={{0,4},{2,6},{4,0},{6,2},{8,12},{10,14},{12,8},{14,10},{16,20},{18,... | collective-permute-start | bytes 1179656 | tf_op jit(solution)/shard_map/ppermute | solution.py:116
  13.2 10.0 %collective-permute-start.7 = (f32[16,32,128]{2,1,0:T(8,128)S(1)}, f32[16,32,128]{2,1,0:T(8,128)S(1)}, u32[]{:S(2)}, u32[]{:S(2)}) collective-permute-start(f32[16,32,128]{2,1,0:T(8,128)S(1)} %get-tuple-element.38), channel_id=1, source_target_pairs={{0,8},{2,10},{4,12},{6,14},{8,0},{10,2},{12,4},{14,6},{16,24},{18,... | collective-permute-start | bytes 786440 | tf_op jit(solution)/shard_map/ppermute | solution.py:116
  19.6 6.4 %collective-permute-start.4 = (f32[4,96,128]{2,1,0:T(8,128)S(1)}, f32[4,96,128]{2,1,0:T(8,128)S(1)}, u32[]{:S(2)}, u32[]{:S(2)}) collective-permute-start(f32[4,96,128]{2,1,0:T(8,128)S(1)} %get-tuple-element.60), channel_id=1, source_target_pairs={{0,4},{2,6},{4,0},{6,2},{8,12},{10,14},{12,8},{14,10},{16,20},{18,... | collective-permute-start | bytes 589832 | tf_op jit(solution)/shard_map/ppermute | solution.py:116
  21.5 15.6 %copy-start.1 = (bf16[1,4,128,128]{3,2,1,0:T(8,128)(2,1)S(1)}, bf16[1,4,128,128]{3,2,1,0:T(8,128)(2,1)}, u32[]{:S(2)}) copy-start(bf16[1,4,128,128]{3,2,1,0:T(8,128)(2,1)} %ql_ref.3) | copy-start | bytes 393220
  21.5 15.6 %copy-start.2 = (bf16[1,4,128,128]{3,2,1,0:T(8,128)(2,1)S(1)}, bf16[1,4,128,128]{3,2,1,0:T(8,128)(2,1)}, u32[]{:S(2)}) copy-start(bf16[1,4,128,128]{3,2,1,0:T(8,128)(2,1)} %qr_ref.3) | copy-start | bytes 393220
  21.5 15.6 %copy-start.3 = (f32[1,4,128,128]{3,2,1,0:T(8,128)S(1)}, f32[1,4,128,128]{3,2,1,0:T(8,128)}, u32[]{:S(2)}) copy-start(f32[1,4,128,128]{3,2,1,0:T(8,128)} %m_ref.1) | copy-start | bytes 786436
  21.5 15.6 %copy-start.4 = (f32[1,4,128,128]{3,2,1,0:T(8,128)S(1)}, f32[1,4,128,128]{3,2,1,0:T(8,128)}, u32[]{:S(2)}) copy-start(f32[1,4,128,128]{3,2,1,0:T(8,128)} %v_ref.1) | copy-start | bytes 786436
  21.5 15.6 %copy-start.5 = (f32[1,4,128,128]{3,2,1,0:T(8,128)S(1)}, f32[1,4,128,128]{3,2,1,0:T(8,128)}, u32[]{:S(2)}) copy-start(f32[1,4,128,128]{3,2,1,0:T(8,128)} %l_ref.1) | copy-start | bytes 786436
  21.5 15.6 %copy-start.6 = (f32[1,4,128,128]{3,2,1,0:T(8,128)S(1)}, f32[1,4,128,128]{3,2,1,0:T(8,128)}, u32[]{:S(2)}) copy-start(f32[1,4,128,128]{3,2,1,0:T(8,128)} %r_ref.1) | copy-start | bytes 786436
  21.6 5.9 %collective-permute-start.5 = (f32[4,96,128]{2,1,0:T(8,128)S(1)}, f32[4,96,128]{2,1,0:T(8,128)S(1)}, u32[]{:S(2)}, u32[]{:S(2)}) collective-permute-start(f32[4,96,128]{2,1,0:T(8,128)S(1)} %get-tuple-element.62), channel_id=1, source_target_pairs={{0,2},{2,0},{4,6},{6,4},{8,10},{10,8},{12,14},{14,12},{16,18},{18,... | collective-permute-start | bytes 589832 | tf_op jit(solution)/shard_map/ppermute | solution.py:116
  23.2 8.0 %collective-permute-start.8 = (f32[8,32,128]{2,1,0:T(8,128)S(1)}, f32[8,32,128]{2,1,0:T(8,128)S(1)}, u32[]{:S(2)}, u32[]{:S(2)}) collective-permute-start(f32[8,32,128]{2,1,0:T(8,128)S(1)} %get-tuple-element.64), channel_id=1, source_target_pairs={{0,16},{2,18},{4,20},{6,22},{8,24},{10,26},{12,28},{14,30},{16,0},... | collective-permute-start | bytes 393224 | tf_op jit(solution)/shard_map/ppermute | solution.py:116
  27.5 6.4 %collective-permute-start.6 = (f32[2,2,96,128]{3,2,1,0:T(8,128)S(1)}, f32[2,2,96,128]{3,2,1,0:T(8,128)S(1)}, u32[]{:S(2)}, u32[]{:S(2)}) collective-permute-start(f32[2,2,96,128]{3,2,1,0:T(8,128)S(1)} %get-tuple-element.58), channel_id=1, source_target_pairs={{0,8},{2,10},{4,12},{6,14},{8,0},{10,2},{12,4},{14,6},{16,24},{18,... | collective-permute-start | bytes 589832 | tf_op jit(solution)/shard_map/ppermute | solution.py:116
  31.2 4.8 %collective-permute-start.10 = (f32[4,32,128]{2,1,0:T(8,128)S(1)}, f32[4,32,128]{2,1,0:T(8,128)S(1)}, u32[]{:S(2)}, u32[]{:S(2)}) collective-permute-start(f32[4,32,128]{2,1,0:T(8,128)S(1)} %get-tuple-element.68), channel_id=1, source_target_pairs={{0,2},{2,0},{4,6},{6,4},{8,10},{10,8},{12,14},{14,12},{16,18},{18,... | collective-permute-start | bytes 196616 | tf_op jit(solution)/shard_map/ppermute | solution.py:116
  33.9 6.9 %collective-permute-start.9 = (f32[2,96,128]{2,1,0:T(8,128)S(1)}, f32[2,96,128]{2,1,0:T(8,128)S(1)}, u32[]{:S(2)}, u32[]{:S(2)}) collective-permute-start(f32[2,96,128]{2,1,0:T(8,128)S(1)} %bitcast.17), channel_id=1, source_target_pairs={{0,16},{2,18},{4,20},{6,22},{8,24},{10,26},{12,28},{14,30},{16,0},... | collective-permute-start | bytes 294920 | tf_op jit(solution)/shard_map/ppermute | solution.py:116
  36.0 4.0 %collective-permute-start.11 = (f32[2,32,128]{2,1,0:T(8,128)S(1)}, f32[2,32,128]{2,1,0:T(8,128)S(1)}, u32[]{:S(2)}, u32[]{:S(2)}) collective-permute-start(f32[2,32,128]{2,1,0:T(8,128)S(1)} %get-tuple-element.69), channel_id=1, source_target_pairs={{0,4},{2,6},{4,0},{6,2},{8,12},{10,14},{12,8},{14,10},{16,20},{18,... | collective-permute-start | bytes 98312 | tf_op jit(solution)/shard_map/ppermute | solution.py:116
  41.5 7.2 %collective-permute-start.14 = (bf16[2,128,128]{2,1,0:T(8,128)(2,1)S(1)}, bf16[2,128,128]{2,1,0:T(8,128)(2,1)S(1)}, u32[]{:S(2)}, u32[]{:S(2)}) collective-permute-start(bf16[2,128,128]{2,1,0:T(8,128)(2,1)S(1)} %get-tuple-element.42), channel_id=1, source_target_pairs={{0,24},{2,26},{4,28},{6,30},{8,16},{10,18},{12,20},{14,22},{16,8},... | collective-permute-start | bytes 196616 | tf_op jit(solution)/shard_map/ppermute | solution.py:116
  44.3 4.5 %collective-permute-start.13 = (bf16[2,128,128]{2,1,0:T(8,128)(2,1)S(1)}, bf16[2,128,128]{2,1,0:T(8,128)(2,1)S(1)}, u32[]{:S(2)}, u32[]{:S(2)}) collective-permute-start(bf16[2,128,128]{2,1,0:T(8,128)(2,1)S(1)} %get-tuple-element.42), channel_id=1, source_target_pairs={{0,8},{2,10},{4,12},{6,14},{8,0},{10,2},{12,4},{14,6},{16,24},{18,... | collective-permute-start | bytes 196616 | tf_op jit(solution)/shard_map/ppermute | solution.py:116
  44.3 5.2 %collective-permute-start.12 = (bf16[2,128,128]{2,1,0:T(8,128)(2,1)S(1)}, bf16[2,128,128]{2,1,0:T(8,128)(2,1)S(1)}, u32[]{:S(2)}, u32[]{:S(2)}) collective-permute-start(bf16[2,128,128]{2,1,0:T(8,128)(2,1)S(1)} %get-tuple-element.42), channel_id=1, source_target_pairs={{0,16},{2,18},{4,20},{6,22},{8,24},{10,26},{12,28},{14,30},{16,0},... | collective-permute-start | bytes 196616 | tf_op jit(solution)/shard_map/ppermute | solution.py:116
  49.5 5.9 %collective-permute-start.15 = (bf16[4,128,128]{2,1,0:T(8,128)(2,1)S(1)}, bf16[4,128,128]{2,1,0:T(8,128)(2,1)S(1)}, u32[]{:S(2)}, u32[]{:S(2)}) collective-permute-start(bf16[4,128,128]{2,1,0:T(8,128)(2,1)S(1)} %get-tuple-element.45), channel_id=1, source_target_pairs={{0,4},{2,6},{4,0},{6,2},{8,12},{10,14},{12,8},{14,10},{16,20},{18,... | collective-permute-start | bytes 393224 | tf_op jit(solution)/shard_map/ppermute | solution.py:116
  50.5 6.4 %collective-permute-start.16 = (bf16[4,128,128]{2,1,0:T(8,128)(2,1)S(1)}, bf16[4,128,128]{2,1,0:T(8,128)(2,1)S(1)}, u32[]{:S(2)}, u32[]{:S(2)}) collective-permute-start(bf16[4,128,128]{2,1,0:T(8,128)(2,1)S(1)} %get-tuple-element.46), channel_id=1, source_target_pairs={{0,2},{2,0},{4,6},{6,4},{8,10},{10,8},{12,14},{14,12},{16,18},{18,... | collective-permute-start | bytes 393224 | tf_op jit(solution)/shard_map/ppermute | solution.py:116
  56.9 6.4 %collective-permute-start.18 = (bf16[8,128,128]{2,1,0:T(8,128)(2,1)S(1)}, bf16[8,128,128]{2,1,0:T(8,128)(2,1)S(1)}, u32[]{:S(2)}, u32[]{:S(2)}) collective-permute-start(bf16[8,128,128]{2,1,0:T(8,128)(2,1)S(1)} %pad_maximum_fusion.refs_0_), channel_id=1, source_target_pairs={{0,2},{2,0},{4,6},{6,4},{8,10},{10,8},{12,14},{14,12},{16,18},{18,... | collective-permute-start | bytes 786440 | tf_op jit(solution)/shard_map/ppermute | solution.py:116
  57.9 6.4 %collective-permute-start.19 = (bf16[8,128,128]{2,1,0:T(8,128)(2,1)S(1)}, bf16[8,128,128]{2,1,0:T(8,128)(2,1)S(1)}, u32[]{:S(2)}, u32[]{:S(2)}) collective-permute-start(bf16[8,128,128]{2,1,0:T(8,128)(2,1)S(1)} %pad_maximum_fusion.1.refs_1_), channel_id=1, source_target_pairs={{0,4},{2,6},{4,0},{6,2},{8,12},{10,14},{12,8},{14,10},{16,20},{18,... | collective-permute-start | bytes 786440 | tf_op jit(solution)/shard_map/ppermute | solution.py:116
  59.6 1.3 %collective-permute-start.17 = (bf16[4,128,128]{2,1,0:T(8,128)(2,1)S(1)}, bf16[4,128,128]{2,1,0:T(8,128)(2,1)S(1)}, u32[]{:S(2)}, u32[]{:S(2)}) collective-permute-start(bf16[4,128,128]{2,1,0:T(8,128)(2,1)S(1)} %finish.1.own_ref), channel_id=1, source_target_pairs={{0,1},{1,0},{2,3},{3,2},{4,5},{5,4},{6,7},{7,6},{8,9},{9,8},{10,11... | collective-permute-start | bytes 393224 | tf_op jit(solution)/shard_map/ppermute | solution.py:116
  59.6 5.2 %collective-permute-start.22 = (bf16[8,128,128]{2,1,0:T(8,128)(2,1)S(1)}, bf16[8,128,128]{2,1,0:T(8,128)(2,1)S(1)}, u32[]{:S(2)}, u32[]{:S(2)}) collective-permute-start(bf16[8,128,128]{2,1,0:T(8,128)(2,1)S(1)} %pad_maximum_fusion.refs_0_), channel_id=1, source_target_pairs={{0,1},{1,0},{2,3},{3,2},{4,5},{5,4},{6,7},{7,6},{8,9},{9,8},{10,11... | collective-permute-start | bytes 786440 | tf_op jit(solution)/shard_map/ppermute | solution.py:116
  60.1 4.7 %collective-permute-start.23 = (bf16[8,128,128]{2,1,0:T(8,128)(2,1)S(1)}, bf16[8,128,128]{2,1,0:T(8,128)(2,1)S(1)}, u32[]{:S(2)}, u32[]{:S(2)}) collective-permute-start(bf16[8,128,128]{2,1,0:T(8,128)(2,1)S(1)} %pad_maximum_fusion.1.refs_1_), channel_id=1, source_target_pairs={{0,1},{1,0},{2,3},{3,2},{4,5},{5,4},{6,7},{7,6},{8,9},{9,8},{10,11... | collective-permute-start | bytes 786440 | tf_op jit(solution)/shard_map/ppermute | solution.py:116
  64.3 2.3 %collective-permute-start.20 = (bf16[8,128,128]{2,1,0:T(8,128)(2,1)S(1)}, bf16[8,128,128]{2,1,0:T(8,128)(2,1)S(1)}, u32[]{:S(2)}, u32[]{:S(2)}) collective-permute-start(bf16[8,128,128]{2,1,0:T(8,128)(2,1)S(1)} %collective-permute-done.18.refs_2_), channel_id=1, source_target_pairs={{0,1},{1,0},{2,3},{3,2},{4,5},{5,4},{6,7},{7,6},{8,9},{9,8},{10,11... | collective-permute-start | bytes 786440 | tf_op jit(solution)/shard_map/ppermute | solution.py:116
  64.3 2.3 %collective-permute-start.21 = (bf16[8,128,128]{2,1,0:T(8,128)(2,1)S(1)}, bf16[8,128,128]{2,1,0:T(8,128)(2,1)S(1)}, u32[]{:S(2)}, u32[]{:S(2)}) collective-permute-start(bf16[8,128,128]{2,1,0:T(8,128)(2,1)S(1)} %collective-permute-done.19.refs_3_), channel_id=1, source_target_pairs={{0,1},{1,0},{2,3},{3,2},{4,5},{5,4},{6,7},{7,6},{8,9},{9,8},{10,11... | collective-permute-start | bytes 786440 | tf_op jit(solution)/shard_map/ppermute | solution.py:116

commit v13 on v12

--- a/solution.py
+++ b/solution.py
@@ -433,6 +433,10 @@
 
     f_sib = swap_along(features, "inner", 2, 1)
     kv_sib = swap_along(kv_cotangent, "inner", 2, 1)
+    f_own, kv_own, owner_own = [
+        lax.ppermute(x, "inner", [(0, 0), (1, 1)])
+        for x in (features, kv_cotangent, owner_of_block)
+    ]
     flipped = pltpu.VMEM((width, rows), jnp.bfloat16)
     part = jax.ShapeDtypeStruct((near, tile - EDGE, tile), jnp.float32)
     edge = jax.ShapeDtypeStruct((owners, EDGE, tile), jnp.float32)
@@ -452,10 +456,10 @@
         ],
         cost_estimate=pl.CostEstimate(flops=0, bytes_accessed=1_000_000, transcendentals=0),
         name="table",
-    )(place, owner_of_block, kv_cotangent)
+    )(place, owner_own, kv_own)
 
     def tiles_from(first, outs, *more):
-        inputs = (features, f_sib, own_rows, kv_sib, *more)
+        inputs = (f_own, f_sib, own_rows, kv_sib, *more)
         return pl.pallas_call(
             functools.partial(tiles_kernel, owners, first),
             out_shape=outs,

time: 68.3 us -> 69.5 us (1.018)
  starting transfers between devices: 28.3 us -> 31.5 us
  local copies, waits for them, and re-layouts: 2.88 us -> 0.05 us
  waiting for transfers between devices: 19.4 us -> 20.2 us
    ppermute x0 -> x3, starting transfers between devices: none -> 2.83 us  [per_device_dealt(): lax.ppermute(x, 'inner', [(0, 0), (1, 1)])]
    unnamed x18 -> x12, local copies, waits for them, and re-layouts: 2.85 us -> 0.03 us
    ppermute x24, waiting for transfers between devices: 19.4 us -> 20.2 us  [swap_along(): return lax.ppermute(values, axis, [(i, i ^ bit) for i in range(size)])]
  transfers between devices with their start and end apart: 24 -> 27, of which waited for: 13 -> 13; matrix products, arithmetic and copies ran while one was open for 1% -> 1% of each run, Pallas kernels for 19% -> 18%
where the time goes in v13:
time: 69.5 us; the launch traced here: 69.3 us
  starting transfers between devices  31.5 us (45%)
  waiting for transfers between devices  20.2 us (29%)
  Pallas kernels  16.3 us (23%)
  between operations  0.86 us (1%)
    ppermute x24, starting transfers between devices, swap_along(): return lax.ppermute(values, axis, [(i, i ^ bit) for i in range(size)])  28.6 us
    ppermute x24, waiting for transfers between devices, swap_along(): return lax.ppermute(values, axis, [(i, i ^ bit) for i in range(size)])  20.2 us
    pallas_call x3, Pallas kernels, on_slots(): pl.pallas_call(kernel, out_shape=tuple(outs), grid_spec=pltpu.PrefetchSca...  3.98 us
    pallas_call x2, Pallas kernels, place_more(): pl.pallas_call(functools.partial(more_kernel, col_tiles, entries), out_sh...  3.25 us
    pallas_call x1, Pallas kernels, sweeping(): pl.pallas_call(kernel, out_shape=jax.ShapeDtypeStruct(values.shape, dtype...  2.9 us
    ppermute x3, starting transfers between devices, per_device_dealt(): lax.ppermute(x, 'inner', [(0, 0), (1, 1)])  2.83 us
    pallas_call x2, Pallas kernels, tiles_from(): pl.pallas_call(functools.partial(tiles_kernel, owners, first), out_shape=...  2.83 us
    pallas_call x1, Pallas kernels, per_device_dealt(): pl.pallas_call(functools.partial(table_kernel, owners, capacity), out_sha...  1.67 us
  transfers between devices with their start and end apart: 27, of which 13 were waited for; matrix products, arithmetic and copies ran while one was open for 1% of the time, Pallas kernels for 18%

profile of v13, /device:TPU:0, one launch (start us, length us, event | category | flops | bytes accessed | tf_op | source)
XLA Modules:
  0.0 69.3 jit_solution(5313654290938838135)
XLA Ops:
  0.6 1.2 %collective-permute-start.2 = (bf16[256,2048]{1,0:T(8,128)(2,1)}, bf16[256,2048]{1,0:T(8,128)(2,1)S(1)}, u32[]{:S(2)}, u32[]{:S(2)}) collective-permute-start(bf16[256,2048]{1,0:T(8,128)(2,1)} %param.9), channel_id=1, source_target_pairs={{0,0},{1,1},{2,2},{3,3},{4,4},{5,5},{6,6},{7,7},{8,8},{9,9},{10,10... | collective-permute-start | bytes 3145736 | tf_op jit(solution)/shard_map/ppermute | solution.py:437
  1.9 0.5 collective-permute-start.3
  2.3 1.0 %collective-permute-start.1 = (bf16[256,512]{1,0:T(8,128)(2,1)}, bf16[256,512]{1,0:T(8,128)(2,1)S(1)}, u32[]{:S(2)}, u32[]{:S(2)}) collective-permute-start(bf16[256,512]{1,0:T(8,128)(2,1)} %param.10), channel_id=1, source_target_pairs={{0,0},{1,1},{2,2},{3,3},{4,4},{5,5},{6,6},{7,7},{8,8},{9,9},{10,10... | collective-permute-start | bytes 786440 | tf_op jit(solution)/shard_map/ppermute | solution.py:437
  3.3 0.7 collective-permute-start
  4.0 0.1 pad_add_fusion.place_ref
  4.1 1.7 %table.1 = (s32[64]{0:T(128)S(1)}, bf16[512,256]{1,0:T(8,128)(2,1)S(1)}) custom-call(s32[2]{0:T(128)S(1)} %pad_add_fusion.place_ref, s32[64]{0:T(128)S(1)} %collective-permute-done.owner_ref, bf16[256,512]{1,0:T(8,128)(2,1)S(1)} %collective-permute-done.1.kv_ref), custom_call_target="tpu_custom_call" | custom-call | bytes 1000000 | tf_op jit(solution)/shard_map/table/pallas_call | solution.py:445
  5.8 1.4 %tiles.2 = (f32[8,96,128]{2,1,0:T(8,128)S(1)}, f32[8,96,128]{2,1,0:T(8,128)S(1)}, f32[32,32,128]{2,1,0:T(8,128)S(1)}) custom-call(s32[64]{0:T(128)S(1)} %get-tuple-element.30.table_ref, bf16[256,2048]{1,0:T(8,128)(2,1)S(1)} %collective-permute-done.2.f_own, bf16[256,2048]{1,0:T(8,128)(2,1)S(1)} %collective-permute-done.3.f_sib, ...), custom_call_target="tpu_custom_call" | custom-call | flops 536870912 | bytes 3500000 | tf_op jit(solution)/shard_map/tiles/pallas_call | solution.py:463
  7.2 3.0 %collective-permute-start.6 = (f32[8,96,128]{2,1,0:T(8,128)S(1)}, f32[8,96,128]{2,1,0:T(8,128)S(1)}, u32[]{:S(2)}, u32[]{:S(2)}) collective-permute-start(f32[8,96,128]{2,1,0:T(8,128)S(1)} %get-tuple-element.36), channel_id=1, source_target_pairs={{0,4},{2,6},{4,0},{6,2},{8,12},{10,14},{12,8},{14,10},{16,20},{18,... | collective-permute-start | bytes 1179656 | tf_op jit(solution)/shard_map/ppermute | solution.py:116
  10.2 1.5 %collective-permute-start.5 = (f32[8,96,128]{2,1,0:T(8,128)S(1)}, f32[8,96,128]{2,1,0:T(8,128)S(1)}, u32[]{:S(2)}, u32[]{:S(2)}) collective-permute-start(f32[8,96,128]{2,1,0:T(8,128)S(1)} %get-tuple-element.34), channel_id=1, source_target_pairs={{0,2},{2,0},{4,6},{6,4},{8,10},{10,8},{12,14},{14,12},{16,18},{18,... | collective-permute-start | bytes 1179656 | tf_op jit(solution)/shard_map/ppermute | solution.py:116
  11.7 1.4 %tiles.3 = (f32[8,96,128]{2,1,0:T(8,128)S(1)}, f32[8,96,128]{2,1,0:T(8,128)S(1)}, f32[16,32,128]{2,1,0:T(8,128)S(1)}, f32[16,32,128]{2,1,0:T(8,128)S(1)}) custom-call(s32[64]{0:T(128)S(1)} %get-tuple-element.30.table_ref, bf16[256,2048]{1,0:T(8,128)(2,1)S(1)} %collective-permute-done.2.f_own, bf16[256,2048]{1,0:T(8,128)(2,1)S(1)} %collective-permute-done.3.f_sib, ...), custom_call_target="tpu_custom_call" | custom-call | flops 536870912 | bytes 3500000 | tf_op jit(solution)/shard_map/tiles/pallas_call | solution.py:463
  13.1 1.6 %collective-permute-start.10 = (f32[16,32,128]{2,1,0:T(8,128)S(1)}, f32[16,32,128]{2,1,0:T(8,128)S(1)}, u32[]{:S(2)}, u32[]{:S(2)}) collective-permute-start(f32[16,32,128]{2,1,0:T(8,128)S(1)} %get-tuple-element.38), channel_id=1, source_target_pairs={{0,8},{2,10},{4,12},{6,14},{8,0},{10,2},{12,4},{14,6},{16,24},{18,... | collective-permute-start | bytes 786440 | tf_op jit(solution)/shard_map/ppermute | solution.py:116
  14.8 4.7 %collective-permute-done.6 = f32[8,96,128]{2,1,0:T(8,128)S(1)} collective-permute-done((f32[8,96,128]{2,1,0:T(8,128)S(1)}, f32[8,96,128]{2,1,0:T(8,128)S(1)}, u32[]{:S(2)}, u32[]{:S(2)}) %collective-permute-start.6) | collective-permute-done | bytes 393248 | tf_op jit(solution)/shard_map/ppermute | solution.py:116
  19.6 1.8 %collective-permute-start.8 = (f32[4,96,128]{2,1,0:T(8,128)S(1)}, f32[4,96,128]{2,1,0:T(8,128)S(1)}, u32[]{:S(2)}, u32[]{:S(2)}) collective-permute-start(f32[4,96,128]{2,1,0:T(8,128)S(1)} %get-tuple-element.62), channel_id=1, source_target_pairs={{0,2},{2,0},{4,6},{6,4},{8,10},{10,8},{12,14},{14,12},{16,18},{18,... | collective-permute-start | bytes 589832 | tf_op jit(solution)/shard_map/ppermute | solution.py:116
  21.4 0.1 fusion.5
  21.5 1.6 %collective-permute-start.7 = (f32[4,96,128]{2,1,0:T(8,128)S(1)}, f32[4,96,128]{2,1,0:T(8,128)S(1)}, u32[]{:S(2)}, u32[]{:S(2)}) collective-permute-start(f32[4,96,128]{2,1,0:T(8,128)S(1)} %get-tuple-element.60), channel_id=1, source_target_pairs={{0,4},{2,6},{4,0},{6,2},{8,12},{10,14},{12,8},{14,10},{16,20},{18,... | collective-permute-start | bytes 589832 | tf_op jit(solution)/shard_map/ppermute | solution.py:116
  23.1 2.7 %collective-permute-start.11 = (f32[8,32,128]{2,1,0:T(8,128)S(1)}, f32[8,32,128]{2,1,0:T(8,128)S(1)}, u32[]{:S(2)}, u32[]{:S(2)}) collective-permute-start(f32[8,32,128]{2,1,0:T(8,128)S(1)} %get-tuple-element.64), channel_id=1, source_target_pairs={{0,16},{2,18},{4,20},{6,22},{8,24},{10,26},{12,28},{14,30},{16,0},... | collective-permute-start | bytes 393224 | tf_op jit(solution)/shard_map/ppermute | solution.py:116
  25.7 0.2 collective-permute-done.8
  25.9 1.3 %collective-permute-done.7 = f32[4,96,128]{2,1,0:T(8,128)S(1)} collective-permute-done((f32[4,96,128]{2,1,0:T(8,128)S(1)}, f32[4,96,128]{2,1,0:T(8,128)S(1)}, u32[]{:S(2)}, u32[]{:S(2)}) %collective-permute-start.7) | collective-permute-done | bytes 196640 | tf_op jit(solution)/shard_map/ppermute | solution.py:116
  27.3 1.7 %collective-permute-start.9 = (f32[2,2,96,128]{3,2,1,0:T(8,128)S(1)}, f32[2,2,96,128]{3,2,1,0:T(8,128)S(1)}, u32[]{:S(2)}, u32[]{:S(2)}) collective-permute-start(f32[2,2,96,128]{3,2,1,0:T(8,128)S(1)} %get-tuple-element.58), channel_id=1, source_target_pairs={{0,8},{2,10},{4,12},{6,14},{8,0},{10,2},{12,4},{14,6},{16,24},{18,... | collective-permute-start | bytes 589832 | tf_op jit(solution)/shard_map/ppermute | solution.py:116
  28.9 2.0 %collective-permute-done.11 = f32[8,32,128]{2,1,0:T(8,128)S(1)} collective-permute-done((f32[8,32,128]{2,1,0:T(8,128)S(1)}, f32[8,32,128]{2,1,0:T(8,128)S(1)}, u32[]{:S(2)}, u32[]{:S(2)}) %collective-permute-start.11) | collective-permute-done | bytes 131104 | tf_op jit(solution)/shard_map/ppermute | solution.py:116
  31.0 0.6 collective-permute-start.13
  31.6 2.1 %collective-permute-done.9 = f32[2,2,96,128]{3,2,1,0:T(8,128)S(1)} collective-permute-done((f32[2,2,96,128]{3,2,1,0:T(8,128)S(1)}, f32[2,2,96,128]{3,2,1,0:T(8,128)S(1)}, u32[]{:S(2)}, u32[]{:S(2)}) %collective-permute-start.9) | collective-permute-done | bytes 196640 | tf_op jit(solution)/shard_map/ppermute | solution.py:116
  33.7 2.0 %collective-permute-start.12 = (f32[2,96,128]{2,1,0:T(8,128)S(1)}, f32[2,96,128]{2,1,0:T(8,128)S(1)}, u32[]{:S(2)}, u32[]{:S(2)}) collective-permute-start(f32[2,96,128]{2,1,0:T(8,128)S(1)} %bitcast.17), channel_id=1, source_target_pairs={{0,16},{2,18},{4,20},{6,22},{8,24},{10,26},{12,28},{14,30},{16,0},... | collective-permute-start | bytes 294920 | tf_op jit(solution)/shard_map/ppermute | solution.py:116
  35.7 1.6 %collective-permute-start.14 = (f32[2,32,128]{2,1,0:T(8,128)S(1)}, f32[2,32,128]{2,1,0:T(8,128)S(1)}, u32[]{:S(2)}, u32[]{:S(2)}) collective-permute-start(f32[2,32,128]{2,1,0:T(8,128)S(1)} %get-tuple-element.69), channel_id=1, source_target_pairs={{0,4},{2,6},{4,0},{6,2},{8,12},{10,14},{12,8},{14,10},{16,20},{18,... | collective-permute-start | bytes 98312 | tf_op jit(solution)/shard_map/ppermute | solution.py:116
  37.3 0.5 rotated.1
  37.8 1.9 %collective-permute-done.14.d_ref = f32[2,32,128]{2,1,0:T(8,128)S(1)} collective-permute-done((f32[2,32,128]{2,1,0:T(8,128)S(1)}, f32[2,32,128]{2,1,0:T(8,128)S(1)}, u32[]{:S(2)}, u32[]{:S(2)}) %collective-permute-start.14) | collective-permute-done | bytes 32800 | tf_op jit(solution)/shard_map/ppermute | solution.py:116
  39.7 0.7 collective-permute-done.12.b_ref
  40.4 0.7 %direction.1 = (bf16[2,128,128]{2,1,0:T(8,128)(2,1)S(1)}, f32[2,128,128]{2,1,0:T(8,128)S(1)}) custom-call(s32[1]{0:T(128)} %bitcast.1.side_ref, f32[2,96,128]{2,1,0:T(8,128)S(1)} %get-tuple-element.66.a_ref, f32[2,96,128]{2,1,0:T(8,128)S(1)} %collective-permute-done.12.b_ref, f32[2,32,128]{2,1,0:T(8,128)S(1)} %get-tuple-element.70.c_ref, ...), custom_call_target="tpu_custom_call" | custom-call | flops 67108864 | bytes 800000 | tf_op jit(solution)/shard_map/direction/pallas_call | solution.py:294
  41.1 0.9 %collective-permute-start.15 = (bf16[2,128,128]{2,1,0:T(8,128)(2,1)S(1)}, bf16[2,128,128]{2,1,0:T(8,128)(2,1)S(1)}, u32[]{:S(2)}, u32[]{:S(2)}) collective-permute-start(bf16[2,128,128]{2,1,0:T(8,128)(2,1)S(1)} %get-tuple-element.42), channel_id=1, source_target_pairs={{0,16},{2,18},{4,20},{6,22},{8,24},{10,26},{12,28},{14,30},{16,0},... | collective-permute-start | bytes 196616 | tf_op jit(solution)/shard_map/ppermute | solution.py:116
  42.0 2.5 %collective-permute-start.16 = (bf16[2,128,128]{2,1,0:T(8,128)(2,1)S(1)}, bf16[2,128,128]{2,1,0:T(8,128)(2,1)S(1)}, u32[]{:S(2)}, u32[]{:S(2)}) collective-permute-start(bf16[2,128,128]{2,1,0:T(8,128)(2,1)S(1)} %get-tuple-element.42), channel_id=1, source_target_pairs={{0,8},{2,10},{4,12},{6,14},{8,0},{10,2},{12,4},{14,6},{16,24},{18,... | collective-permute-start | bytes 196616 | tf_op jit(solution)/shard_map/ppermute | solution.py:116
  44.5 1.0 %collective-permute-start.17 = (bf16[2,128,128]{2,1,0:T(8,128)(2,1)S(1)}, bf16[2,128,128]{2,1,0:T(8,128)(2,1)S(1)}, u32[]{:S(2)}, u32[]{:S(2)}) collective-permute-start(bf16[2,128,128]{2,1,0:T(8,128)(2,1)S(1)} %get-tuple-element.42), channel_id=1, source_target_pairs={{0,24},{2,26},{4,28},{6,30},{8,16},{10,18},{12,20},{14,22},{16,8},... | collective-permute-start | bytes 196616 | tf_op jit(solution)/shard_map/ppermute | solution.py:116
  45.6 2.8 %refresh.1.iter_ref = f32[4,128,128]{2,1,0:T(8,128)S(1)} custom-call(s32[1]{0:T(128)} %bitcast.1.side_ref, f32[2,128,128]{2,1,0:T(8,128)S(1)} %get-tuple-element.43.g_ref, f32[4,128,128]{2,1,0:T(8,128)S(1)} %get-tuple-element.44.power_ref, bf16[1,4,128,128]{3,2,1,0:T(8,128)(2,1)S(1)} %copy-done, bf16[1,4,128,128]{3,2,1,0:T(8,128)(2,1)S(1)} %copy-done.1), custom_call_target="tpu_custom_call" | custom-call | flops 939524096 | bytes 800000 | tf_op jit(solution)/shard_map/refresh/pallas_call | solution.py:294
  48.4 2.2 %collective-permute-done.17 = bf16[2,128,128]{2,1,0:T(8,128)(2,1)S(1)} collective-permute-done((bf16[2,128,128]{2,1,0:T(8,128)(2,1)S(1)}, bf16[2,128,128]{2,1,0:T(8,128)(2,1)S(1)}, u32[]{:S(2)}, u32[]{:S(2)}) %collective-permute-start.17) | collective-permute-done | bytes 65568 | tf_op jit(solution)/shard_map/ppermute | solution.py:116
  50.6 1.1 %collective-permute-start.19 = (bf16[4,128,128]{2,1,0:T(8,128)(2,1)S(1)}, bf16[4,128,128]{2,1,0:T(8,128)(2,1)S(1)}, u32[]{:S(2)}, u32[]{:S(2)}) collective-permute-start(bf16[4,128,128]{2,1,0:T(8,128)(2,1)S(1)} %get-tuple-element.46), channel_id=1, source_target_pairs={{0,2},{2,0},{4,6},{6,4},{8,10},{10,8},{12,14},{14,12},{16,18},{18,... | collective-permute-start | bytes 393224 | tf_op jit(solution)/shard_map/ppermute | solution.py:116
  51.7 1.0 %collective-permute-start.18 = (bf16[4,128,128]{2,1,0:T(8,128)(2,1)S(1)}, bf16[4,128,128]{2,1,0:T(8,128)(2,1)S(1)}, u32[]{:S(2)}, u32[]{:S(2)}) collective-permute-start(bf16[4,128,128]{2,1,0:T(8,128)(2,1)S(1)} %get-tuple-element.45), channel_id=1, source_target_pairs={{0,4},{2,6},{4,0},{6,2},{8,12},{10,14},{12,8},{14,10},{16,20},{18,... | collective-permute-start | bytes 393224 | tf_op jit(solution)/shard_map/ppermute | solution.py:116
  52.7 2.9 %finish.1.own_ref = bf16[4,128,128]{2,1,0:T(8,128)(2,1)S(1)} custom-call(f32[4,128,128]{2,1,0:T(8,128)S(1)} %refresh.1.iter_ref), custom_call_target="tpu_custom_call" | custom-call | flops 939524096 | bytes 400000 | tf_op jit(solution)/shard_map/finish/pallas_call | solution.py:344
  55.6 1.4 %collective-permute-done.19 = bf16[4,128,128]{2,1,0:T(8,128)(2,1)S(1)} collective-permute-done((bf16[4,128,128]{2,1,0:T(8,128)(2,1)S(1)}, bf16[4,128,128]{2,1,0:T(8,128)(2,1)S(1)}, u32[]{:S(2)}, u32[]{:S(2)}) %collective-permute-start.19) | collective-permute-done | bytes 131104 | tf_op jit(solution)/shard_map/ppermute | solution.py:116
  57.1 1.0 %collective-permute-done.18 = bf16[4,128,128]{2,1,0:T(8,128)(2,1)S(1)} collective-permute-done((bf16[4,128,128]{2,1,0:T(8,128)(2,1)S(1)}, bf16[4,128,128]{2,1,0:T(8,128)(2,1)S(1)}, u32[]{:S(2)}, u32[]{:S(2)}) %collective-permute-start.18) | collective-permute-done | bytes 131104 | tf_op jit(solution)/shard_map/ppermute | solution.py:116
  58.1 1.0 %collective-permute-start.21 = (bf16[8,128,128]{2,1,0:T(8,128)(2,1)S(1)}, bf16[8,128,128]{2,1,0:T(8,128)(2,1)S(1)}, u32[]{:S(2)}, u32[]{:S(2)}) collective-permute-start(bf16[8,128,128]{2,1,0:T(8,128)(2,1)S(1)} %pad_maximum_fusion.refs_0_), channel_id=1, source_target_pairs={{0,2},{2,0},{4,6},{6,4},{8,10},{10,8},{12,14},{14,12},{16,18},{18,... | collective-permute-start | bytes 786440 | tf_op jit(solution)/shard_map/ppermute | solution.py:116
  59.1 1.6 %collective-permute-start.22 = (bf16[8,128,128]{2,1,0:T(8,128)(2,1)S(1)}, bf16[8,128,128]{2,1,0:T(8,128)(2,1)S(1)}, u32[]{:S(2)}, u32[]{:S(2)}) collective-permute-start(bf16[8,128,128]{2,1,0:T(8,128)(2,1)S(1)} %pad_maximum_fusion.1.refs_1_), channel_id=1, source_target_pairs={{0,4},{2,6},{4,0},{6,2},{8,12},{10,14},{12,8},{14,10},{16,20},{18,... | collective-permute-start | bytes 786440 | tf_op jit(solution)/shard_map/ppermute | solution.py:116
  60.7 0.5 collective-permute-start.25
  61.2 0.8 %collective-permute-done.20.sib_ref = bf16[4,128,128]{2,1,0:T(8,128)(2,1)S(1)} collective-permute-done((bf16[4,128,128]{2,1,0:T(8,128)(2,1)S(1)}, bf16[4,128,128]{2,1,0:T(8,128)(2,1)S(1)}, u32[]{:S(2)}, u32[]{:S(2)}) %collective-permute-start.20) | collective-permute-done | bytes 131104 | tf_op jit(solution)/shard_map/ppermute | solution.py:116
  62.0 1.6 %begin.1 = (bf16[2048,512]{1,0:T(8,128)(2,1)}, bf16[1,4,128,128]{3,2,1,0:T(8,128)(2,1)}, bf16[1,4,128,128]{3,2,1,0:T(8,128)(2,1)}) custom-call(s32[64]{0:T(128)S(1)} %get-tuple-element.30.table_ref, s32[2]{0:T(128)S(1)} %pad_add_fusion.place_ref, bf16[4,128,128]{2,1,0:T(8,128)(2,1)S(1)} %finish.1.own_ref, ...), custom_call_target="tpu_custom_call" | custom-call | bytes 800000 | tf_op jit(solution)/shard_map/begin/pallas_call | solution.py:552
  63.7 0.9 %collective-permute-done.21.refs_2_ = bf16[8,128,128]{2,1,0:T(8,128)(2,1)S(1)} collective-permute-done((bf16[8,128,128]{2,1,0:T(8,128)(2,1)S(1)}, bf16[8,128,128]{2,1,0:T(8,128)(2,1)S(1)}, u32[]{:S(2)}, u32[]{:S(2)}) %collective-permute-start.21) | collective-permute-done | bytes 262176 | tf_op jit(solution)/shard_map/ppermute | solution.py:116
  64.6 0.9 %collective-permute-done.22.refs_3_ = bf16[8,128,128]{2,1,0:T(8,128)(2,1)S(1)} collective-permute-done((bf16[8,128,128]{2,1,0:T(8,128)(2,1)S(1)}, bf16[8,128,128]{2,1,0:T(8,128)(2,1)S(1)}, u32[]{:S(2)}, u32[]{:S(2)}) %collective-permute-start.22) | collective-permute-done | bytes 262176 | tf_op jit(solution)/shard_map/ppermute | solution.py:116
  65.5 0.5 collective-permute-start.24
  66.0 1.8 %more.2.refs_2_ = bf16[2048,512]{1,0:T(8,128)(2,1)} custom-call(s32[64]{0:T(128)S(1)} %get-tuple-element.30.table_ref, bf16[8,128,128]{2,1,0:T(8,128)(2,1)S(1)} %collective-permute-done.25.refs_0_, bf16[8,128,128]{2,1,0:T(8,128)(2,1)S(1)} %collective-permute-done.26.refs_1_, ...), custom_call_target="tpu_custom_call", output_to_operand_aliasing={{}: (5, {})} | custom-call | bytes 1000000 | tf_op jit(solution)/shard_map/more/pallas_call | solution.py:396
  67.8 1.5 %more.3 = bf16[2048,512]{1,0:T(8,128)(2,1)} custom-call(s32[64]{0:T(128)S(1)} %get-tuple-element.30.table_ref, bf16[8,128,128]{2,1,0:T(8,128)(2,1)S(1)} %collective-permute-done.23.refs_0_, bf16[8,128,128]{2,1,0:T(8,128)(2,1)S(1)} %collective-permute-done.24.refs_1_, bf16[2048,512]{1,0:T(8,128)(2,1)} %more.2.refs_2_), custom_call_target="tpu_custom_call", output_to_operand_aliasing={{}: (3, {})} | custom-call | bytes 1000000 | tf_op jit(solution)/shard_map/more/pallas_call | solution.py:396
  (43 shorter events, 0.4 us)
Async XLA Ops:
  0.6 5.1 %collective-permute-start.2 = (bf16[256,2048]{1,0:T(8,128)(2,1)}, bf16[256,2048]{1,0:T(8,128)(2,1)S(1)}, u32[]{:S(2)}, u32[]{:S(2)}) collective-permute-start(bf16[256,2048]{1,0:T(8,128)(2,1)} %param.9), channel_id=1, source_target_pairs={{0,0},{1,1},{2,2},{3,3},{4,4},{5,5},{6,6},{7,7},{8,8},{9,9},{10,10... | collective-permute-start | bytes 3145736 | tf_op jit(solution)/shard_map/ppermute | solution.py:437
  1.9 3.9 %collective-permute-start.3 = (bf16[256,2048]{1,0:T(8,128)(2,1)}, bf16[256,2048]{1,0:T(8,128)(2,1)S(1)}, u32[]{:S(2)}, u32[]{:S(2)}) collective-permute-start(bf16[256,2048]{1,0:T(8,128)(2,1)} %param.9), channel_id=1, source_target_pairs={{0,1},{1,0},{2,3},{3,2},{4,5},{5,4},{6,7},{7,6},{8,9},{9,8},{10,11... | collective-permute-start | bytes 3145736 | tf_op jit(solution)/shard_map/ppermute | solution.py:116
  2.3 1.7 %collective-permute-start.1 = (bf16[256,512]{1,0:T(8,128)(2,1)}, bf16[256,512]{1,0:T(8,128)(2,1)S(1)}, u32[]{:S(2)}, u32[]{:S(2)}) collective-permute-start(bf16[256,512]{1,0:T(8,128)(2,1)} %param.10), channel_id=1, source_target_pairs={{0,0},{1,1},{2,2},{3,3},{4,4},{5,5},{6,6},{7,7},{8,8},{9,9},{10,10... | collective-permute-start | bytes 786440 | tf_op jit(solution)/shard_map/ppermute | solution.py:437
  3.3 2.5 %collective-permute-start.4 = (bf16[256,512]{1,0:T(8,128)(2,1)}, bf16[256,512]{1,0:T(8,128)(2,1)S(1)}, u32[]{:S(2)}, u32[]{:S(2)}) collective-permute-start(bf16[256,512]{1,0:T(8,128)(2,1)} %param.10), channel_id=1, source_target_pairs={{0,1},{1,0},{2,3},{3,2},{4,5},{5,4},{6,7},{7,6},{8,9},{9,8},{10,11... | collective-permute-start | bytes 786440 | tf_op jit(solution)/shard_map/ppermute | solution.py:116
  3.3 0.7 %collective-permute-start = (s32[64]{0:T(128)}, s32[64]{0:T(128)S(1)}, u32[]{:S(2)}, u32[]{:S(2)}) collective-permute-start(s32[64]{0:T(128)} %param.11), channel_id=1, source_target_pairs={{0,0},{1,1},{2,2},{3,3},{4,4},{5,5},{6,6},{7,7},{8,8},{9,9},{10,10... | collective-permute-start | bytes 776 | tf_op jit(solution)/shard_map/ppermute | solution.py:437
  7.2 12.3 %collective-permute-start.6 = (f32[8,96,128]{2,1,0:T(8,128)S(1)}, f32[8,96,128]{2,1,0:T(8,128)S(1)}, u32[]{:S(2)}, u32[]{:S(2)}) collective-permute-start(f32[8,96,128]{2,1,0:T(8,128)S(1)} %get-tuple-element.36), channel_id=1, source_target_pairs={{0,4},{2,6},{4,0},{6,2},{8,12},{10,14},{12,8},{14,10},{16,20},{18,... | collective-permute-start | bytes 1179656 | tf_op jit(solution)/shard_map/ppermute | solution.py:116
  10.2 11.1 %collective-permute-start.5 = (f32[8,96,128]{2,1,0:T(8,128)S(1)}, f32[8,96,128]{2,1,0:T(8,128)S(1)}, u32[]{:S(2)}, u32[]{:S(2)}) collective-permute-start(f32[8,96,128]{2,1,0:T(8,128)S(1)} %get-tuple-element.34), channel_id=1, source_target_pairs={{0,2},{2,0},{4,6},{6,4},{8,10},{10,8},{12,14},{14,12},{16,18},{18,... | collective-permute-start | bytes 1179656 | tf_op jit(solution)/shard_map/ppermute | solution.py:116
  13.1 9.9 %collective-permute-start.10 = (f32[16,32,128]{2,1,0:T(8,128)S(1)}, f32[16,32,128]{2,1,0:T(8,128)S(1)}, u32[]{:S(2)}, u32[]{:S(2)}) collective-permute-start(f32[16,32,128]{2,1,0:T(8,128)S(1)} %get-tuple-element.38), channel_id=1, source_target_pairs={{0,8},{2,10},{4,12},{6,14},{8,0},{10,2},{12,4},{14,6},{16,24},{18,... | collective-permute-start | bytes 786440 | tf_op jit(solution)/shard_map/ppermute | solution.py:116
  19.6 6.4 %collective-permute-start.8 = (f32[4,96,128]{2,1,0:T(8,128)S(1)}, f32[4,96,128]{2,1,0:T(8,128)S(1)}, u32[]{:S(2)}, u32[]{:S(2)}) collective-permute-start(f32[4,96,128]{2,1,0:T(8,128)S(1)} %get-tuple-element.62), channel_id=1, source_target_pairs={{0,2},{2,0},{4,6},{6,4},{8,10},{10,8},{12,14},{14,12},{16,18},{18,... | collective-permute-start | bytes 589832 | tf_op jit(solution)/shard_map/ppermute | solution.py:116
  21.3 15.9 %copy-start = (bf16[1,4,128,128]{3,2,1,0:T(8,128)(2,1)S(1)}, bf16[1,4,128,128]{3,2,1,0:T(8,128)(2,1)}, u32[]{:S(2)}) copy-start(bf16[1,4,128,128]{3,2,1,0:T(8,128)(2,1)} %ql_ref.3) | copy-start | bytes 393220
  21.3 15.9 %copy-start.1 = (bf16[1,4,128,128]{3,2,1,0:T(8,128)(2,1)S(1)}, bf16[1,4,128,128]{3,2,1,0:T(8,128)(2,1)}, u32[]{:S(2)}) copy-start(bf16[1,4,128,128]{3,2,1,0:T(8,128)(2,1)} %qr_ref.3) | copy-start | bytes 393220
  21.3 15.9 %copy-start.2 = (f32[1,4,128,128]{3,2,1,0:T(8,128)S(1)}, f32[1,4,128,128]{3,2,1,0:T(8,128)}, u32[]{:S(2)}) copy-start(f32[1,4,128,128]{3,2,1,0:T(8,128)} %m_ref.1) | copy-start | bytes 786436
  21.4 15.9 %copy-start.3 = (f32[1,4,128,128]{3,2,1,0:T(8,128)S(1)}, f32[1,4,128,128]{3,2,1,0:T(8,128)}, u32[]{:S(2)}) copy-start(f32[1,4,128,128]{3,2,1,0:T(8,128)} %v_ref.1) | copy-start | bytes 786436
  21.4 15.9 %copy-start.4 = (f32[1,4,128,128]{3,2,1,0:T(8,128)S(1)}, f32[1,4,128,128]{3,2,1,0:T(8,128)}, u32[]{:S(2)}) copy-start(f32[1,4,128,128]{3,2,1,0:T(8,128)} %l_ref.1) | copy-start | bytes 786436
  21.4 15.9 %copy-start.5 = (f32[1,4,128,128]{3,2,1,0:T(8,128)S(1)}, f32[1,4,128,128]{3,2,1,0:T(8,128)}, u32[]{:S(2)}) copy-start(f32[1,4,128,128]{3,2,1,0:T(8,128)} %r_ref.1) | copy-start | bytes 786436
  21.5 5.7 %collective-permute-start.7 = (f32[4,96,128]{2,1,0:T(8,128)S(1)}, f32[4,96,128]{2,1,0:T(8,128)S(1)}, u32[]{:S(2)}, u32[]{:S(2)}) collective-permute-start(f32[4,96,128]{2,1,0:T(8,128)S(1)} %get-tuple-element.60), channel_id=1, source_target_pairs={{0,4},{2,6},{4,0},{6,2},{8,12},{10,14},{12,8},{14,10},{16,20},{18,... | collective-permute-start | bytes 589832 | tf_op jit(solution)/shard_map/ppermute | solution.py:116
  23.1 7.9 %collective-permute-start.11 = (f32[8,32,128]{2,1,0:T(8,128)S(1)}, f32[8,32,128]{2,1,0:T(8,128)S(1)}, u32[]{:S(2)}, u32[]{:S(2)}) collective-permute-start(f32[8,32,128]{2,1,0:T(8,128)S(1)} %get-tuple-element.64), channel_id=1, source_target_pairs={{0,16},{2,18},{4,20},{6,22},{8,24},{10,26},{12,28},{14,30},{16,0},... | collective-permute-start | bytes 393224 | tf_op jit(solution)/shard_map/ppermute | solution.py:116
  27.3 6.4 %collective-permute-start.9 = (f32[2,2,96,128]{3,2,1,0:T(8,128)S(1)}, f32[2,2,96,128]{3,2,1,0:T(8,128)S(1)}, u32[]{:S(2)}, u32[]{:S(2)}) collective-permute-start(f32[2,2,96,128]{3,2,1,0:T(8,128)S(1)} %get-tuple-element.58), channel_id=1, source_target_pairs={{0,8},{2,10},{4,12},{6,14},{8,0},{10,2},{12,4},{14,6},{16,24},{18,... | collective-permute-start | bytes 589832 | tf_op jit(solution)/shard_map/ppermute | solution.py:116
  31.0 4.7 %collective-permute-start.13 = (f32[4,32,128]{2,1,0:T(8,128)S(1)}, f32[4,32,128]{2,1,0:T(8,128)S(1)}, u32[]{:S(2)}, u32[]{:S(2)}) collective-permute-start(f32[4,32,128]{2,1,0:T(8,128)S(1)} %get-tuple-element.68), channel_id=1, source_target_pairs={{0,2},{2,0},{4,6},{6,4},{8,10},{10,8},{12,14},{14,12},{16,18},{18,... | collective-permute-start | bytes 196616 | tf_op jit(solution)/shard_map/ppermute | solution.py:116
  33.7 6.7 %collective-permute-start.12 = (f32[2,96,128]{2,1,0:T(8,128)S(1)}, f32[2,96,128]{2,1,0:T(8,128)S(1)}, u32[]{:S(2)}, u32[]{:S(2)}) collective-permute-start(f32[2,96,128]{2,1,0:T(8,128)S(1)} %bitcast.17), channel_id=1, source_target_pairs={{0,16},{2,18},{4,20},{6,22},{8,24},{10,26},{12,28},{14,30},{16,0},... | collective-permute-start | bytes 294920 | tf_op jit(solution)/shard_map/ppermute | solution.py:116
  35.7 4.0 %collective-permute-start.14 = (f32[2,32,128]{2,1,0:T(8,128)S(1)}, f32[2,32,128]{2,1,0:T(8,128)S(1)}, u32[]{:S(2)}, u32[]{:S(2)}) collective-permute-start(f32[2,32,128]{2,1,0:T(8,128)S(1)} %get-tuple-element.69), channel_id=1, source_target_pairs={{0,4},{2,6},{4,0},{6,2},{8,12},{10,14},{12,8},{14,10},{16,20},{18,... | collective-permute-start | bytes 98312 | tf_op jit(solution)/shard_map/ppermute | solution.py:116
  41.1 7.2 %collective-permute-start.15 = (bf16[2,128,128]{2,1,0:T(8,128)(2,1)S(1)}, bf16[2,128,128]{2,1,0:T(8,128)(2,1)S(1)}, u32[]{:S(2)}, u32[]{:S(2)}) collective-permute-start(bf16[2,128,128]{2,1,0:T(8,128)(2,1)S(1)} %get-tuple-element.42), channel_id=1, source_target_pairs={{0,16},{2,18},{4,20},{6,22},{8,24},{10,26},{12,28},{14,30},{16,0},... | collective-permute-start | bytes 196616 | tf_op jit(solution)/shard_map/ppermute | solution.py:116
  42.0 6.4 %collective-permute-start.16 = (bf16[2,128,128]{2,1,0:T(8,128)(2,1)S(1)}, bf16[2,128,128]{2,1,0:T(8,128)(2,1)S(1)}, u32[]{:S(2)}, u32[]{:S(2)}) collective-permute-start(bf16[2,128,128]{2,1,0:T(8,128)(2,1)S(1)} %get-tuple-element.42), channel_id=1, source_target_pairs={{0,8},{2,10},{4,12},{6,14},{8,0},{10,2},{12,4},{14,6},{16,24},{18,... | collective-permute-start | bytes 196616 | tf_op jit(solution)/shard_map/ppermute | solution.py:116
  44.5 6.1 %collective-permute-start.17 = (bf16[2,128,128]{2,1,0:T(8,128)(2,1)S(1)}, bf16[2,128,128]{2,1,0:T(8,128)(2,1)S(1)}, u32[]{:S(2)}, u32[]{:S(2)}) collective-permute-start(bf16[2,128,128]{2,1,0:T(8,128)(2,1)S(1)} %get-tuple-element.42), channel_id=1, source_target_pairs={{0,24},{2,26},{4,28},{6,30},{8,16},{10,18},{12,20},{14,22},{16,8},... | collective-permute-start | bytes 196616 | tf_op jit(solution)/shard_map/ppermute | solution.py:116
  50.6 6.4 %collective-permute-start.19 = (bf16[4,128,128]{2,1,0:T(8,128)(2,1)S(1)}, bf16[4,128,128]{2,1,0:T(8,128)(2,1)S(1)}, u32[]{:S(2)}, u32[]{:S(2)}) collective-permute-start(bf16[4,128,128]{2,1,0:T(8,128)(2,1)S(1)} %get-tuple-element.46), channel_id=1, source_target_pairs={{0,2},{2,0},{4,6},{6,4},{8,10},{10,8},{12,14},{14,12},{16,18},{18,... | collective-permute-start | bytes 393224 | tf_op jit(solution)/shard_map/ppermute | solution.py:116
  51.7 6.4 %collective-permute-start.18 = (bf16[4,128,128]{2,1,0:T(8,128)(2,1)S(1)}, bf16[4,128,128]{2,1,0:T(8,128)(2,1)S(1)}, u32[]{:S(2)}, u32[]{:S(2)}) collective-permute-start(bf16[4,128,128]{2,1,0:T(8,128)(2,1)S(1)} %get-tuple-element.45), channel_id=1, source_target_pairs={{0,4},{2,6},{4,0},{6,2},{8,12},{10,14},{12,8},{14,10},{16,20},{18,... | collective-permute-start | bytes 393224 | tf_op jit(solution)/shard_map/ppermute | solution.py:116
  58.1 6.4 %collective-permute-start.21 = (bf16[8,128,128]{2,1,0:T(8,128)(2,1)S(1)}, bf16[8,128,128]{2,1,0:T(8,128)(2,1)S(1)}, u32[]{:S(2)}, u32[]{:S(2)}) collective-permute-start(bf16[8,128,128]{2,1,0:T(8,128)(2,1)S(1)} %pad_maximum_fusion.refs_0_), channel_id=1, source_target_pairs={{0,2},{2,0},{4,6},{6,4},{8,10},{10,8},{12,14},{14,12},{16,18},{18,... | collective-permute-start | bytes 786440 | tf_op jit(solution)/shard_map/ppermute | solution.py:116
  59.1 6.4 %collective-permute-start.22 = (bf16[8,128,128]{2,1,0:T(8,128)(2,1)S(1)}, bf16[8,128,128]{2,1,0:T(8,128)(2,1)S(1)}, u32[]{:S(2)}, u32[]{:S(2)}) collective-permute-start(bf16[8,128,128]{2,1,0:T(8,128)(2,1)S(1)} %pad_maximum_fusion.1.refs_1_), channel_id=1, source_target_pairs={{0,4},{2,6},{4,0},{6,2},{8,12},{10,14},{12,8},{14,10},{16,20},{18,... | collective-permute-start | bytes 786440 | tf_op jit(solution)/shard_map/ppermute | solution.py:116
  60.7 1.3 %collective-permute-start.20 = (bf16[4,128,128]{2,1,0:T(8,128)(2,1)S(1)}, bf16[4,128,128]{2,1,0:T(8,128)(2,1)S(1)}, u32[]{:S(2)}, u32[]{:S(2)}) collective-permute-start(bf16[4,128,128]{2,1,0:T(8,128)(2,1)S(1)} %finish.1.own_ref), channel_id=1, source_target_pairs={{0,1},{1,0},{2,3},{3,2},{4,5},{5,4},{6,7},{7,6},{8,9},{9,8},{10,11... | collective-permute-start | bytes 393224 | tf_op jit(solution)/shard_map/ppermute | solution.py:116
  60.7 5.3 %collective-permute-start.25 = (bf16[8,128,128]{2,1,0:T(8,128)(2,1)S(1)}, bf16[8,128,128]{2,1,0:T(8,128)(2,1)S(1)}, u32[]{:S(2)}, u32[]{:S(2)}) collective-permute-start(bf16[8,128,128]{2,1,0:T(8,128)(2,1)S(1)} %pad_maximum_fusion.refs_0_), channel_id=1, source_target_pairs={{0,1},{1,0},{2,3},{3,2},{4,5},{5,4},{6,7},{7,6},{8,9},{9,8},{10,11... | collective-permute-start | bytes 786440 | tf_op jit(solution)/shard_map/ppermute | solution.py:116
  61.2 4.8 %collective-permute-start.26 = (bf16[8,128,128]{2,1,0:T(8,128)(2,1)S(1)}, bf16[8,128,128]{2,1,0:T(8,128)(2,1)S(1)}, u32[]{:S(2)}, u32[]{:S(2)}) collective-permute-start(bf16[8,128,128]{2,1,0:T(8,128)(2,1)S(1)} %pad_maximum_fusion.1.refs_1_), channel_id=1, source_target_pairs={{0,1},{1,0},{2,3},{3,2},{4,5},{5,4},{6,7},{7,6},{8,9},{9,8},{10,11... | collective-permute-start | bytes 786440 | tf_op jit(solution)/shard_map/ppermute | solution.py:116
  65.5 2.3 %collective-permute-start.23 = (bf16[8,128,128]{2,1,0:T(8,128)(2,1)S(1)}, bf16[8,128,128]{2,1,0:T(8,128)(2,1)S(1)}, u32[]{:S(2)}, u32[]{:S(2)}) collective-permute-start(bf16[8,128,128]{2,1,0:T(8,128)(2,1)S(1)} %collective-permute-done.21.refs_2_), channel_id=1, source_target_pairs={{0,1},{1,0},{2,3},{3,2},{4,5},{5,4},{6,7},{7,6},{8,9},{9,8},{10,11... | collective-permute-start | bytes 786440 | tf_op jit(solution)/shard_map/ppermute | solution.py:116
  65.5 2.3 %collective-permute-start.24 = (bf16[8,128,128]{2,1,0:T(8,128)(2,1)S(1)}, bf16[8,128,128]{2,1,0:T(8,128)(2,1)S(1)}, u32[]{:S(2)}, u32[]{:S(2)}) collective-permute-start(bf16[8,128,128]{2,1,0:T(8,128)(2,1)S(1)} %collective-permute-done.22.refs_3_), channel_id=1, source_target_pairs={{0,1},{1,0},{2,3},{3,2},{4,5},{5,4},{6,7},{7,6},{8,9},{9,8},{10,11... | collective-permute-start | bytes 786440 | tf_op jit(solution)/shard_map/ppermute | solution.py:116

commit v14 on v11

--- a/solution.py
+++ b/solution.py
@@ -112,8 +112,17 @@
 TM = ((0,), (0,))
 
 
+def turned(offset, core):
+    if core == 0:
+        return offset
+    return (offset & ~12) | ((offset & 4) << 1) | ((offset & 8) >> 1)
+
+
 def swap_along(values, axis, size, bit):
-    return lax.ppermute(values, axis, [(i, i ^ bit) for i in range(size)])
+    if axis == "inner":
+        return lax.ppermute(values, axis, [(i, i ^ bit) for i in range(size)])
+    pairs = [(2 * i + c, 2 * (i ^ turned(bit, c)) + c) for i in range(size) for c in range(2)]
+    return lax.ppermute(values, (axis, "inner"), pairs)
 
 
 def dot(left, right, dims):
@@ -189,11 +198,14 @@
     here, core = place_ref[0], place_ref[1]
     offsets = stream_offsets(owners)[1]
     for side in range(2):
-        first_slot = 2 * (core ^ side)
+        at = core ^ side
+        first_slot = 2 * at
         for stream in range(2):
             for p in range(owners):
                 entry = (side * 2 + stream) * owners + p
-                table_ref[entry] = held[(here ^ offsets[stream][p]) * capacity + first_slot + stream]
+                plain = offsets[stream][p]
+                offset = plain + at * (turned(plain, 1) - plain)
+                table_ref[entry] = held[(here ^ offset) * capacity + first_slot + stream]
 
 
 EDGE = 32
@@ -576,7 +588,7 @@
     def per_device(*args):
         capacity = args[-1].shape[1]
         full = args[2].shape[0] == owners * capacity
-        if full and inner == 2 and capacity == 4 and owners >= 8 and owners & (owners - 1) == 0:
+        if full and inner == 2 and capacity == 4 and owners >= 16 and owners & (owners - 1) == 0:
             return per_device_dealt(owners, *args)
         return per_device_plain(*args)
 

time: 68.3 us -> 69.5 us (1.018)
  waiting for transfers between devices: 19.5 us -> 22 us
  starting transfers between devices: 28.2 us -> 27 us
    ppermute x24 -> x7, starting transfers between devices: 28.2 us -> 1.62 us  [swap_along(): return lax.ppermute(values, axis, [(i, i ^ bit) for i in range(size)])]
    ppermute x0 -> x17, starting transfers between devices: none -> 25.4 us  [swap_along(): return lax.ppermute(values, (axis, 'inner'), pairs)]
    ppermute x0 -> x17, waiting for transfers between devices: none -> 21.1 us  [swap_along(): return lax.ppermute(values, (axis, 'inner'), pairs)]
    ppermute x24 -> x7, waiting for transfers between devices: 19.5 us -> 0.85 us  [swap_along(): return lax.ppermute(values, axis, [(i, i ^ bit) for i in range(size)])]
  transfers between devices with their start and end apart: 24 -> 24, of which waited for: 13 -> 12; matrix products, arithmetic and copies ran while one was open for 1% -> 0% of each run, Pallas kernels for 19% -> 18%
where the time goes in v14:
time: 69.5 us; the launch traced here: 69.4 us
  starting transfers between devices  27 us (39%)
  waiting for transfers between devices  22 us (32%)
  Pallas kernels  16.3 us (23%)
  local copies, waits for them, and re-layouts  2.88 us (4%)
  between operations  0.88 us (1%)
    ppermute x17, starting transfers between devices, swap_along(): return lax.ppermute(values, (axis, 'inner'), pairs)  25.4 us
    ppermute x17, waiting for transfers between devices, swap_along(): return lax.ppermute(values, (axis, 'inner'), pairs)  21.1 us
    pallas_call x3, Pallas kernels, on_slots(): pl.pallas_call(kernel, out_shape=tuple(outs), grid_spec=pltpu.PrefetchSca...  3.98 us
    pallas_call x2, Pallas kernels, place_more(): pl.pallas_call(functools.partial(more_kernel, col_tiles, entries), out_sh...  3.25 us
    pallas_call x1, Pallas kernels, sweeping(): pl.pallas_call(kernel, out_shape=jax.ShapeDtypeStruct(values.shape, dtype...  2.9 us
    unnamed x18, local copies, waits for them, and re-layouts  2.85 us
    pallas_call x2, Pallas kernels, tiles_from(): pl.pallas_call(functools.partial(tiles_kernel, owners, first), out_shape=...  2.84 us
    pallas_call x1, Pallas kernels, per_device_dealt(): pl.pallas_call(functools.partial(table_kernel, owners, capacity), out_sha...  1.65 us
  transfers between devices with their start and end apart: 24, of which 12 were waited for; matrix products, arithmetic and copies ran while one was open for 0% of the time, Pallas kernels for 18%

profile of v14, /device:TPU:0, one launch (start us, length us, event | category | flops | bytes accessed | tf_op | source)
XLA Modules:
  0.0 69.4 jit_solution(3339582841932053164)
XLA Ops:
  0.6 0.5 collective-permute-start
  1.1 0.1 collective-permute-start.1
  1.2 0.1 pad_add_fusion.place_ref
  1.3 0.9 %copy-done.7 = bf16[256,512]{1,0:T(8,128)(2,1)S(1)} copy-done((bf16[256,512]{1,0:T(8,128)(2,1)S(1)}, bf16[256,512]{1,0:T(8,128)(2,1)}, u32[]{:S(2)}) %copy-start.7) | copy-done | bytes 262168
  2.3 0.7 copy-done.8
  2.9 1.7 %table.1 = (s32[64]{0:T(128)S(1)}, bf16[512,256]{1,0:T(8,128)(2,1)S(1)}) custom-call(s32[2]{0:T(128)S(1)} %pad_add_fusion.place_ref, s32[64]{0:T(128)S(1)} %copy-done.8, bf16[256,512]{1,0:T(8,128)(2,1)S(1)} %copy-done.7), custom_call_target="tpu_custom_call" | custom-call | bytes 1000000 | tf_op jit(solution)/shard_map/table/pallas_call | solution.py:450
  4.6 0.0 copy-start
  4.6 1.2 %copy-done = bf16[256,2048]{1,0:T(8,128)(2,1)S(1)} copy-done((bf16[256,2048]{1,0:T(8,128)(2,1)S(1)}, bf16[256,2048]{1,0:T(8,128)(2,1)}, u32[]{:S(2)}) %copy-start) | copy-done | bytes 1048600
  5.8 1.4 %tiles.2 = (f32[8,96,128]{2,1,0:T(8,128)S(1)}, f32[8,96,128]{2,1,0:T(8,128)S(1)}, f32[32,32,128]{2,1,0:T(8,128)S(1)}) custom-call(s32[64]{0:T(128)S(1)} %get-tuple-element.30.table_ref, bf16[256,2048]{1,0:T(8,128)(2,1)S(1)} %copy-done, bf16[256,2048]{1,0:T(8,128)(2,1)S(1)} %collective-permute-done.f_sib, bf16[512,256]{1,0:T(8,128)(2,1)S(1)} %get-tuple-element.31.own_rows, ...), custom_call_target="tpu_custom_call" | custom-call | flops 536870912 | bytes 3500000 | tf_op jit(solution)/shard_map/tiles/pallas_call | solution.py:469
  7.2 3.0 %collective-permute-start.2 = (f32[8,96,128]{2,1,0:T(8,128)S(1)}, f32[8,96,128]{2,1,0:T(8,128)S(1)}, u32[]{:S(2)}, u32[]{:S(2)}) collective-permute-start(f32[8,96,128]{2,1,0:T(8,128)S(1)} %get-tuple-element.34), channel_id=1, source_target_pairs={{0,2},{1,3},{2,0},{3,1},{4,6},{5,7},{6,4},{7,5},{8,10},{9,11},{10,... | collective-permute-start | bytes 1179656 | tf_op jit(solution)/shard_map/ppermute | solution.py:125
  10.2 1.5 %collective-permute-start.3 = (f32[8,96,128]{2,1,0:T(8,128)S(1)}, f32[8,96,128]{2,1,0:T(8,128)S(1)}, u32[]{:S(2)}, u32[]{:S(2)}) collective-permute-start(f32[8,96,128]{2,1,0:T(8,128)S(1)} %get-tuple-element.36), channel_id=1, source_target_pairs={{0,4},{1,5},{2,6},{3,7},{4,0},{5,1},{6,2},{7,3},{8,12},{9,13},{10,... | collective-permute-start | bytes 1179656 | tf_op jit(solution)/shard_map/ppermute | solution.py:125
  11.7 1.4 %tiles.3 = (f32[8,96,128]{2,1,0:T(8,128)S(1)}, f32[8,96,128]{2,1,0:T(8,128)S(1)}, f32[16,32,128]{2,1,0:T(8,128)S(1)}, f32[16,32,128]{2,1,0:T(8,128)S(1)}) custom-call(s32[64]{0:T(128)S(1)} %get-tuple-element.30.table_ref, bf16[256,2048]{1,0:T(8,128)(2,1)S(1)} %copy-done, bf16[256,2048]{1,0:T(8,128)(2,1)S(1)} %collective-permute-done.f_sib, ...), custom_call_target="tpu_custom_call" | custom-call | flops 536870912 | bytes 3500000 | tf_op jit(solution)/shard_map/tiles/pallas_call | solution.py:469
  13.2 1.6 %collective-permute-start.7 = (f32[16,32,128]{2,1,0:T(8,128)S(1)}, f32[16,32,128]{2,1,0:T(8,128)S(1)}, u32[]{:S(2)}, u32[]{:S(2)}) collective-permute-start(f32[16,32,128]{2,1,0:T(8,128)S(1)} %get-tuple-element.38), channel_id=1, source_target_pairs={{0,8},{1,17},{2,10},{3,19},{4,12},{5,21},{6,14},{7,23},{8,0},{9,25... | collective-permute-start | bytes 786440 | tf_op jit(solution)/shard_map/ppermute | solution.py:125
  14.8 4.8 %collective-permute-done.2 = f32[8,96,128]{2,1,0:T(8,128)S(1)} collective-permute-done((f32[8,96,128]{2,1,0:T(8,128)S(1)}, f32[8,96,128]{2,1,0:T(8,128)S(1)}, u32[]{:S(2)}, u32[]{:S(2)}) %collective-permute-start.2) | collective-permute-done | bytes 393248 | tf_op jit(solution)/shard_map/ppermute | solution.py:125
  19.6 1.8 %collective-permute-start.4 = (f32[4,96,128]{2,1,0:T(8,128)S(1)}, f32[4,96,128]{2,1,0:T(8,128)S(1)}, u32[]{:S(2)}, u32[]{:S(2)}) collective-permute-start(f32[4,96,128]{2,1,0:T(8,128)S(1)} %get-tuple-element.60), channel_id=1, source_target_pairs={{0,4},{1,5},{2,6},{3,7},{4,0},{5,1},{6,2},{7,3},{8,12},{9,13},{10,... | collective-permute-start | bytes 589832 | tf_op jit(solution)/shard_map/ppermute | solution.py:125
  21.6 1.6 %collective-permute-start.5 = (f32[4,96,128]{2,1,0:T(8,128)S(1)}, f32[4,96,128]{2,1,0:T(8,128)S(1)}, u32[]{:S(2)}, u32[]{:S(2)}) collective-permute-start(f32[4,96,128]{2,1,0:T(8,128)S(1)} %get-tuple-element.62), channel_id=1, source_target_pairs={{0,2},{1,3},{2,0},{3,1},{4,6},{5,7},{6,4},{7,5},{8,10},{9,11},{10,... | collective-permute-start | bytes 589832 | tf_op jit(solution)/shard_map/ppermute | solution.py:125
  23.2 2.7 %collective-permute-start.8 = (f32[8,32,128]{2,1,0:T(8,128)S(1)}, f32[8,32,128]{2,1,0:T(8,128)S(1)}, u32[]{:S(2)}, u32[]{:S(2)}) collective-permute-start(f32[8,32,128]{2,1,0:T(8,128)S(1)} %get-tuple-element.64), channel_id=1, source_target_pairs={{0,16},{1,9},{2,18},{3,11},{4,20},{5,13},{6,22},{7,15},{8,24},{9,1... | collective-permute-start | bytes 393224 | tf_op jit(solution)/shard_map/ppermute | solution.py:125
  25.8 0.2 collective-permute-done.4
  26.1 1.3 %collective-permute-done.5 = f32[4,96,128]{2,1,0:T(8,128)S(1)} collective-permute-done((f32[4,96,128]{2,1,0:T(8,128)S(1)}, f32[4,96,128]{2,1,0:T(8,128)S(1)}, u32[]{:S(2)}, u32[]{:S(2)}) %collective-permute-start.5) | collective-permute-done | bytes 196640 | tf_op jit(solution)/shard_map/ppermute | solution.py:125
  27.4 0.1 fusion.1
  27.4 1.6 %collective-permute-start.6 = (f32[2,2,96,128]{3,2,1,0:T(8,128)S(1)}, f32[2,2,96,128]{3,2,1,0:T(8,128)S(1)}, u32[]{:S(2)}, u32[]{:S(2)}) collective-permute-start(f32[2,2,96,128]{3,2,1,0:T(8,128)S(1)} %get-tuple-element.58), channel_id=1, source_target_pairs={{0,8},{1,17},{2,10},{3,19},{4,12},{5,21},{6,14},{7,23},{8,0},{9,25... | collective-permute-start | bytes 589832 | tf_op jit(solution)/shard_map/ppermute | solution.py:125
  29.1 3.9 %collective-permute-done.8 = f32[8,32,128]{2,1,0:T(8,128)S(1)} collective-permute-done((f32[8,32,128]{2,1,0:T(8,128)S(1)}, f32[8,32,128]{2,1,0:T(8,128)S(1)}, u32[]{:S(2)}, u32[]{:S(2)}) %collective-permute-start.8) | collective-permute-done | bytes 131104 | tf_op jit(solution)/shard_map/ppermute | solution.py:125
  33.0 0.1 collective-permute-start.10
  33.1 2.5 %collective-permute-done.6 = f32[2,2,96,128]{3,2,1,0:T(8,128)S(1)} collective-permute-done((f32[2,2,96,128]{3,2,1,0:T(8,128)S(1)}, f32[2,2,96,128]{3,2,1,0:T(8,128)S(1)}, u32[]{:S(2)}, u32[]{:S(2)}) %collective-permute-start.6) | collective-permute-done | bytes 196640 | tf_op jit(solution)/shard_map/ppermute | solution.py:125
  35.6 2.7 %collective-permute-start.9 = (f32[2,96,128]{2,1,0:T(8,128)S(1)}, f32[2,96,128]{2,1,0:T(8,128)S(1)}, u32[]{:S(2)}, u32[]{:S(2)}) collective-permute-start(f32[2,96,128]{2,1,0:T(8,128)S(1)} %bitcast.17), channel_id=1, source_target_pairs={{0,16},{1,9},{2,18},{3,11},{4,20},{5,13},{6,22},{7,15},{8,24},{9,1... | collective-permute-start | bytes 294920 | tf_op jit(solution)/shard_map/ppermute | solution.py:125
  38.4 0.7 collective-permute-start.11
  39.1 0.5 rotated.1
  39.6 2.8 %collective-permute-done.11.d_ref = f32[2,32,128]{2,1,0:T(8,128)S(1)} collective-permute-done((f32[2,32,128]{2,1,0:T(8,128)S(1)}, f32[2,32,128]{2,1,0:T(8,128)S(1)}, u32[]{:S(2)}, u32[]{:S(2)}) %collective-permute-start.11) | collective-permute-done | bytes 32800 | tf_op jit(solution)/shard_map/ppermute | solution.py:125
  42.4 0.7 %direction.1 = (bf16[2,128,128]{2,1,0:T(8,128)(2,1)S(1)}, f32[2,128,128]{2,1,0:T(8,128)S(1)}) custom-call(s32[1]{0:T(128)} %bitcast.1.side_ref, f32[2,96,128]{2,1,0:T(8,128)S(1)} %get-tuple-element.66.a_ref, f32[2,96,128]{2,1,0:T(8,128)S(1)} %collective-permute-done.9.b_ref, f32[2,32,128]{2,1,0:T(8,128)S(1)} %get-tuple-element.70.c_ref, ...), custom_call_target="tpu_custom_call" | custom-call | flops 67108864 | bytes 800000 | tf_op jit(solution)/shard_map/direction/pallas_call | solution.py:303
  43.1 3.7 %collective-permute-start.14 = (bf16[2,128,128]{2,1,0:T(8,128)(2,1)S(1)}, bf16[2,128,128]{2,1,0:T(8,128)(2,1)S(1)}, u32[]{:S(2)}, u32[]{:S(2)}) collective-permute-start(bf16[2,128,128]{2,1,0:T(8,128)(2,1)S(1)} %get-tuple-element.42), channel_id=1, source_target_pairs={{0,24},{1,25},{2,26},{3,27},{4,28},{5,29},{6,30},{7,31},{8,16},{9,... | collective-permute-start | bytes 196616 | tf_op jit(solution)/shard_map/ppermute | solution.py:125
  46.8 0.7 %collective-permute-start.12 = (bf16[2,128,128]{2,1,0:T(8,128)(2,1)S(1)}, bf16[2,128,128]{2,1,0:T(8,128)(2,1)S(1)}, u32[]{:S(2)}, u32[]{:S(2)}) collective-permute-start(bf16[2,128,128]{2,1,0:T(8,128)(2,1)S(1)} %get-tuple-element.42), channel_id=1, source_target_pairs={{0,16},{1,9},{2,18},{3,11},{4,20},{5,13},{6,22},{7,15},{8,24},{9,1... | collective-permute-start | bytes 196616 | tf_op jit(solution)/shard_map/ppermute | solution.py:125
  47.5 2.8 %refresh.1.iter_ref = f32[4,128,128]{2,1,0:T(8,128)S(1)} custom-call(s32[1]{0:T(128)} %bitcast.1.side_ref, f32[2,128,128]{2,1,0:T(8,128)S(1)} %get-tuple-element.43.g_ref, f32[4,128,128]{2,1,0:T(8,128)S(1)} %get-tuple-element.44.power_ref, bf16[1,4,128,128]{3,2,1,0:T(8,128)(2,1)S(1)} %copy-done.1, bf16[1,4,128,128]{3,2,1,0:T(8,128)(2,1)S(1)} %copy-done.2), custom_call_target="tpu_custom_call" | custom-call | flops 939524096 | bytes 800000 | tf_op jit(solution)/shard_map/refresh/pallas_call | solution.py:303
  50.3 0.7 %collective-permute-done.13 = bf16[2,128,128]{2,1,0:T(8,128)(2,1)S(1)} collective-permute-done((bf16[2,128,128]{2,1,0:T(8,128)(2,1)S(1)}, bf16[2,128,128]{2,1,0:T(8,128)(2,1)S(1)}, u32[]{:S(2)}, u32[]{:S(2)}) %collective-permute-start.13) | collective-permute-done | bytes 65568 | tf_op jit(solution)/shard_map/ppermute | solution.py:125
  51.1 0.9 %collective-permute-done.12 = bf16[2,128,128]{2,1,0:T(8,128)(2,1)S(1)} collective-permute-done((bf16[2,128,128]{2,1,0:T(8,128)(2,1)S(1)}, bf16[2,128,128]{2,1,0:T(8,128)(2,1)S(1)}, u32[]{:S(2)}, u32[]{:S(2)}) %collective-permute-start.12) | collective-permute-done | bytes 65568 | tf_op jit(solution)/shard_map/ppermute | solution.py:125
  52.0 0.8 %collective-permute-start.15 = (bf16[4,128,128]{2,1,0:T(8,128)(2,1)S(1)}, bf16[4,128,128]{2,1,0:T(8,128)(2,1)S(1)}, u32[]{:S(2)}, u32[]{:S(2)}) collective-permute-start(bf16[4,128,128]{2,1,0:T(8,128)(2,1)S(1)} %get-tuple-element.45), channel_id=1, source_target_pairs={{0,4},{1,5},{2,6},{3,7},{4,0},{5,1},{6,2},{7,3},{8,12},{9,13},{10,... | collective-permute-start | bytes 393224 | tf_op jit(solution)/shard_map/ppermute | solution.py:125
  52.8 1.0 %collective-permute-start.16 = (bf16[4,128,128]{2,1,0:T(8,128)(2,1)S(1)}, bf16[4,128,128]{2,1,0:T(8,128)(2,1)S(1)}, u32[]{:S(2)}, u32[]{:S(2)}) collective-permute-start(bf16[4,128,128]{2,1,0:T(8,128)(2,1)S(1)} %get-tuple-element.46), channel_id=1, source_target_pairs={{0,2},{1,3},{2,0},{3,1},{4,6},{5,7},{6,4},{7,5},{8,10},{9,11},{10,... | collective-permute-start | bytes 393224 | tf_op jit(solution)/shard_map/ppermute | solution.py:125
  53.9 2.9 %finish.1.own_ref = bf16[4,128,128]{2,1,0:T(8,128)(2,1)S(1)} custom-call(f32[4,128,128]{2,1,0:T(8,128)S(1)} %refresh.1.iter_ref), custom_call_target="tpu_custom_call" | custom-call | flops 939524096 | bytes 400000 | tf_op jit(solution)/shard_map/finish/pallas_call | solution.py:353
  56.8 1.7 %collective-permute-done.15 = bf16[4,128,128]{2,1,0:T(8,128)(2,1)S(1)} collective-permute-done((bf16[4,128,128]{2,1,0:T(8,128)(2,1)S(1)}, bf16[4,128,128]{2,1,0:T(8,128)(2,1)S(1)}, u32[]{:S(2)}, u32[]{:S(2)}) %collective-permute-start.15) | collective-permute-done | bytes 131104 | tf_op jit(solution)/shard_map/ppermute | solution.py:125
  58.5 0.7 collective-permute-start.18
  59.2 1.1 %collective-permute-start.19 = (bf16[8,128,128]{2,1,0:T(8,128)(2,1)S(1)}, bf16[8,128,128]{2,1,0:T(8,128)(2,1)S(1)}, u32[]{:S(2)}, u32[]{:S(2)}) collective-permute-start(bf16[8,128,128]{2,1,0:T(8,128)(2,1)S(1)} %pad_maximum_fusion.1.refs_1_), channel_id=1, source_target_pairs={{0,4},{1,5},{2,6},{3,7},{4,0},{5,1},{6,2},{7,3},{8,12},{9,13},{10,... | collective-permute-start | bytes 786440 | tf_op jit(solution)/shard_map/ppermute | solution.py:125
  60.3 0.5 collective-permute-start.22
  60.8 0.8 %collective-permute-done.17.sib_ref = bf16[4,128,128]{2,1,0:T(8,128)(2,1)S(1)} collective-permute-done((bf16[4,128,128]{2,1,0:T(8,128)(2,1)S(1)}, bf16[4,128,128]{2,1,0:T(8,128)(2,1)S(1)}, u32[]{:S(2)}, u32[]{:S(2)}) %collective-permute-start.17) | collective-permute-done | bytes 131104 | tf_op jit(solution)/shard_map/ppermute | solution.py:123
  61.6 1.6 %begin.1 = (bf16[2048,512]{1,0:T(8,128)(2,1)}, bf16[1,4,128,128]{3,2,1,0:T(8,128)(2,1)}, bf16[1,4,128,128]{3,2,1,0:T(8,128)(2,1)}) custom-call(s32[64]{0:T(128)S(1)} %get-tuple-element.30.table_ref, s32[2]{0:T(128)S(1)} %pad_add_fusion.place_ref, bf16[4,128,128]{2,1,0:T(8,128)(2,1)S(1)} %finish.1.own_ref, ...), custom_call_target="tpu_custom_call" | custom-call | bytes 800000 | tf_op jit(solution)/shard_map/begin/pallas_call | solution.py:558
  63.3 1.7 %collective-permute-done.18.refs_2_ = bf16[8,128,128]{2,1,0:T(8,128)(2,1)S(1)} collective-permute-done((bf16[8,128,128]{2,1,0:T(8,128)(2,1)S(1)}, bf16[8,128,128]{2,1,0:T(8,128)(2,1)S(1)}, u32[]{:S(2)}, u32[]{:S(2)}) %collective-permute-start.18) | collective-permute-done | bytes 262176 | tf_op jit(solution)/shard_map/ppermute | solution.py:125
  65.0 0.6 collective-permute-done.19.refs_3_
  65.6 0.5 collective-permute-start.21
  66.1 1.8 %more.2.refs_2_ = bf16[2048,512]{1,0:T(8,128)(2,1)} custom-call(s32[64]{0:T(128)S(1)} %get-tuple-element.30.table_ref, bf16[8,128,128]{2,1,0:T(8,128)(2,1)S(1)} %collective-permute-done.22.refs_0_, bf16[8,128,128]{2,1,0:T(8,128)(2,1)S(1)} %collective-permute-done.23.refs_1_, ...), custom_call_target="tpu_custom_call", output_to_operand_aliasing={{}: (5, {})} | custom-call | bytes 1000000 | tf_op jit(solution)/shard_map/more/pallas_call | solution.py:405
  67.9 1.5 %more.3 = bf16[2048,512]{1,0:T(8,128)(2,1)} custom-call(s32[64]{0:T(128)S(1)} %get-tuple-element.30.table_ref, bf16[8,128,128]{2,1,0:T(8,128)(2,1)S(1)} %collective-permute-done.20.refs_0_, bf16[8,128,128]{2,1,0:T(8,128)(2,1)S(1)} %collective-permute-done.21.refs_1_, bf16[2048,512]{1,0:T(8,128)(2,1)} %more.2.refs_2_), custom_call_target="tpu_custom_call", output_to_operand_aliasing={{}: (3, {})} | custom-call | bytes 1000000 | tf_op jit(solution)/shard_map/more/pallas_call | solution.py:405
  (43 shorter events, 0.4 us)
Async XLA Ops:
  0.6 4.0 %collective-permute-start = (bf16[256,2048]{1,0:T(8,128)(2,1)}, bf16[256,2048]{1,0:T(8,128)(2,1)S(1)}, u32[]{:S(2)}, u32[]{:S(2)}) collective-permute-start(bf16[256,2048]{1,0:T(8,128)(2,1)} %f_own.3), channel_id=1, source_target_pairs={{0,1},{1,0},{2,3},{3,2},{4,5},{5,4},{6,7},{7,6},{8,9},{9,8},{10,11... | collective-permute-start | bytes 3145736 | tf_op jit(solution)/shard_map/ppermute | solution.py:123
  1.1 3.4 %collective-permute-start.1 = (bf16[256,512]{1,0:T(8,128)(2,1)}, bf16[256,512]{1,0:T(8,128)(2,1)S(1)}, u32[]{:S(2)}, u32[]{:S(2)}) collective-permute-start(bf16[256,512]{1,0:T(8,128)(2,1)} %kv_ref.1), channel_id=1, source_target_pairs={{0,1},{1,0},{2,3},{3,2},{4,5},{5,4},{6,7},{7,6},{8,9},{9,8},{10,11... | collective-permute-start | bytes 786440 | tf_op jit(solution)/shard_map/ppermute | solution.py:123
  1.3 0.9 %copy-start.7 = (bf16[256,512]{1,0:T(8,128)(2,1)S(1)}, bf16[256,512]{1,0:T(8,128)(2,1)}, u32[]{:S(2)}) copy-start(bf16[256,512]{1,0:T(8,128)(2,1)} %kv_ref.1) | copy-start | bytes 786436
  2.3 0.7 copy-start.8
  4.6 1.2 %copy-start = (bf16[256,2048]{1,0:T(8,128)(2,1)S(1)}, bf16[256,2048]{1,0:T(8,128)(2,1)}, u32[]{:S(2)}) copy-start(bf16[256,2048]{1,0:T(8,128)(2,1)} %f_own.3) | copy-start | bytes 3145732
  7.2 12.3 %collective-permute-start.2 = (f32[8,96,128]{2,1,0:T(8,128)S(1)}, f32[8,96,128]{2,1,0:T(8,128)S(1)}, u32[]{:S(2)}, u32[]{:S(2)}) collective-permute-start(f32[8,96,128]{2,1,0:T(8,128)S(1)} %get-tuple-element.34), channel_id=1, source_target_pairs={{0,2},{1,3},{2,0},{3,1},{4,6},{5,7},{6,4},{7,5},{8,10},{9,11},{10,... | collective-permute-start | bytes 1179656 | tf_op jit(solution)/shard_map/ppermute | solution.py:125
  10.2 11.3 %collective-permute-start.3 = (f32[8,96,128]{2,1,0:T(8,128)S(1)}, f32[8,96,128]{2,1,0:T(8,128)S(1)}, u32[]{:S(2)}, u32[]{:S(2)}) collective-permute-start(f32[8,96,128]{2,1,0:T(8,128)S(1)} %get-tuple-element.36), channel_id=1, source_target_pairs={{0,4},{1,5},{2,6},{3,7},{4,0},{5,1},{6,2},{7,3},{8,12},{9,13},{10,... | collective-permute-start | bytes 1179656 | tf_op jit(solution)/shard_map/ppermute | solution.py:125
  13.2 10.0 %collective-permute-start.7 = (f32[16,32,128]{2,1,0:T(8,128)S(1)}, f32[16,32,128]{2,1,0:T(8,128)S(1)}, u32[]{:S(2)}, u32[]{:S(2)}) collective-permute-start(f32[16,32,128]{2,1,0:T(8,128)S(1)} %get-tuple-element.38), channel_id=1, source_target_pairs={{0,8},{1,17},{2,10},{3,19},{4,12},{5,21},{6,14},{7,23},{8,0},{9,25... | collective-permute-start | bytes 786440 | tf_op jit(solution)/shard_map/ppermute | solution.py:125
  19.6 6.4 %collective-permute-start.4 = (f32[4,96,128]{2,1,0:T(8,128)S(1)}, f32[4,96,128]{2,1,0:T(8,128)S(1)}, u32[]{:S(2)}, u32[]{:S(2)}) collective-permute-start(f32[4,96,128]{2,1,0:T(8,128)S(1)} %get-tuple-element.60), channel_id=1, source_target_pairs={{0,4},{1,5},{2,6},{3,7},{4,0},{5,1},{6,2},{7,3},{8,12},{9,13},{10,... | collective-permute-start | bytes 589832 | tf_op jit(solution)/shard_map/ppermute | solution.py:125
  21.5 17.6 %copy-start.1 = (bf16[1,4,128,128]{3,2,1,0:T(8,128)(2,1)S(1)}, bf16[1,4,128,128]{3,2,1,0:T(8,128)(2,1)}, u32[]{:S(2)}) copy-start(bf16[1,4,128,128]{3,2,1,0:T(8,128)(2,1)} %ql_ref.3) | copy-start | bytes 393220
  21.5 17.6 %copy-start.2 = (bf16[1,4,128,128]{3,2,1,0:T(8,128)(2,1)S(1)}, bf16[1,4,128,128]{3,2,1,0:T(8,128)(2,1)}, u32[]{:S(2)}) copy-start(bf16[1,4,128,128]{3,2,1,0:T(8,128)(2,1)} %qr_ref.3) | copy-start | bytes 393220
  21.5 17.6 %copy-start.3 = (f32[1,4,128,128]{3,2,1,0:T(8,128)S(1)}, f32[1,4,128,128]{3,2,1,0:T(8,128)}, u32[]{:S(2)}) copy-start(f32[1,4,128,128]{3,2,1,0:T(8,128)} %m_ref.1) | copy-start | bytes 786436
  21.5 17.6 %copy-start.4 = (f32[1,4,128,128]{3,2,1,0:T(8,128)S(1)}, f32[1,4,128,128]{3,2,1,0:T(8,128)}, u32[]{:S(2)}) copy-start(f32[1,4,128,128]{3,2,1,0:T(8,128)} %v_ref.1) | copy-start | bytes 786436
  21.5 17.6 %copy-start.5 = (f32[1,4,128,128]{3,2,1,0:T(8,128)S(1)}, f32[1,4,128,128]{3,2,1,0:T(8,128)}, u32[]{:S(2)}) copy-start(f32[1,4,128,128]{3,2,1,0:T(8,128)} %l_ref.1) | copy-start | bytes 786436
  21.5 17.6 %copy-start.6 = (f32[1,4,128,128]{3,2,1,0:T(8,128)S(1)}, f32[1,4,128,128]{3,2,1,0:T(8,128)}, u32[]{:S(2)}) copy-start(f32[1,4,128,128]{3,2,1,0:T(8,128)} %r_ref.1) | copy-start | bytes 786436
  21.6 5.8 %collective-permute-start.5 = (f32[4,96,128]{2,1,0:T(8,128)S(1)}, f32[4,96,128]{2,1,0:T(8,128)S(1)}, u32[]{:S(2)}, u32[]{:S(2)}) collective-permute-start(f32[4,96,128]{2,1,0:T(8,128)S(1)} %get-tuple-element.62), channel_id=1, source_target_pairs={{0,2},{1,3},{2,0},{3,1},{4,6},{5,7},{6,4},{7,5},{8,10},{9,11},{10,... | collective-permute-start | bytes 589832 | tf_op jit(solution)/shard_map/ppermute | solution.py:125
  23.2 9.8 %collective-permute-start.8 = (f32[8,32,128]{2,1,0:T(8,128)S(1)}, f32[8,32,128]{2,1,0:T(8,128)S(1)}, u32[]{:S(2)}, u32[]{:S(2)}) collective-permute-start(f32[8,32,128]{2,1,0:T(8,128)S(1)} %get-tuple-element.64), channel_id=1, source_target_pairs={{0,16},{1,9},{2,18},{3,11},{4,20},{5,13},{6,22},{7,15},{8,24},{9,1... | collective-permute-start | bytes 393224 | tf_op jit(solution)/shard_map/ppermute | solution.py:125
  27.4 8.1 %collective-permute-start.6 = (f32[2,2,96,128]{3,2,1,0:T(8,128)S(1)}, f32[2,2,96,128]{3,2,1,0:T(8,128)S(1)}, u32[]{:S(2)}, u32[]{:S(2)}) collective-permute-start(f32[2,2,96,128]{3,2,1,0:T(8,128)S(1)} %get-tuple-element.58), channel_id=1, source_target_pairs={{0,8},{1,17},{2,10},{3,19},{4,12},{5,21},{6,14},{7,23},{8,0},{9,25... | collective-permute-start | bytes 589832 | tf_op jit(solution)/shard_map/ppermute | solution.py:125
  33.0 5.4 %collective-permute-start.10 = (f32[4,32,128]{2,1,0:T(8,128)S(1)}, f32[4,32,128]{2,1,0:T(8,128)S(1)}, u32[]{:S(2)}, u32[]{:S(2)}) collective-permute-start(f32[4,32,128]{2,1,0:T(8,128)S(1)} %get-tuple-element.68), channel_id=1, source_target_pairs={{0,2},{1,3},{2,0},{3,1},{4,6},{5,7},{6,4},{7,5},{8,10},{9,11},{10,... | collective-permute-start | bytes 196616 | tf_op jit(solution)/shard_map/ppermute | solution.py:125
  35.6 6.7 %collective-permute-start.9 = (f32[2,96,128]{2,1,0:T(8,128)S(1)}, f32[2,96,128]{2,1,0:T(8,128)S(1)}, u32[]{:S(2)}, u32[]{:S(2)}) collective-permute-start(f32[2,96,128]{2,1,0:T(8,128)S(1)} %bitcast.17), channel_id=1, source_target_pairs={{0,16},{1,9},{2,18},{3,11},{4,20},{5,13},{6,22},{7,15},{8,24},{9,1... | collective-permute-start | bytes 294920 | tf_op jit(solution)/shard_map/ppermute | solution.py:125
  38.4 4.0 %collective-permute-start.11 = (f32[2,32,128]{2,1,0:T(8,128)S(1)}, f32[2,32,128]{2,1,0:T(8,128)S(1)}, u32[]{:S(2)}, u32[]{:S(2)}) collective-permute-start(f32[2,32,128]{2,1,0:T(8,128)S(1)} %get-tuple-element.69), channel_id=1, source_target_pairs={{0,4},{1,5},{2,6},{3,7},{4,0},{5,1},{6,2},{7,3},{8,12},{9,13},{10,... | collective-permute-start | bytes 98312 | tf_op jit(solution)/shard_map/ppermute | solution.py:125
  43.1 7.2 %collective-permute-start.14 = (bf16[2,128,128]{2,1,0:T(8,128)(2,1)S(1)}, bf16[2,128,128]{2,1,0:T(8,128)(2,1)S(1)}, u32[]{:S(2)}, u32[]{:S(2)}) collective-permute-start(bf16[2,128,128]{2,1,0:T(8,128)(2,1)S(1)} %get-tuple-element.42), channel_id=1, source_target_pairs={{0,24},{1,25},{2,26},{3,27},{4,28},{5,29},{6,30},{7,31},{8,16},{9,... | collective-permute-start | bytes 196616 | tf_op jit(solution)/shard_map/ppermute | solution.py:125
  46.8 4.3 %collective-permute-start.13 = (bf16[2,128,128]{2,1,0:T(8,128)(2,1)S(1)}, bf16[2,128,128]{2,1,0:T(8,128)(2,1)S(1)}, u32[]{:S(2)}, u32[]{:S(2)}) collective-permute-start(bf16[2,128,128]{2,1,0:T(8,128)(2,1)S(1)} %get-tuple-element.42), channel_id=1, source_target_pairs={{0,8},{1,17},{2,10},{3,19},{4,12},{5,21},{6,14},{7,23},{8,0},{9,25... | collective-permute-start | bytes 196616 | tf_op jit(solution)/shard_map/ppermute | solution.py:125
  46.8 5.2 %collective-permute-start.12 = (bf16[2,128,128]{2,1,0:T(8,128)(2,1)S(1)}, bf16[2,128,128]{2,1,0:T(8,128)(2,1)S(1)}, u32[]{:S(2)}, u32[]{:S(2)}) collective-permute-start(bf16[2,128,128]{2,1,0:T(8,128)(2,1)S(1)} %get-tuple-element.42), channel_id=1, source_target_pairs={{0,16},{1,9},{2,18},{3,11},{4,20},{5,13},{6,22},{7,15},{8,24},{9,1... | collective-permute-start | bytes 196616 | tf_op jit(solution)/shard_map/ppermute | solution.py:125
  52.0 6.4 %collective-permute-start.15 = (bf16[4,128,128]{2,1,0:T(8,128)(2,1)S(1)}, bf16[4,128,128]{2,1,0:T(8,128)(2,1)S(1)}, u32[]{:S(2)}, u32[]{:S(2)}) collective-permute-start(bf16[4,128,128]{2,1,0:T(8,128)(2,1)S(1)} %get-tuple-element.45), channel_id=1, source_target_pairs={{0,4},{1,5},{2,6},{3,7},{4,0},{5,1},{6,2},{7,3},{8,12},{9,13},{10,... | collective-permute-start | bytes 393224 | tf_op jit(solution)/shard_map/ppermute | solution.py:125
  52.8 5.7 %collective-permute-start.16 = (bf16[4,128,128]{2,1,0:T(8,128)(2,1)S(1)}, bf16[4,128,128]{2,1,0:T(8,128)(2,1)S(1)}, u32[]{:S(2)}, u32[]{:S(2)}) collective-permute-start(bf16[4,128,128]{2,1,0:T(8,128)(2,1)S(1)} %get-tuple-element.46), channel_id=1, source_target_pairs={{0,2},{1,3},{2,0},{3,1},{4,6},{5,7},{6,4},{7,5},{8,10},{9,11},{10,... | collective-permute-start | bytes 393224 | tf_op jit(solution)/shard_map/ppermute | solution.py:125
  58.5 6.4 %collective-permute-start.18 = (bf16[8,128,128]{2,1,0:T(8,128)(2,1)S(1)}, bf16[8,128,128]{2,1,0:T(8,128)(2,1)S(1)}, u32[]{:S(2)}, u32[]{:S(2)}) collective-permute-start(bf16[8,128,128]{2,1,0:T(8,128)(2,1)S(1)} %pad_maximum_fusion.refs_0_), channel_id=1, source_target_pairs={{0,2},{1,3},{2,0},{3,1},{4,6},{5,7},{6,4},{7,5},{8,10},{9,11},{10,... | collective-permute-start | bytes 786440 | tf_op jit(solution)/shard_map/ppermute | solution.py:125
  59.2 6.4 %collective-permute-start.19 = (bf16[8,128,128]{2,1,0:T(8,128)(2,1)S(1)}, bf16[8,128,128]{2,1,0:T(8,128)(2,1)S(1)}, u32[]{:S(2)}, u32[]{:S(2)}) collective-permute-start(bf16[8,128,128]{2,1,0:T(8,128)(2,1)S(1)} %pad_maximum_fusion.1.refs_1_), channel_id=1, source_target_pairs={{0,4},{1,5},{2,6},{3,7},{4,0},{5,1},{6,2},{7,3},{8,12},{9,13},{10,... | collective-permute-start | bytes 786440 | tf_op jit(solution)/shard_map/ppermute | solution.py:125
  60.3 1.3 %collective-permute-start.17 = (bf16[4,128,128]{2,1,0:T(8,128)(2,1)S(1)}, bf16[4,128,128]{2,1,0:T(8,128)(2,1)S(1)}, u32[]{:S(2)}, u32[]{:S(2)}) collective-permute-start(bf16[4,128,128]{2,1,0:T(8,128)(2,1)S(1)} %finish.1.own_ref), channel_id=1, source_target_pairs={{0,1},{1,0},{2,3},{3,2},{4,5},{5,4},{6,7},{7,6},{8,9},{9,8},{10,11... | collective-permute-start | bytes 393224 | tf_op jit(solution)/shard_map/ppermute | solution.py:123
  60.3 5.8 %collective-permute-start.22 = (bf16[8,128,128]{2,1,0:T(8,128)(2,1)S(1)}, bf16[8,128,128]{2,1,0:T(8,128)(2,1)S(1)}, u32[]{:S(2)}, u32[]{:S(2)}) collective-permute-start(bf16[8,128,128]{2,1,0:T(8,128)(2,1)S(1)} %pad_maximum_fusion.refs_0_), channel_id=1, source_target_pairs={{0,1},{1,0},{2,3},{3,2},{4,5},{5,4},{6,7},{7,6},{8,9},{9,8},{10,11... | collective-permute-start | bytes 786440 | tf_op jit(solution)/shard_map/ppermute | solution.py:123
  60.8 5.3 %collective-permute-start.23 = (bf16[8,128,128]{2,1,0:T(8,128)(2,1)S(1)}, bf16[8,128,128]{2,1,0:T(8,128)(2,1)S(1)}, u32[]{:S(2)}, u32[]{:S(2)}) collective-permute-start(bf16[8,128,128]{2,1,0:T(8,128)(2,1)S(1)} %pad_maximum_fusion.1.refs_1_), channel_id=1, source_target_pairs={{0,1},{1,0},{2,3},{3,2},{4,5},{5,4},{6,7},{7,6},{8,9},{9,8},{10,11... | collective-permute-start | bytes 786440 | tf_op jit(solution)/shard_map/ppermute | solution.py:123
  65.6 2.3 %collective-permute-start.20 = (bf16[8,128,128]{2,1,0:T(8,128)(2,1)S(1)}, bf16[8,128,128]{2,1,0:T(8,128)(2,1)S(1)}, u32[]{:S(2)}, u32[]{:S(2)}) collective-permute-start(bf16[8,128,128]{2,1,0:T(8,128)(2,1)S(1)} %collective-permute-done.18.refs_2_), channel_id=1, source_target_pairs={{0,1},{1,0},{2,3},{3,2},{4,5},{5,4},{6,7},{7,6},{8,9},{9,8},{10,11... | collective-permute-start | bytes 786440 | tf_op jit(solution)/shard_map/ppermute | solution.py:123
  65.6 2.3 %collective-permute-start.21 = (bf16[8,128,128]{2,1,0:T(8,128)(2,1)S(1)}, bf16[8,128,128]{2,1,0:T(8,128)(2,1)S(1)}, u32[]{:S(2)}, u32[]{:S(2)}) collective-permute-start(bf16[8,128,128]{2,1,0:T(8,128)(2,1)S(1)} %collective-permute-done.19.refs_3_), channel_id=1, source_target_pairs={{0,1},{1,0},{2,3},{3,2},{4,5},{5,4},{6,7},{7,6},{8,9},{9,8},{10,11... | collective-permute-start | bytes 786440 | tf_op jit(solution)/shard_map/ppermute | solution.py:123

commit v15 on v11

--- a/solution.py
+++ b/solution.py
@@ -196,7 +196,7 @@
                 table_ref[entry] = held[(here ^ offsets[stream][p]) * capacity + first_slot + stream]
 
 
-EDGE = 32
+EDGE = 40
 
 
 def tiles_kernel(owners, first, table_ref, f_own, f_sib, own_rows, kv_sib, *rest):

time: 68.3 us -> 67.3 us (0.985)
  starting transfers between devices: 28.2 us -> 27.5 us
    ppermute x24, starting transfers between devices: 28.2 us -> 27.5 us  [swap_along(): return lax.ppermute(values, axis, [(i, i ^ bit) for i in range(size)])]
where the time goes in v15:
time: 67.3 us; the launch traced here: 66.9 us
  starting transfers between devices  27.5 us (41%)
  waiting for transfers between devices  19 us (28%)
  Pallas kernels  16.2 us (24%)
  local copies, waits for them, and re-layouts  2.88 us (4%)
  between operations  0.86 us (1%)
    ppermute x24, starting transfers between devices, swap_along(): return lax.ppermute(values, axis, [(i, i ^ bit) for i in range(size)])  27.5 us
    ppermute x24, waiting for transfers between devices, swap_along(): return lax.ppermute(values, axis, [(i, i ^ bit) for i in range(size)])  19 us
    pallas_call x3, Pallas kernels, on_slots(): pl.pallas_call(kernel, out_shape=tuple(outs), grid_spec=pltpu.PrefetchSca...  3.99 us
    pallas_call x2, Pallas kernels, place_more(): pl.pallas_call(functools.partial(more_kernel, col_tiles, entries), out_sh...  3.25 us
    pallas_call x1, Pallas kernels, sweeping(): pl.pallas_call(kernel, out_shape=jax.ShapeDtypeStruct(values.shape, dtype...  2.89 us
    unnamed x18, local copies, waits for them, and re-layouts  2.85 us
    pallas_call x2, Pallas kernels, tiles_from(): pl.pallas_call(functools.partial(tiles_kernel, owners, first), out_shape=...  2.83 us
    pallas_call x1, Pallas kernels, per_device_dealt(): pl.pallas_call(functools.partial(table_kernel, owners, capacity), out_sha...  1.65 us
  transfers between devices with their start and end apart: 24, of which 13 were waited for; matrix products, arithmetic and copies ran while one was open for 1% of the time, Pallas kernels for 19%

profile of v15, /device:TPU:0, one launch (start us, length us, event | category | flops | bytes accessed | tf_op | source)
XLA Modules:
  0.0 66.9 jit_solution(12336655636412889167)
XLA Ops:
  0.6 0.5 collective-permute-start
  1.1 0.1 collective-permute-start.1
  1.2 0.1 pad_add_fusion.place_ref
  1.3 0.9 %copy-done.7 = bf16[256,512]{1,0:T(8,128)(2,1)S(1)} copy-done((bf16[256,512]{1,0:T(8,128)(2,1)S(1)}, bf16[256,512]{1,0:T(8,128)(2,1)}, u32[]{:S(2)}) %copy-start.7) | copy-done | bytes 262168
  2.3 0.7 copy-done.8
  2.9 1.7 %table.1 = (s32[64]{0:T(128)S(1)}, bf16[512,256]{1,0:T(8,128)(2,1)S(1)}) custom-call(s32[2]{0:T(128)S(1)} %pad_add_fusion.place_ref, s32[64]{0:T(128)S(1)} %copy-done.8, bf16[256,512]{1,0:T(8,128)(2,1)S(1)} %copy-done.7), custom_call_target="tpu_custom_call" | custom-call | bytes 1000000 | tf_op jit(solution)/shard_map/table/pallas_call | solution.py:438
  4.6 1.2 %copy-done = bf16[256,2048]{1,0:T(8,128)(2,1)S(1)} copy-done((bf16[256,2048]{1,0:T(8,128)(2,1)S(1)}, bf16[256,2048]{1,0:T(8,128)(2,1)}, u32[]{:S(2)}) %copy-start) | copy-done | bytes 1048600
  5.8 1.4 %tiles.2 = (f32[8,88,128]{2,1,0:T(8,128)S(1)}, f32[8,88,128]{2,1,0:T(8,128)S(1)}, f32[32,40,128]{2,1,0:T(8,128)S(1)}) custom-call(s32[64]{0:T(128)S(1)} %get-tuple-element.30.table_ref, bf16[256,2048]{1,0:T(8,128)(2,1)S(1)} %copy-done, bf16[256,2048]{1,0:T(8,128)(2,1)S(1)} %collective-permute-done.f_sib, bf16[512,256]{1,0:T(8,128)(2,1)S(1)} %get-tuple-element.31.own_rows, ...), custom_call_target="tpu_custom_call" | custom-call | flops 536870912 | bytes 3500000 | tf_op jit(solution)/shard_map/tiles/pallas_call | solution.py:457
  7.2 3.0 %collective-permute-start.2 = (f32[8,88,128]{2,1,0:T(8,128)S(1)}, f32[8,88,128]{2,1,0:T(8,128)S(1)}, u32[]{:S(2)}, u32[]{:S(2)}) collective-permute-start(f32[8,88,128]{2,1,0:T(8,128)S(1)} %get-tuple-element.34), channel_id=1, source_target_pairs={{0,2},{2,0},{4,6},{6,4},{8,10},{10,8},{12,14},{14,12},{16,18},{18,... | collective-permute-start | bytes 1081352 | tf_op jit(solution)/shard_map/ppermute | solution.py:116
  10.2 1.5 %collective-permute-start.3 = (f32[8,88,128]{2,1,0:T(8,128)S(1)}, f32[8,88,128]{2,1,0:T(8,128)S(1)}, u32[]{:S(2)}, u32[]{:S(2)}) collective-permute-start(f32[8,88,128]{2,1,0:T(8,128)S(1)} %get-tuple-element.36), channel_id=1, source_target_pairs={{0,4},{2,6},{4,0},{6,2},{8,12},{10,14},{12,8},{14,10},{16,20},{18,... | collective-permute-start | bytes 1081352 | tf_op jit(solution)/shard_map/ppermute | solution.py:116
  11.7 1.4 %tiles.3 = (f32[8,88,128]{2,1,0:T(8,128)S(1)}, f32[8,88,128]{2,1,0:T(8,128)S(1)}, f32[16,40,128]{2,1,0:T(8,128)S(1)}, f32[16,40,128]{2,1,0:T(8,128)S(1)}) custom-call(s32[64]{0:T(128)S(1)} %get-tuple-element.30.table_ref, bf16[256,2048]{1,0:T(8,128)(2,1)S(1)} %copy-done, bf16[256,2048]{1,0:T(8,128)(2,1)S(1)} %collective-permute-done.f_sib, ...), custom_call_target="tpu_custom_call" | custom-call | flops 536870912 | bytes 3500000 | tf_op jit(solution)/shard_map/tiles/pallas_call | solution.py:457
  13.2 1.6 %collective-permute-start.7 = (f32[16,40,128]{2,1,0:T(8,128)S(1)}, f32[16,40,128]{2,1,0:T(8,128)S(1)}, u32[]{:S(2)}, u32[]{:S(2)}) collective-permute-start(f32[16,40,128]{2,1,0:T(8,128)S(1)} %get-tuple-element.38), channel_id=1, source_target_pairs={{0,8},{2,10},{4,12},{6,14},{8,0},{10,2},{12,4},{14,6},{16,24},{18,... | collective-permute-start | bytes 983048 | tf_op jit(solution)/shard_map/ppermute | solution.py:116
  14.8 4.1 %collective-permute-done.2 = f32[8,88,128]{2,1,0:T(8,128)S(1)} collective-permute-done((f32[8,88,128]{2,1,0:T(8,128)S(1)}, f32[8,88,128]{2,1,0:T(8,128)S(1)}, u32[]{:S(2)}, u32[]{:S(2)}) %collective-permute-start.2) | collective-permute-done | bytes 360480 | tf_op jit(solution)/shard_map/ppermute | solution.py:116
  18.9 1.8 %collective-permute-start.4 = (f32[4,88,128]{2,1,0:T(8,128)S(1)}, f32[4,88,128]{2,1,0:T(8,128)S(1)}, u32[]{:S(2)}, u32[]{:S(2)}) collective-permute-start(f32[4,88,128]{2,1,0:T(8,128)S(1)} %get-tuple-element.60), channel_id=1, source_target_pairs={{0,4},{2,6},{4,0},{6,2},{8,12},{10,14},{12,8},{14,10},{16,20},{18,... | collective-permute-start | bytes 540680 | tf_op jit(solution)/shard_map/ppermute | solution.py:116
  20.8 1.6 %collective-permute-start.5 = (f32[4,88,128]{2,1,0:T(8,128)S(1)}, f32[4,88,128]{2,1,0:T(8,128)S(1)}, u32[]{:S(2)}, u32[]{:S(2)}) collective-permute-start(f32[4,88,128]{2,1,0:T(8,128)S(1)} %get-tuple-element.62), channel_id=1, source_target_pairs={{0,2},{2,0},{4,6},{6,4},{8,10},{10,8},{12,14},{14,12},{16,18},{18,... | collective-permute-start | bytes 540680 | tf_op jit(solution)/shard_map/ppermute | solution.py:116
  22.5 2.6 %collective-permute-start.8 = (f32[8,40,128]{2,1,0:T(8,128)S(1)}, f32[8,40,128]{2,1,0:T(8,128)S(1)}, u32[]{:S(2)}, u32[]{:S(2)}) collective-permute-start(f32[8,40,128]{2,1,0:T(8,128)S(1)} %get-tuple-element.64), channel_id=1, source_target_pairs={{0,16},{2,18},{4,20},{6,22},{8,24},{10,26},{12,28},{14,30},{16,0},... | collective-permute-start | bytes 491528 | tf_op jit(solution)/shard_map/ppermute | solution.py:116
  25.1 1.3 %collective-permute-done.5 = f32[4,88,128]{2,1,0:T(8,128)S(1)} collective-permute-done((f32[4,88,128]{2,1,0:T(8,128)S(1)}, f32[4,88,128]{2,1,0:T(8,128)S(1)}, u32[]{:S(2)}, u32[]{:S(2)}) %collective-permute-start.5) | collective-permute-done | bytes 180256 | tf_op jit(solution)/shard_map/ppermute | solution.py:116
  26.4 0.1 fusion.1
  26.5 1.6 %collective-permute-start.6 = (f32[2,2,88,128]{3,2,1,0:T(8,128)S(1)}, f32[2,2,88,128]{3,2,1,0:T(8,128)S(1)}, u32[]{:S(2)}, u32[]{:S(2)}) collective-permute-start(f32[2,2,88,128]{3,2,1,0:T(8,128)S(1)} %get-tuple-element.58), channel_id=1, source_target_pairs={{0,8},{2,10},{4,12},{6,14},{8,0},{10,2},{12,4},{14,6},{16,24},{18,... | collective-permute-start | bytes 540680 | tf_op jit(solution)/shard_map/ppermute | solution.py:116
  28.1 3.7 %collective-permute-done.8 = f32[8,40,128]{2,1,0:T(8,128)S(1)} collective-permute-done((f32[8,40,128]{2,1,0:T(8,128)S(1)}, f32[8,40,128]{2,1,0:T(8,128)S(1)}, u32[]{:S(2)}, u32[]{:S(2)}) %collective-permute-start.8) | collective-permute-done | bytes 163872 | tf_op jit(solution)/shard_map/ppermute | solution.py:116
  31.8 0.6 collective-permute-start.10
  32.4 1.1 %collective-permute-done.6 = f32[2,2,88,128]{3,2,1,0:T(8,128)S(1)} collective-permute-done((f32[2,2,88,128]{3,2,1,0:T(8,128)S(1)}, f32[2,2,88,128]{3,2,1,0:T(8,128)S(1)}, u32[]{:S(2)}, u32[]{:S(2)}) %collective-permute-start.6) | collective-permute-done | bytes 180256 | tf_op jit(solution)/shard_map/ppermute | solution.py:116
  33.6 2.1 %collective-permute-start.9 = (f32[2,88,128]{2,1,0:T(8,128)S(1)}, f32[2,88,128]{2,1,0:T(8,128)S(1)}, u32[]{:S(2)}, u32[]{:S(2)}) collective-permute-start(f32[2,88,128]{2,1,0:T(8,128)S(1)} %bitcast.17), channel_id=1, source_target_pairs={{0,16},{2,18},{4,20},{6,22},{8,24},{10,26},{12,28},{14,30},{16,0},... | collective-permute-start | bytes 270344 | tf_op jit(solution)/shard_map/ppermute | solution.py:116
  35.7 0.6 collective-permute-done.10
  36.4 0.6 collective-permute-start.11
  37.0 0.5 rotated.1
  37.5 3.0 %collective-permute-done.11.d_ref = f32[2,40,128]{2,1,0:T(8,128)S(1)} collective-permute-done((f32[2,40,128]{2,1,0:T(8,128)S(1)}, f32[2,40,128]{2,1,0:T(8,128)S(1)}, u32[]{:S(2)}, u32[]{:S(2)}) %collective-permute-start.11) | collective-permute-done | bytes 40992 | tf_op jit(solution)/shard_map/ppermute | solution.py:116
  40.4 0.7 %direction.1 = (bf16[2,128,128]{2,1,0:T(8,128)(2,1)S(1)}, f32[2,128,128]{2,1,0:T(8,128)S(1)}) custom-call(s32[1]{0:T(128)} %bitcast.1.side_ref, f32[2,88,128]{2,1,0:T(8,128)S(1)} %get-tuple-element.66.a_ref, f32[2,88,128]{2,1,0:T(8,128)S(1)} %collective-permute-done.9.b_ref, f32[2,40,128]{2,1,0:T(8,128)S(1)} %get-tuple-element.70.c_ref, ...), custom_call_target="tpu_custom_call" | custom-call | flops 67108864 | bytes 800000 | tf_op jit(solution)/shard_map/direction/pallas_call | solution.py:291
  41.2 3.5 %collective-permute-start.14 = (bf16[2,128,128]{2,1,0:T(8,128)(2,1)S(1)}, bf16[2,128,128]{2,1,0:T(8,128)(2,1)S(1)}, u32[]{:S(2)}, u32[]{:S(2)}) collective-permute-start(bf16[2,128,128]{2,1,0:T(8,128)(2,1)S(1)} %get-tuple-element.42), channel_id=1, source_target_pairs={{0,24},{2,26},{4,28},{6,30},{8,16},{10,18},{12,20},{14,22},{16,8},... | collective-permute-start | bytes 196616 | tf_op jit(solution)/shard_map/ppermute | solution.py:116
  44.7 0.9 %collective-permute-start.12 = (bf16[2,128,128]{2,1,0:T(8,128)(2,1)S(1)}, bf16[2,128,128]{2,1,0:T(8,128)(2,1)S(1)}, u32[]{:S(2)}, u32[]{:S(2)}) collective-permute-start(bf16[2,128,128]{2,1,0:T(8,128)(2,1)S(1)} %get-tuple-element.42), channel_id=1, source_target_pairs={{0,16},{2,18},{4,20},{6,22},{8,24},{10,26},{12,28},{14,30},{16,0},... | collective-permute-start | bytes 196616 | tf_op jit(solution)/shard_map/ppermute | solution.py:116
  45.6 2.8 %refresh.1.iter_ref = f32[4,128,128]{2,1,0:T(8,128)S(1)} custom-call(s32[1]{0:T(128)} %bitcast.1.side_ref, f32[2,128,128]{2,1,0:T(8,128)S(1)} %get-tuple-element.43.g_ref, f32[4,128,128]{2,1,0:T(8,128)S(1)} %get-tuple-element.44.power_ref, bf16[1,4,128,128]{3,2,1,0:T(8,128)(2,1)S(1)} %copy-done.1, bf16[1,4,128,128]{3,2,1,0:T(8,128)(2,1)S(1)} %copy-done.2), custom_call_target="tpu_custom_call" | custom-call | flops 939524096 | bytes 800000 | tf_op jit(solution)/shard_map/refresh/pallas_call | solution.py:291
  48.4 0.6 collective-permute-done.13
  49.0 0.9 %collective-permute-done.12 = bf16[2,128,128]{2,1,0:T(8,128)(2,1)S(1)} collective-permute-done((bf16[2,128,128]{2,1,0:T(8,128)(2,1)S(1)}, bf16[2,128,128]{2,1,0:T(8,128)(2,1)S(1)}, u32[]{:S(2)}, u32[]{:S(2)}) %collective-permute-start.12) | collective-permute-done | bytes 65568 | tf_op jit(solution)/shard_map/ppermute | solution.py:116
  49.9 0.6 collective-permute-start.15
  50.5 1.0 %collective-permute-start.16 = (bf16[4,128,128]{2,1,0:T(8,128)(2,1)S(1)}, bf16[4,128,128]{2,1,0:T(8,128)(2,1)S(1)}, u32[]{:S(2)}, u32[]{:S(2)}) collective-permute-start(bf16[4,128,128]{2,1,0:T(8,128)(2,1)S(1)} %get-tuple-element.46), channel_id=1, source_target_pairs={{0,2},{2,0},{4,6},{6,4},{8,10},{10,8},{12,14},{14,12},{16,18},{18,... | collective-permute-start | bytes 393224 | tf_op jit(solution)/shard_map/ppermute | solution.py:116
  51.6 2.9 %finish.1.own_ref = bf16[4,128,128]{2,1,0:T(8,128)(2,1)S(1)} custom-call(f32[4,128,128]{2,1,0:T(8,128)S(1)} %refresh.1.iter_ref), custom_call_target="tpu_custom_call" | custom-call | flops 939524096 | bytes 400000 | tf_op jit(solution)/shard_map/finish/pallas_call | solution.py:341
  54.5 0.5 collective-permute-done.15
  55.0 0.7 %collective-permute-done.16 = bf16[4,128,128]{2,1,0:T(8,128)(2,1)S(1)} collective-permute-done((bf16[4,128,128]{2,1,0:T(8,128)(2,1)S(1)}, bf16[4,128,128]{2,1,0:T(8,128)(2,1)S(1)}, u32[]{:S(2)}, u32[]{:S(2)}) %collective-permute-start.16) | collective-permute-done | bytes 131104 | tf_op jit(solution)/shard_map/ppermute | solution.py:116
  55.7 1.0 %collective-permute-start.18 = (bf16[8,128,128]{2,1,0:T(8,128)(2,1)S(1)}, bf16[8,128,128]{2,1,0:T(8,128)(2,1)S(1)}, u32[]{:S(2)}, u32[]{:S(2)}) collective-permute-start(bf16[8,128,128]{2,1,0:T(8,128)(2,1)S(1)} %pad_maximum_fusion.refs_0_), channel_id=1, source_target_pairs={{0,2},{2,0},{4,6},{6,4},{8,10},{10,8},{12,14},{14,12},{16,18},{18,... | collective-permute-start | bytes 786440 | tf_op jit(solution)/shard_map/ppermute | solution.py:116
  56.7 1.7 %collective-permute-start.19 = (bf16[8,128,128]{2,1,0:T(8,128)(2,1)S(1)}, bf16[8,128,128]{2,1,0:T(8,128)(2,1)S(1)}, u32[]{:S(2)}, u32[]{:S(2)}) collective-permute-start(bf16[8,128,128]{2,1,0:T(8,128)(2,1)S(1)} %pad_maximum_fusion.1.refs_1_), channel_id=1, source_target_pairs={{0,4},{2,6},{4,0},{6,2},{8,12},{10,14},{12,8},{14,10},{16,20},{18,... | collective-permute-start | bytes 786440 | tf_op jit(solution)/shard_map/ppermute | solution.py:116
  58.4 0.5 collective-permute-start.22
  58.9 0.8 %collective-permute-done.17.sib_ref = bf16[4,128,128]{2,1,0:T(8,128)(2,1)S(1)} collective-permute-done((bf16[4,128,128]{2,1,0:T(8,128)(2,1)S(1)}, bf16[4,128,128]{2,1,0:T(8,128)(2,1)S(1)}, u32[]{:S(2)}, u32[]{:S(2)}) %collective-permute-start.17) | collective-permute-done | bytes 131104 | tf_op jit(solution)/shard_map/ppermute | solution.py:116
  59.7 1.6 %begin.1 = (bf16[2048,512]{1,0:T(8,128)(2,1)}, bf16[1,4,128,128]{3,2,1,0:T(8,128)(2,1)}, bf16[1,4,128,128]{3,2,1,0:T(8,128)(2,1)}) custom-call(s32[64]{0:T(128)S(1)} %get-tuple-element.30.table_ref, s32[2]{0:T(128)S(1)} %pad_add_fusion.place_ref, bf16[4,128,128]{2,1,0:T(8,128)(2,1)S(1)} %finish.1.own_ref, ...), custom_call_target="tpu_custom_call" | custom-call | bytes 800000 | tf_op jit(solution)/shard_map/begin/pallas_call | solution.py:546
  61.4 0.8 %collective-permute-done.18.refs_2_ = bf16[8,128,128]{2,1,0:T(8,128)(2,1)S(1)} collective-permute-done((bf16[8,128,128]{2,1,0:T(8,128)(2,1)S(1)}, bf16[8,128,128]{2,1,0:T(8,128)(2,1)S(1)}, u32[]{:S(2)}, u32[]{:S(2)}) %collective-permute-start.18) | collective-permute-done | bytes 262176 | tf_op jit(solution)/shard_map/ppermute | solution.py:116
  62.2 0.9 %collective-permute-done.19.refs_3_ = bf16[8,128,128]{2,1,0:T(8,128)(2,1)S(1)} collective-permute-done((bf16[8,128,128]{2,1,0:T(8,128)(2,1)S(1)}, bf16[8,128,128]{2,1,0:T(8,128)(2,1)S(1)}, u32[]{:S(2)}, u32[]{:S(2)}) %collective-permute-start.19) | collective-permute-done | bytes 262176 | tf_op jit(solution)/shard_map/ppermute | solution.py:116
  63.1 0.5 collective-permute-start.21
  63.6 1.8 %more.2.refs_2_ = bf16[2048,512]{1,0:T(8,128)(2,1)} custom-call(s32[64]{0:T(128)S(1)} %get-tuple-element.30.table_ref, bf16[8,128,128]{2,1,0:T(8,128)(2,1)S(1)} %collective-permute-done.22.refs_0_, bf16[8,128,128]{2,1,0:T(8,128)(2,1)S(1)} %collective-permute-done.23.refs_1_, ...), custom_call_target="tpu_custom_call", output_to_operand_aliasing={{}: (5, {})} | custom-call | bytes 1000000 | tf_op jit(solution)/shard_map/more/pallas_call | solution.py:393
  65.4 1.5 %more.3 = bf16[2048,512]{1,0:T(8,128)(2,1)} custom-call(s32[64]{0:T(128)S(1)} %get-tuple-element.30.table_ref, bf16[8,128,128]{2,1,0:T(8,128)(2,1)S(1)} %collective-permute-done.20.refs_0_, bf16[8,128,128]{2,1,0:T(8,128)(2,1)S(1)} %collective-permute-done.21.refs_1_, bf16[2048,512]{1,0:T(8,128)(2,1)} %more.2.refs_2_), custom_call_target="tpu_custom_call", output_to_operand_aliasing={{}: (3, {})} | custom-call | bytes 1000000 | tf_op jit(solution)/shard_map/more/pallas_call | solution.py:393
  (43 shorter events, 0.4 us)
Async XLA Ops:
  0.6 4.0 %collective-permute-start = (bf16[256,2048]{1,0:T(8,128)(2,1)}, bf16[256,2048]{1,0:T(8,128)(2,1)S(1)}, u32[]{:S(2)}, u32[]{:S(2)}) collective-permute-start(bf16[256,2048]{1,0:T(8,128)(2,1)} %f_own.3), channel_id=1, source_target_pairs={{0,1},{1,0},{2,3},{3,2},{4,5},{5,4},{6,7},{7,6},{8,9},{9,8},{10,11... | collective-permute-start | bytes 3145736 | tf_op jit(solution)/shard_map/ppermute | solution.py:116
  1.1 3.4 %collective-permute-start.1 = (bf16[256,512]{1,0:T(8,128)(2,1)}, bf16[256,512]{1,0:T(8,128)(2,1)S(1)}, u32[]{:S(2)}, u32[]{:S(2)}) collective-permute-start(bf16[256,512]{1,0:T(8,128)(2,1)} %kv_ref.1), channel_id=1, source_target_pairs={{0,1},{1,0},{2,3},{3,2},{4,5},{5,4},{6,7},{7,6},{8,9},{9,8},{10,11... | collective-permute-start | bytes 786440 | tf_op jit(solution)/shard_map/ppermute | solution.py:116
  1.3 0.9 %copy-start.7 = (bf16[256,512]{1,0:T(8,128)(2,1)S(1)}, bf16[256,512]{1,0:T(8,128)(2,1)}, u32[]{:S(2)}) copy-start(bf16[256,512]{1,0:T(8,128)(2,1)} %kv_ref.1) | copy-start | bytes 786436
  2.3 0.7 copy-start.8
  4.6 1.2 %copy-start = (bf16[256,2048]{1,0:T(8,128)(2,1)S(1)}, bf16[256,2048]{1,0:T(8,128)(2,1)}, u32[]{:S(2)}) copy-start(bf16[256,2048]{1,0:T(8,128)(2,1)} %f_own.3) | copy-start | bytes 3145732
  7.2 11.6 %collective-permute-start.2 = (f32[8,88,128]{2,1,0:T(8,128)S(1)}, f32[8,88,128]{2,1,0:T(8,128)S(1)}, u32[]{:S(2)}, u32[]{:S(2)}) collective-permute-start(f32[8,88,128]{2,1,0:T(8,128)S(1)} %get-tuple-element.34), channel_id=1, source_target_pairs={{0,2},{2,0},{4,6},{6,4},{8,10},{10,8},{12,14},{14,12},{16,18},{18,... | collective-permute-start | bytes 1081352 | tf_op jit(solution)/shard_map/ppermute | solution.py:116
  10.2 10.5 %collective-permute-start.3 = (f32[8,88,128]{2,1,0:T(8,128)S(1)}, f32[8,88,128]{2,1,0:T(8,128)S(1)}, u32[]{:S(2)}, u32[]{:S(2)}) collective-permute-start(f32[8,88,128]{2,1,0:T(8,128)S(1)} %get-tuple-element.36), channel_id=1, source_target_pairs={{0,4},{2,6},{4,0},{6,2},{8,12},{10,14},{12,8},{14,10},{16,20},{18,... | collective-permute-start | bytes 1081352 | tf_op jit(solution)/shard_map/ppermute | solution.py:116
  13.2 9.2 %collective-permute-start.7 = (f32[16,40,128]{2,1,0:T(8,128)S(1)}, f32[16,40,128]{2,1,0:T(8,128)S(1)}, u32[]{:S(2)}, u32[]{:S(2)}) collective-permute-start(f32[16,40,128]{2,1,0:T(8,128)S(1)} %get-tuple-element.38), channel_id=1, source_target_pairs={{0,8},{2,10},{4,12},{6,14},{8,0},{10,2},{12,4},{14,6},{16,24},{18,... | collective-permute-start | bytes 983048 | tf_op jit(solution)/shard_map/ppermute | solution.py:116
  18.9 6.2 %collective-permute-start.4 = (f32[4,88,128]{2,1,0:T(8,128)S(1)}, f32[4,88,128]{2,1,0:T(8,128)S(1)}, u32[]{:S(2)}, u32[]{:S(2)}) collective-permute-start(f32[4,88,128]{2,1,0:T(8,128)S(1)} %get-tuple-element.60), channel_id=1, source_target_pairs={{0,4},{2,6},{4,0},{6,2},{8,12},{10,14},{12,8},{14,10},{16,20},{18,... | collective-permute-start | bytes 540680 | tf_op jit(solution)/shard_map/ppermute | solution.py:116
  20.7 16.2 %copy-start.1 = (bf16[1,4,128,128]{3,2,1,0:T(8,128)(2,1)S(1)}, bf16[1,4,128,128]{3,2,1,0:T(8,128)(2,1)}, u32[]{:S(2)}) copy-start(bf16[1,4,128,128]{3,2,1,0:T(8,128)(2,1)} %ql_ref.3) | copy-start | bytes 393220
  20.7 16.2 %copy-start.2 = (bf16[1,4,128,128]{3,2,1,0:T(8,128)(2,1)S(1)}, bf16[1,4,128,128]{3,2,1,0:T(8,128)(2,1)}, u32[]{:S(2)}) copy-start(bf16[1,4,128,128]{3,2,1,0:T(8,128)(2,1)} %qr_ref.3) | copy-start | bytes 393220
  20.8 16.2 %copy-start.3 = (f32[1,4,128,128]{3,2,1,0:T(8,128)S(1)}, f32[1,4,128,128]{3,2,1,0:T(8,128)}, u32[]{:S(2)}) copy-start(f32[1,4,128,128]{3,2,1,0:T(8,128)} %m_ref.1) | copy-start | bytes 786436
  20.8 16.2 %copy-start.4 = (f32[1,4,128,128]{3,2,1,0:T(8,128)S(1)}, f32[1,4,128,128]{3,2,1,0:T(8,128)}, u32[]{:S(2)}) copy-start(f32[1,4,128,128]{3,2,1,0:T(8,128)} %v_ref.1) | copy-start | bytes 786436
  20.8 16.2 %copy-start.5 = (f32[1,4,128,128]{3,2,1,0:T(8,128)S(1)}, f32[1,4,128,128]{3,2,1,0:T(8,128)}, u32[]{:S(2)}) copy-start(f32[1,4,128,128]{3,2,1,0:T(8,128)} %l_ref.1) | copy-start | bytes 786436
  20.8 16.2 %copy-start.6 = (f32[1,4,128,128]{3,2,1,0:T(8,128)S(1)}, f32[1,4,128,128]{3,2,1,0:T(8,128)}, u32[]{:S(2)}) copy-start(f32[1,4,128,128]{3,2,1,0:T(8,128)} %r_ref.1) | copy-start | bytes 786436
  20.8 5.6 %collective-permute-start.5 = (f32[4,88,128]{2,1,0:T(8,128)S(1)}, f32[4,88,128]{2,1,0:T(8,128)S(1)}, u32[]{:S(2)}, u32[]{:S(2)}) collective-permute-start(f32[4,88,128]{2,1,0:T(8,128)S(1)} %get-tuple-element.62), channel_id=1, source_target_pairs={{0,2},{2,0},{4,6},{6,4},{8,10},{10,8},{12,14},{14,12},{16,18},{18,... | collective-permute-start | bytes 540680 | tf_op jit(solution)/shard_map/ppermute | solution.py:116
  22.5 9.4 %collective-permute-start.8 = (f32[8,40,128]{2,1,0:T(8,128)S(1)}, f32[8,40,128]{2,1,0:T(8,128)S(1)}, u32[]{:S(2)}, u32[]{:S(2)}) collective-permute-start(f32[8,40,128]{2,1,0:T(8,128)S(1)} %get-tuple-element.64), channel_id=1, source_target_pairs={{0,16},{2,18},{4,20},{6,22},{8,24},{10,26},{12,28},{14,30},{16,0},... | collective-permute-start | bytes 491528 | tf_op jit(solution)/shard_map/ppermute | solution.py:116
  26.5 7.1 %collective-permute-start.6 = (f32[2,2,88,128]{3,2,1,0:T(8,128)S(1)}, f32[2,2,88,128]{3,2,1,0:T(8,128)S(1)}, u32[]{:S(2)}, u32[]{:S(2)}) collective-permute-start(f32[2,2,88,128]{3,2,1,0:T(8,128)S(1)} %get-tuple-element.58), channel_id=1, source_target_pairs={{0,8},{2,10},{4,12},{6,14},{8,0},{10,2},{12,4},{14,6},{16,24},{18,... | collective-permute-start | bytes 540680 | tf_op jit(solution)/shard_map/ppermute | solution.py:116
  31.8 4.5 %collective-permute-start.10 = (f32[4,40,128]{2,1,0:T(8,128)S(1)}, f32[4,40,128]{2,1,0:T(8,128)S(1)}, u32[]{:S(2)}, u32[]{:S(2)}) collective-permute-start(f32[4,40,128]{2,1,0:T(8,128)S(1)} %get-tuple-element.68), channel_id=1, source_target_pairs={{0,2},{2,0},{4,6},{6,4},{8,10},{10,8},{12,14},{14,12},{16,18},{18,... | collective-permute-start | bytes 245768 | tf_op jit(solution)/shard_map/ppermute | solution.py:116
  33.6 6.8 %collective-permute-start.9 = (f32[2,88,128]{2,1,0:T(8,128)S(1)}, f32[2,88,128]{2,1,0:T(8,128)S(1)}, u32[]{:S(2)}, u32[]{:S(2)}) collective-permute-start(f32[2,88,128]{2,1,0:T(8,128)S(1)} %bitcast.17), channel_id=1, source_target_pairs={{0,16},{2,18},{4,20},{6,22},{8,24},{10,26},{12,28},{14,30},{16,0},... | collective-permute-start | bytes 270344 | tf_op jit(solution)/shard_map/ppermute | solution.py:116
  36.4 4.1 %collective-permute-start.11 = (f32[2,40,128]{2,1,0:T(8,128)S(1)}, f32[2,40,128]{2,1,0:T(8,128)S(1)}, u32[]{:S(2)}, u32[]{:S(2)}) collective-permute-start(f32[2,40,128]{2,1,0:T(8,128)S(1)} %get-tuple-element.69), channel_id=1, source_target_pairs={{0,4},{2,6},{4,0},{6,2},{8,12},{10,14},{12,8},{14,10},{16,20},{18,... | collective-permute-start | bytes 122888 | tf_op jit(solution)/shard_map/ppermute | solution.py:116
  41.2 7.2 %collective-permute-start.14 = (bf16[2,128,128]{2,1,0:T(8,128)(2,1)S(1)}, bf16[2,128,128]{2,1,0:T(8,128)(2,1)S(1)}, u32[]{:S(2)}, u32[]{:S(2)}) collective-permute-start(bf16[2,128,128]{2,1,0:T(8,128)(2,1)S(1)} %get-tuple-element.42), channel_id=1, source_target_pairs={{0,24},{2,26},{4,28},{6,30},{8,16},{10,18},{12,20},{14,22},{16,8},... | collective-permute-start | bytes 196616 | tf_op jit(solution)/shard_map/ppermute | solution.py:116
  44.7 4.3 %collective-permute-start.13 = (bf16[2,128,128]{2,1,0:T(8,128)(2,1)S(1)}, bf16[2,128,128]{2,1,0:T(8,128)(2,1)S(1)}, u32[]{:S(2)}, u32[]{:S(2)}) collective-permute-start(bf16[2,128,128]{2,1,0:T(8,128)(2,1)S(1)} %get-tuple-element.42), channel_id=1, source_target_pairs={{0,8},{2,10},{4,12},{6,14},{8,0},{10,2},{12,4},{14,6},{16,24},{18,... | collective-permute-start | bytes 196616 | tf_op jit(solution)/shard_map/ppermute | solution.py:116
  44.7 5.2 %collective-permute-start.12 = (bf16[2,128,128]{2,1,0:T(8,128)(2,1)S(1)}, bf16[2,128,128]{2,1,0:T(8,128)(2,1)S(1)}, u32[]{:S(2)}, u32[]{:S(2)}) collective-permute-start(bf16[2,128,128]{2,1,0:T(8,128)(2,1)S(1)} %get-tuple-element.42), channel_id=1, source_target_pairs={{0,16},{2,18},{4,20},{6,22},{8,24},{10,26},{12,28},{14,30},{16,0},... | collective-permute-start | bytes 196616 | tf_op jit(solution)/shard_map/ppermute | solution.py:116
  49.9 5.0 %collective-permute-start.15 = (bf16[4,128,128]{2,1,0:T(8,128)(2,1)S(1)}, bf16[4,128,128]{2,1,0:T(8,128)(2,1)S(1)}, u32[]{:S(2)}, u32[]{:S(2)}) collective-permute-start(bf16[4,128,128]{2,1,0:T(8,128)(2,1)S(1)} %get-tuple-element.45), channel_id=1, source_target_pairs={{0,4},{2,6},{4,0},{6,2},{8,12},{10,14},{12,8},{14,10},{16,20},{18,... | collective-permute-start | bytes 393224 | tf_op jit(solution)/shard_map/ppermute | solution.py:116
  50.5 5.1 %collective-permute-start.16 = (bf16[4,128,128]{2,1,0:T(8,128)(2,1)S(1)}, bf16[4,128,128]{2,1,0:T(8,128)(2,1)S(1)}, u32[]{:S(2)}, u32[]{:S(2)}) collective-permute-start(bf16[4,128,128]{2,1,0:T(8,128)(2,1)S(1)} %get-tuple-element.46), channel_id=1, source_target_pairs={{0,2},{2,0},{4,6},{6,4},{8,10},{10,8},{12,14},{14,12},{16,18},{18,... | collective-permute-start | bytes 393224 | tf_op jit(solution)/shard_map/ppermute | solution.py:116
  55.7 6.4 %collective-permute-start.18 = (bf16[8,128,128]{2,1,0:T(8,128)(2,1)S(1)}, bf16[8,128,128]{2,1,0:T(8,128)(2,1)S(1)}, u32[]{:S(2)}, u32[]{:S(2)}) collective-permute-start(bf16[8,128,128]{2,1,0:T(8,128)(2,1)S(1)} %pad_maximum_fusion.refs_0_), channel_id=1, source_target_pairs={{0,2},{2,0},{4,6},{6,4},{8,10},{10,8},{12,14},{14,12},{16,18},{18,... | collective-permute-start | bytes 786440 | tf_op jit(solution)/shard_map/ppermute | solution.py:116
  56.7 6.4 %collective-permute-start.19 = (bf16[8,128,128]{2,1,0:T(8,128)(2,1)S(1)}, bf16[8,128,128]{2,1,0:T(8,128)(2,1)S(1)}, u32[]{:S(2)}, u32[]{:S(2)}) collective-permute-start(bf16[8,128,128]{2,1,0:T(8,128)(2,1)S(1)} %pad_maximum_fusion.1.refs_1_), channel_id=1, source_target_pairs={{0,4},{2,6},{4,0},{6,2},{8,12},{10,14},{12,8},{14,10},{16,20},{18,... | collective-permute-start | bytes 786440 | tf_op jit(solution)/shard_map/ppermute | solution.py:116
  58.4 1.3 %collective-permute-start.17 = (bf16[4,128,128]{2,1,0:T(8,128)(2,1)S(1)}, bf16[4,128,128]{2,1,0:T(8,128)(2,1)S(1)}, u32[]{:S(2)}, u32[]{:S(2)}) collective-permute-start(bf16[4,128,128]{2,1,0:T(8,128)(2,1)S(1)} %finish.1.own_ref), channel_id=1, source_target_pairs={{0,1},{1,0},{2,3},{3,2},{4,5},{5,4},{6,7},{7,6},{8,9},{9,8},{10,11... | collective-permute-start | bytes 393224 | tf_op jit(solution)/shard_map/ppermute | solution.py:116
  58.4 5.2 %collective-permute-start.22 = (bf16[8,128,128]{2,1,0:T(8,128)(2,1)S(1)}, bf16[8,128,128]{2,1,0:T(8,128)(2,1)S(1)}, u32[]{:S(2)}, u32[]{:S(2)}) collective-permute-start(bf16[8,128,128]{2,1,0:T(8,128)(2,1)S(1)} %pad_maximum_fusion.refs_0_), channel_id=1, source_target_pairs={{0,1},{1,0},{2,3},{3,2},{4,5},{5,4},{6,7},{7,6},{8,9},{9,8},{10,11... | collective-permute-start | bytes 786440 | tf_op jit(solution)/shard_map/ppermute | solution.py:116
  58.9 4.7 %collective-permute-start.23 = (bf16[8,128,128]{2,1,0:T(8,128)(2,1)S(1)}, bf16[8,128,128]{2,1,0:T(8,128)(2,1)S(1)}, u32[]{:S(2)}, u32[]{:S(2)}) collective-permute-start(bf16[8,128,128]{2,1,0:T(8,128)(2,1)S(1)} %pad_maximum_fusion.1.refs_1_), channel_id=1, source_target_pairs={{0,1},{1,0},{2,3},{3,2},{4,5},{5,4},{6,7},{7,6},{8,9},{9,8},{10,11... | collective-permute-start | bytes 786440 | tf_op jit(solution)/shard_map/ppermute | solution.py:116
  63.1 2.3 %collective-permute-start.20 = (bf16[8,128,128]{2,1,0:T(8,128)(2,1)S(1)}, bf16[8,128,128]{2,1,0:T(8,128)(2,1)S(1)}, u32[]{:S(2)}, u32[]{:S(2)}) collective-permute-start(bf16[8,128,128]{2,1,0:T(8,128)(2,1)S(1)} %collective-permute-done.18.refs_2_), channel_id=1, source_target_pairs={{0,1},{1,0},{2,3},{3,2},{4,5},{5,4},{6,7},{7,6},{8,9},{9,8},{10,11... | collective-permute-start | bytes 786440 | tf_op jit(solution)/shard_map/ppermute | solution.py:116
  63.1 2.3 %collective-permute-start.21 = (bf16[8,128,128]{2,1,0:T(8,128)(2,1)S(1)}, bf16[8,128,128]{2,1,0:T(8,128)(2,1)S(1)}, u32[]{:S(2)}, u32[]{:S(2)}) collective-permute-start(bf16[8,128,128]{2,1,0:T(8,128)(2,1)S(1)} %collective-permute-done.19.refs_3_), channel_id=1, source_target_pairs={{0,1},{1,0},{2,3},{3,2},{4,5},{5,4},{6,7},{7,6},{8,9},{9,8},{10,11... | collective-permute-start | bytes 786440 | tf_op jit(solution)/shard_map/ppermute | solution.py:116

commit v16 on v15

--- a/solution.py
+++ b/solution.py
@@ -196,7 +196,7 @@
                 table_ref[entry] = held[(here ^ offsets[stream][p]) * capacity + first_slot + stream]
 
 
-EDGE = 40
+EDGE = 48
 
 
 def tiles_kernel(owners, first, table_ref, f_own, f_sib, own_rows, kv_sib, *rest):

time: 67.3 us -> 70.4 us (1.046)
  waiting for transfers between devices: 19 us -> 25.7 us
  starting transfers between devices: 27.5 us -> 24.2 us
    ppermute x24, waiting for transfers between devices: 19 us -> 25.7 us  [swap_along(): return lax.ppermute(values, axis, [(i, i ^ bit) for i in range(size)])]
    ppermute x24, starting transfers between devices: 27.5 us -> 24.2 us  [swap_along(): return lax.ppermute(values, axis, [(i, i ^ bit) for i in range(size)])]
  transfers between devices with their start and end apart: 24 -> 24, of which waited for: 13 -> 13; matrix products, arithmetic and copies ran while one was open for 1% -> 0% of each run, Pallas kernels for 19% -> 18%
where the time goes in v16:
time: 70.4 us; the launch traced here: 70.3 us
  waiting for transfers between devices  25.7 us (37%)
  starting transfers between devices  24.2 us (34%)
  Pallas kernels  16.2 us (23%)
  local copies, waits for them, and re-layouts  2.88 us (4%)
  between operations  0.86 us (1%)
    ppermute x24, waiting for transfers between devices, swap_along(): return lax.ppermute(values, axis, [(i, i ^ bit) for i in range(size)])  25.7 us
    ppermute x24, starting transfers between devices, swap_along(): return lax.ppermute(values, axis, [(i, i ^ bit) for i in range(size)])  24.2 us
    pallas_call x3, Pallas kernels, on_slots(): pl.pallas_call(kernel, out_shape=tuple(outs), grid_spec=pltpu.PrefetchSca...  3.99 us
    pallas_call x2, Pallas kernels, place_more(): pl.pallas_call(functools.partial(more_kernel, col_tiles, entries), out_sh...  3.25 us
    pallas_call x1, Pallas kernels, sweeping(): pl.pallas_call(kernel, out_shape=jax.ShapeDtypeStruct(values.shape, dtype...  2.89 us
    unnamed x18, local copies, waits for them, and re-layouts  2.85 us
    pallas_call x2, Pallas kernels, tiles_from(): pl.pallas_call(functools.partial(tiles_kernel, owners, first), out_shape=...  2.84 us
    pallas_call x1, Pallas kernels, per_device_dealt(): pl.pallas_call(functools.partial(table_kernel, owners, capacity), out_sha...  1.65 us
  transfers between devices with their start and end apart: 24, of which 13 were waited for; matrix products, arithmetic and copies ran while one was open for 0% of the time, Pallas kernels for 18%

profile of v16, /device:TPU:0, one launch (start us, length us, event | category | flops | bytes accessed | tf_op | source)
XLA Modules:
  0.0 70.3 jit_solution(14886298914604593744)
XLA Ops:
  0.6 0.5 collective-permute-start
  1.1 0.1 collective-permute-start.1
  1.2 0.1 pad_add_fusion.place_ref
  1.3 0.9 %copy-done.7 = bf16[256,512]{1,0:T(8,128)(2,1)S(1)} copy-done((bf16[256,512]{1,0:T(8,128)(2,1)S(1)}, bf16[256,512]{1,0:T(8,128)(2,1)}, u32[]{:S(2)}) %copy-start.7) | copy-done | bytes 262168
  2.3 0.7 copy-done.8
  2.9 1.7 %table.1 = (s32[64]{0:T(128)S(1)}, bf16[512,256]{1,0:T(8,128)(2,1)S(1)}) custom-call(s32[2]{0:T(128)S(1)} %pad_add_fusion.place_ref, s32[64]{0:T(128)S(1)} %copy-done.8, bf16[256,512]{1,0:T(8,128)(2,1)S(1)} %copy-done.7), custom_call_target="tpu_custom_call" | custom-call | bytes 1000000 | tf_op jit(solution)/shard_map/table/pallas_call | solution.py:438
  4.6 1.2 %copy-done = bf16[256,2048]{1,0:T(8,128)(2,1)S(1)} copy-done((bf16[256,2048]{1,0:T(8,128)(2,1)S(1)}, bf16[256,2048]{1,0:T(8,128)(2,1)}, u32[]{:S(2)}) %copy-start) | copy-done | bytes 1048600
  5.8 1.4 %tiles.2 = (f32[8,80,128]{2,1,0:T(8,128)S(1)}, f32[8,80,128]{2,1,0:T(8,128)S(1)}, f32[32,48,128]{2,1,0:T(8,128)S(1)}) custom-call(s32[64]{0:T(128)S(1)} %get-tuple-element.30.table_ref, bf16[256,2048]{1,0:T(8,128)(2,1)S(1)} %copy-done, bf16[256,2048]{1,0:T(8,128)(2,1)S(1)} %collective-permute-done.f_sib, bf16[512,256]{1,0:T(8,128)(2,1)S(1)} %get-tuple-element.31.own_rows, ...), custom_call_target="tpu_custom_call" | custom-call | flops 536870912 | bytes 3500000 | tf_op jit(solution)/shard_map/tiles/pallas_call | solution.py:457
  7.2 3.0 %collective-permute-start.2 = (f32[8,80,128]{2,1,0:T(8,128)S(1)}, f32[8,80,128]{2,1,0:T(8,128)S(1)}, u32[]{:S(2)}, u32[]{:S(2)}) collective-permute-start(f32[8,80,128]{2,1,0:T(8,128)S(1)} %get-tuple-element.34), channel_id=1, source_target_pairs={{0,2},{2,0},{4,6},{6,4},{8,10},{10,8},{12,14},{14,12},{16,18},{18,... | collective-permute-start | bytes 983048 | tf_op jit(solution)/shard_map/ppermute | solution.py:116
  10.2 1.5 %collective-permute-start.3 = (f32[8,80,128]{2,1,0:T(8,128)S(1)}, f32[8,80,128]{2,1,0:T(8,128)S(1)}, u32[]{:S(2)}, u32[]{:S(2)}) collective-permute-start(f32[8,80,128]{2,1,0:T(8,128)S(1)} %get-tuple-element.36), channel_id=1, source_target_pairs={{0,4},{2,6},{4,0},{6,2},{8,12},{10,14},{12,8},{14,10},{16,20},{18,... | collective-permute-start | bytes 983048 | tf_op jit(solution)/shard_map/ppermute | solution.py:116
  11.7 1.4 %tiles.3 = (f32[8,80,128]{2,1,0:T(8,128)S(1)}, f32[8,80,128]{2,1,0:T(8,128)S(1)}, f32[16,48,128]{2,1,0:T(8,128)S(1)}, f32[16,48,128]{2,1,0:T(8,128)S(1)}) custom-call(s32[64]{0:T(128)S(1)} %get-tuple-element.30.table_ref, bf16[256,2048]{1,0:T(8,128)(2,1)S(1)} %copy-done, bf16[256,2048]{1,0:T(8,128)(2,1)S(1)} %collective-permute-done.f_sib, ...), custom_call_target="tpu_custom_call" | custom-call | flops 536870912 | bytes 3500000 | tf_op jit(solution)/shard_map/tiles/pallas_call | solution.py:457
  13.2 1.6 %collective-permute-start.7 = (f32[16,48,128]{2,1,0:T(8,128)S(1)}, f32[16,48,128]{2,1,0:T(8,128)S(1)}, u32[]{:S(2)}, u32[]{:S(2)}) collective-permute-start(f32[16,48,128]{2,1,0:T(8,128)S(1)} %get-tuple-element.38), channel_id=1, source_target_pairs={{0,8},{2,10},{4,12},{6,14},{8,0},{10,2},{12,4},{14,6},{16,24},{18,... | collective-permute-start | bytes 1179656 | tf_op jit(solution)/shard_map/ppermute | solution.py:116
  14.8 3.4 %collective-permute-done.2 = f32[8,80,128]{2,1,0:T(8,128)S(1)} collective-permute-done((f32[8,80,128]{2,1,0:T(8,128)S(1)}, f32[8,80,128]{2,1,0:T(8,128)S(1)}, u32[]{:S(2)}, u32[]{:S(2)}) %collective-permute-start.2) | collective-permute-done | bytes 327712 | tf_op jit(solution)/shard_map/ppermute | solution.py:116
  18.2 1.8 %collective-permute-start.4 = (f32[4,80,128]{2,1,0:T(8,128)S(1)}, f32[4,80,128]{2,1,0:T(8,128)S(1)}, u32[]{:S(2)}, u32[]{:S(2)}) collective-permute-start(f32[4,80,128]{2,1,0:T(8,128)S(1)} %get-tuple-element.62), channel_id=1, source_target_pairs={{0,4},{2,6},{4,0},{6,2},{8,12},{10,14},{12,8},{14,10},{16,20},{18,... | collective-permute-start | bytes 491528 | tf_op jit(solution)/shard_map/ppermute | solution.py:116
  20.1 1.6 %collective-permute-start.5 = (f32[4,80,128]{2,1,0:T(8,128)S(1)}, f32[4,80,128]{2,1,0:T(8,128)S(1)}, u32[]{:S(2)}, u32[]{:S(2)}) collective-permute-start(f32[4,80,128]{2,1,0:T(8,128)S(1)} %get-tuple-element.64), channel_id=1, source_target_pairs={{0,2},{2,0},{4,6},{6,4},{8,10},{10,8},{12,14},{14,12},{16,18},{18,... | collective-permute-start | bytes 491528 | tf_op jit(solution)/shard_map/ppermute | solution.py:116
  21.7 2.1 %collective-permute-done.7 = f32[16,48,128]{2,1,0:T(8,128)S(1)} collective-permute-done((f32[16,48,128]{2,1,0:T(8,128)S(1)}, f32[16,48,128]{2,1,0:T(8,128)S(1)}, u32[]{:S(2)}, u32[]{:S(2)}) %collective-permute-start.7) | collective-permute-done | bytes 393248 | tf_op jit(solution)/shard_map/ppermute | solution.py:116
  23.8 0.1 slice_add_fusion
  23.8 2.7 %collective-permute-start.8 = (f32[8,48,128]{2,1,0:T(8,128)S(1)}, f32[8,48,128]{2,1,0:T(8,128)S(1)}, u32[]{:S(2)}, u32[]{:S(2)}) collective-permute-start(f32[8,48,128]{2,1,0:T(8,128)S(1)} %get-tuple-element.58), channel_id=1, source_target_pairs={{0,16},{2,18},{4,20},{6,22},{8,24},{10,26},{12,28},{14,30},{16,0},... | collective-permute-start | bytes 589832 | tf_op jit(solution)/shard_map/ppermute | solution.py:116
  26.5 1.6 %collective-permute-start.6 = (f32[2,2,80,128]{3,2,1,0:T(8,128)S(1)}, f32[2,2,80,128]{3,2,1,0:T(8,128)S(1)}, u32[]{:S(2)}, u32[]{:S(2)}) collective-permute-start(f32[2,2,80,128]{3,2,1,0:T(8,128)S(1)} %get-tuple-element.60), channel_id=1, source_target_pairs={{0,8},{2,10},{4,12},{6,14},{8,0},{10,2},{12,4},{14,6},{16,24},{18,... | collective-permute-start | bytes 491528 | tf_op jit(solution)/shard_map/ppermute | solution.py:116
  28.2 6.3 %collective-permute-done.8 = f32[8,48,128]{2,1,0:T(8,128)S(1)} collective-permute-done((f32[8,48,128]{2,1,0:T(8,128)S(1)}, f32[8,48,128]{2,1,0:T(8,128)S(1)}, u32[]{:S(2)}, u32[]{:S(2)}) %collective-permute-start.8) | collective-permute-done | bytes 196640 | tf_op jit(solution)/shard_map/ppermute | solution.py:116
  34.5 0.6 collective-permute-start.10
  35.1 0.3 collective-permute-start.9
  35.5 3.7 %collective-permute-done.10 = f32[4,48,128]{2,1,0:T(8,128)S(1)} collective-permute-done((f32[4,48,128]{2,1,0:T(8,128)S(1)}, f32[4,48,128]{2,1,0:T(8,128)S(1)}, u32[]{:S(2)}, u32[]{:S(2)}) %collective-permute-start.10) | collective-permute-done | bytes 98336 | tf_op jit(solution)/shard_map/ppermute | solution.py:116
  39.2 0.6 collective-permute-start.11
  39.8 0.5 rotated.1
  40.3 1.4 %collective-permute-done.9.b_ref = f32[2,80,128]{2,1,0:T(8,128)S(1)} collective-permute-done((f32[2,80,128]{2,1,0:T(8,128)S(1)}, f32[2,80,128]{2,1,0:T(8,128)S(1)}, u32[]{:S(2)}, u32[]{:S(2)}) %collective-permute-start.9) | collective-permute-done | bytes 81952 | tf_op jit(solution)/shard_map/ppermute | solution.py:116
  41.7 1.7 %collective-permute-done.11.d_ref = f32[2,48,128]{2,1,0:T(8,128)S(1)} collective-permute-done((f32[2,48,128]{2,1,0:T(8,128)S(1)}, f32[2,48,128]{2,1,0:T(8,128)S(1)}, u32[]{:S(2)}, u32[]{:S(2)}) %collective-permute-start.11) | collective-permute-done | bytes 49184 | tf_op jit(solution)/shard_map/ppermute | solution.py:116
  43.3 0.7 %direction.1 = (bf16[2,128,128]{2,1,0:T(8,128)(2,1)S(1)}, f32[2,128,128]{2,1,0:T(8,128)S(1)}) custom-call(s32[1]{0:T(128)} %bitcast.1.side_ref, f32[2,80,128]{2,1,0:T(8,128)S(1)} %get-tuple-element.68.a_ref, f32[2,80,128]{2,1,0:T(8,128)S(1)} %collective-permute-done.9.b_ref, f32[2,48,128]{2,1,0:T(8,128)S(1)} %get-tuple-element.70.c_ref, ...), custom_call_target="tpu_custom_call" | custom-call | flops 67108864 | bytes 800000 | tf_op jit(solution)/shard_map/direction/pallas_call | solution.py:291
  44.1 3.6 %collective-permute-start.14 = (bf16[2,128,128]{2,1,0:T(8,128)(2,1)S(1)}, bf16[2,128,128]{2,1,0:T(8,128)(2,1)S(1)}, u32[]{:S(2)}, u32[]{:S(2)}) collective-permute-start(bf16[2,128,128]{2,1,0:T(8,128)(2,1)S(1)} %get-tuple-element.42), channel_id=1, source_target_pairs={{0,24},{2,26},{4,28},{6,30},{8,16},{10,18},{12,20},{14,22},{16,8},... | collective-permute-start | bytes 196616 | tf_op jit(solution)/shard_map/ppermute | solution.py:116
  47.7 0.8 %collective-permute-start.12 = (bf16[2,128,128]{2,1,0:T(8,128)(2,1)S(1)}, bf16[2,128,128]{2,1,0:T(8,128)(2,1)S(1)}, u32[]{:S(2)}, u32[]{:S(2)}) collective-permute-start(bf16[2,128,128]{2,1,0:T(8,128)(2,1)S(1)} %get-tuple-element.42), channel_id=1, source_target_pairs={{0,16},{2,18},{4,20},{6,22},{8,24},{10,26},{12,28},{14,30},{16,0},... | collective-permute-start | bytes 196616 | tf_op jit(solution)/shard_map/ppermute | solution.py:116
  48.5 2.8 %refresh.1.iter_ref = f32[4,128,128]{2,1,0:T(8,128)S(1)} custom-call(s32[1]{0:T(128)} %bitcast.1.side_ref, f32[2,128,128]{2,1,0:T(8,128)S(1)} %get-tuple-element.43.g_ref, f32[4,128,128]{2,1,0:T(8,128)S(1)} %get-tuple-element.44.power_ref, bf16[1,4,128,128]{3,2,1,0:T(8,128)(2,1)S(1)} %copy-done.1, bf16[1,4,128,128]{3,2,1,0:T(8,128)(2,1)S(1)} %copy-done.2), custom_call_target="tpu_custom_call" | custom-call | flops 939524096 | bytes 800000 | tf_op jit(solution)/shard_map/refresh/pallas_call | solution.py:291
  51.3 0.6 collective-permute-done.13
  52.0 0.9 %collective-permute-done.12 = bf16[2,128,128]{2,1,0:T(8,128)(2,1)S(1)} collective-permute-done((bf16[2,128,128]{2,1,0:T(8,128)(2,1)S(1)}, bf16[2,128,128]{2,1,0:T(8,128)(2,1)S(1)}, u32[]{:S(2)}, u32[]{:S(2)}) %collective-permute-start.12) | collective-permute-done | bytes 65568 | tf_op jit(solution)/shard_map/ppermute | solution.py:116
  52.9 0.6 collective-permute-start.15
  53.5 0.5 collective-permute-start.16
  54.0 2.9 %finish.1.own_ref = bf16[4,128,128]{2,1,0:T(8,128)(2,1)S(1)} custom-call(f32[4,128,128]{2,1,0:T(8,128)S(1)} %refresh.1.iter_ref), custom_call_target="tpu_custom_call" | custom-call | flops 939524096 | bytes 400000 | tf_op jit(solution)/shard_map/finish/pallas_call | solution.py:341
  56.9 1.2 %collective-permute-done.15 = bf16[4,128,128]{2,1,0:T(8,128)(2,1)S(1)} collective-permute-done((bf16[4,128,128]{2,1,0:T(8,128)(2,1)S(1)}, bf16[4,128,128]{2,1,0:T(8,128)(2,1)S(1)}, u32[]{:S(2)}, u32[]{:S(2)}) %collective-permute-start.15) | collective-permute-done | bytes 131104 | tf_op jit(solution)/shard_map/ppermute | solution.py:116
  58.1 1.7 %collective-permute-done.16 = bf16[4,128,128]{2,1,0:T(8,128)(2,1)S(1)} collective-permute-done((bf16[4,128,128]{2,1,0:T(8,128)(2,1)S(1)}, bf16[4,128,128]{2,1,0:T(8,128)(2,1)S(1)}, u32[]{:S(2)}, u32[]{:S(2)}) %collective-permute-start.16) | collective-permute-done | bytes 131104 | tf_op jit(solution)/shard_map/ppermute | solution.py:116
  59.9 0.2 collective-permute-start.18
  60.1 1.4 %collective-permute-start.19 = (bf16[8,128,128]{2,1,0:T(8,128)(2,1)S(1)}, bf16[8,128,128]{2,1,0:T(8,128)(2,1)S(1)}, u32[]{:S(2)}, u32[]{:S(2)}) collective-permute-start(bf16[8,128,128]{2,1,0:T(8,128)(2,1)S(1)} %pad_maximum_fusion.1.refs_1_), channel_id=1, source_target_pairs={{0,4},{2,6},{4,0},{6,2},{8,12},{10,14},{12,8},{14,10},{16,20},{18,... | collective-permute-start | bytes 786440 | tf_op jit(solution)/shard_map/ppermute | solution.py:116
  61.6 0.5 collective-permute-start.22
  62.1 0.8 %collective-permute-done.17.sib_ref = bf16[4,128,128]{2,1,0:T(8,128)(2,1)S(1)} collective-permute-done((bf16[4,128,128]{2,1,0:T(8,128)(2,1)S(1)}, bf16[4,128,128]{2,1,0:T(8,128)(2,1)S(1)}, u32[]{:S(2)}, u32[]{:S(2)}) %collective-permute-start.17) | collective-permute-done | bytes 131104 | tf_op jit(solution)/shard_map/ppermute | solution.py:116
  62.9 1.6 %begin.1 = (bf16[2048,512]{1,0:T(8,128)(2,1)}, bf16[1,4,128,128]{3,2,1,0:T(8,128)(2,1)}, bf16[1,4,128,128]{3,2,1,0:T(8,128)(2,1)}) custom-call(s32[64]{0:T(128)S(1)} %get-tuple-element.30.table_ref, s32[2]{0:T(128)S(1)} %pad_add_fusion.place_ref, bf16[4,128,128]{2,1,0:T(8,128)(2,1)S(1)} %finish.1.own_ref, ...), custom_call_target="tpu_custom_call" | custom-call | bytes 800000 | tf_op jit(solution)/shard_map/begin/pallas_call | solution.py:546
  64.5 1.8 %collective-permute-done.18.refs_2_ = bf16[8,128,128]{2,1,0:T(8,128)(2,1)S(1)} collective-permute-done((bf16[8,128,128]{2,1,0:T(8,128)(2,1)S(1)}, bf16[8,128,128]{2,1,0:T(8,128)(2,1)S(1)}, u32[]{:S(2)}, u32[]{:S(2)}) %collective-permute-start.18) | collective-permute-done | bytes 262176 | tf_op jit(solution)/shard_map/ppermute | solution.py:116
  66.3 0.2 collective-permute-done.19.refs_3_
  66.5 0.5 collective-permute-start.21
  67.0 1.8 %more.2.refs_2_ = bf16[2048,512]{1,0:T(8,128)(2,1)} custom-call(s32[64]{0:T(128)S(1)} %get-tuple-element.30.table_ref, bf16[8,128,128]{2,1,0:T(8,128)(2,1)S(1)} %collective-permute-done.22.refs_0_, bf16[8,128,128]{2,1,0:T(8,128)(2,1)S(1)} %collective-permute-done.23.refs_1_, ...), custom_call_target="tpu_custom_call", output_to_operand_aliasing={{}: (5, {})} | custom-call | bytes 1000000 | tf_op jit(solution)/shard_map/more/pallas_call | solution.py:393
  68.8 1.5 %more.3 = bf16[2048,512]{1,0:T(8,128)(2,1)} custom-call(s32[64]{0:T(128)S(1)} %get-tuple-element.30.table_ref, bf16[8,128,128]{2,1,0:T(8,128)(2,1)S(1)} %collective-permute-done.20.refs_0_, bf16[8,128,128]{2,1,0:T(8,128)(2,1)S(1)} %collective-permute-done.21.refs_1_, bf16[2048,512]{1,0:T(8,128)(2,1)} %more.2.refs_2_), custom_call_target="tpu_custom_call", output_to_operand_aliasing={{}: (3, {})} | custom-call | bytes 1000000 | tf_op jit(solution)/shard_map/more/pallas_call | solution.py:393
  (43 shorter events, 0.4 us)
Async XLA Ops:
  0.6 4.0 %collective-permute-start = (bf16[256,2048]{1,0:T(8,128)(2,1)}, bf16[256,2048]{1,0:T(8,128)(2,1)S(1)}, u32[]{:S(2)}, u32[]{:S(2)}) collective-permute-start(bf16[256,2048]{1,0:T(8,128)(2,1)} %f_own.3), channel_id=1, source_target_pairs={{0,1},{1,0},{2,3},{3,2},{4,5},{5,4},{6,7},{7,6},{8,9},{9,8},{10,11... | collective-permute-start | bytes 3145736 | tf_op jit(solution)/shard_map/ppermute | solution.py:116
  1.1 3.4 %collective-permute-start.1 = (bf16[256,512]{1,0:T(8,128)(2,1)}, bf16[256,512]{1,0:T(8,128)(2,1)S(1)}, u32[]{:S(2)}, u32[]{:S(2)}) collective-permute-start(bf16[256,512]{1,0:T(8,128)(2,1)} %kv_ref.1), channel_id=1, source_target_pairs={{0,1},{1,0},{2,3},{3,2},{4,5},{5,4},{6,7},{7,6},{8,9},{9,8},{10,11... | collective-permute-start | bytes 786440 | tf_op jit(solution)/shard_map/ppermute | solution.py:116
  1.3 0.9 %copy-start.7 = (bf16[256,512]{1,0:T(8,128)(2,1)S(1)}, bf16[256,512]{1,0:T(8,128)(2,1)}, u32[]{:S(2)}) copy-start(bf16[256,512]{1,0:T(8,128)(2,1)} %kv_ref.1) | copy-start | bytes 786436
  2.3 0.7 copy-start.8
  4.6 1.2 %copy-start = (bf16[256,2048]{1,0:T(8,128)(2,1)S(1)}, bf16[256,2048]{1,0:T(8,128)(2,1)}, u32[]{:S(2)}) copy-start(bf16[256,2048]{1,0:T(8,128)(2,1)} %f_own.3) | copy-start | bytes 3145732
  7.2 10.9 %collective-permute-start.2 = (f32[8,80,128]{2,1,0:T(8,128)S(1)}, f32[8,80,128]{2,1,0:T(8,128)S(1)}, u32[]{:S(2)}, u32[]{:S(2)}) collective-permute-start(f32[8,80,128]{2,1,0:T(8,128)S(1)} %get-tuple-element.34), channel_id=1, source_target_pairs={{0,2},{2,0},{4,6},{6,4},{8,10},{10,8},{12,14},{14,12},{16,18},{18,... | collective-permute-start | bytes 983048 | tf_op jit(solution)/shard_map/ppermute | solution.py:116
  10.2 9.8 %collective-permute-start.3 = (f32[8,80,128]{2,1,0:T(8,128)S(1)}, f32[8,80,128]{2,1,0:T(8,128)S(1)}, u32[]{:S(2)}, u32[]{:S(2)}) collective-permute-start(f32[8,80,128]{2,1,0:T(8,128)S(1)} %get-tuple-element.36), channel_id=1, source_target_pairs={{0,4},{2,6},{4,0},{6,2},{8,12},{10,14},{12,8},{14,10},{16,20},{18,... | collective-permute-start | bytes 983048 | tf_op jit(solution)/shard_map/ppermute | solution.py:116
  13.2 10.6 %collective-permute-start.7 = (f32[16,48,128]{2,1,0:T(8,128)S(1)}, f32[16,48,128]{2,1,0:T(8,128)S(1)}, u32[]{:S(2)}, u32[]{:S(2)}) collective-permute-start(f32[16,48,128]{2,1,0:T(8,128)S(1)} %get-tuple-element.38), channel_id=1, source_target_pairs={{0,8},{2,10},{4,12},{6,14},{8,0},{10,2},{12,4},{14,6},{16,24},{18,... | collective-permute-start | bytes 1179656 | tf_op jit(solution)/shard_map/ppermute | solution.py:116
  18.2 8.3 %collective-permute-start.4 = (f32[4,80,128]{2,1,0:T(8,128)S(1)}, f32[4,80,128]{2,1,0:T(8,128)S(1)}, u32[]{:S(2)}, u32[]{:S(2)}) collective-permute-start(f32[4,80,128]{2,1,0:T(8,128)S(1)} %get-tuple-element.62), channel_id=1, source_target_pairs={{0,4},{2,6},{4,0},{6,2},{8,12},{10,14},{12,8},{14,10},{16,20},{18,... | collective-permute-start | bytes 491528 | tf_op jit(solution)/shard_map/ppermute | solution.py:116
  20.0 19.7 %copy-start.1 = (bf16[1,4,128,128]{3,2,1,0:T(8,128)(2,1)S(1)}, bf16[1,4,128,128]{3,2,1,0:T(8,128)(2,1)}, u32[]{:S(2)}) copy-start(bf16[1,4,128,128]{3,2,1,0:T(8,128)(2,1)} %ql_ref.3) | copy-start | bytes 393220
  20.1 19.7 %copy-start.2 = (bf16[1,4,128,128]{3,2,1,0:T(8,128)(2,1)S(1)}, bf16[1,4,128,128]{3,2,1,0:T(8,128)(2,1)}, u32[]{:S(2)}) copy-start(bf16[1,4,128,128]{3,2,1,0:T(8,128)(2,1)} %qr_ref.3) | copy-start | bytes 393220
  20.1 19.7 %copy-start.3 = (f32[1,4,128,128]{3,2,1,0:T(8,128)S(1)}, f32[1,4,128,128]{3,2,1,0:T(8,128)}, u32[]{:S(2)}) copy-start(f32[1,4,128,128]{3,2,1,0:T(8,128)} %m_ref.1) | copy-start | bytes 786436
  20.1 19.7 %copy-start.4 = (f32[1,4,128,128]{3,2,1,0:T(8,128)S(1)}, f32[1,4,128,128]{3,2,1,0:T(8,128)}, u32[]{:S(2)}) copy-start(f32[1,4,128,128]{3,2,1,0:T(8,128)} %v_ref.1) | copy-start | bytes 786436
  20.1 19.7 %copy-start.5 = (f32[1,4,128,128]{3,2,1,0:T(8,128)S(1)}, f32[1,4,128,128]{3,2,1,0:T(8,128)}, u32[]{:S(2)}) copy-start(f32[1,4,128,128]{3,2,1,0:T(8,128)} %l_ref.1) | copy-start | bytes 786436
  20.1 19.7 %copy-start.6 = (f32[1,4,128,128]{3,2,1,0:T(8,128)S(1)}, f32[1,4,128,128]{3,2,1,0:T(8,128)}, u32[]{:S(2)}) copy-start(f32[1,4,128,128]{3,2,1,0:T(8,128)} %r_ref.1) | copy-start | bytes 786436
  20.1 6.4 %collective-permute-start.5 = (f32[4,80,128]{2,1,0:T(8,128)S(1)}, f32[4,80,128]{2,1,0:T(8,128)S(1)}, u32[]{:S(2)}, u32[]{:S(2)}) collective-permute-start(f32[4,80,128]{2,1,0:T(8,128)S(1)} %get-tuple-element.64), channel_id=1, source_target_pairs={{0,2},{2,0},{4,6},{6,4},{8,10},{10,8},{12,14},{14,12},{16,18},{18,... | collective-permute-start | bytes 491528 | tf_op jit(solution)/shard_map/ppermute | solution.py:116
  23.8 10.6 %collective-permute-start.8 = (f32[8,48,128]{2,1,0:T(8,128)S(1)}, f32[8,48,128]{2,1,0:T(8,128)S(1)}, u32[]{:S(2)}, u32[]{:S(2)}) collective-permute-start(f32[8,48,128]{2,1,0:T(8,128)S(1)} %get-tuple-element.58), channel_id=1, source_target_pairs={{0,16},{2,18},{4,20},{6,22},{8,24},{10,26},{12,28},{14,30},{16,0},... | collective-permute-start | bytes 589832 | tf_op jit(solution)/shard_map/ppermute | solution.py:116
  26.5 8.6 %collective-permute-start.6 = (f32[2,2,80,128]{3,2,1,0:T(8,128)S(1)}, f32[2,2,80,128]{3,2,1,0:T(8,128)S(1)}, u32[]{:S(2)}, u32[]{:S(2)}) collective-permute-start(f32[2,2,80,128]{3,2,1,0:T(8,128)S(1)} %get-tuple-element.60), channel_id=1, source_target_pairs={{0,8},{2,10},{4,12},{6,14},{8,0},{10,2},{12,4},{14,6},{16,24},{18,... | collective-permute-start | bytes 491528 | tf_op jit(solution)/shard_map/ppermute | solution.py:116
  34.5 4.7 %collective-permute-start.10 = (f32[4,48,128]{2,1,0:T(8,128)S(1)}, f32[4,48,128]{2,1,0:T(8,128)S(1)}, u32[]{:S(2)}, u32[]{:S(2)}) collective-permute-start(f32[4,48,128]{2,1,0:T(8,128)S(1)} %get-tuple-element.66), channel_id=1, source_target_pairs={{0,2},{2,0},{4,6},{6,4},{8,10},{10,8},{12,14},{14,12},{16,18},{18,... | collective-permute-start | bytes 294920 | tf_op jit(solution)/shard_map/ppermute | solution.py:116
  35.1 6.5 %collective-permute-start.9 = (f32[2,80,128]{2,1,0:T(8,128)S(1)}, f32[2,80,128]{2,1,0:T(8,128)S(1)}, u32[]{:S(2)}, u32[]{:S(2)}) collective-permute-start(f32[2,80,128]{2,1,0:T(8,128)S(1)} %bitcast.17), channel_id=1, source_target_pairs={{0,16},{2,18},{4,20},{6,22},{8,24},{10,26},{12,28},{14,30},{16,0},... | collective-permute-start | bytes 245768 | tf_op jit(solution)/shard_map/ppermute | solution.py:116
  39.2 4.2 %collective-permute-start.11 = (f32[2,48,128]{2,1,0:T(8,128)S(1)}, f32[2,48,128]{2,1,0:T(8,128)S(1)}, u32[]{:S(2)}, u32[]{:S(2)}) collective-permute-start(f32[2,48,128]{2,1,0:T(8,128)S(1)} %get-tuple-element.69), channel_id=1, source_target_pairs={{0,4},{2,6},{4,0},{6,2},{8,12},{10,14},{12,8},{14,10},{16,20},{18,... | collective-permute-start | bytes 147464 | tf_op jit(solution)/shard_map/ppermute | solution.py:116
  44.1 7.2 %collective-permute-start.14 = (bf16[2,128,128]{2,1,0:T(8,128)(2,1)S(1)}, bf16[2,128,128]{2,1,0:T(8,128)(2,1)S(1)}, u32[]{:S(2)}, u32[]{:S(2)}) collective-permute-start(bf16[2,128,128]{2,1,0:T(8,128)(2,1)S(1)} %get-tuple-element.42), channel_id=1, source_target_pairs={{0,24},{2,26},{4,28},{6,30},{8,16},{10,18},{12,20},{14,22},{16,8},... | collective-permute-start | bytes 196616 | tf_op jit(solution)/shard_map/ppermute | solution.py:116
  47.7 4.3 %collective-permute-start.13 = (bf16[2,128,128]{2,1,0:T(8,128)(2,1)S(1)}, bf16[2,128,128]{2,1,0:T(8,128)(2,1)S(1)}, u32[]{:S(2)}, u32[]{:S(2)}) collective-permute-start(bf16[2,128,128]{2,1,0:T(8,128)(2,1)S(1)} %get-tuple-element.42), channel_id=1, source_target_pairs={{0,8},{2,10},{4,12},{6,14},{8,0},{10,2},{12,4},{14,6},{16,24},{18,... | collective-permute-start | bytes 196616 | tf_op jit(solution)/shard_map/ppermute | solution.py:116
  47.7 5.2 %collective-permute-start.12 = (bf16[2,128,128]{2,1,0:T(8,128)(2,1)S(1)}, bf16[2,128,128]{2,1,0:T(8,128)(2,1)S(1)}, u32[]{:S(2)}, u32[]{:S(2)}) collective-permute-start(bf16[2,128,128]{2,1,0:T(8,128)(2,1)S(1)} %get-tuple-element.42), channel_id=1, source_target_pairs={{0,16},{2,18},{4,20},{6,22},{8,24},{10,26},{12,28},{14,30},{16,0},... | collective-permute-start | bytes 196616 | tf_op jit(solution)/shard_map/ppermute | solution.py:116
  52.9 5.2 %collective-permute-start.15 = (bf16[4,128,128]{2,1,0:T(8,128)(2,1)S(1)}, bf16[4,128,128]{2,1,0:T(8,128)(2,1)S(1)}, u32[]{:S(2)}, u32[]{:S(2)}) collective-permute-start(bf16[4,128,128]{2,1,0:T(8,128)(2,1)S(1)} %get-tuple-element.45), channel_id=1, source_target_pairs={{0,4},{2,6},{4,0},{6,2},{8,12},{10,14},{12,8},{14,10},{16,20},{18,... | collective-permute-start | bytes 393224 | tf_op jit(solution)/shard_map/ppermute | solution.py:116
  53.5 6.4 %collective-permute-start.16 = (bf16[4,128,128]{2,1,0:T(8,128)(2,1)S(1)}, bf16[4,128,128]{2,1,0:T(8,128)(2,1)S(1)}, u32[]{:S(2)}, u32[]{:S(2)}) collective-permute-start(bf16[4,128,128]{2,1,0:T(8,128)(2,1)S(1)} %get-tuple-element.46), channel_id=1, source_target_pairs={{0,2},{2,0},{4,6},{6,4},{8,10},{10,8},{12,14},{14,12},{16,18},{18,... | collective-permute-start | bytes 393224 | tf_op jit(solution)/shard_map/ppermute | solution.py:116
  59.9 6.4 %collective-permute-start.18 = (bf16[8,128,128]{2,1,0:T(8,128)(2,1)S(1)}, bf16[8,128,128]{2,1,0:T(8,128)(2,1)S(1)}, u32[]{:S(2)}, u32[]{:S(2)}) collective-permute-start(bf16[8,128,128]{2,1,0:T(8,128)(2,1)S(1)} %pad_maximum_fusion.refs_0_), channel_id=1, source_target_pairs={{0,2},{2,0},{4,6},{6,4},{8,10},{10,8},{12,14},{14,12},{16,18},{18,... | collective-permute-start | bytes 786440 | tf_op jit(solution)/shard_map/ppermute | solution.py:116
  60.1 6.4 %collective-permute-start.19 = (bf16[8,128,128]{2,1,0:T(8,128)(2,1)S(1)}, bf16[8,128,128]{2,1,0:T(8,128)(2,1)S(1)}, u32[]{:S(2)}, u32[]{:S(2)}) collective-permute-start(bf16[8,128,128]{2,1,0:T(8,128)(2,1)S(1)} %pad_maximum_fusion.1.refs_1_), channel_id=1, source_target_pairs={{0,4},{2,6},{4,0},{6,2},{8,12},{10,14},{12,8},{14,10},{16,20},{18,... | collective-permute-start | bytes 786440 | tf_op jit(solution)/shard_map/ppermute | solution.py:116
  61.6 1.3 %collective-permute-start.17 = (bf16[4,128,128]{2,1,0:T(8,128)(2,1)S(1)}, bf16[4,128,128]{2,1,0:T(8,128)(2,1)S(1)}, u32[]{:S(2)}, u32[]{:S(2)}) collective-permute-start(bf16[4,128,128]{2,1,0:T(8,128)(2,1)S(1)} %finish.1.own_ref), channel_id=1, source_target_pairs={{0,1},{1,0},{2,3},{3,2},{4,5},{5,4},{6,7},{7,6},{8,9},{9,8},{10,11... | collective-permute-start | bytes 393224 | tf_op jit(solution)/shard_map/ppermute | solution.py:116
  61.6 5.5 %collective-permute-start.22 = (bf16[8,128,128]{2,1,0:T(8,128)(2,1)S(1)}, bf16[8,128,128]{2,1,0:T(8,128)(2,1)S(1)}, u32[]{:S(2)}, u32[]{:S(2)}) collective-permute-start(bf16[8,128,128]{2,1,0:T(8,128)(2,1)S(1)} %pad_maximum_fusion.refs_0_), channel_id=1, source_target_pairs={{0,1},{1,0},{2,3},{3,2},{4,5},{5,4},{6,7},{7,6},{8,9},{9,8},{10,11... | collective-permute-start | bytes 786440 | tf_op jit(solution)/shard_map/ppermute | solution.py:116
  62.1 4.9 %collective-permute-start.23 = (bf16[8,128,128]{2,1,0:T(8,128)(2,1)S(1)}, bf16[8,128,128]{2,1,0:T(8,128)(2,1)S(1)}, u32[]{:S(2)}, u32[]{:S(2)}) collective-permute-start(bf16[8,128,128]{2,1,0:T(8,128)(2,1)S(1)} %pad_maximum_fusion.1.refs_1_), channel_id=1, source_target_pairs={{0,1},{1,0},{2,3},{3,2},{4,5},{5,4},{6,7},{7,6},{8,9},{9,8},{10,11... | collective-permute-start | bytes 786440 | tf_op jit(solution)/shard_map/ppermute | solution.py:116
  66.5 2.3 %collective-permute-start.20 = (bf16[8,128,128]{2,1,0:T(8,128)(2,1)S(1)}, bf16[8,128,128]{2,1,0:T(8,128)(2,1)S(1)}, u32[]{:S(2)}, u32[]{:S(2)}) collective-permute-start(bf16[8,128,128]{2,1,0:T(8,128)(2,1)S(1)} %collective-permute-done.18.refs_2_), channel_id=1, source_target_pairs={{0,1},{1,0},{2,3},{3,2},{4,5},{5,4},{6,7},{7,6},{8,9},{9,8},{10,11... | collective-permute-start | bytes 786440 | tf_op jit(solution)/shard_map/ppermute | solution.py:116
  66.5 2.3 %collective-permute-start.21 = (bf16[8,128,128]{2,1,0:T(8,128)(2,1)S(1)}, bf16[8,128,128]{2,1,0:T(8,128)(2,1)S(1)}, u32[]{:S(2)}, u32[]{:S(2)}) collective-permute-start(bf16[8,128,128]{2,1,0:T(8,128)(2,1)S(1)} %collective-permute-done.19.refs_3_), channel_id=1, source_target_pairs={{0,1},{1,0},{2,3},{3,2},{4,5},{5,4},{6,7},{7,6},{8,9},{9,8},{10,11... | collective-permute-start | bytes 786440 | tf_op jit(solution)/shard_map/ppermute | solution.py:116
